TPU v7x, 32 devices: a whole 2x2x4 slice. The times are simulated.
32 devices in a mesh: depth: 8 (over y, x, core), mode: 4 (over z).
Axes of the slice: x: 2, y: 2, z: 4, core: 2. Of those that a mesh axis runs over, the one named last changes fastest.
Arguments:
- blocks: float32 [128, 2, 128, 128], P(('depth', 'mode')), may hold values from -6 to 6
- live_slots: int32 [128], P(('depth', 'mode')), may hold values from 0 to 1, as said below
- parent_index: int32 [128], P(('depth', 'mode')), may hold values from 0 to 15, as said below
- bath_mode: int32 [128], P(('depth', 'mode')), may hold values from 0 to 7, as said below
- hamiltonian: float32 [128, 128], replicated, may hold values from -0.5 to 0.5
- coupling: float32 [8, 128, 128], P('mode'), may hold values from -0.5 to 0.5
- correlation: float32 [8, 2], P('mode'), may hold values from -1 to 1
- damping: float32 [128], P(('depth', 'mode')), may hold values from 0.01 to 0.1
- link_weight: float32 [128], P(('depth', 'mode')), may hold values from 0.5 to 2
Outputs:
- evolved: float32 [128, 2, 128, 128], P(('depth', 'mode'))
Inputs may be any that keep to these rules, and one draw needn't show every extreme that they name: `live_slots`: on each device the live slots come first and slot 0 is live; every slot of the deepest depth is live in every draw. `parent_index`: for a block of depth d >= 1, m * 4 + s names a live block of depth d - 1, held on index m of mode in slot s; 0 at depth 0. `bath_mode`: A block held on index m of mode links through a bath mode from m * 2 to m * 2 + 1.
All inputs are finite; a program needn't handle non-finite values.
Results may differ from a plain program's by a relative error of at most 0.0001.
Values sent between devices are 32-bit elements; how exact they have to be, the bound alone decides.
No kernel may reach another device: no remote copies, remote signals or barrier semaphores. Data moves between devices by JAX's collectives and lax.ppermute only.
A program may use at most 64 MiB of HBM per device.

v0:
```python
import functools
import math
import jax
import jax.numpy as jnp
from jax import lax
from jax.experimental import pallas as pl
from jax.experimental.pallas import tpu as pltpu
from jax.sharding import PartitionSpec as P

SUBSTEPS = 2
ORDER = 4
substep = 0.7
couple_step = 0.2

AXES = ("depth", "mode")
VMEM = pltpu.VMEM
SMEM = pltpu.SMEM
bf16 = jnp.bfloat16
f32 = jnp.float32

PARENT, MODE, LIVE, FACTOR, WEIGHT, WEIGHT_A, WEIGHT_C = range(7)
ROWS, LANES = 8, 128


def split(value):
    high = value.astype(bf16)
    return high, (value - high.astype(f32)).astype(bf16)


def stack_rows(value):
    high, low = split(value)
    return jnp.concatenate([high, high, low], axis=0)


def stack_cols(value):
    high, low = split(value)
    return jnp.concatenate([high, low, high], axis=1)


def dot(first, second):
    return jnp.dot(first, second, preferred_element_type=f32)


def exact(first, second):
    return jnp.dot(first, second, preferred_element_type=f32, precision=lax.Precision.HIGHEST)


def odd_depth():
    return lax.rem(lax.axis_index("depth"), 2)


def pack_kernel(live_ref, parent_ref, mode_ref, damping_ref, weight_ref, corr_ref, blocks_ref, coupling_ref, out_ref, table_ref):
    slots, modes = blocks_ref.shape[0], coupling_ref.shape[0]
    out_ref[pl.ds(0, 2 * slots)] = blocks_ref[...].reshape(2 * slots, *blocks_ref.shape[2:])
    out_ref[pl.ds(2 * slots + 1, modes)] = coupling_ref[...]
    row = lax.broadcasted_iota(jnp.int32, (ROWS, LANES), 0)
    lane = lax.broadcasted_iota(jnp.int32, (ROWS, LANES), 1)
    table = jnp.zeros((ROWS, LANES), f32)
    first_mode = lax.axis_index("mode") * modes
    for s in range(slots):
        mode = mode_ref[s] - first_mode
        live = live_ref[s].astype(f32)
        weight = weight_ref[s]
        values = {
            PARENT: parent_ref[s].astype(f32),
            MODE: mode.astype(f32),
            LIVE: live,
            FACTOR: damping_ref[s] * (-SUBSTEPS * substep),
            WEIGHT: weight * live,
            WEIGHT_A: weight * corr_ref[mode, 0],
            WEIGHT_C: weight * corr_ref[mode, 1],
        }
        for at, value in values.items():
            table = jnp.where(jnp.logical_and(row == at, lane == s), value, table)
    live_row = table[LIVE : LIVE + 1]
    table = jnp.where(row == FACTOR, live_row * jnp.exp(table), table)
    table_ref[...] = table
    out_ref[2 * slots] = jnp.zeros(out_ref.shape[1:], f32)
    out_ref[2 * slots, :ROWS, :LANES] = table


def powers_kernel(ham_ref, right_ref, left_ref):
    n = ham_ref.shape[0]
    ham = (ham_ref[...] + ham_ref[...].T) * 0.5
    power = ham
    for k in range(1, ORDER + 1):
        if k > 1:
            power = exact(power, ham)
        scaled = power * (substep**k / math.factorial(k))
        right_ref[:, (k - 1) * n : k * n] = stack_rows(scaled)
        left_ref[:, (k - 1) * 3 * n : k * 3 * n] = stack_cols(scaled)


def pull(sources, smem_ref, sem_ref):
    copies = [pltpu.make_async_copy(source, smem_ref.at[i], sem_ref.at[i]) for i, source in enumerate(sources)]
    for copy in copies:
        copy.start()
    for copy in copies:
        copy.wait()


def table_at(ref, slab):
    return ref.at[slab, pl.ds(0, ROWS), pl.ds(0, LANES)]


def operators_kernel(group, modes, skip, parity, own_ref, *refs):
    sources, outs = refs[: -2 - (parity is None)], refs[-2 - (parity is None) :]
    right_ref, left_ref = outs[0], outs[1]

    def fill(value_of):
        for k in range(group):
            for i in range(modes):
                value = own_ref[i] if k == 0 else value_of(k, i)
                sym = (value + value.T) * 0.5
                right_ref[k * modes + i] = stack_rows(sym)
                left_ref[k * modes + i] = stack_cols(sym)
                if parity is None and k:
                    outs[2][(k - 1) * modes + i] = value

    if parity is None:
        fill(lambda k, i: sources[k - 1][skip + i])
    else:
        pl.when(odd_depth() == parity)(lambda: fill(lambda k, i: sources[0][(k - 1) * modes + i]))


def taylor(real, imag, right, left):
    n = real.shape[0]
    out = dot(stack_cols(jnp.concatenate([real, imag], axis=0)), right)
    rp = [out[:n, k * n : (k + 1) * n] for k in range(ORDER)]
    ip = [out[n:, k * n : (k + 1) * n] for k in range(ORDER)]
    u_real, u_imag = real, imag
    stacked = [None] * ORDER
    for k in range(ORDER + 1):
        if k:
            turn = k % 4
            if turn == 1:
                u_real, u_imag = u_real - ip[k - 1], u_imag + rp[k - 1]
            elif turn == 2:
                u_real, u_imag = u_real - rp[k - 1], u_imag - ip[k - 1]
            elif turn == 3:
                u_real, u_imag = u_real + ip[k - 1], u_imag - rp[k - 1]
            else:
                u_real, u_imag = u_real + rp[k - 1], u_imag + ip[k - 1]
        j = ORDER - k
        if j:
            turn = j % 4
            if turn == 1:
                pair = (u_imag, -u_real)
            elif turn == 2:
                pair = (-u_real, -u_imag)
            elif turn == 3:
                pair = (-u_imag, u_real)
            else:
                pair = (u_real, u_imag)
            stacked[j - 1] = stack_rows(jnp.concatenate(pair, axis=1))
    done = dot(left, jnp.concatenate(stacked, axis=0))
    return u_real + done[:, :n], u_imag + done[:, n:]


def free_kernel(run_parity, times, slots, states_ref, right_ref, left_ref, out_ref):
    pair = 2 if slots % 2 == 0 else 1

    @pl.when(odd_depth() == run_parity)
    def _():
        right, left = right_ref[...], left_ref[...]
        out_ref[...] = states_ref[pl.ds(0, 2 * slots)]

        @pl.loop(0, slots // pair)
        def _(step):
            @pl.loop(0, times * SUBSTEPS)
            def _(turn):
                at = [2 * (step * pair + u) for u in range(pair)]
                done = [taylor(out_ref[s], out_ref[s + 1], right, left) for s in at]
                for s, (real, imag) in zip(at, done):
                    out_ref[s] = real
                    out_ref[s + 1] = imag

        factors = states_ref[2 * slots, FACTOR : FACTOR + 1, :LANES]
        for s in range(slots):
            scale = factors[:, s : s + 1] ** times
            out_ref[2 * s] = out_ref[2 * s] * scale
            out_ref[2 * s + 1] = out_ref[2 * s + 1] * scale


def sided(real, imag, right, left):
    n = real.shape[0]
    after = dot(stack_cols(jnp.concatenate([real, imag], axis=0)), right)
    before = dot(left, stack_rows(jnp.concatenate([real, imag], axis=1)))
    return after[:n], after[n:], before[:, :n], before[:, n:]


class Layout:
    def __init__(self, refs, slots, group):
        self.refs, self.slots, self.group = refs, slots, group
        self.held = group // len(refs)
        self.stride = 2 * slots + 1

    def base(self, k):
        return self.refs[k // self.held], (k % self.held) * self.stride

    def table(self, k):
        ref, base = self.base(k)
        return table_at(ref, base + 2 * self.slots)

    def fetch(self, index, stage_ref, at):
        for k in range(self.group):
            ref, base = self.base(k)
            local = index - k * self.slots

            @pl.when(jnp.logical_and(local >= 0, local < self.slots))
            def _():
                stage_ref[pl.ds(at, 2)] = ref[pl.ds(base + 2 * local, 2)]


def entry(tab, row, c, slots):
    if isinstance(c, int):
        return tab[c // slots, row, c % slots]
    return tab[lax.div(c, slots), row, lax.rem(c, slots)]


def operator_of(tab, c, slots, modes):
    back = c // slots if isinstance(c, int) else lax.div(c, slots)
    return back * modes + entry(tab, MODE, c, slots).astype(jnp.int32)


def parent_of(tab, c, slots, group):
    parent = entry(tab, PARENT, c, slots).astype(jnp.int32)
    back = lax.rem(lax.axis_index("mode") - lax.div(parent, slots) + group, group)
    return back * slots + lax.rem(parent, slots)


def child_pair(stage_ref, at, mode, weight, right_ref, left_ref):
    ra, ia, rb, ib = sided(stage_ref[at], stage_ref[at + 1], right_ref[mode], left_ref[mode])
    return weight * (ib - ia), weight * (ra - rb)


def parent_pair(stage_ref, at, mode, wa, wc, right_ref, left_ref):
    ra, ia, rb, ib = sided(stage_ref[at], stage_ref[at + 1], right_ref[mode], left_ref[mode])
    return wa * (ib - ia) + wc * (rb + ra), wa * (ra - rb) + wc * (ib + ia)


def part_of(parts, s):
    size = parts[0].shape[0] // 2
    return parts[s // size], 2 * (s % size)


def send_kernel(sender, slots, group, modes, sum_parts, pick_parts, near_ref, right_ref, left_ref, *refs):
    acc_ref, stage_ref, list_ref, tab, sem_ref = refs[-5:]
    tabs_ref = refs[-6]
    outs = refs[-6 - sum_parts - pick_parts : -6]
    sums, picks = outs[:sum_parts], outs[sum_parts:]
    groups = Layout(refs[: -6 - sum_parts - pick_parts], slots, group)

    @pl.when(odd_depth() == sender)
    def _():
        pull([groups.table(k) for k in range(group)] + [near_ref], tab, sem_ref)
        for k in range(group):
            ref, base = groups.base(k)
            tabs_ref[k] = ref[base + 2 * slots, :ROWS, :LANES]
        acc_ref[...] = jnp.zeros_like(acc_ref)
        for s in range(slots):
            pick, at = part_of(picks, s)
            groups.fetch(parent_of(tab, group * slots + s, slots, group), pick, at)

        def collect(c, count):
            mine = parent_of(tab, c, slots, group) < slots

            @pl.when(mine)
            def _():
                list_ref[count] = c

            return count + mine.astype(jnp.int32)

        count = lax.fori_loop(0, group * slots, collect, jnp.int32(0))

        @pl.loop(0, lax.div(count + slots - 1, slots))
        def _(batch):
            children = []
            for u in range(slots):
                place = batch * slots + u
                c = list_ref[jnp.minimum(place, count - 1)]
                groups.fetch(c, stage_ref, 2 * u)
                children.append((c, jnp.where(place < count, entry(tab, WEIGHT, c, slots), 0.0)))
            terms = [
                child_pair(stage_ref, 2 * u, operator_of(tab, c, slots, modes), weight, right_ref, left_ref)
                for u, (c, weight) in enumerate(children)
            ]
            for (c, _), (real, imag) in zip(children, terms):
                target = 2 * parent_of(tab, c, slots, group)
                acc_ref[target] = acc_ref[target] + real
                acc_ref[target + 1] = acc_ref[target + 1] + imag

        for s in range(slots):
            part, at = part_of(sums, s)
            part[pl.ds(at, 2)] = acc_ref[pl.ds(2 * s, 2)]


def join_kernel(receiver, slots, modes, sum_parts, pick_parts, own_ref, right_ref, left_ref, *refs):
    out_ref, tab, sem_ref = refs[-3:]
    picks = refs[-3 - pick_parts : -3]
    sums = refs[-3 - pick_parts - sum_parts : -3 - pick_parts]
    frees = refs[: -3 - pick_parts - sum_parts]
    final = len(frees) > 1

    def store(at, value):
        if final:
            out_ref[at // 2, at % 2] = value
        else:
            out_ref[at] = value

    @pl.when(odd_depth() == receiver)
    def _():
        pull([own_ref], tab, sem_ref)
        terms = []
        for s in range(slots):
            pick, at = part_of(picks, s)
            wa, wc = tab[0, WEIGHT_A, s], tab[0, WEIGHT_C, s]
            terms.append(parent_pair(pick, at, operator_of(tab, s, slots, modes), wa, wc, right_ref, left_ref))
        for s in range(slots):
            scale = tab[0, LIVE, s] * couple_step
            part, at = part_of(sums, s)
            for i in range(2):
                store(2 * s + i, frees[0][2 * s + i] + scale * (part[at + i] + terms[s][i]))
        if not final:
            out_ref[2 * slots] = jnp.zeros(out_ref.shape[1:], f32)
            out_ref[2 * slots, :ROWS, :LANES] = own_ref[...]

    if final:

        @pl.when(odd_depth() != receiver)
        def _():
            for at in range(2 * slots):
                store(at, frees[1][at])


def side_kernel(side, receiver, slots, group, modes, base_count, group_count, tab_count, right_ref, left_ref, *refs):
    stage_ref, tab, sem_ref = refs[-3:]
    bases = refs[:base_count]
    groups = Layout(refs[base_count : base_count + group_count], slots, group)
    tab_refs = refs[base_count + group_count : base_count + group_count + tab_count]
    outs = refs[base_count + group_count + tab_count : -3]
    second = len(outs) > 2 or base_count == 1
    if second:
        out = Layout(outs, slots, group)

        def at_slot(k):
            return out.base(k)

    else:
        acc_ref, tabs_ref = outs

        def at_slot(k):
            return acc_ref, 2 * slots * k

    own_tables = [tab_refs[0].at[k] for k in range(group)]
    if tab_count > 1:
        gathered = Layout(tab_refs, slots, group)
        own_tables = [gathered.table(k) for k in range(group)]

    @pl.when(odd_depth() == receiver)
    def _():
        below = [groups.table(k) for k in range(group)] if side == "children" else []
        pull(own_tables + below, tab, sem_ref)
        for k in range(group):
            ref, base = at_slot(k)
            if base_count == 1:
                ref[pl.ds(base, 2 * slots)] = bases[0][pl.ds(2 * slots * k, 2 * slots)]
            else:
                ref[pl.ds(base, 2 * slots)] = bases[k][...]
            if second:
                ref[base + 2 * slots] = jnp.zeros(ref.shape[1:], f32)
                ref[base + 2 * slots, :ROWS, :LANES] = tab_refs[0][k]
            elif tab_count > 1:
                source, origin = gathered.base(k)
                tabs_ref[k] = source[origin + 2 * slots, :ROWS, :LANES]

        def add(index, pair):
            for k in range(group):
                ref, base = at_slot(k)
                local = index - k * slots

                @pl.when(jnp.logical_and(local >= 0, local < slots))
                def _():
                    for i in range(2):
                        ref[base + 2 * local + i] = ref[base + 2 * local + i] + pair[i]

        @pl.loop(0, group)
        def _(k):
            at = k * slots
            targets, terms = [], []
            for s in range(slots):
                c = at + s
                if side == "children":
                    groups.fetch(c, stage_ref, 2 * s)
                else:
                    groups.fetch(parent_of(tab, c, slots, group), stage_ref, 2 * s)
            for s in range(slots):
                c = at + s
                if side == "children":
                    b = c + group * slots
                    target = parent_of(tab, b, slots, group)
                    weight = entry(tab, WEIGHT, b, slots) * (entry(tab, LIVE, target, slots) * couple_step)
                    mode = operator_of(tab, b, slots, modes) - group * modes
                    terms.append(child_pair(stage_ref, 2 * s, mode, weight, right_ref, left_ref))
                else:
                    target = c
                    scale = entry(tab, LIVE, c, slots) * couple_step
                    wa, wc = entry(tab, WEIGHT_A, c, slots) * scale, entry(tab, WEIGHT_C, c, slots) * scale
                    mode = operator_of(tab, c, slots, modes)
                    terms.append(parent_pair(stage_ref, 2 * s, mode, wa, wc, right_ref, left_ref))
                targets.append(target)
            for target, pair in zip(targets, terms):
                if second:
                    add(target, pair)
                else:
                    acc_ref[2 * target] = acc_ref[2 * target] + pair[0]
                    acc_ref[2 * target + 1] = acc_ref[2 * target + 1] + pair[1]


def call(kernel, out_shapes, limit, args, smem=0, us=1.0, scratch=()):
    specs = [pl.BlockSpec(memory_space=SMEM)] * smem
    specs += [pl.BlockSpec(memory_space=VMEM)] * (len(args) - smem)
    return pl.pallas_call(
        kernel,
        out_shape=out_shapes,
        in_specs=specs,
        out_specs=jax.tree.map(lambda _: pl.BlockSpec(memory_space=VMEM), out_shapes),
        scratch_shapes=scratch,
        compiler_params=pltpu.CompilerParams(vmem_limit_bytes=limit),
        cost_estimate=pl.CostEstimate(flops=int(us * 1.1e9), bytes_accessed=1 << 19, transcendentals=0),
    )(*args)


def turn_order(group):
    return sorted(range(1, group), key=lambda k: abs(k - group / 2))


def shards(sizes, blocks, live_slots, parent_index, bath_mode, hamiltonian, coupling, correlation, damping, link_weight):
    depths, group = sizes
    slots, _, n, _ = blocks.shape
    modes = coupling.shape[0]
    total = group * slots
    limit = 8 * total * 2 * n * n * 4
    order = turn_order(group)
    split_hop = 2 if slots % 2 == 0 else 1
    ranks = range(group)

    def place(d, m):
        return d * group + m

    def turn(value, k, parity):
        pairs = [(place(d, m), place(d, (m + k) % group)) for d in range(parity, depths, 2) for m in ranks]
        return lax.ppermute(value, AXES, pairs)

    def shift(value, step, parity=None):
        pairs = [
            (place(d, m), place(d + step, m))
            for d in range(depths)
            for m in ranks
            if 0 <= d + step < depths and (parity is None or d % 2 == parity)
        ]
        return lax.ppermute(value, AXES, pairs)

    def slabs(count):
        return jax.ShapeDtypeStruct((count, n, n), f32)

    def sds(*shape, dtype=f32):
        return jax.ShapeDtypeStruct(shape, dtype)

    own, plain = 2 * slots + 1, 2 * slots
    table_shape = sds(ROWS, LANES)
    stage = VMEM((plain, n, n), f32)

    def tables(count):
        return [SMEM((count, ROWS, LANES), f32), pltpu.SemaphoreType.DMA((count,))]

    operator_shapes = (sds(group * modes, 3 * n, n, dtype=bf16), sds(group * modes, n, 3 * n, dtype=bf16))

    packed, own_table = call(
        pack_kernel,
        (slabs(own + modes), table_shape),
        limit,
        (live_slots, parent_index, bath_mode, damping, link_weight, correlation, blocks, coupling),
        smem=6,
    )
    turned = {k: turn(packed, k, 1) for k in order}
    first = [packed] + [turned[k] for k in range(1, group)]
    near_table = shift(own_table, -1)
    powers = call(
        powers_kernel, (sds(3 * n, ORDER * n, dtype=bf16), sds(n, 3 * ORDER * n, dtype=bf16)), limit, (hamiltonian,)
    )
    *operators_odd, raw = call(
        functools.partial(operators_kernel, group, modes, own, None),
        (*operator_shapes, slabs((group - 1) * modes)),
        limit,
        (coupling, *first[1:]),
    )

    def free(states, parity, times):
        return call(
            functools.partial(free_kernel, parity, times, slots), slabs(plain), limit, (states, *powers), us=4.7 * times
        )

    def send(groups, sender, sum_parts, pick_parts, operators):
        shapes = [slabs(plain // sum_parts)] * sum_parts + [slabs(plain // pick_parts)] * pick_parts
        outs = call(
            functools.partial(send_kernel, sender, slots, group, modes, sum_parts, pick_parts),
            [*shapes, sds(group, ROWS, LANES)],
            limit,
            (near_table, *operators, *groups),
            us=2,
            scratch=[stage, stage, SMEM((total,), jnp.int32), *tables(group + 1)],
        )
        return outs[:sum_parts], outs[sum_parts:-1], outs[-1]

    def join(frees, sums, picks, receiver, operators):
        return call(
            functools.partial(join_kernel, receiver, slots, modes, len(sums), len(picks)),
            sds(*blocks.shape) if len(frees) > 1 else slabs(own),
            limit,
            (own_table, *operators, *frees, *sums, *picks),
            scratch=tables(1),
        )

    def side(kind, bases, groups, tabs, receiver, operators):
        second = len(bases) == 1
        halves = 2 if group % 2 == 0 else 1
        return call(
            functools.partial(side_kernel, kind, receiver, slots, group, modes, len(bases), len(groups), len(tabs)),
            [slabs(group * own // halves)] * halves if second else [slabs(2 * total), sds(group, ROWS, LANES)],
            limit,
            (*operators, *bases, *groups, *tabs),
            us=3,
            scratch=[stage, *tables(2 * group if kind == "children" else group)],
        )

    free_even = free(packed, 0, 1)
    free_odd = [free(first[k], 1, 2) for k in ranks]
    sums, picks, tabs_odd = send(first, 1, 1, split_hop, operators_odd)
    picks = [shift(value, 1, 1) for value in picks]
    sums = [shift(value, -1, 1) for value in sums]
    own_state = join([free_even], sums, picks, 0, operators_odd)

    turned = {k: turn(own_state, k, 0) for k in order}
    gathered = [own_state] + [turned[k] for k in range(1, group)]
    from_below = [shift(value, -1, 0) for value in gathered]
    from_above = [shift(value, 1, 0) for value in gathered]
    free_even = [free(gathered[k], 0, 2) for k in ranks]
    passed = shift(raw, -1, 1)
    operators_even = call(
        functools.partial(operators_kernel, group, modes, own, 0), operator_shapes, limit, (coupling, passed)
    )
    states, _ = side("parents", free_odd, from_above, [tabs_odd], 1, operators_odd)
    states = side("children", [states], from_below, [tabs_odd], 1, operators_odd)

    from_above = [shift(value, 1, 1) for value in states]
    from_below = [shift(value, -1, 1) for value in states]
    last_odd = free(states[0], 1, 2)
    states, tabs_even = side("children", free_even, from_below, gathered, 0, operators_even)
    states = side("parents", [states], from_above, [tabs_even], 0, operators_even)

    sums, picks, _ = send(states, 0, split_hop, 1, operators_even)
    sums = [shift(value, -1, 0) for value in sums]
    picks = [shift(value, 1, 0) for value in picks]
    last_even = free(states[0], 0, 1)
    return join([last_odd, last_even], sums, picks, 1, operators_odd)


def solution(mesh):
    sizes = (mesh.shape["depth"], mesh.shape["mode"])

    def whole(*args):
        return shards(sizes, *args)

    return jax.shard_map(
        whole,
        mesh=mesh,
        in_specs=(
            P(("depth", "mode"), None, None, None),
            P(("depth", "mode")),
            P(("depth", "mode")),
            P(("depth", "mode")),
            P(),
            P("mode", None, None),
            P("mode", None),
            P(("depth", "mode")),
            P(("depth", "mode")),
        ),
        out_specs=P(("depth", "mode"), None, None, None),
        check_vma=False,
    )
```

profile of v0, /device:TPU:11, one launch (start us, length us, event | category | flops | bytes accessed | tf_op | source)
XLA Modules:
  0.0 181.7 jit_solution(5910919271772014433)
XLA Ops:
  0.0 1.0 copy-done
  1.0 0.9 copy-done.1
  1.9 0.7 copy-done.4
  2.6 0.7 copy-done.5
  3.3 0.7 copy-done.6
  3.9 0.7 copy-done.7
  4.6 0.7 copy-done.8
  5.3 0.7 copy-done.9
  5.9 0.6 shard_map.91
  6.6 3.2 %collective-permute-start = (f32[11,128,128]{2,1,0:T(8,128)S(1)}, f32[11,128,128]{2,1,0:T(8,128)S(1)}, u32[]{:S(2)}, u32[]{:S(2)}) collective-permute-start(f32[11,128,128]{2,1,0:T(8,128)S(1)} %get-tuple-element.29.states_ref.refs_0_), channel_id=1, source_target_pairs={{4,5},{5,6},{6,7},{7,4},{12,13},{13,14},{14,15},{15,12},{20,21},{2... | collective-permute-start | bytes 2162696 | tf_op jit(solution)/shard_map/ppermute | solution.py:453
  9.8 2.9 %collective-permute-start.1 = (f32[11,128,128]{2,1,0:T(8,128)S(1)}, f32[11,128,128]{2,1,0:T(8,128)S(1)}, u32[]{:S(2)}, u32[]{:S(2)}) collective-permute-start(f32[11,128,128]{2,1,0:T(8,128)S(1)} %get-tuple-element.29.states_ref.refs_0_), channel_id=1, source_target_pairs={{4,6},{5,7},{6,4},{7,5},{12,14},{13,15},{14,12},{15,13},{20,22},{2... | collective-permute-start | bytes 2162696 | tf_op jit(solution)/shard_map/ppermute | solution.py:453
  12.7 3.4 %collective-permute-start.2 = (f32[11,128,128]{2,1,0:T(8,128)S(1)}, f32[11,128,128]{2,1,0:T(8,128)S(1)}, u32[]{:S(2)}, u32[]{:S(2)}) collective-permute-start(f32[11,128,128]{2,1,0:T(8,128)S(1)} %get-tuple-element.29.states_ref.refs_0_), channel_id=1, source_target_pairs={{4,7},{5,4},{6,5},{7,6},{12,15},{13,12},{14,13},{15,14},{20,23},{2... | collective-permute-start | bytes 2162696 | tf_op jit(solution)/shard_map/ppermute | solution.py:453
  16.1 1.9 %collective-permute-start.3 = (f32[8,128]{1,0:T(8,128)S(1)}, f32[8,128]{1,0:T(8,128)S(1)}, u32[]{:S(2)}, u32[]{:S(2)}) collective-permute-start(f32[8,128]{1,0:T(8,128)S(1)} %get-tuple-element.28.own_ref), channel_id=1, source_target_pairs={{4,0},{5,1},{6,2},{7,3},{8,4},{9,5},{10,6},{11,7},{12,8},{13,9},{1... | collective-permute-start | bytes 12296 | tf_op jit(solution)/shard_map/ppermute | solution.py:462
  18.0 0.7 shard_map.93
  18.8 8.2 %shard_map.94.refs_0_ = f32[8,128,128]{2,1,0:T(8,128)S(1)} custom-call(f32[11,128,128]{2,1,0:T(8,128)S(1)} %get-tuple-element.29.states_ref.refs_0_, bf16[384,512]{1,0:T(8,128)(2,1)S(1)} %get-tuple-element.32.right_ref, bf16[128,1536]{1,0:T(8,128)(2,1)S(1)} %get-tuple-element.33.left_ref), custom_call_target="tpu_custom_call" | custom-call | flops 10339999744 | bytes 524288 | tf_op jit(solution)/shard_map/pallas_call | solution.py:423
  27.0 14.1 %collective-permute-done.1.refs_1_.states_ref.refs_2_ = f32[11,128,128]{2,1,0:T(8,128)S(1)} collective-permute-done((f32[11,128,128]{2,1,0:T(8,128)S(1)}, f32[11,128,128]{2,1,0:T(8,128)S(1)}, u32[]{:S(2)}, u32[]{:S(2)}) %collective-permute-start.1) | collective-permute-done | bytes 720928 | tf_op jit(solution)/shard_map/ppermute | solution.py:453
  41.2 1.5 collective-permute-done.2.refs_2_.states_ref.refs_3_
  42.7 0.2 shard_map.92
  42.9 2.2 %shard_map.99 = (f32[8,128,128]{2,1,0:T(8,128)S(1)}, f32[4,128,128]{2,1,0:T(8,128)S(1)}, f32[4,128,128]{2,1,0:T(8,128)S(1)}, f32[4,8,128]{2,1,0:T(8,128)S(1)}) custom-call(f32[8,128]{1,0:T(8,128)S(1)} %collective-permute-done.3.near_ref, bf16[8,384,128]{2,1,0:T(8,128)(2,1)S(1)} %get-tuple-element.30.right_ref, ...), custom_call_target="tpu_custom_call" | custom-call | flops 2200000000 | bytes 524288 | tf_op jit(solution)/shard_map/pallas_call | solution.py:423
  45.1 1.3 collective-permute-start.4
  46.5 1.3 collective-permute-start.5
  47.8 1.3 collective-permute-start.6
  49.1 1.3 collective-permute-start.18
  50.4 8.2 %shard_map.95.refs_1_ = f32[8,128,128]{2,1,0:T(8,128)S(1)} custom-call(f32[11,128,128]{2,1,0:T(8,128)S(1)} %collective-permute-done.refs_0_.states_ref.refs_1_, bf16[384,512]{1,0:T(8,128)(2,1)S(1)} %get-tuple-element.32.right_ref, bf16[128,1536]{1,0:T(8,128)(2,1)S(1)} %get-tuple-element.33.left_ref), custom_call_target="tpu_custom_call" | custom-call | flops 10339999744 | bytes 524288 | tf_op jit(solution)/shard_map/pallas_call | solution.py:423
  58.7 8.2 %shard_map.96.refs_2_ = f32[8,128,128]{2,1,0:T(8,128)S(1)} custom-call(f32[11,128,128]{2,1,0:T(8,128)S(1)} %collective-permute-done.1.refs_1_.states_ref.refs_2_, bf16[384,512]{1,0:T(8,128)(2,1)S(1)} %get-tuple-element.32.right_ref, bf16[128,1536]{1,0:T(8,128)(2,1)S(1)} %get-tuple-element.33.left_ref), custom_call_target="tpu_custom_call" | custom-call | flops 10339999744 | bytes 524288 | tf_op jit(solution)/shard_map/pallas_call | solution.py:423
  66.9 0.0 collective-permute-done.6.refs_3_
  66.9 0.0 collective-permute-done.4.refs_1_
  66.9 0.0 copy-start.2
  67.0 0.8 collective-permute-start.10
  67.8 0.7 collective-permute-start.12
  68.5 8.2 %shard_map.97.refs_3_ = f32[8,128,128]{2,1,0:T(8,128)S(1)} custom-call(f32[11,128,128]{2,1,0:T(8,128)S(1)} %collective-permute-done.2.refs_2_.states_ref.refs_3_, bf16[384,512]{1,0:T(8,128)(2,1)S(1)} %get-tuple-element.32.right_ref, bf16[128,1536]{1,0:T(8,128)(2,1)S(1)} %get-tuple-element.33.left_ref), custom_call_target="tpu_custom_call" | custom-call | flops 10339999744 | bytes 524288 | tf_op jit(solution)/shard_map/pallas_call | solution.py:423
  76.7 0.0 collective-permute-done.18.refs_0_
  76.8 0.7 collective-permute-start.8
  77.5 1.3 collective-permute-start.7
  78.8 1.3 collective-permute-start.14
  80.1 1.3 collective-permute-start.11
  81.4 1.3 collective-permute-start.13
  82.7 0.0 collective-permute-done.8.states_ref.refs_7_
  82.7 1.3 collective-permute-start.9
  84.1 1.3 collective-permute-start.15
  85.4 1.3 collective-permute-start.16
  86.7 1.3 collective-permute-done.13.refs_7_
  87.9 1.3 collective-permute-start.17
  89.3 8.2 %collective-permute-done.9.refs_5_ = f32[9,128,128]{2,1,0:T(8,128)S(1)} collective-permute-done((f32[9,128,128]{2,1,0:T(8,128)S(1)}, f32[9,128,128]{2,1,0:T(8,128)S(1)}, u32[]{:S(2)}, u32[]{:S(2)}) %collective-permute-start.9) | collective-permute-done | bytes 589856 | tf_op jit(solution)/shard_map/ppermute | solution.py:462
  97.5 4.4 %shard_map.101 = (f32[32,128,128]{2,1,0:T(8,128)S(1)}, f32[4,8,128]{2,1,0:T(8,128)}) custom-call(bf16[8,384,128]{2,1,0:T(8,128)(2,1)S(1)} %get-tuple-element.30.right_ref, bf16[8,128,384]{2,1,0:T(8,128)(2,1)S(1)} %get-tuple-element.31.left_ref, f32[8,128,128]{2,1,0:T(8,128)S(1)} %shard_map.94.refs_0_, f32[8,128,128]{2,1,0:T(8,128)S(1)} %shard_map.95.refs_1_, ...), custom_call_target="tpu_custom_call" | custom-call | flops 3300000000 | bytes 524288 | tf_op jit(solution)/shard_map/pallas_call | solution.py:423
  101.9 5.0 %collective-permute-done.15.refs_2_ = f32[9,128,128]{2,1,0:T(8,128)S(1)} collective-permute-done((f32[9,128,128]{2,1,0:T(8,128)S(1)}, f32[9,128,128]{2,1,0:T(8,128)S(1)}, u32[]{:S(2)}, u32[]{:S(2)}) %collective-permute-start.15) | collective-permute-done | bytes 589856 | tf_op jit(solution)/shard_map/ppermute | solution.py:462
  106.9 6.3 %collective-permute-done.16.refs_3_ = f32[9,128,128]{2,1,0:T(8,128)S(1)} collective-permute-done((f32[9,128,128]{2,1,0:T(8,128)S(1)}, f32[9,128,128]{2,1,0:T(8,128)S(1)}, u32[]{:S(2)}, u32[]{:S(2)}) %collective-permute-start.16) | collective-permute-done | bytes 589856 | tf_op jit(solution)/shard_map/ppermute | solution.py:462
  113.2 6.3 %collective-permute-done.17.refs_4_ = f32[9,128,128]{2,1,0:T(8,128)S(1)} collective-permute-done((f32[9,128,128]{2,1,0:T(8,128)S(1)}, f32[9,128,128]{2,1,0:T(8,128)S(1)}, u32[]{:S(2)}, u32[]{:S(2)}) %collective-permute-start.17) | collective-permute-done | bytes 589856 | tf_op jit(solution)/shard_map/ppermute | solution.py:462
  119.5 4.4 %shard_map.102 = (f32[18,128,128]{2,1,0:T(8,128)S(1)}, f32[18,128,128]{2,1,0:T(8,128)S(1)}) custom-call(bf16[8,384,128]{2,1,0:T(8,128)(2,1)S(1)} %get-tuple-element.30.right_ref, bf16[8,128,384]{2,1,0:T(8,128)(2,1)S(1)} %get-tuple-element.31.left_ref, f32[32,128,128]{2,1,0:T(8,128)S(1)} %get-tuple-element.38.refs_0_, ...), custom_call_target="tpu_custom_call" | custom-call | flops 3300000000 | bytes 524288 | tf_op jit(solution)/shard_map/pallas_call | solution.py:423
  123.9 1.4 collective-permute-start.19
  125.3 1.4 collective-permute-start.20
  126.7 5.5 %collective-permute-start.21 = (f32[18,128,128]{2,1,0:T(8,128)S(1)}, f32[18,128,128]{2,1,0:T(8,128)S(1)}, u32[]{:S(2)}, u32[]{:S(2)}) collective-permute-start(f32[18,128,128]{2,1,0:T(8,128)S(1)} %get-tuple-element.39.states_ref), channel_id=1, source_target_pairs={{4,8},{5,9},{6,10},{7,11},{12,16},{13,17},{14,18},{15,19},{20,24},... | collective-permute-start | bytes 3538952 | tf_op jit(solution)/shard_map/ppermute | solution.py:462
  132.2 1.4 collective-permute-start.22
  133.7 0.1 shard_map.109
  133.8 11.5 %collective-permute-done.21.refs_1_ = f32[18,128,128]{2,1,0:T(8,128)S(1)} collective-permute-done((f32[18,128,128]{2,1,0:T(8,128)S(1)}, f32[18,128,128]{2,1,0:T(8,128)S(1)}, u32[]{:S(2)}, u32[]{:S(2)}) %collective-permute-start.21) | collective-permute-done | bytes 1179680 | tf_op jit(solution)/shard_map/ppermute | solution.py:462
  145.3 12.6 %collective-permute-done.22.refs_2_ = f32[18,128,128]{2,1,0:T(8,128)S(1)} collective-permute-done((f32[18,128,128]{2,1,0:T(8,128)S(1)}, f32[18,128,128]{2,1,0:T(8,128)S(1)}, u32[]{:S(2)}, u32[]{:S(2)}) %collective-permute-start.22) | collective-permute-done | bytes 1179680 | tf_op jit(solution)/shard_map/ppermute | solution.py:462
  158.0 0.7 shard_map.112
  158.7 1.3 collective-permute-start.25
  160.0 8.2 %shard_map.103.refs_0_ = f32[8,128,128]{2,1,0:T(8,128)S(1)} custom-call(f32[18,128,128]{2,1,0:T(8,128)S(1)} %get-tuple-element.39.states_ref, bf16[384,512]{1,0:T(8,128)(2,1)S(1)} %get-tuple-element.32.right_ref, bf16[128,1536]{1,0:T(8,128)(2,1)S(1)} %get-tuple-element.33.left_ref), custom_call_target="tpu_custom_call" | custom-call | flops 10339999744 | bytes 524288 | tf_op jit(solution)/shard_map/pallas_call | solution.py:423
  168.2 1.3 collective-permute-start.23
  169.5 1.3 collective-permute-start.24
  170.8 6.0 %collective-permute-done.23.refs_2_ = f32[4,128,128]{2,1,0:T(8,128)S(1)} collective-permute-done((f32[4,128,128]{2,1,0:T(8,128)S(1)}, f32[4,128,128]{2,1,0:T(8,128)S(1)}, u32[]{:S(2)}, u32[]{:S(2)}) %collective-permute-start.23) | collective-permute-done | bytes 262176 | tf_op jit(solution)/shard_map/ppermute | solution.py:462
  176.8 2.8 %collective-permute-done.24.refs_3_ = f32[4,128,128]{2,1,0:T(8,128)S(1)} collective-permute-done((f32[4,128,128]{2,1,0:T(8,128)S(1)}, f32[4,128,128]{2,1,0:T(8,128)S(1)}, u32[]{:S(2)}, u32[]{:S(2)}) %collective-permute-start.24) | collective-permute-done | bytes 262176 | tf_op jit(solution)/shard_map/ppermute | solution.py:462
  179.6 1.9 %shard_map.113 = f32[4,2,128,128]{3,2,1,0:T(8,128)} custom-call(f32[8,128]{1,0:T(8,128)S(1)} %get-tuple-element.28.own_ref, bf16[8,384,128]{2,1,0:T(8,128)(2,1)S(1)} %get-tuple-element.30.right_ref, bf16[8,128,384]{2,1,0:T(8,128)(2,1)S(1)} %get-tuple-element.31.left_ref, f32[8,128,128]{2,1,0:T(8,128)S(1)} %shard_map.103.refs_0_, ...), custom_call_target="tpu_custom_call" | custom-call | flops 1100000000 | bytes 524288 | tf_op jit(solution)/shard_map/pallas_call | solution.py:423
  (31 shorter events, 0.2 us)
Async XLA Ops:
  0.0 1.0 copy-start
  1.0 0.9 copy-start.1
  1.9 0.7 copy-start.4
  2.6 0.7 copy-start.5
  3.3 0.7 copy-start.6
  3.9 0.7 copy-start.7
  4.6 0.7 copy-start.8
  5.2 0.7 copy-start.9
  5.9 12.1 %copy-start.3 = (f32[128,128]{1,0:T(8,128)S(1)}, f32[128,128]{1,0:T(8,128)}, u32[]{:S(2)}) copy-start(f32[128,128]{1,0:T(8,128)} %ham_ref.1) | copy-start | bytes 196612
  6.6 20.5 %collective-permute-start = (f32[11,128,128]{2,1,0:T(8,128)S(1)}, f32[11,128,128]{2,1,0:T(8,128)S(1)}, u32[]{:S(2)}, u32[]{:S(2)}) collective-permute-start(f32[11,128,128]{2,1,0:T(8,128)S(1)} %get-tuple-element.29.states_ref.refs_0_), channel_id=1, source_target_pairs={{4,5},{5,6},{6,7},{7,4},{12,13},{13,14},{14,15},{15,12},{20,21},{2... | collective-permute-start | bytes 2162696 | tf_op jit(solution)/shard_map/ppermute | solution.py:453
  9.8 31.4 %collective-permute-start.1 = (f32[11,128,128]{2,1,0:T(8,128)S(1)}, f32[11,128,128]{2,1,0:T(8,128)S(1)}, u32[]{:S(2)}, u32[]{:S(2)}) collective-permute-start(f32[11,128,128]{2,1,0:T(8,128)S(1)} %get-tuple-element.29.states_ref.refs_0_), channel_id=1, source_target_pairs={{4,6},{5,7},{6,4},{7,5},{12,14},{13,15},{14,12},{15,13},{20,22},{2... | collective-permute-start | bytes 2162696 | tf_op jit(solution)/shard_map/ppermute | solution.py:453
  12.7 29.9 %collective-permute-start.2 = (f32[11,128,128]{2,1,0:T(8,128)S(1)}, f32[11,128,128]{2,1,0:T(8,128)S(1)}, u32[]{:S(2)}, u32[]{:S(2)}) collective-permute-start(f32[11,128,128]{2,1,0:T(8,128)S(1)} %get-tuple-element.29.states_ref.refs_0_), channel_id=1, source_target_pairs={{4,7},{5,4},{6,5},{7,6},{12,15},{13,12},{14,13},{15,14},{20,23},{2... | collective-permute-start | bytes 2162696 | tf_op jit(solution)/shard_map/ppermute | solution.py:453
  16.1 26.8 %collective-permute-start.3 = (f32[8,128]{1,0:T(8,128)S(1)}, f32[8,128]{1,0:T(8,128)S(1)}, u32[]{:S(2)}, u32[]{:S(2)}) collective-permute-start(f32[8,128]{1,0:T(8,128)S(1)} %get-tuple-element.28.own_ref), channel_id=1, source_target_pairs={{4,0},{5,1},{6,2},{7,3},{8,4},{9,5},{10,6},{11,7},{12,8},{13,9},{1... | collective-permute-start | bytes 12296 | tf_op jit(solution)/shard_map/ppermute | solution.py:462
  45.1 21.8 %collective-permute-start.4 = (f32[8,128,128]{2,1,0:T(8,128)S(1)}, f32[8,128,128]{2,1,0:T(8,128)S(1)}, u32[]{:S(2)}, u32[]{:S(2)}) collective-permute-start(f32[8,128,128]{2,1,0:T(8,128)S(1)} %get-tuple-element.34), channel_id=1, source_target_pairs={{4,0},{5,1},{6,2},{7,3},{12,8},{13,9},{14,10},{15,11},{20,16},{21,... | collective-permute-start | bytes 1572872 | tf_op jit(solution)/shard_map/ppermute | solution.py:462
  46.5 20.4 %collective-permute-start.5 = (f32[4,128,128]{2,1,0:T(8,128)S(1)}, f32[4,128,128]{2,1,0:T(8,128)S(1)}, u32[]{:S(2)}, u32[]{:S(2)}) collective-permute-start(f32[4,128,128]{2,1,0:T(8,128)S(1)} %get-tuple-element.35), channel_id=1, source_target_pairs={{4,8},{5,9},{6,10},{7,11},{12,16},{13,17},{14,18},{15,19},{20,24},... | collective-permute-start | bytes 786440 | tf_op jit(solution)/shard_map/ppermute | solution.py:462
  47.8 19.1 %collective-permute-start.6 = (f32[4,128,128]{2,1,0:T(8,128)S(1)}, f32[4,128,128]{2,1,0:T(8,128)S(1)}, u32[]{:S(2)}, u32[]{:S(2)}) collective-permute-start(f32[4,128,128]{2,1,0:T(8,128)S(1)} %get-tuple-element.36), channel_id=1, source_target_pairs={{4,8},{5,9},{6,10},{7,11},{12,16},{13,17},{14,18},{15,19},{20,24},... | collective-permute-start | bytes 786440 | tf_op jit(solution)/shard_map/ppermute | solution.py:462
  49.1 27.6 %collective-permute-start.18 = (f32[6,128,128]{2,1,0:T(8,128)S(1)}, f32[6,128,128]{2,1,0:T(8,128)S(1)}, u32[]{:S(2)}, u32[]{:S(2)}) collective-permute-start(f32[6,128,128]{2,1,0:T(8,128)S(1)} %get-tuple-element.40), channel_id=1, source_target_pairs={{4,0},{5,1},{6,2},{7,3},{12,8},{13,9},{14,10},{15,11},{20,16},{21,... | collective-permute-start | bytes 1179656 | tf_op jit(solution)/shard_map/ppermute | solution.py:462
  66.9 9.8 %copy-start.2 = (f32[2,128,128]{2,1,0:T(8,128)S(1)}, f32[2,128,128]{2,1,0:T(8,128)}, u32[]{:S(2)}) copy-start(f32[2,128,128]{2,1,0:T(8,128)} %own_ref.3) | copy-start | bytes 393220
  67.0 13.1 %collective-permute-start.10 = (f32[9,128,128]{2,1,0:T(8,128)S(1)}, f32[9,128,128]{2,1,0:T(8,128)S(1)}, u32[]{:S(2)}, u32[]{:S(2)}) collective-permute-start(f32[9,128,128]{2,1,0:T(8,128)S(1)} %shard_map.100.states_ref.refs_6_), channel_id=1, source_target_pairs={{0,2},{1,3},{2,0},{3,1},{8,10},{9,11},{10,8},{11,9},{16,18},{17,19... | collective-permute-start | bytes 1769480 | tf_op jit(solution)/shard_map/ppermute | solution.py:453
  67.8 13.6 %collective-permute-start.12 = (f32[9,128,128]{2,1,0:T(8,128)S(1)}, f32[9,128,128]{2,1,0:T(8,128)S(1)}, u32[]{:S(2)}, u32[]{:S(2)}) collective-permute-start(f32[9,128,128]{2,1,0:T(8,128)S(1)} %shard_map.100.states_ref.refs_6_), channel_id=1, source_target_pairs={{0,3},{1,0},{2,1},{3,2},{8,11},{9,8},{10,9},{11,10},{16,19},{17,16... | collective-permute-start | bytes 1769480 | tf_op jit(solution)/shard_map/ppermute | solution.py:453
  76.8 6.0 %collective-permute-start.8 = (f32[9,128,128]{2,1,0:T(8,128)S(1)}, f32[9,128,128]{2,1,0:T(8,128)S(1)}, u32[]{:S(2)}, u32[]{:S(2)}) collective-permute-start(f32[9,128,128]{2,1,0:T(8,128)S(1)} %shard_map.100.states_ref.refs_6_), channel_id=1, source_target_pairs={{0,1},{1,2},{2,3},{3,0},{8,9},{9,10},{10,11},{11,8},{16,17},{17,18... | collective-permute-start | bytes 1769480 | tf_op jit(solution)/shard_map/ppermute | solution.py:453
  77.5 6.6 %collective-permute-start.7 = (f32[9,128,128]{2,1,0:T(8,128)S(1)}, f32[9,128,128]{2,1,0:T(8,128)S(1)}, u32[]{:S(2)}, u32[]{:S(2)}) collective-permute-start(f32[9,128,128]{2,1,0:T(8,128)S(1)} %shard_map.100.states_ref.refs_6_), channel_id=1, source_target_pairs={{0,4},{1,5},{2,6},{3,7},{8,12},{9,13},{10,14},{11,15},{16,20},{17,... | collective-permute-start | bytes 1769480 | tf_op jit(solution)/shard_map/ppermute | solution.py:462
  78.8 23.1 %collective-permute-start.14 = (f32[9,128,128]{2,1,0:T(8,128)S(1)}, f32[9,128,128]{2,1,0:T(8,128)S(1)}, u32[]{:S(2)}, u32[]{:S(2)}) collective-permute-start(f32[9,128,128]{2,1,0:T(8,128)S(1)} %shard_map.100.states_ref.refs_6_), channel_id=1, source_target_pairs={{8,4},{9,5},{10,6},{11,7},{16,12},{17,13},{18,14},{19,15},{24,20},... | collective-permute-start | bytes 1769480 | tf_op jit(solution)/shard_map/ppermute | solution.py:462
  80.1 5.3 %collective-permute-start.11 = (f32[9,128,128]{2,1,0:T(8,128)S(1)}, f32[9,128,128]{2,1,0:T(8,128)S(1)}, u32[]{:S(2)}, u32[]{:S(2)}) collective-permute-start(f32[9,128,128]{2,1,0:T(8,128)S(1)} %collective-permute-done.10.states_ref.refs_8_), channel_id=1, source_target_pairs={{0,4},{1,5},{2,6},{3,7},{8,12},{9,13},{10,14},{11,15},{16,20},{17,... | collective-permute-start | bytes 1769480 | tf_op jit(solution)/shard_map/ppermute | solution.py:462
  81.4 6.5 %collective-permute-start.13 = (f32[9,128,128]{2,1,0:T(8,128)S(1)}, f32[9,128,128]{2,1,0:T(8,128)S(1)}, u32[]{:S(2)}, u32[]{:S(2)}) collective-permute-start(f32[9,128,128]{2,1,0:T(8,128)S(1)} %collective-permute-done.12.states_ref.refs_9_), channel_id=1, source_target_pairs={{0,4},{1,5},{2,6},{3,7},{8,12},{9,13},{10,14},{11,15},{16,20},{17,... | collective-permute-start | bytes 1769480 | tf_op jit(solution)/shard_map/ppermute | solution.py:462
  82.7 14.8 %collective-permute-start.9 = (f32[9,128,128]{2,1,0:T(8,128)S(1)}, f32[9,128,128]{2,1,0:T(8,128)S(1)}, u32[]{:S(2)}, u32[]{:S(2)}) collective-permute-start(f32[9,128,128]{2,1,0:T(8,128)S(1)} %collective-permute-done.8.states_ref.refs_7_), channel_id=1, source_target_pairs={{0,4},{1,5},{2,6},{3,7},{8,12},{9,13},{10,14},{11,15},{16,20},{17,... | collective-permute-start | bytes 1769480 | tf_op jit(solution)/shard_map/ppermute | solution.py:462
  84.1 22.8 %collective-permute-start.15 = (f32[9,128,128]{2,1,0:T(8,128)S(1)}, f32[9,128,128]{2,1,0:T(8,128)S(1)}, u32[]{:S(2)}, u32[]{:S(2)}) collective-permute-start(f32[9,128,128]{2,1,0:T(8,128)S(1)} %collective-permute-done.8.states_ref.refs_7_), channel_id=1, source_target_pairs={{8,4},{9,5},{10,6},{11,7},{16,12},{17,13},{18,14},{19,15},{24,20},... | collective-permute-start | bytes 1769480 | tf_op jit(solution)/shard_map/ppermute | solution.py:462
  85.4 27.8 %collective-permute-start.16 = (f32[9,128,128]{2,1,0:T(8,128)S(1)}, f32[9,128,128]{2,1,0:T(8,128)S(1)}, u32[]{:S(2)}, u32[]{:S(2)}) collective-permute-start(f32[9,128,128]{2,1,0:T(8,128)S(1)} %collective-permute-done.10.states_ref.refs_8_), channel_id=1, source_target_pairs={{8,4},{9,5},{10,6},{11,7},{16,12},{17,13},{18,14},{19,15},{24,20},... | collective-permute-start | bytes 1769480 | tf_op jit(solution)/shard_map/ppermute | solution.py:462
  87.9 31.6 %collective-permute-start.17 = (f32[9,128,128]{2,1,0:T(8,128)S(1)}, f32[9,128,128]{2,1,0:T(8,128)S(1)}, u32[]{:S(2)}, u32[]{:S(2)}) collective-permute-start(f32[9,128,128]{2,1,0:T(8,128)S(1)} %collective-permute-done.12.states_ref.refs_9_), channel_id=1, source_target_pairs={{8,4},{9,5},{10,6},{11,7},{16,12},{17,13},{18,14},{19,15},{24,20},... | collective-permute-start | bytes 1769480 | tf_op jit(solution)/shard_map/ppermute | solution.py:462
  123.9 9.7 %collective-permute-start.19 = (f32[18,128,128]{2,1,0:T(8,128)S(1)}, f32[18,128,128]{2,1,0:T(8,128)S(1)}, u32[]{:S(2)}, u32[]{:S(2)}) collective-permute-start(f32[18,128,128]{2,1,0:T(8,128)S(1)} %get-tuple-element.39.states_ref), channel_id=1, source_target_pairs={{4,0},{5,1},{6,2},{7,3},{12,8},{13,9},{14,10},{15,11},{20,16},{21,... | collective-permute-start | bytes 3538952 | tf_op jit(solution)/shard_map/ppermute | solution.py:462
  125.3 8.3 %collective-permute-start.20 = (f32[18,128,128]{2,1,0:T(8,128)S(1)}, f32[18,128,128]{2,1,0:T(8,128)S(1)}, u32[]{:S(2)}, u32[]{:S(2)}) collective-permute-start(f32[18,128,128]{2,1,0:T(8,128)S(1)} %get-tuple-element.43), channel_id=1, source_target_pairs={{4,0},{5,1},{6,2},{7,3},{12,8},{13,9},{14,10},{15,11},{20,16},{21,... | collective-permute-start | bytes 3538952 | tf_op jit(solution)/shard_map/ppermute | solution.py:462
  126.7 18.6 %collective-permute-start.21 = (f32[18,128,128]{2,1,0:T(8,128)S(1)}, f32[18,128,128]{2,1,0:T(8,128)S(1)}, u32[]{:S(2)}, u32[]{:S(2)}) collective-permute-start(f32[18,128,128]{2,1,0:T(8,128)S(1)} %get-tuple-element.39.states_ref), channel_id=1, source_target_pairs={{4,8},{5,9},{6,10},{7,11},{12,16},{13,17},{14,18},{15,19},{20,24},... | collective-permute-start | bytes 3538952 | tf_op jit(solution)/shard_map/ppermute | solution.py:462
  132.2 25.7 %collective-permute-start.22 = (f32[18,128,128]{2,1,0:T(8,128)S(1)}, f32[18,128,128]{2,1,0:T(8,128)S(1)}, u32[]{:S(2)}, u32[]{:S(2)}) collective-permute-start(f32[18,128,128]{2,1,0:T(8,128)S(1)} %get-tuple-element.43), channel_id=1, source_target_pairs={{4,8},{5,9},{6,10},{7,11},{12,16},{13,17},{14,18},{15,19},{20,24},... | collective-permute-start | bytes 3538952 | tf_op jit(solution)/shard_map/ppermute | solution.py:462
  158.7 20.9 %collective-permute-start.25 = (f32[8,128,128]{2,1,0:T(8,128)S(1)}, f32[8,128,128]{2,1,0:T(8,128)S(1)}, u32[]{:S(2)}, u32[]{:S(2)}) collective-permute-start(f32[8,128,128]{2,1,0:T(8,128)S(1)} %get-tuple-element.50), channel_id=1, source_target_pairs={{0,4},{1,5},{2,6},{3,7},{8,12},{9,13},{10,14},{11,15},{16,20},{17,... | collective-permute-start | bytes 1572872 | tf_op jit(solution)/shard_map/ppermute | solution.py:462
  168.2 8.6 %collective-permute-start.23 = (f32[4,128,128]{2,1,0:T(8,128)S(1)}, f32[4,128,128]{2,1,0:T(8,128)S(1)}, u32[]{:S(2)}, u32[]{:S(2)}) collective-permute-start(f32[4,128,128]{2,1,0:T(8,128)S(1)} %get-tuple-element.48), channel_id=1, source_target_pairs={{8,4},{9,5},{10,6},{11,7},{16,12},{17,13},{18,14},{19,15},{24,20},... | collective-permute-start | bytes 786440 | tf_op jit(solution)/shard_map/ppermute | solution.py:462
  169.5 10.1 %collective-permute-start.24 = (f32[4,128,128]{2,1,0:T(8,128)S(1)}, f32[4,128,128]{2,1,0:T(8,128)S(1)}, u32[]{:S(2)}, u32[]{:S(2)}) collective-permute-start(f32[4,128,128]{2,1,0:T(8,128)S(1)} %get-tuple-element.49), channel_id=1, source_target_pairs={{8,4},{9,5},{10,6},{11,7},{16,12},{17,13},{18,14},{19,15},{24,20},... | collective-permute-start | bytes 786440 | tf_op jit(solution)/shard_map/ppermute | solution.py:462
where the time goes:
time: 182 us
  waiting for transfers between devices  75.7 us (42%)
  Pallas kernels  56.7 us (31%)
  starting transfers between devices  42.7 us (23%)
  local copies, waits for them, and re-layouts  5.91 us (3%)
    ppermute x20, waiting for transfers between devices, shift(): return lax.ppermute(value, AXES, pairs)  60.1 us
    pallas_call x23, Pallas kernels, call(): pl.pallas_call(kernel, out_shape=out_shapes, in_specs=specs, out_specs=ja...  56.7 us
    ppermute x20, starting transfers between devices, shift(): return lax.ppermute(value, AXES, pairs)  31 us
    ppermute x6, waiting for transfers between devices, turn(): return lax.ppermute(value, AXES, pairs)  15.6 us
    ppermute x6, starting transfers between devices, turn(): return lax.ppermute(value, AXES, pairs)  11.7 us
    unnamed x20, local copies, waits for them, and re-layouts  5.91 us
  transfers between devices with their start and end apart: 26, of which 11 were waited for; matrix products, arithmetic and copies ran while one was open for 0% of the time, Pallas kernels for 26%

commit v1 on v0

v1 whole, which is shorter than its diff:
```python
import functools
import math
import jax
import jax.numpy as jnp
from jax import lax
from jax.experimental import pallas as pl
from jax.experimental.pallas import tpu as pltpu
from jax.sharding import PartitionSpec as P

SUBSTEPS = 2
ORDER = 4
substep = 0.7
couple_step = 0.2

AXES = ("depth", "mode")
VMEM = pltpu.VMEM
SMEM = pltpu.SMEM
bf16 = jnp.bfloat16
f32 = jnp.float32

PARENT, MODE, LIVE, FACTOR, WEIGHT, WEIGHT_A, WEIGHT_C = range(7)
ROWS, LANES = 8, 128
PACK_LIMIT = 56 << 20


def split(value):
    high = value.astype(bf16)
    return high, (value - high.astype(f32)).astype(bf16)


def stack_rows(value):
    high, low = split(value)
    return jnp.concatenate([high, high, low], axis=0)


def stack_cols(value):
    high, low = split(value)
    return jnp.concatenate([high, low, high], axis=1)


def dot(first, second):
    return jnp.dot(first, second, preferred_element_type=f32)


def exact(first, second):
    return jnp.dot(first, second, preferred_element_type=f32, precision=lax.Precision.HIGHEST)


def odd_depth():
    return lax.rem(lax.axis_index("depth"), 2)


def rows(at, n, count=1):
    if not isinstance(at, int):
        at = pl.multiple_of(at, ROWS)
    return pl.ds(at, count * n)


def pack_kernel(live_ref, parent_ref, mode_ref, damping_ref, weight_ref, corr_ref, blocks_ref, coupling_ref, out_ref, table_ref):
    slots, n = live_ref.shape[0], blocks_ref.shape[1]
    size = blocks_ref.shape[0]
    out_ref[pl.ds(0, size)] = blocks_ref[...]
    out_ref[pl.ds(size + ROWS, coupling_ref.shape[0])] = coupling_ref[...]
    row = lax.broadcasted_iota(jnp.int32, (ROWS, n), 0)
    lane = lax.broadcasted_iota(jnp.int32, (ROWS, n), 1)
    table = jnp.zeros((ROWS, n), f32)
    first_mode = lax.axis_index("mode") * corr_ref.shape[0]
    for s in range(slots):
        mode = mode_ref[s] - first_mode
        live = live_ref[s].astype(f32)
        weight = weight_ref[s]
        values = {
            PARENT: parent_ref[s].astype(f32),
            MODE: mode.astype(f32),
            LIVE: live,
            FACTOR: damping_ref[s] * (-SUBSTEPS * substep),
            WEIGHT: weight * live,
            WEIGHT_A: weight * corr_ref[mode, 0],
            WEIGHT_C: weight * corr_ref[mode, 1],
        }
        for at, value in values.items():
            table = jnp.where(jnp.logical_and(row == at, lane == s), value, table)
    live_row = table[LIVE : LIVE + 1]
    table = jnp.where(row == FACTOR, live_row * jnp.exp(table), table)
    table_ref[...] = table
    out_ref[pl.ds(size, ROWS)] = table


def powers_kernel(ham_ref, right_ref, left_ref):
    n = ham_ref.shape[0]
    ham = (ham_ref[...] + ham_ref[...].T) * 0.5
    power = ham
    for k in range(1, ORDER + 1):
        if k > 1:
            power = exact(power, ham)
        scaled = power * (substep**k / math.factorial(k))
        right_ref[:, (k - 1) * n : k * n] = stack_rows(scaled)
        left_ref[:, (k - 1) * 3 * n : k * 3 * n] = stack_cols(scaled)


class Layout:
    def __init__(self, refs, slots, group):
        self.refs, self.slots, self.group = refs, slots, group
        self.n = refs[0].shape[1]
        self.relay = len(refs) == group + 1
        self.held = 1 if self.relay else group // len(refs)
        self.size = 2 * slots * self.n
        self.stride = self.size + ROWS

    def places(self, k):
        if self.relay and k in (1, self.group - 1):
            edge = lax.axis_index("mode") == (0 if k == 1 else self.group - 1)
            return [(jnp.logical_not(edge), self.refs[k], 0), (edge, self.refs[-1], 0)]
        return [(None, self.refs[k // self.held], (k % self.held) * self.stride)]

    def each(self, k, body):
        for condition, ref, base in self.places(k):
            if condition is None:
                body(ref, base)
            else:
                pl.when(condition)(functools.partial(body, ref, base))

    def table(self, k):
        return [
            (condition, ref.at[pl.ds(base + self.size, ROWS), pl.ds(0, LANES)]) for condition, ref, base in self.places(k)
        ]

    def copy_table(self, k, target_ref, at):
        def body(ref, base):
            target_ref[at] = ref[pl.ds(base + self.size, ROWS)]

        self.each(k, body)

    def fetch(self, index, stage_ref, at):
        for k in range(self.group):
            local = index - k * self.slots
            inside = jnp.logical_and(local >= 0, local < self.slots)
            for condition, ref, base in self.places(k):
                here = inside if condition is None else jnp.logical_and(inside, condition)

                @pl.when(here)
                def _():
                    stage_ref[rows(at * self.n, self.n, 2)] = ref[rows(base + 2 * local * self.n, self.n, 2)]


def pull(sources, smem_ref, sem_ref):
    copies = []
    for i, source in enumerate(sources):
        for condition, ref in source if isinstance(source, list) else [(None, source)]:
            copy = pltpu.make_async_copy(ref, smem_ref.at[i], sem_ref.at[i])
            if condition is None:
                copy.start()
            else:
                pl.when(condition)(copy.start)
        copies.append(copy)
    for copy in copies:
        copy.wait()


def narrow(ref):
    return ref.at[pl.ds(0, ROWS), pl.ds(0, LANES)]


def operators_kernel(slots, group, modes, parity, own_ref, *refs):
    outs = refs[-2 - (parity is None) :]
    sources = refs[: -len(outs)]
    right_ref, left_ref = outs[0], outs[1]
    n = own_ref.shape[1]

    def put(at, value):
        sym = (value + value.T) * 0.5
        right_ref[at] = stack_rows(sym)
        left_ref[at] = stack_cols(sym)

    def own():
        for i in range(modes):
            put(i, own_ref[rows(i * n, n)])

    if parity is None:
        own()
        groups = Layout(sources, slots, group)
        for k in range(1, group):

            def body(ref, base, k=k):
                for i in range(modes):
                    value = ref[rows(base + groups.stride + i * n, n)]
                    put(k * modes + i, value)
                    outs[2][rows(((k - 1) * modes + i) * n, n)] = value

            groups.each(k, body)
    else:

        @pl.when(odd_depth() == parity)
        def _():
            own()
            for at in range(modes, group * modes):
                put(at, sources[0][rows((at - modes) * n, n)])


def taylor(real, imag, right, left):
    n = real.shape[0]
    out = dot(stack_cols(jnp.concatenate([real, imag], axis=0)), right)
    rp = [out[:n, k * n : (k + 1) * n] for k in range(ORDER)]
    ip = [out[n:, k * n : (k + 1) * n] for k in range(ORDER)]
    u_real, u_imag = real, imag
    stacked = [None] * ORDER
    for k in range(ORDER + 1):
        if k:
            turn = k % 4
            if turn == 1:
                u_real, u_imag = u_real - ip[k - 1], u_imag + rp[k - 1]
            elif turn == 2:
                u_real, u_imag = u_real - rp[k - 1], u_imag - ip[k - 1]
            elif turn == 3:
                u_real, u_imag = u_real + ip[k - 1], u_imag - rp[k - 1]
            else:
                u_real, u_imag = u_real + rp[k - 1], u_imag + ip[k - 1]
        j = ORDER - k
        if j:
            turn = j % 4
            if turn == 1:
                pair = (u_imag, -u_real)
            elif turn == 2:
                pair = (-u_real, -u_imag)
            elif turn == 3:
                pair = (-u_imag, u_real)
            else:
                pair = (u_real, u_imag)
            stacked[j - 1] = stack_rows(jnp.concatenate(pair, axis=1))
    done = dot(left, jnp.concatenate(stacked, axis=0))
    return u_real + done[:, :n], u_imag + done[:, n:]


def free_kernel(run_parity, times, slots, group, k, right_ref, left_ref, *refs):
    out_ref = refs[-1]
    pair = 2 if slots % 2 == 0 else 1
    n = out_ref.shape[1]
    size = 2 * slots * n
    edge = lax.axis_index("mode") == (0 if k == 1 else group - 1)

    def each(body):
        if len(refs) == 2:
            body(refs[0])
        else:
            pl.when(jnp.logical_not(edge))(lambda: body(refs[0]))
            pl.when(edge)(lambda: body(refs[1]))

    @pl.when(odd_depth() == run_parity)
    def _():
        right, left = right_ref[...], left_ref[...]

        def load(ref):
            out_ref[...] = ref[pl.ds(0, size)]

        each(load)

        @pl.loop(0, slots // pair)
        def _(step):
            @pl.loop(0, times * SUBSTEPS)
            def _(turn):
                at = [(rows(2 * s * n, n), rows((2 * s + 1) * n, n)) for s in [step * pair + u for u in range(pair)]]
                done = [taylor(out_ref[r], out_ref[i], right, left) for r, i in at]
                for (r, i), (real, imag) in zip(at, done):
                    out_ref[r] = real
                    out_ref[i] = imag

        def damp(ref):
            factors = ref[pl.ds(size, ROWS)][FACTOR : FACTOR + 1]
            for s in range(slots):
                scale = factors[:, s : s + 1] ** times
                at = rows(2 * s * n, n, 2)
                out_ref[at] = out_ref[at] * scale

        each(damp)


def sided(real, imag, right, left):
    n = real.shape[0]
    after = dot(stack_cols(jnp.concatenate([real, imag], axis=0)), right)
    before = dot(left, stack_rows(jnp.concatenate([real, imag], axis=1)))
    return after[:n], after[n:], before[:, :n], before[:, n:]


def entry(tab, row, c, slots):
    if isinstance(c, int):
        return tab[c // slots, row, c % slots]
    return tab[lax.div(c, slots), row, lax.rem(c, slots)]


def operator_of(tab, c, slots, modes):
    back = c // slots if isinstance(c, int) else lax.div(c, slots)
    return back * modes + entry(tab, MODE, c, slots).astype(jnp.int32)


def parent_of(tab, c, slots, group):
    parent = entry(tab, PARENT, c, slots).astype(jnp.int32)
    back = lax.rem(lax.axis_index("mode") - lax.div(parent, slots) + group, group)
    return back * slots + lax.rem(parent, slots)


def child_pair(stage_ref, at, mode, weight, right_ref, left_ref):
    n = stage_ref.shape[1]
    ra, ia, rb, ib = sided(stage_ref[rows(at * n, n)], stage_ref[rows((at + 1) * n, n)], right_ref[mode], left_ref[mode])
    return weight * (ib - ia), weight * (ra - rb)


def parent_pair(stage_ref, at, mode, wa, wc, right_ref, left_ref):
    n = stage_ref.shape[1]
    ra, ia, rb, ib = sided(stage_ref[rows(at * n, n)], stage_ref[rows((at + 1) * n, n)], right_ref[mode], left_ref[mode])
    return wa * (ib - ia) + wc * (rb + ra), wa * (ra - rb) + wc * (ib + ia)


def add_pair(acc_ref, at, pair):
    n = acc_ref.shape[1]
    for i in range(2):
        where = rows(at + i * n, n)
        acc_ref[where] = acc_ref[where] + pair[i]


def part_of(parts, s):
    size = parts[0].shape[0] // (2 * parts[0].shape[1])
    return parts[s // size], 2 * (s % size)


def send_kernel(sender, slots, group, modes, sum_parts, pick_parts, near_ref, right_ref, left_ref, *refs):
    acc_ref, stage_ref, list_ref, tab, sem_ref = refs[-5:]
    tabs_ref = refs[-6]
    n = acc_ref.shape[1]
    outs = refs[-6 - sum_parts - pick_parts : -6]
    sums, picks = outs[:sum_parts], outs[sum_parts:]
    groups = Layout(refs[: -6 - sum_parts - pick_parts], slots, group)

    @pl.when(odd_depth() == sender)
    def _():
        pull([groups.table(k) for k in range(group)] + [narrow(near_ref)], tab, sem_ref)
        for k in range(group):
            groups.copy_table(k, tabs_ref, k)
        acc_ref[...] = jnp.zeros_like(acc_ref)
        for s in range(slots):
            pick, at = part_of(picks, s)
            groups.fetch(parent_of(tab, group * slots + s, slots, group), pick, at)

        def collect(c, count):
            mine = parent_of(tab, c, slots, group) < slots

            @pl.when(mine)
            def _():
                list_ref[count] = c

            return count + mine.astype(jnp.int32)

        count = lax.fori_loop(0, group * slots, collect, jnp.int32(0))

        @pl.loop(0, lax.div(count + slots - 1, slots))
        def _(batch):
            children = []
            for u in range(slots):
                place = batch * slots + u
                c = list_ref[jnp.minimum(place, count - 1)]
                groups.fetch(c, stage_ref, 2 * u)
                children.append((c, jnp.where(place < count, entry(tab, WEIGHT, c, slots), 0.0)))
            terms = [
                child_pair(stage_ref, 2 * u, operator_of(tab, c, slots, modes), weight, right_ref, left_ref)
                for u, (c, weight) in enumerate(children)
            ]
            for (c, _), pair in zip(children, terms):
                add_pair(acc_ref, 2 * parent_of(tab, c, slots, group) * n, pair)

        for s in range(slots):
            part, at = part_of(sums, s)
            part[rows(at * n, n, 2)] = acc_ref[rows(2 * s * n, n, 2)]


def join_kernel(receiver, slots, modes, sum_parts, pick_parts, own_ref, right_ref, left_ref, *refs):
    out_ref, tab, sem_ref = refs[-3:]
    picks = refs[-3 - pick_parts : -3]
    sums = refs[-3 - pick_parts - sum_parts : -3 - pick_parts]
    frees = refs[: -3 - pick_parts - sum_parts]
    n = frees[0].shape[1]
    final = len(frees) > 1

    @pl.when(odd_depth() == receiver)
    def _():
        pull([narrow(own_ref)], tab, sem_ref)
        terms = []
        for s in range(slots):
            pick, at = part_of(picks, s)
            wa, wc = tab[0, WEIGHT_A, s], tab[0, WEIGHT_C, s]
            terms.append(parent_pair(pick, at, operator_of(tab, s, slots, modes), wa, wc, right_ref, left_ref))
        for s in range(slots):
            scale = tab[0, LIVE, s] * couple_step
            part, at = part_of(sums, s)
            for i in range(2):
                here = rows((2 * s + i) * n, n)
                out_ref[here] = frees[0][here] + scale * (part[rows((at + i) * n, n)] + terms[s][i])
        if not final:
            out_ref[pl.ds(2 * slots * n, ROWS)] = own_ref[...]

    if final:

        @pl.when(odd_depth() != receiver)
        def _():
            out_ref[...] = frees[1][...]


def side_kernel(side, receiver, slots, group, modes, base_count, group_count, tab_count, right_ref, left_ref, *refs):
    stage_ref, tab, sem_ref = refs[-3:]
    bases = refs[:base_count]
    groups = Layout(refs[base_count : base_count + group_count], slots, group)
    tab_refs = refs[base_count + group_count : base_count + group_count + tab_count]
    outs = refs[base_count + group_count + tab_count : -3]
    second = base_count == 1
    n = stage_ref.shape[1]
    size = 2 * slots * n
    gathered = Layout(tab_refs, slots, group) if tab_count > 1 else None
    own_tables = [gathered.table(k) if gathered else tab_refs[0].at[k, pl.ds(0, ROWS), pl.ds(0, LANES)] for k in range(group)]
    held = group // len(outs) if second else group
    stride = size + ROWS if second else size

    def spot(k):
        return outs[k // held], (k % held) * stride

    @pl.when(odd_depth() == receiver)
    def _():
        below = [groups.table(k) for k in range(group)] if side == "children" else []
        pull(own_tables + below, tab, sem_ref)
        for k in range(group):
            ref, base = spot(k)
            ref[pl.ds(base, size)] = bases[0][pl.ds(k * size, size)] if second else bases[k][...]
            if second:
                ref[pl.ds(base + size, ROWS)] = tab_refs[0][k]
            elif gathered:
                gathered.copy_table(k, outs[1], k)
            else:
                outs[1][k] = tab_refs[0][k]

        def add(index, pair):
            if not second:
                add_pair(outs[0], 2 * index * n, pair)
                return
            for half, ref in enumerate(outs):
                local = index - half * held * slots
                at = lax.div(local, slots) * stride + lax.rem(local, slots) * (2 * n)

                @pl.when(jnp.logical_and(local >= 0, local < held * slots))
                def _():
                    add_pair(ref, at, pair)

        @pl.loop(0, group)
        def _(k):
            at = k * slots
            targets, terms = [], []
            for s in range(slots):
                c = at + s
                groups.fetch(c if side == "children" else parent_of(tab, c, slots, group), stage_ref, 2 * s)
            for s in range(slots):
                c = at + s
                if side == "children":
                    b = c + group * slots
                    target = parent_of(tab, b, slots, group)
                    weight = entry(tab, WEIGHT, b, slots) * (entry(tab, LIVE, target, slots) * couple_step)
                    mode = operator_of(tab, b, slots, modes) - group * modes
                    terms.append(child_pair(stage_ref, 2 * s, mode, weight, right_ref, left_ref))
                else:
                    target = c
                    scale = entry(tab, LIVE, c, slots) * couple_step
                    wa, wc = entry(tab, WEIGHT_A, c, slots) * scale, entry(tab, WEIGHT_C, c, slots) * scale
                    mode = operator_of(tab, c, slots, modes)
                    terms.append(parent_pair(stage_ref, 2 * s, mode, wa, wc, right_ref, left_ref))
                targets.append(target)
            for target, pair in zip(targets, terms):
                add(target, pair)


def call(kernel, out_shapes, limit, args, smem=0, us=1.0, scratch=()):
    specs = [pl.BlockSpec(memory_space=SMEM)] * smem
    specs += [pl.BlockSpec(memory_space=VMEM)] * (len(args) - smem)
    return pl.pallas_call(
        kernel,
        out_shape=out_shapes,
        in_specs=specs,
        out_specs=jax.tree.map(lambda _: pl.BlockSpec(memory_space=VMEM), out_shapes),
        scratch_shapes=scratch,
        compiler_params=pltpu.CompilerParams(vmem_limit_bytes=limit),
        cost_estimate=pl.CostEstimate(flops=int(us * 1.1e9), bytes_accessed=1 << 19, transcendentals=0),
    )(*args)


def turn_order(group):
    return sorted(range(1, group), key=lambda k: abs(k - group / 2))


def has_relay(group):
    return group - 2 == 2


def shards(sizes, blocks, live_slots, parent_index, bath_mode, hamiltonian, coupling, correlation, damping, link_weight):
    depths, group = sizes
    slots, _, n, _ = blocks.shape
    modes = coupling.shape[0]
    total = group * slots
    limit = 8 * total * 2 * n * n * 4
    order = turn_order(group)
    split_hop = 2 if slots % 2 == 0 else 1
    ranks = range(group)
    relay = has_relay(group)

    def place(d, m):
        return d * group + m

    def permute(value, pairs):
        return lax.ppermute(value, AXES, pairs)

    def gather(value, parity):
        def turn(k):
            wraps = {1: group - 1, group - 1: 0}
            pairs = [
                (place(d, m), place(d, (m + k) % group))
                for d in range(parity, depths, 2)
                for m in ranks
                if not (relay and wraps.get(k) == m)
            ]
            return permute(value, pairs)

        turned = {k: turn(k) for k in order}
        groups = [value] + [turned[k] for k in range(1, group)]
        if relay:
            pairs = [
                (place(d, source), place(d, target))
                for d in range(parity, depths, 2)
                for source, target in ((1, 0), (group - 2, group - 1))
            ]
            groups.append(permute(turned[2], pairs))
        return groups

    def shift(value, step, parity=None, k=None):
        def sent(m):
            if not relay or k is None:
                return True
            edge = {1: 0, group - 1: group - 1}
            return m in edge.values() if k == group else edge.get(k) != m

        pairs = [
            (place(d, m), place(d + step, m))
            for d in range(depths)
            for m in ranks
            if 0 <= d + step < depths and (parity is None or d % 2 == parity) and sent(m)
        ]
        return permute(value, pairs)

    def mats(count, tables=0):
        return jax.ShapeDtypeStruct((count * n + tables * ROWS, n), f32)

    def sds(*shape, dtype=f32):
        return jax.ShapeDtypeStruct(shape, dtype)

    plain = 2 * slots
    stage = VMEM((plain * n, n), f32)

    def tables(count):
        return [SMEM((count, ROWS, LANES), f32), pltpu.SemaphoreType.DMA((count,))]

    operator_shapes = (sds(group * modes, 3 * n, n, dtype=bf16), sds(group * modes, n, 3 * n, dtype=bf16))
    couplings = coupling.reshape(modes * n, n)

    packed, own_table = call(
        pack_kernel,
        (mats(plain + modes, 1), sds(ROWS, n)),
        PACK_LIMIT,
        (live_slots, parent_index, bath_mode, damping, link_weight, correlation, blocks.reshape(plain * n, n), couplings),
        smem=6,
    )
    first = gather(packed, 1)
    near_table = shift(own_table, -1)
    powers = call(
        powers_kernel, (sds(3 * n, ORDER * n, dtype=bf16), sds(n, 3 * ORDER * n, dtype=bf16)), limit, (hamiltonian,)
    )
    *operators_odd, raw = call(
        functools.partial(operators_kernel, slots, group, modes, None),
        (*operator_shapes, mats((group - 1) * modes)),
        limit,
        (couplings, *first),
    )

    def free(groups, k, parity, times):
        sources = [groups[k]]
        if len(groups) == group + 1 and k in (1, group - 1):
            sources.append(groups[group])
        return call(
            functools.partial(free_kernel, parity, times, slots, group, k),
            mats(plain),
            limit,
            (*powers, *sources),
            us=4.7 * times,
        )

    def send(groups, sender, sum_parts, pick_parts, operators):
        shapes = [mats(plain // sum_parts)] * sum_parts + [mats(plain // pick_parts)] * pick_parts
        outs = call(
            functools.partial(send_kernel, sender, slots, group, modes, sum_parts, pick_parts),
            [*shapes, sds(group, ROWS, n)],
            limit,
            (near_table, *operators, *groups),
            us=2,
            scratch=[stage, stage, SMEM((total,), jnp.int32), *tables(group + 1)],
        )
        return outs[:sum_parts], outs[sum_parts:-1], outs[-1]

    def join(frees, sums, picks, receiver, operators):
        return call(
            functools.partial(join_kernel, receiver, slots, modes, len(sums), len(picks)),
            mats(plain) if len(frees) > 1 else mats(plain, 1),
            limit,
            (own_table, *operators, *frees, *sums, *picks),
            scratch=tables(1),
        )

    def side(kind, bases, groups, tabs, receiver, operators):
        second = len(bases) == 1
        halves = 2 if group % 2 == 0 else 1
        return call(
            functools.partial(side_kernel, kind, receiver, slots, group, modes, len(bases), len(groups), len(tabs)),
            [mats(2 * total // halves, group // halves)] * halves if second else [mats(2 * total), sds(group, ROWS, n)],
            limit,
            (*operators, *bases, *groups, *tabs),
            us=3,
            scratch=[stage, *tables(2 * group if kind == "children" else group)],
        )

    free_even = free([packed], 0, 0, 1)
    free_odd = [free(first, k, 1, 2) for k in ranks]
    sums, picks, tabs_odd = send(first, 1, 1, split_hop, operators_odd)
    picks = [shift(value, 1, 1) for value in picks]
    sums = [shift(value, -1, 1) for value in sums]
    own_state = join([free_even], sums, picks, 0, operators_odd)

    gathered = gather(own_state, 0)
    from_below = [shift(value, -1, 0, k) for k, value in enumerate(gathered)]
    from_above = [shift(value, 1, 0, k) for k, value in enumerate(gathered)]
    free_even = [free(gathered, k, 0, 2) for k in ranks]
    states, _ = side("parents", free_odd, from_above, [tabs_odd], 1, operators_odd)
    states = side("children", [states], from_below, [tabs_odd], 1, operators_odd)

    from_above = [shift(value, 1, 1) for value in states]
    from_below = [shift(value, -1, 1) for value in states]
    passed = shift(raw, -1, 1)
    operators_even = call(
        functools.partial(operators_kernel, slots, group, modes, 0), operator_shapes, limit, (couplings, passed)
    )
    last_odd = free(states[:1], 0, 1, 2)
    states, tabs_even = side("children", free_even, from_below, gathered, 0, operators_even)
    states = side("parents", [states], from_above, [tabs_even], 0, operators_even)

    sums, picks, _ = send(states, 0, split_hop, 1, operators_even)
    sums = [shift(value, -1, 0) for value in sums]
    picks = [shift(value, 1, 0) for value in picks]
    last_even = free(states[:1], 0, 0, 1)
    return join([last_odd, last_even], sums, picks, 1, operators_odd).reshape(blocks.shape)


def solution(mesh):
    sizes = (mesh.shape["depth"], mesh.shape["mode"])

    def whole(*args):
        return shards(sizes, *args)

    return jax.shard_map(
        whole,
        mesh=mesh,
        in_specs=(
            P(("depth", "mode"), None, None, None),
            P(("depth", "mode")),
            P(("depth", "mode")),
            P(("depth", "mode")),
            P(),
            P("mode", None, None),
            P("mode", None),
            P(("depth", "mode")),
            P(("depth", "mode")),
        ),
        out_specs=P(("depth", "mode"), None, None, None),
        check_vma=False,
    )
```

time: 182 us -> 174 us (0.956)
  the two profiles are of different devices: /device:TPU:11 before, /device:TPU:3 now
where the time goes in v1:
time: 174 us; the launch traced here: 173 us
  waiting for transfers between devices  67.6 us (39%)
  Pallas kernels  59.6 us (34%)
  starting transfers between devices  45.3 us (26%)
    ppermute x30, waiting for transfers between devices, permute(): return lax.ppermute(value, AXES, pairs)  67.6 us
    pallas_call x23, Pallas kernels, call(): pl.pallas_call(kernel, out_shape=out_shapes, in_specs=specs, out_specs=ja...  59.6 us
    ppermute x30, starting transfers between devices, permute(): return lax.ppermute(value, AXES, pairs)  45.3 us
  transfers between devices with their start and end apart: 30, of which 10 were waited for; matrix products, arithmetic and copies ran while one was open for 0% of the time, Pallas kernels for 27%

profile of v1, /device:TPU:3, one launch (start us, length us, event | category | flops | bytes accessed | tf_op | source)
XLA Modules:
  0.0 173.3 jit_solution(4841214513780366761)
XLA Ops:
  0.0 2.0 %shard_map.91 = (f32[1288,128]{1,0:T(8,128)}, f32[8,128]{1,0:T(8,128)}) custom-call(s32[4]{0:T(128)} %live_ref.1, s32[4]{0:T(128)} %parent_ref.1, s32[4]{0:T(128)} %mode_ref.1, f32[4]{0:T(128)} %damping_ref.1, f32[4]{0:T(128)} %weight_ref.1, f32[2,2]{1,0:T(2,128)} %corr_ref.1, f32[1024,128]{1,0:T(8,128)} %bitcast.6, f32[256,128]{1,0:T(8,128)} %bitcast.3), custom_call_target="tpu_custom_call" | custom-call | flops 1100000000 | bytes 524288 | tf_op jit(solution)/shard_map/pallas_call | solution.py:478
  2.0 4.2 %collective-permute-start.1 = (f32[1288,128]{1,0:T(8,128)}, f32[1288,128]{1,0:T(8,128)S(1)}, u32[]{:S(2)}, u32[]{:S(2)}) collective-permute-start(f32[1288,128]{1,0:T(8,128)} %get-tuple-element.29.refs_0_), channel_id=1, source_target_pairs={{4,6},{5,7},{6,4},{7,5},{12,14},{13,15},{14,12},{15,13},{20,22},{2... | collective-permute-start | bytes 1978376 | tf_op jit(solution)/shard_map/ppermute | solution.py:512
  6.2 3.2 %collective-permute-start = (f32[1288,128]{1,0:T(8,128)}, f32[1288,128]{1,0:T(8,128)S(1)}, u32[]{:S(2)}, u32[]{:S(2)}) collective-permute-start(f32[1288,128]{1,0:T(8,128)} %get-tuple-element.29.refs_0_), channel_id=1, source_target_pairs={{4,5},{5,6},{6,7},{12,13},{13,14},{14,15},{20,21},{21,22},{22,23},... | collective-permute-start | bytes 1978376 | tf_op jit(solution)/shard_map/ppermute | solution.py:512
  9.5 1.3 collective-permute-start.2
  10.8 2.1 %collective-permute-start.4 = (f32[8,128]{1,0:T(8,128)}, f32[8,128]{1,0:T(8,128)S(1)}, u32[]{:S(2)}, u32[]{:S(2)}) collective-permute-start(f32[8,128]{1,0:T(8,128)} %get-tuple-element.28.own_ref), channel_id=1, source_target_pairs={{4,0},{5,1},{6,2},{7,3},{8,4},{9,5},{10,6},{11,7},{12,8},{13,9},{1... | collective-permute-start | bytes 12296 | tf_op jit(solution)/shard_map/ppermute | solution.py:512
  12.8 0.7 shard_map.93
  13.6 8.1 %collective-permute-done.1.refs_2_.refs_0_ = f32[1288,128]{1,0:T(8,128)S(1)} collective-permute-done((f32[1288,128]{1,0:T(8,128)}, f32[1288,128]{1,0:T(8,128)S(1)}, u32[]{:S(2)}, u32[]{:S(2)}) %collective-permute-start.1) | collective-permute-done | bytes 659488 | tf_op jit(solution)/shard_map/ppermute | solution.py:512
  21.6 1.3 collective-permute-start.3
  22.9 8.2 %shard_map.94.refs_0_ = f32[1024,128]{1,0:T(8,128)S(1)} custom-call(bf16[384,512]{1,0:T(8,128)(2,1)S(1)} %get-tuple-element.32.right_ref, bf16[128,1536]{1,0:T(8,128)(2,1)S(1)} %get-tuple-element.33.left_ref, f32[1288,128]{1,0:T(8,128)S(1)} %copy-done.1), custom_call_target="tpu_custom_call" | custom-call | flops 10339999744 | bytes 524288 | tf_op jit(solution)/shard_map/pallas_call | solution.py:478
  31.2 0.0 copy-start.2
  31.2 0.0 collective-permute-done.2.refs_3_.refs_0_
  31.2 2.8 %collective-permute-done.3.refs_4_.refs_1_ = f32[1288,128]{1,0:T(8,128)S(1)} collective-permute-done((f32[1288,128]{1,0:T(8,128)S(1)}, f32[1288,128]{1,0:T(8,128)S(1)}, u32[]{:S(2)}, u32[]{:S(2)}) %collective-permute-start.3) | collective-permute-done | bytes 659488 | tf_op jit(solution)/shard_map/ppermute | solution.py:512
  34.1 0.4 shard_map.92
  34.5 0.0 collective-permute-done.4.near_ref
  34.5 3.1 %shard_map.99 = (f32[1024,128]{1,0:T(8,128)S(1)}, f32[512,128]{1,0:T(8,128)S(1)}, f32[512,128]{1,0:T(8,128)S(1)}, f32[4,8,128]{2,1,0:T(8,128)S(1)}) custom-call(f32[8,128]{1,0:T(8,128)S(1)} %collective-permute-done.4.near_ref, bf16[8,384,128]{2,1,0:T(8,128)(2,1)S(1)} %get-tuple-element.30.right_ref, bf16[8,128,384]{2,1,0:T(8,128)(2,1)S(1)} %get-tuple-element.31.left_ref, ...), custom_call_target="tpu_custom_call" | custom-call | flops 2200000000 | bytes 524288 | tf_op jit(solution)/shard_map/pallas_call | solution.py:478
  37.6 1.3 collective-permute-start.5
  38.9 1.3 collective-permute-start.6
  40.3 0.0 copy-start
  40.3 1.3 collective-permute-start.7
  41.6 8.2 %shard_map.96.refs_2_ = f32[1024,128]{1,0:T(8,128)S(1)} custom-call(bf16[384,512]{1,0:T(8,128)(2,1)S(1)} %get-tuple-element.32.right_ref, bf16[128,1536]{1,0:T(8,128)(2,1)S(1)} %get-tuple-element.33.left_ref, f32[1288,128]{1,0:T(8,128)S(1)} %collective-permute-done.1.refs_2_.refs_0_), custom_call_target="tpu_custom_call" | custom-call | flops 10339999744 | bytes 524288 | tf_op jit(solution)/shard_map/pallas_call | solution.py:478
  49.8 1.3 collective-permute-start.22
  51.1 0.0 collective-permute-done.6.refs_2_
  51.2 0.0 collective-permute-done.5.refs_1_
  51.2 0.7 collective-permute-start.11
  51.9 8.3 %shard_map.95.refs_1_ = f32[1024,128]{1,0:T(8,128)S(1)} custom-call(bf16[384,512]{1,0:T(8,128)(2,1)S(1)} %get-tuple-element.32.right_ref, bf16[128,1536]{1,0:T(8,128)(2,1)S(1)} %get-tuple-element.33.left_ref, f32[1288,128]{1,0:T(8,128)S(1)} %collective-permute-done.refs_1_.refs_0_, f32[1288,128]{1,0:T(8,128)S(1)} %collective-permute-done.3.refs_4_.refs_1_), custom_call_target="tpu_custom_call" | custom-call | flops 10339999744 | bytes 524288 | tf_op jit(solution)/shard_map/pallas_call | solution.py:478
  60.2 0.7 collective-permute-start.9
  60.9 0.7 collective-permute-start.13
  61.6 0.0 collective-permute-done.11.refs_0_.refs_8_
  61.6 0.7 collective-permute-start.15
  62.3 8.2 %shard_map.97.refs_3_ = f32[1024,128]{1,0:T(8,128)S(1)} custom-call(bf16[384,512]{1,0:T(8,128)(2,1)S(1)} %get-tuple-element.32.right_ref, bf16[128,1536]{1,0:T(8,128)(2,1)S(1)} %get-tuple-element.33.left_ref, f32[1288,128]{1,0:T(8,128)S(1)} %collective-permute-done.2.refs_3_.refs_0_, f32[1288,128]{1,0:T(8,128)S(1)} %collective-permute-done.3.refs_4_.refs_1_), custom_call_target="tpu_custom_call" | custom-call | flops 10339999744 | bytes 524288 | tf_op jit(solution)/shard_map/pallas_call | solution.py:478
  70.5 0.0 collective-permute-done.22.refs_0_
  70.6 1.3 collective-permute-start.8
  71.9 1.3 collective-permute-start.12
  73.2 0.7 collective-permute-start.10
  73.9 1.3 collective-permute-start.14
  75.2 0.0 collective-permute-done.15.refs_1_.refs_10_
  75.2 1.3 collective-permute-start.16
  76.5 1.3 collective-permute-start.17
  77.8 0.7 collective-permute-start.18
  78.6 1.3 collective-permute-start.19
  79.9 1.3 collective-permute-start.20
  81.2 1.3 collective-permute-start.21
  82.5 0.2 shard_map.107.refs_2_
  82.7 4.7 %shard_map.101 = (f32[4096,128]{1,0:T(8,128)S(1)}, f32[4,8,128]{2,1,0:T(8,128)}) custom-call(bf16[8,384,128]{2,1,0:T(8,128)(2,1)S(1)} %get-tuple-element.30.right_ref, bf16[8,128,384]{2,1,0:T(8,128)(2,1)S(1)} %get-tuple-element.31.left_ref, f32[1024,128]{1,0:T(8,128)S(1)} %shard_map.94.refs_0_, f32[1024,128]{1,0:T(8,128)S(1)} %shard_map.95.refs_1_, ...), custom_call_target="tpu_custom_call" | custom-call | flops 3300000000 | bytes 524288 | tf_op jit(solution)/shard_map/pallas_call | solution.py:478
  87.4 9.4 %collective-permute-done.17.refs_1_ = f32[1032,128]{1,0:T(8,128)S(1)} collective-permute-done((f32[1032,128]{1,0:T(8,128)S(1)}, f32[1032,128]{1,0:T(8,128)S(1)}, u32[]{:S(2)}, u32[]{:S(2)}) %collective-permute-start.17) | collective-permute-done | bytes 528416 | tf_op jit(solution)/shard_map/ppermute | solution.py:512
  96.8 5.7 %collective-permute-done.19.refs_3_ = f32[1032,128]{1,0:T(8,128)S(1)} collective-permute-done((f32[1032,128]{1,0:T(8,128)S(1)}, f32[1032,128]{1,0:T(8,128)S(1)}, u32[]{:S(2)}, u32[]{:S(2)}) %collective-permute-start.19) | collective-permute-done | bytes 528416 | tf_op jit(solution)/shard_map/ppermute | solution.py:512
  102.4 5.7 %collective-permute-done.20.refs_4_ = f32[1032,128]{1,0:T(8,128)S(1)} collective-permute-done((f32[1032,128]{1,0:T(8,128)S(1)}, f32[1032,128]{1,0:T(8,128)S(1)}, u32[]{:S(2)}, u32[]{:S(2)}) %collective-permute-start.20) | collective-permute-done | bytes 528416 | tf_op jit(solution)/shard_map/ppermute | solution.py:512
  108.1 5.7 %collective-permute-done.21.refs_5_ = f32[1032,128]{1,0:T(8,128)S(1)} collective-permute-done((f32[1032,128]{1,0:T(8,128)S(1)}, f32[1032,128]{1,0:T(8,128)S(1)}, u32[]{:S(2)}, u32[]{:S(2)}) %collective-permute-start.21) | collective-permute-done | bytes 528416 | tf_op jit(solution)/shard_map/ppermute | solution.py:512
  113.8 4.4 %shard_map.102 = (f32[2064,128]{1,0:T(8,128)S(1)}, f32[2064,128]{1,0:T(8,128)S(1)}) custom-call(bf16[8,384,128]{2,1,0:T(8,128)(2,1)S(1)} %get-tuple-element.30.right_ref, bf16[8,128,384]{2,1,0:T(8,128)(2,1)S(1)} %get-tuple-element.31.left_ref, f32[4096,128]{1,0:T(8,128)S(1)} %get-tuple-element.38.refs_0_, f32[1032,128]{1,0:T(8,128)S(1)} %collective-permute-done.17.refs_1_, ...), custom_call_target="tpu_custom_call" | custom-call | flops 3300000000 | bytes 524288 | tf_op jit(solution)/shard_map/pallas_call | solution.py:478
  118.2 1.4 collective-permute-start.23
  119.6 1.4 collective-permute-start.24
  121.0 5.5 %collective-permute-start.25 = (f32[2064,128]{1,0:T(8,128)S(1)}, f32[2064,128]{1,0:T(8,128)S(1)}, u32[]{:S(2)}, u32[]{:S(2)}) collective-permute-start(f32[2064,128]{1,0:T(8,128)S(1)} %get-tuple-element.39.refs_0_), channel_id=1, source_target_pairs={{4,8},{5,9},{6,10},{7,11},{12,16},{13,17},{14,18},{15,19},{20,24},... | collective-permute-start | bytes 3170312 | tf_op jit(solution)/shard_map/ppermute | solution.py:512
  126.5 1.4 collective-permute-start.26
  127.9 0.1 shard_map.109
  128.0 10.2 %collective-permute-done.25.refs_1_ = f32[2064,128]{1,0:T(8,128)S(1)} collective-permute-done((f32[2064,128]{1,0:T(8,128)S(1)}, f32[2064,128]{1,0:T(8,128)S(1)}, u32[]{:S(2)}, u32[]{:S(2)}) %collective-permute-start.25) | collective-permute-done | bytes 1056800 | tf_op jit(solution)/shard_map/ppermute | solution.py:512
  138.2 11.3 %collective-permute-done.26.refs_2_ = f32[2064,128]{1,0:T(8,128)S(1)} collective-permute-done((f32[2064,128]{1,0:T(8,128)S(1)}, f32[2064,128]{1,0:T(8,128)S(1)}, u32[]{:S(2)}, u32[]{:S(2)}) %collective-permute-start.26) | collective-permute-done | bytes 1056800 | tf_op jit(solution)/shard_map/ppermute | solution.py:512
  149.6 0.7 shard_map.112
  150.3 1.3 collective-permute-start.29
  151.6 8.2 %shard_map.103.refs_0_ = f32[1024,128]{1,0:T(8,128)S(1)} custom-call(bf16[384,512]{1,0:T(8,128)(2,1)S(1)} %get-tuple-element.32.right_ref, bf16[128,1536]{1,0:T(8,128)(2,1)S(1)} %get-tuple-element.33.left_ref, f32[2064,128]{1,0:T(8,128)S(1)} %get-tuple-element.39.refs_0_), custom_call_target="tpu_custom_call" | custom-call | flops 10339999744 | bytes 524288 | tf_op jit(solution)/shard_map/pallas_call | solution.py:478
  159.8 1.3 collective-permute-start.27
  161.1 1.3 collective-permute-start.28
  162.4 6.0 %collective-permute-done.27.refs_2_ = f32[512,128]{1,0:T(8,128)S(1)} collective-permute-done((f32[512,128]{1,0:T(8,128)S(1)}, f32[512,128]{1,0:T(8,128)S(1)}, u32[]{:S(2)}, u32[]{:S(2)}) %collective-permute-start.27) | collective-permute-done | bytes 262176 | tf_op jit(solution)/shard_map/ppermute | solution.py:512
  168.4 2.8 %collective-permute-done.28.refs_3_ = f32[512,128]{1,0:T(8,128)S(1)} collective-permute-done((f32[512,128]{1,0:T(8,128)S(1)}, f32[512,128]{1,0:T(8,128)S(1)}, u32[]{:S(2)}, u32[]{:S(2)}) %collective-permute-start.28) | collective-permute-done | bytes 262176 | tf_op jit(solution)/shard_map/ppermute | solution.py:512
  171.2 1.9 %shard_map.113 = f32[1024,128]{1,0:T(8,128)} custom-call(f32[8,128]{1,0:T(8,128)S(1)} %copy-done, bf16[8,384,128]{2,1,0:T(8,128)(2,1)S(1)} %get-tuple-element.30.right_ref, bf16[8,128,384]{2,1,0:T(8,128)(2,1)S(1)} %get-tuple-element.31.left_ref, f32[1024,128]{1,0:T(8,128)S(1)} %shard_map.103.refs_0_, f32[1024,128]{1,0:T(8,128)S(1)} %shard_map.111.refs_1_, ...), custom_call_target="tpu_custom_call" | custom-call | flops 1100000000 | bytes 524288 | tf_op jit(solution)/shard_map/pallas_call | solution.py:478
  (27 shorter events, 0.2 us)
Async XLA Ops:
  0.0 12.8 %copy-start.3 = (f32[128,128]{1,0:T(8,128)S(1)}, f32[128,128]{1,0:T(8,128)}, u32[]{:S(2)}) copy-start(f32[128,128]{1,0:T(8,128)} %ham_ref.1) | copy-start | bytes 196612
  2.0 19.6 %collective-permute-start.1 = (f32[1288,128]{1,0:T(8,128)}, f32[1288,128]{1,0:T(8,128)S(1)}, u32[]{:S(2)}, u32[]{:S(2)}) collective-permute-start(f32[1288,128]{1,0:T(8,128)} %get-tuple-element.29.refs_0_), channel_id=1, source_target_pairs={{4,6},{5,7},{6,4},{7,5},{12,14},{13,15},{14,12},{15,13},{20,22},{2... | collective-permute-start | bytes 1978376 | tf_op jit(solution)/shard_map/ppermute | solution.py:512
  6.2 25.0 %collective-permute-start = (f32[1288,128]{1,0:T(8,128)}, f32[1288,128]{1,0:T(8,128)S(1)}, u32[]{:S(2)}, u32[]{:S(2)}) collective-permute-start(f32[1288,128]{1,0:T(8,128)} %get-tuple-element.29.refs_0_), channel_id=1, source_target_pairs={{4,5},{5,6},{6,7},{12,13},{13,14},{14,15},{20,21},{21,22},{22,23},... | collective-permute-start | bytes 1978376 | tf_op jit(solution)/shard_map/ppermute | solution.py:512
  9.5 21.8 %collective-permute-start.2 = (f32[1288,128]{1,0:T(8,128)}, f32[1288,128]{1,0:T(8,128)S(1)}, u32[]{:S(2)}, u32[]{:S(2)}) collective-permute-start(f32[1288,128]{1,0:T(8,128)} %get-tuple-element.29.refs_0_), channel_id=1, source_target_pairs={{5,4},{6,5},{7,6},{13,12},{14,13},{15,14},{21,20},{22,21},{23,22},... | collective-permute-start | bytes 1978376 | tf_op jit(solution)/shard_map/ppermute | solution.py:512
  10.8 12.2 %copy-start.1 = (f32[1288,128]{1,0:T(8,128)S(1)}, f32[1288,128]{1,0:T(8,128)}, u32[]{:S(2)}) copy-start(f32[1288,128]{1,0:T(8,128)} %get-tuple-element.29.refs_0_) | copy-start | bytes 1978372
  10.8 23.7 %collective-permute-start.4 = (f32[8,128]{1,0:T(8,128)}, f32[8,128]{1,0:T(8,128)S(1)}, u32[]{:S(2)}, u32[]{:S(2)}) collective-permute-start(f32[8,128]{1,0:T(8,128)} %get-tuple-element.28.own_ref), channel_id=1, source_target_pairs={{4,0},{5,1},{6,2},{7,3},{8,4},{9,5},{10,6},{11,7},{12,8},{13,9},{1... | collective-permute-start | bytes 12296 | tf_op jit(solution)/shard_map/ppermute | solution.py:512
  21.6 12.4 %collective-permute-start.3 = (f32[1288,128]{1,0:T(8,128)S(1)}, f32[1288,128]{1,0:T(8,128)S(1)}, u32[]{:S(2)}, u32[]{:S(2)}) collective-permute-start(f32[1288,128]{1,0:T(8,128)S(1)} %collective-permute-done.1.refs_2_.refs_0_), channel_id=1, source_target_pairs={{5,4},{6,7},{13,12},{14,15},{21,20},{22,23},{29,28},{30,31}} | collective-permute-start | bytes 1978376 | tf_op jit(solution)/shard_map/ppermute | solution.py:512
  31.2 2.9 %copy-start.2 = (f32[2,128,128]{2,1,0:T(8,128)S(1)}, f32[2,128,128]{2,1,0:T(8,128)}, u32[]{:S(2)}) copy-start(f32[2,128,128]{2,1,0:T(8,128)} %param.14) | copy-start | bytes 393220
  37.6 13.6 %collective-permute-start.5 = (f32[1024,128]{1,0:T(8,128)S(1)}, f32[1024,128]{1,0:T(8,128)S(1)}, u32[]{:S(2)}, u32[]{:S(2)}) collective-permute-start(f32[1024,128]{1,0:T(8,128)S(1)} %get-tuple-element.34), channel_id=1, source_target_pairs={{4,0},{5,1},{6,2},{7,3},{12,8},{13,9},{14,10},{15,11},{20,16},{21,... | collective-permute-start | bytes 1572872 | tf_op jit(solution)/shard_map/ppermute | solution.py:512
  38.9 12.2 %collective-permute-start.6 = (f32[512,128]{1,0:T(8,128)S(1)}, f32[512,128]{1,0:T(8,128)S(1)}, u32[]{:S(2)}, u32[]{:S(2)}) collective-permute-start(f32[512,128]{1,0:T(8,128)S(1)} %get-tuple-element.35), channel_id=1, source_target_pairs={{4,8},{5,9},{6,10},{7,11},{12,16},{13,17},{14,18},{15,19},{20,24},... | collective-permute-start | bytes 786440 | tf_op jit(solution)/shard_map/ppermute | solution.py:512
  40.3 10.9 %copy-start = (f32[8,128]{1,0:T(8,128)S(1)}, f32[8,128]{1,0:T(8,128)}, u32[]{:S(2)}) copy-start(f32[8,128]{1,0:T(8,128)} %get-tuple-element.28.own_ref) | copy-start | bytes 12292
  40.3 10.9 %collective-permute-start.7 = (f32[512,128]{1,0:T(8,128)S(1)}, f32[512,128]{1,0:T(8,128)S(1)}, u32[]{:S(2)}, u32[]{:S(2)}) collective-permute-start(f32[512,128]{1,0:T(8,128)S(1)} %get-tuple-element.36), channel_id=1, source_target_pairs={{4,8},{5,9},{6,10},{7,11},{12,16},{13,17},{14,18},{15,19},{20,24},... | collective-permute-start | bytes 786440 | tf_op jit(solution)/shard_map/ppermute | solution.py:512
  49.8 20.7 %collective-permute-start.22 = (f32[768,128]{1,0:T(8,128)S(1)}, f32[768,128]{1,0:T(8,128)S(1)}, u32[]{:S(2)}, u32[]{:S(2)}) collective-permute-start(f32[768,128]{1,0:T(8,128)S(1)} %get-tuple-element.40), channel_id=1, source_target_pairs={{4,0},{5,1},{6,2},{7,3},{12,8},{13,9},{14,10},{15,11},{20,16},{21,... | collective-permute-start | bytes 1179656 | tf_op jit(solution)/shard_map/ppermute | solution.py:512
  51.2 10.4 %collective-permute-start.11 = (f32[1032,128]{1,0:T(8,128)S(1)}, f32[1032,128]{1,0:T(8,128)S(1)}, u32[]{:S(2)}, u32[]{:S(2)}) collective-permute-start(f32[1032,128]{1,0:T(8,128)S(1)} %shard_map.100.refs_0_.refs_6_), channel_id=1, source_target_pairs={{0,2},{1,3},{2,0},{3,1},{8,10},{9,11},{10,8},{11,9},{16,18},{17,19... | collective-permute-start | bytes 1585160 | tf_op jit(solution)/shard_map/ppermute | solution.py:512
  60.2 13.0 %collective-permute-start.9 = (f32[1032,128]{1,0:T(8,128)S(1)}, f32[1032,128]{1,0:T(8,128)S(1)}, u32[]{:S(2)}, u32[]{:S(2)}) collective-permute-start(f32[1032,128]{1,0:T(8,128)S(1)} %shard_map.100.refs_0_.refs_6_), channel_id=1, source_target_pairs={{0,1},{1,2},{2,3},{8,9},{9,10},{10,11},{16,17},{17,18},{18,19},{24... | collective-permute-start | bytes 1585160 | tf_op jit(solution)/shard_map/ppermute | solution.py:512
  60.9 13.0 %collective-permute-start.13 = (f32[1032,128]{1,0:T(8,128)S(1)}, f32[1032,128]{1,0:T(8,128)S(1)}, u32[]{:S(2)}, u32[]{:S(2)}) collective-permute-start(f32[1032,128]{1,0:T(8,128)S(1)} %shard_map.100.refs_0_.refs_6_), channel_id=1, source_target_pairs={{1,0},{2,1},{3,2},{9,8},{10,9},{11,10},{17,16},{18,17},{19,18},{25... | collective-permute-start | bytes 1585160 | tf_op jit(solution)/shard_map/ppermute | solution.py:512
  61.6 13.6 %collective-permute-start.15 = (f32[1032,128]{1,0:T(8,128)S(1)}, f32[1032,128]{1,0:T(8,128)S(1)}, u32[]{:S(2)}, u32[]{:S(2)}) collective-permute-start(f32[1032,128]{1,0:T(8,128)S(1)} %collective-permute-done.11.refs_0_.refs_8_), channel_id=1, source_target_pairs={{1,0},{2,3},{9,8},{10,11},{17,16},{18,19},{25,24},{26,27}} | collective-permute-start | bytes 1585160 | tf_op jit(solution)/shard_map/ppermute | solution.py:512
  70.6 6.0 %collective-permute-start.8 = (f32[1032,128]{1,0:T(8,128)S(1)}, f32[1032,128]{1,0:T(8,128)S(1)}, u32[]{:S(2)}, u32[]{:S(2)}) collective-permute-start(f32[1032,128]{1,0:T(8,128)S(1)} %shard_map.100.refs_0_.refs_6_), channel_id=1, source_target_pairs={{0,4},{1,5},{2,6},{3,7},{8,12},{9,13},{10,14},{11,15},{16,20},{17,... | collective-permute-start | bytes 1585160 | tf_op jit(solution)/shard_map/ppermute | solution.py:512
  71.9 6.7 %collective-permute-start.12 = (f32[1032,128]{1,0:T(8,128)S(1)}, f32[1032,128]{1,0:T(8,128)S(1)}, u32[]{:S(2)}, u32[]{:S(2)}) collective-permute-start(f32[1032,128]{1,0:T(8,128)S(1)} %collective-permute-done.11.refs_0_.refs_8_), channel_id=1, source_target_pairs={{0,4},{1,5},{2,6},{3,7},{8,12},{9,13},{10,14},{11,15},{16,20},{17,... | collective-permute-start | bytes 1585160 | tf_op jit(solution)/shard_map/ppermute | solution.py:512
  73.2 4.7 %collective-permute-start.10 = (f32[1032,128]{1,0:T(8,128)S(1)}, f32[1032,128]{1,0:T(8,128)S(1)}, u32[]{:S(2)}, u32[]{:S(2)}) collective-permute-start(f32[1032,128]{1,0:T(8,128)S(1)} %collective-permute-done.9.refs_0_.refs_7_), channel_id=1, source_target_pairs={{1,5},{2,6},{3,7},{9,13},{10,14},{11,15},{17,21},{18,22},{19,23},{... | collective-permute-start | bytes 1585160 | tf_op jit(solution)/shard_map/ppermute | solution.py:512
  73.9 6.0 %collective-permute-start.14 = (f32[1032,128]{1,0:T(8,128)S(1)}, f32[1032,128]{1,0:T(8,128)S(1)}, u32[]{:S(2)}, u32[]{:S(2)}) collective-permute-start(f32[1032,128]{1,0:T(8,128)S(1)} %collective-permute-done.13.refs_0_.refs_9_), channel_id=1, source_target_pairs={{0,4},{1,5},{2,6},{8,12},{9,13},{10,14},{16,20},{17,21},{18,22},{2... | collective-permute-start | bytes 1585160 | tf_op jit(solution)/shard_map/ppermute | solution.py:512
  75.2 6.0 %collective-permute-start.16 = (f32[1032,128]{1,0:T(8,128)S(1)}, f32[1032,128]{1,0:T(8,128)S(1)}, u32[]{:S(2)}, u32[]{:S(2)}) collective-permute-start(f32[1032,128]{1,0:T(8,128)S(1)} %collective-permute-done.15.refs_1_.refs_10_), channel_id=1, source_target_pairs={{0,4},{3,7},{8,12},{11,15},{16,20},{19,23},{24,28},{27,31}} | collective-permute-start | bytes 1585160 | tf_op jit(solution)/shard_map/ppermute | solution.py:512
  76.5 20.2 %collective-permute-start.17 = (f32[1032,128]{1,0:T(8,128)S(1)}, f32[1032,128]{1,0:T(8,128)S(1)}, u32[]{:S(2)}, u32[]{:S(2)}) collective-permute-start(f32[1032,128]{1,0:T(8,128)S(1)} %shard_map.100.refs_0_.refs_6_), channel_id=1, source_target_pairs={{8,4},{9,5},{10,6},{11,7},{16,12},{17,13},{18,14},{19,15},{24,20},... | collective-permute-start | bytes 1585160 | tf_op jit(solution)/shard_map/ppermute | solution.py:512
  77.8 18.9 %collective-permute-start.18 = (f32[1032,128]{1,0:T(8,128)S(1)}, f32[1032,128]{1,0:T(8,128)S(1)}, u32[]{:S(2)}, u32[]{:S(2)}) collective-permute-start(f32[1032,128]{1,0:T(8,128)S(1)} %collective-permute-done.9.refs_0_.refs_7_), channel_id=1, source_target_pairs={{9,5},{10,6},{11,7},{17,13},{18,14},{19,15},{25,21},{26,22},{27,23}} | collective-permute-start | bytes 1585160 | tf_op jit(solution)/shard_map/ppermute | solution.py:512
  78.6 23.9 %collective-permute-start.19 = (f32[1032,128]{1,0:T(8,128)S(1)}, f32[1032,128]{1,0:T(8,128)S(1)}, u32[]{:S(2)}, u32[]{:S(2)}) collective-permute-start(f32[1032,128]{1,0:T(8,128)S(1)} %collective-permute-done.11.refs_0_.refs_8_), channel_id=1, source_target_pairs={{8,4},{9,5},{10,6},{11,7},{16,12},{17,13},{18,14},{19,15},{24,20},... | collective-permute-start | bytes 1585160 | tf_op jit(solution)/shard_map/ppermute | solution.py:512
  79.9 28.2 %collective-permute-start.20 = (f32[1032,128]{1,0:T(8,128)S(1)}, f32[1032,128]{1,0:T(8,128)S(1)}, u32[]{:S(2)}, u32[]{:S(2)}) collective-permute-start(f32[1032,128]{1,0:T(8,128)S(1)} %collective-permute-done.13.refs_0_.refs_9_), channel_id=1, source_target_pairs={{8,4},{9,5},{10,6},{16,12},{17,13},{18,14},{24,20},{25,21},{26,22}} | collective-permute-start | bytes 1585160 | tf_op jit(solution)/shard_map/ppermute | solution.py:512
  81.2 32.6 %collective-permute-start.21 = (f32[1032,128]{1,0:T(8,128)S(1)}, f32[1032,128]{1,0:T(8,128)S(1)}, u32[]{:S(2)}, u32[]{:S(2)}) collective-permute-start(f32[1032,128]{1,0:T(8,128)S(1)} %collective-permute-done.15.refs_1_.refs_10_), channel_id=1, source_target_pairs={{8,4},{11,7},{16,12},{19,15},{24,20},{27,23}} | collective-permute-start | bytes 1585160 | tf_op jit(solution)/shard_map/ppermute | solution.py:512
  118.2 9.6 %collective-permute-start.23 = (f32[2064,128]{1,0:T(8,128)S(1)}, f32[2064,128]{1,0:T(8,128)S(1)}, u32[]{:S(2)}, u32[]{:S(2)}) collective-permute-start(f32[2064,128]{1,0:T(8,128)S(1)} %get-tuple-element.39.refs_0_), channel_id=1, source_target_pairs={{4,0},{5,1},{6,2},{7,3},{12,8},{13,9},{14,10},{15,11},{20,16},{21,... | collective-permute-start | bytes 3170312 | tf_op jit(solution)/shard_map/ppermute | solution.py:512
  119.6 8.3 %collective-permute-start.24 = (f32[2064,128]{1,0:T(8,128)S(1)}, f32[2064,128]{1,0:T(8,128)S(1)}, u32[]{:S(2)}, u32[]{:S(2)}) collective-permute-start(f32[2064,128]{1,0:T(8,128)S(1)} %get-tuple-element.43), channel_id=1, source_target_pairs={{4,0},{5,1},{6,2},{7,3},{12,8},{13,9},{14,10},{15,11},{20,16},{21,... | collective-permute-start | bytes 3170312 | tf_op jit(solution)/shard_map/ppermute | solution.py:512
  121.0 17.2 %collective-permute-start.25 = (f32[2064,128]{1,0:T(8,128)S(1)}, f32[2064,128]{1,0:T(8,128)S(1)}, u32[]{:S(2)}, u32[]{:S(2)}) collective-permute-start(f32[2064,128]{1,0:T(8,128)S(1)} %get-tuple-element.39.refs_0_), channel_id=1, source_target_pairs={{4,8},{5,9},{6,10},{7,11},{12,16},{13,17},{14,18},{15,19},{20,24},... | collective-permute-start | bytes 3170312 | tf_op jit(solution)/shard_map/ppermute | solution.py:512
  126.5 23.1 %collective-permute-start.26 = (f32[2064,128]{1,0:T(8,128)S(1)}, f32[2064,128]{1,0:T(8,128)S(1)}, u32[]{:S(2)}, u32[]{:S(2)}) collective-permute-start(f32[2064,128]{1,0:T(8,128)S(1)} %get-tuple-element.43), channel_id=1, source_target_pairs={{4,8},{5,9},{6,10},{7,11},{12,16},{13,17},{14,18},{15,19},{20,24},... | collective-permute-start | bytes 3170312 | tf_op jit(solution)/shard_map/ppermute | solution.py:512
  150.3 20.9 %collective-permute-start.29 = (f32[1024,128]{1,0:T(8,128)S(1)}, f32[1024,128]{1,0:T(8,128)S(1)}, u32[]{:S(2)}, u32[]{:S(2)}) collective-permute-start(f32[1024,128]{1,0:T(8,128)S(1)} %get-tuple-element.50), channel_id=1, source_target_pairs={{0,4},{1,5},{2,6},{3,7},{8,12},{9,13},{10,14},{11,15},{16,20},{17,... | collective-permute-start | bytes 1572872 | tf_op jit(solution)/shard_map/ppermute | solution.py:512
  159.8 8.6 %collective-permute-start.27 = (f32[512,128]{1,0:T(8,128)S(1)}, f32[512,128]{1,0:T(8,128)S(1)}, u32[]{:S(2)}, u32[]{:S(2)}) collective-permute-start(f32[512,128]{1,0:T(8,128)S(1)} %get-tuple-element.48), channel_id=1, source_target_pairs={{8,4},{9,5},{10,6},{11,7},{16,12},{17,13},{18,14},{19,15},{24,20},... | collective-permute-start | bytes 786440 | tf_op jit(solution)/shard_map/ppermute | solution.py:512
  161.1 10.1 %collective-permute-start.28 = (f32[512,128]{1,0:T(8,128)S(1)}, f32[512,128]{1,0:T(8,128)S(1)}, u32[]{:S(2)}, u32[]{:S(2)}) collective-permute-start(f32[512,128]{1,0:T(8,128)S(1)} %get-tuple-element.49), channel_id=1, source_target_pairs={{8,4},{9,5},{10,6},{11,7},{16,12},{17,13},{18,14},{19,15},{24,20},... | collective-permute-start | bytes 786440 | tf_op jit(solution)/shard_map/ppermute | solution.py:512

commit v2 on v1

--- a/solution.py
+++ b/solution.py
@@ -102,57 +102,35 @@
     def __init__(self, refs, slots, group):
         self.refs, self.slots, self.group = refs, slots, group
         self.n = refs[0].shape[1]
-        self.relay = len(refs) == group + 1
-        self.held = 1 if self.relay else group // len(refs)
+        self.held = group // len(refs)
         self.size = 2 * slots * self.n
         self.stride = self.size + ROWS
 
-    def places(self, k):
-        if self.relay and k in (1, self.group - 1):
-            edge = lax.axis_index("mode") == (0 if k == 1 else self.group - 1)
-            return [(jnp.logical_not(edge), self.refs[k], 0), (edge, self.refs[-1], 0)]
-        return [(None, self.refs[k // self.held], (k % self.held) * self.stride)]
-
-    def each(self, k, body):
-        for condition, ref, base in self.places(k):
-            if condition is None:
-                body(ref, base)
-            else:
-                pl.when(condition)(functools.partial(body, ref, base))
+    def base(self, k):
+        return self.refs[k // self.held], (k % self.held) * self.stride
 
     def table(self, k):
-        return [
-            (condition, ref.at[pl.ds(base + self.size, ROWS), pl.ds(0, LANES)]) for condition, ref, base in self.places(k)
-        ]
+        ref, base = self.base(k)
+        return ref.at[pl.ds(base + self.size, ROWS), pl.ds(0, LANES)]
 
     def copy_table(self, k, target_ref, at):
-        def body(ref, base):
-            target_ref[at] = ref[pl.ds(base + self.size, ROWS)]
-
-        self.each(k, body)
+        ref, base = self.base(k)
+        target_ref[at] = ref[pl.ds(base + self.size, ROWS)]
 
     def fetch(self, index, stage_ref, at):
         for k in range(self.group):
+            ref, base = self.base(k)
             local = index - k * self.slots
-            inside = jnp.logical_and(local >= 0, local < self.slots)
-            for condition, ref, base in self.places(k):
-                here = inside if condition is None else jnp.logical_and(inside, condition)
-
-                @pl.when(here)
-                def _():
-                    stage_ref[rows(at * self.n, self.n, 2)] = ref[rows(base + 2 * local * self.n, self.n, 2)]
+
+            @pl.when(jnp.logical_and(local >= 0, local < self.slots))
+            def _():
+                stage_ref[rows(at * self.n, self.n, 2)] = ref[rows(base + 2 * local * self.n, self.n, 2)]
 
 
 def pull(sources, smem_ref, sem_ref):
-    copies = []
-    for i, source in enumerate(sources):
-        for condition, ref in source if isinstance(source, list) else [(None, source)]:
-            copy = pltpu.make_async_copy(ref, smem_ref.at[i], sem_ref.at[i])
-            if condition is None:
-                copy.start()
-            else:
-                pl.when(condition)(copy.start)
-        copies.append(copy)
+    copies = [pltpu.make_async_copy(ref, smem_ref.at[i], sem_ref.at[i]) for i, ref in enumerate(sources)]
+    for copy in copies:
+        copy.start()
     for copy in copies:
         copy.wait()
 
@@ -180,14 +158,11 @@
         own()
         groups = Layout(sources, slots, group)
         for k in range(1, group):
-
-            def body(ref, base, k=k):
-                for i in range(modes):
-                    value = ref[rows(base + groups.stride + i * n, n)]
-                    put(k * modes + i, value)
-                    outs[2][rows(((k - 1) * modes + i) * n, n)] = value
-
-            groups.each(k, body)
+            ref, base = groups.base(k)
+            for i in range(modes):
+                value = ref[rows(base + groups.stride + i * n, n)]
+                put(k * modes + i, value)
+                outs[2][rows(((k - 1) * modes + i) * n, n)] = value
     else:
 
         @pl.when(odd_depth() == parity)
@@ -231,30 +206,17 @@
     return u_real + done[:, :n], u_imag + done[:, n:]
 
 
-def free_kernel(run_parity, times, slots, group, k, right_ref, left_ref, *refs):
-    out_ref = refs[-1]
-    pair = 2 if slots % 2 == 0 else 1
+def free_kernel(run_parity, times, slots, first, states_ref, right_ref, left_ref, out_ref):
     n = out_ref.shape[1]
-    size = 2 * slots * n
-    edge = lax.axis_index("mode") == (0 if k == 1 else group - 1)
-
-    def each(body):
-        if len(refs) == 2:
-            body(refs[0])
-        else:
-            pl.when(jnp.logical_not(edge))(lambda: body(refs[0]))
-            pl.when(edge)(lambda: body(refs[1]))
+    count = out_ref.shape[0] // (2 * n)
+    pair = 2 if count % 2 == 0 else 1
 
     @pl.when(odd_depth() == run_parity)
     def _():
         right, left = right_ref[...], left_ref[...]
-
-        def load(ref):
-            out_ref[...] = ref[pl.ds(0, size)]
-
-        each(load)
-
-        @pl.loop(0, slots // pair)
+        out_ref[...] = states_ref[pl.ds(2 * first * n, 2 * count * n)]
+
+        @pl.loop(0, count // pair)
         def _(step):
             @pl.loop(0, times * SUBSTEPS)
             def _(turn):
@@ -264,14 +226,11 @@
                     out_ref[r] = real
                     out_ref[i] = imag
 
-        def damp(ref):
-            factors = ref[pl.ds(size, ROWS)][FACTOR : FACTOR + 1]
-            for s in range(slots):
-                scale = factors[:, s : s + 1] ** times
-                at = rows(2 * s * n, n, 2)
-                out_ref[at] = out_ref[at] * scale
-
-        each(damp)
+        factors = states_ref[pl.ds(2 * slots * n, ROWS)][FACTOR : FACTOR + 1]
+        for s in range(count):
+            scale = factors[:, first + s : first + s + 1] ** times
+            at = rows(2 * s * n, n, 2)
+            out_ref[at] = out_ref[at] * scale
 
 
 def sided(real, imag, right, left):
@@ -292,9 +251,9 @@
     return back * modes + entry(tab, MODE, c, slots).astype(jnp.int32)
 
 
-def parent_of(tab, c, slots, group):
+def parent_of(tab, c, slots):
     parent = entry(tab, PARENT, c, slots).astype(jnp.int32)
-    back = lax.rem(lax.axis_index("mode") - lax.div(parent, slots) + group, group)
+    back = lax.bitwise_xor(lax.axis_index("mode"), lax.div(parent, slots))
     return back * slots + lax.rem(parent, slots)
 
 
@@ -338,10 +297,10 @@
         acc_ref[...] = jnp.zeros_like(acc_ref)
         for s in range(slots):
             pick, at = part_of(picks, s)
-            groups.fetch(parent_of(tab, group * slots + s, slots, group), pick, at)
+            groups.fetch(parent_of(tab, group * slots + s, slots), pick, at)
 
         def collect(c, count):
-            mine = parent_of(tab, c, slots, group) < slots
+            mine = parent_of(tab, c, slots) < slots
 
             @pl.when(mine)
             def _():
@@ -364,7 +323,7 @@
                 for u, (c, weight) in enumerate(children)
             ]
             for (c, _), pair in zip(children, terms):
-                add_pair(acc_ref, 2 * parent_of(tab, c, slots, group) * n, pair)
+                add_pair(acc_ref, 2 * parent_of(tab, c, slots) * n, pair)
 
         for s in range(slots):
             part, at = part_of(sums, s)
@@ -403,13 +362,14 @@
             out_ref[...] = frees[1][...]
 
 
-def side_kernel(side, receiver, slots, group, modes, base_count, group_count, tab_count, right_ref, left_ref, *refs):
+def side_kernel(side, receiver, slots, group, modes, span, base_count, group_count, tab_count, right_ref, left_ref, *refs):
     stage_ref, tab, sem_ref = refs[-3:]
+    start, count = span
     bases = refs[:base_count]
-    groups = Layout(refs[base_count : base_count + group_count], slots, group)
+    groups = Layout(refs[base_count : base_count + group_count], slots, count)
     tab_refs = refs[base_count + group_count : base_count + group_count + tab_count]
     outs = refs[base_count + group_count + tab_count : -3]
-    second = base_count == 1
+    second = len(outs[-1].shape) == 2
     n = stage_ref.shape[1]
     size = 2 * slots * n
     gathered = Layout(tab_refs, slots, group) if tab_count > 1 else None
@@ -417,22 +377,25 @@
     held = group // len(outs) if second else group
     stride = size + ROWS if second else size
 
-    def spot(k):
-        return outs[k // held], (k % held) * stride
-
     @pl.when(odd_depth() == receiver)
     def _():
-        below = [groups.table(k) for k in range(group)] if side == "children" else []
+        below = [groups.table(k) for k in range(count)] if side == "children" else []
         pull(own_tables + below, tab, sem_ref)
-        for k in range(group):
-            ref, base = spot(k)
-            ref[pl.ds(base, size)] = bases[0][pl.ds(k * size, size)] if second else bases[k][...]
-            if second:
+        if second:
+            for k in range(group):
+                ref, base = outs[k // held], (k % held) * stride
+                ref[pl.ds(base, size)] = bases[0][pl.ds(k * size, size)]
                 ref[pl.ds(base + size, ROWS)] = tab_refs[0][k]
-            elif gathered:
-                gathered.copy_table(k, outs[1], k)
-            else:
-                outs[1][k] = tab_refs[0][k]
+        else:
+            offset = 0
+            for base in bases:
+                outs[0][pl.ds(offset, base.shape[0])] = base[...]
+                offset += base.shape[0]
+            for k in range(group):
+                if gathered:
+                    gathered.copy_table(k, outs[1], k)
+                else:
+                    outs[1][k] = tab_refs[0][k]
 
         def add(index, pair):
             if not second:
@@ -446,20 +409,20 @@
                 def _():
                     add_pair(ref, at, pair)
 
-        @pl.loop(0, group)
+        @pl.loop(0, count)
         def _(k):
             at = k * slots
             targets, terms = [], []
             for s in range(slots):
                 c = at + s
-                groups.fetch(c if side == "children" else parent_of(tab, c, slots, group), stage_ref, 2 * s)
+                groups.fetch(c if side == "children" else parent_of(tab, c, slots), stage_ref, 2 * s)
             for s in range(slots):
                 c = at + s
                 if side == "children":
                     b = c + group * slots
-                    target = parent_of(tab, b, slots, group)
+                    target = parent_of(tab, b, slots)
                     weight = entry(tab, WEIGHT, b, slots) * (entry(tab, LIVE, target, slots) * couple_step)
-                    mode = operator_of(tab, b, slots, modes) - group * modes
+                    mode = operator_of(tab, b, slots, modes) + (start - group) * modes
                     terms.append(child_pair(stage_ref, 2 * s, mode, weight, right_ref, left_ref))
                 else:
                     target = c
@@ -487,11 +450,7 @@
 
 
 def turn_order(group):
-    return sorted(range(1, group), key=lambda k: abs(k - group / 2))
-
-
-def has_relay(group):
-    return group - 2 == 2
+    return sorted(range(1, group), key=lambda k: (bin(k).count("1"), -k))
 
 
 def shards(sizes, blocks, live_slots, parent_index, bath_mode, hamiltonian, coupling, correlation, damping, link_weight):
@@ -503,7 +462,6 @@
     order = turn_order(group)
     split_hop = 2 if slots % 2 == 0 else 1
     ranks = range(group)
-    relay = has_relay(group)
 
     def place(d, m):
         return d * group + m
@@ -512,39 +470,19 @@
         return lax.ppermute(value, AXES, pairs)
 
     def gather(value, parity):
-        def turn(k):
-            wraps = {1: group - 1, group - 1: 0}
-            pairs = [
-                (place(d, m), place(d, (m + k) % group))
-                for d in range(parity, depths, 2)
-                for m in ranks
-                if not (relay and wraps.get(k) == m)
-            ]
-            return permute(value, pairs)
-
-        turned = {k: turn(k) for k in order}
-        groups = [value] + [turned[k] for k in range(1, group)]
-        if relay:
-            pairs = [
-                (place(d, source), place(d, target))
-                for d in range(parity, depths, 2)
-                for source, target in ((1, 0), (group - 2, group - 1))
-            ]
-            groups.append(permute(turned[2], pairs))
-        return groups
-
-    def shift(value, step, parity=None, k=None):
-        def sent(m):
-            if not relay or k is None:
-                return True
-            edge = {1: 0, group - 1: group - 1}
-            return m in edge.values() if k == group else edge.get(k) != m
-
+        held = {0: value}
+        for k in order:
+            step = k & -k
+            pairs = [(place(d, m), place(d, m ^ step)) for d in range(parity, depths, 2) for m in ranks]
+            held[k] = permute(held[k ^ step], pairs)
+        return [held[k] for k in ranks]
+
+    def shift(value, step, parity=None):
         pairs = [
             (place(d, m), place(d + step, m))
             for d in range(depths)
             for m in ranks
-            if 0 <= d + step < depths and (parity is None or d % 2 == parity) and sent(m)
+            if 0 <= d + step < depths and (parity is None or d % 2 == parity)
         ]
         return permute(value, pairs)
 
@@ -582,17 +520,18 @@
         (couplings, *first),
     )
 
-    def free(groups, k, parity, times):
-        sources = [groups[k]]
-        if len(groups) == group + 1 and k in (1, group - 1):
-            sources.append(groups[group])
+    def free(states, parity, times, part=0, parts=1):
+        count = slots // parts
         return call(
-            functools.partial(free_kernel, parity, times, slots, group, k),
-            mats(plain),
+            functools.partial(free_kernel, parity, times, slots, part * count),
+            mats(2 * count),
             limit,
-            (*powers, *sources),
-            us=4.7 * times,
+            (states, *powers),
+            us=4.5 * times / parts,
         )
+
+    def free_parts(states, parity, times):
+        return [free(states, parity, times, part, split_hop) for part in range(split_hop)]
 
     def send(groups, sender, sum_parts, pick_parts, operators):
         shapes = [mats(plain // sum_parts)] * sum_parts + [mats(plain // pick_parts)] * pick_parts
@@ -615,31 +554,33 @@
             scratch=tables(1),
         )
 
-    def side(kind, bases, groups, tabs, receiver, operators):
-        second = len(bases) == 1
+    def side(kind, bases, groups, tabs, receiver, operators, second=False, span=None):
         halves = 2 if group % 2 == 0 else 1
+        span = (0, group) if span is None else span
         return call(
-            functools.partial(side_kernel, kind, receiver, slots, group, modes, len(bases), len(groups), len(tabs)),
+            functools.partial(side_kernel, kind, receiver, slots, group, modes, span, len(bases), len(groups), len(tabs)),
             [mats(2 * total // halves, group // halves)] * halves if second else [mats(2 * total), sds(group, ROWS, n)],
             limit,
             (*operators, *bases, *groups, *tabs),
             us=3,
-            scratch=[stage, *tables(2 * group if kind == "children" else group)],
+            scratch=[stage, *tables(group + (span[1] if kind == "children" else 0))],
         )
 
-    free_even = free([packed], 0, 0, 1)
-    free_odd = [free(first, k, 1, 2) for k in ranks]
+    free_even = free(packed, 0, 1)
+    free_odd = [part for k in ranks for part in free_parts(first[k], 1, 2)]
     sums, picks, tabs_odd = send(first, 1, 1, split_hop, operators_odd)
     picks = [shift(value, 1, 1) for value in picks]
     sums = [shift(value, -1, 1) for value in sums]
     own_state = join([free_even], sums, picks, 0, operators_odd)
 
     gathered = gather(own_state, 0)
-    from_below = [shift(value, -1, 0, k) for k, value in enumerate(gathered)]
-    from_above = [shift(value, 1, 0, k) for k, value in enumerate(gathered)]
-    free_even = [free(gathered, k, 0, 2) for k in ranks]
+    from_below = [shift(value, -1, 0) for value in gathered]
+    from_above = [shift(value, 1, 0) for value in gathered]
+    free_even = [part for k in ranks for part in free_parts(gathered[k], 0, 2)]
     states, _ = side("parents", free_odd, from_above, [tabs_odd], 1, operators_odd)
-    states = side("children", [states], from_below, [tabs_odd], 1, operators_odd)
+    ready = group - 1
+    states, _ = side("children", [states], from_below[:ready], [tabs_odd], 1, operators_odd, span=(0, ready))
+    states = side("children", [states], from_below[ready:], [tabs_odd], 1, operators_odd, second=True, span=(ready, 1))
 
     from_above = [shift(value, 1, 1) for value in states]
     from_below = [shift(value, -1, 1) for value in states]
@@ -647,14 +588,14 @@
     operators_even = call(
         functools.partial(operators_kernel, slots, group, modes, 0), operator_shapes, limit, (couplings, passed)
     )
-    last_odd = free(states[:1], 0, 1, 2)
+    last_odd = free(states[0], 1, 2)
     states, tabs_even = side("children", free_even, from_below, gathered, 0, operators_even)
-    states = side("parents", [states], from_above, [tabs_even], 0, operators_even)
+    states = side("parents", [states], from_above, [tabs_even], 0, operators_even, second=True)
 
     sums, picks, _ = send(states, 0, split_hop, 1, operators_even)
     sums = [shift(value, -1, 0) for value in sums]
     picks = [shift(value, 1, 0) for value in picks]
-    last_even = free(states[:1], 0, 0, 1)
+    last_even = free(states[0], 0, 1)
     return join([last_odd, last_even], sums, picks, 1, operators_odd).reshape(blocks.shape)
 
 

time: 174 us -> 170 us (0.977)
  the two profiles are of different devices: /device:TPU:3 before, /device:TPU:11 now
where the time goes in v2:
time: 170 us; the launch traced here: 169 us
  waiting for transfers between devices  67.7 us (40%)
  Pallas kernels  59.8 us (35%)
  starting transfers between devices  40.8 us (24%)
    ppermute x26, waiting for transfers between devices, permute(): return lax.ppermute(value, AXES, pairs)  67.7 us
    pallas_call x32, Pallas kernels, call(): pl.pallas_call(kernel, out_shape=out_shapes, in_specs=specs, out_specs=ja...  59.8 us
    ppermute x26, starting transfers between devices, permute(): return lax.ppermute(value, AXES, pairs)  40.8 us
  transfers between devices with their start and end apart: 26, of which 10 were waited for; matrix products, arithmetic and copies ran while one was open for 0% of the time, Pallas kernels for 30%

profile of v2, /device:TPU:11, one launch (start us, length us, event | category | flops | bytes accessed | tf_op | source)
XLA Modules:
  0.0 169.1 jit_solution(9519490461303940075)
XLA Ops:
  0.0 2.0 %shard_map.91 = (f32[1288,128]{1,0:T(8,128)}, f32[8,128]{1,0:T(8,128)}) custom-call(s32[4]{0:T(128)} %live_ref.1, s32[4]{0:T(128)} %parent_ref.1, s32[4]{0:T(128)} %mode_ref.1, f32[4]{0:T(128)} %damping_ref.1, f32[4]{0:T(128)} %weight_ref.1, f32[2,2]{1,0:T(2,128)} %corr_ref.1, f32[1024,128]{1,0:T(8,128)} %bitcast.6, f32[256,128]{1,0:T(8,128)} %bitcast.3), custom_call_target="tpu_custom_call" | custom-call | flops 1100000000 | bytes 524288 | tf_op jit(solution)/shard_map/pallas_call | solution.py:441
  2.0 4.2 %collective-permute-start.1 = (f32[1288,128]{1,0:T(8,128)}, f32[1288,128]{1,0:T(8,128)S(1)}, u32[]{:S(2)}, u32[]{:S(2)}) collective-permute-start(f32[1288,128]{1,0:T(8,128)} %get-tuple-element.30.refs_0_.states_ref), channel_id=1, source_target_pairs={{4,6},{5,7},{6,4},{7,5},{12,14},{13,15},{14,12},{15,13},{20,22},{2... | collective-permute-start | bytes 1978376 | tf_op jit(solution)/shard_map/ppermute | solution.py:470
  6.2 2.1 %collective-permute-start = (f32[1288,128]{1,0:T(8,128)}, f32[1288,128]{1,0:T(8,128)S(1)}, u32[]{:S(2)}, u32[]{:S(2)}) collective-permute-start(f32[1288,128]{1,0:T(8,128)} %get-tuple-element.30.refs_0_.states_ref), channel_id=1, source_target_pairs={{4,5},{5,4},{6,7},{7,6},{12,13},{13,12},{14,15},{15,14},{20,21},{2... | collective-permute-start | bytes 1978376 | tf_op jit(solution)/shard_map/ppermute | solution.py:470
  8.3 2.1 %collective-permute-start.3 = (f32[8,128]{1,0:T(8,128)}, f32[8,128]{1,0:T(8,128)S(1)}, u32[]{:S(2)}, u32[]{:S(2)}) collective-permute-start(f32[8,128]{1,0:T(8,128)} %get-tuple-element.29.own_ref), channel_id=1, source_target_pairs={{4,0},{5,1},{6,2},{7,3},{8,4},{9,5},{10,6},{11,7},{12,8},{13,9},{1... | collective-permute-start | bytes 12296 | tf_op jit(solution)/shard_map/ppermute | solution.py:470
  10.4 0.7 shard_map.93
  11.2 4.2 %shard_map.94.refs_0_ = f32[512,128]{1,0:T(8,128)S(1)} custom-call(f32[1288,128]{1,0:T(8,128)S(1)} %copy-done.1, bf16[384,512]{1,0:T(8,128)(2,1)S(1)} %get-tuple-element.33.right_ref, bf16[128,1536]{1,0:T(8,128)(2,1)S(1)} %get-tuple-element.34.left_ref), custom_call_target="tpu_custom_call" | custom-call | flops 4950000128 | bytes 524288 | tf_op jit(solution)/shard_map/pallas_call | solution.py:441
  15.4 4.2 %shard_map.95.refs_1_ = f32[512,128]{1,0:T(8,128)S(1)} custom-call(f32[1288,128]{1,0:T(8,128)S(1)} %copy-done.1, bf16[384,512]{1,0:T(8,128)(2,1)S(1)} %get-tuple-element.33.right_ref, bf16[128,1536]{1,0:T(8,128)(2,1)S(1)} %get-tuple-element.34.left_ref), custom_call_target="tpu_custom_call" | custom-call | flops 4950000128 | bytes 524288 | tf_op jit(solution)/shard_map/pallas_call | solution.py:441
  19.6 1.5 collective-permute-done.1.refs_2_.states_ref
  21.1 2.6 %collective-permute-start.2 = (f32[1288,128]{1,0:T(8,128)S(1)}, f32[1288,128]{1,0:T(8,128)S(1)}, u32[]{:S(2)}, u32[]{:S(2)}) collective-permute-start(f32[1288,128]{1,0:T(8,128)S(1)} %collective-permute-done.1.refs_2_.states_ref), channel_id=1, source_target_pairs={{4,5},{5,4},{6,7},{7,6},{12,13},{13,12},{14,15},{15,14},{20,21},{2... | collective-permute-start | bytes 1978376 | tf_op jit(solution)/shard_map/ppermute | solution.py:470
  23.7 4.2 %shard_map.98.refs_4_ = f32[512,128]{1,0:T(8,128)S(1)} custom-call(f32[1288,128]{1,0:T(8,128)S(1)} %collective-permute-done.1.refs_2_.states_ref, bf16[384,512]{1,0:T(8,128)(2,1)S(1)} %get-tuple-element.33.right_ref, bf16[128,1536]{1,0:T(8,128)(2,1)S(1)} %get-tuple-element.34.left_ref), custom_call_target="tpu_custom_call" | custom-call | flops 4950000128 | bytes 524288 | tf_op jit(solution)/shard_map/pallas_call | solution.py:441
  27.9 4.2 %shard_map.99.refs_5_ = f32[512,128]{1,0:T(8,128)S(1)} custom-call(f32[1288,128]{1,0:T(8,128)S(1)} %collective-permute-done.1.refs_2_.states_ref, bf16[384,512]{1,0:T(8,128)(2,1)S(1)} %get-tuple-element.33.right_ref, bf16[128,1536]{1,0:T(8,128)(2,1)S(1)} %get-tuple-element.34.left_ref), custom_call_target="tpu_custom_call" | custom-call | flops 4950000128 | bytes 524288 | tf_op jit(solution)/shard_map/pallas_call | solution.py:441
  32.2 0.0 collective-permute-done.refs_1_.states_ref
  32.2 4.2 %shard_map.96.refs_2_ = f32[512,128]{1,0:T(8,128)S(1)} custom-call(f32[1288,128]{1,0:T(8,128)S(1)} %collective-permute-done.refs_1_.states_ref, bf16[384,512]{1,0:T(8,128)(2,1)S(1)} %get-tuple-element.33.right_ref, bf16[128,1536]{1,0:T(8,128)(2,1)S(1)} %get-tuple-element.34.left_ref), custom_call_target="tpu_custom_call" | custom-call | flops 4950000128 | bytes 524288 | tf_op jit(solution)/shard_map/pallas_call | solution.py:441
  36.4 0.0 copy-start.2
  36.4 4.2 %shard_map.97.refs_3_ = f32[512,128]{1,0:T(8,128)S(1)} custom-call(f32[1288,128]{1,0:T(8,128)S(1)} %collective-permute-done.refs_1_.states_ref, bf16[384,512]{1,0:T(8,128)(2,1)S(1)} %get-tuple-element.33.right_ref, bf16[128,1536]{1,0:T(8,128)(2,1)S(1)} %get-tuple-element.34.left_ref), custom_call_target="tpu_custom_call" | custom-call | flops 4950000128 | bytes 524288 | tf_op jit(solution)/shard_map/pallas_call | solution.py:441
  40.6 0.2 shard_map.92
  40.9 0.0 collective-permute-done.3.near_ref
  40.9 2.2 %shard_map.103 = (f32[1024,128]{1,0:T(8,128)S(1)}, f32[512,128]{1,0:T(8,128)S(1)}, f32[512,128]{1,0:T(8,128)S(1)}, f32[4,8,128]{2,1,0:T(8,128)S(1)}) custom-call(f32[8,128]{1,0:T(8,128)S(1)} %collective-permute-done.3.near_ref, bf16[8,384,128]{2,1,0:T(8,128)(2,1)S(1)} %get-tuple-element.31.right_ref, bf16[8,128,384]{2,1,0:T(8,128)(2,1)S(1)} %get-tuple-element.32.left_ref, ...), custom_call_target="tpu_custom_call" | custom-call | flops 2200000000 | bytes 524288 | tf_op jit(solution)/shard_map/pallas_call | solution.py:441
  43.0 1.3 collective-permute-start.4
  44.4 1.3 collective-permute-start.5
  45.7 1.3 collective-permute-start.6
  47.0 1.3 collective-permute-start.18
  48.3 4.2 %shard_map.100.refs_6_ = f32[512,128]{1,0:T(8,128)S(1)} custom-call(f32[1288,128]{1,0:T(8,128)S(1)} %collective-permute-done.2.refs_3_.states_ref, bf16[384,512]{1,0:T(8,128)(2,1)S(1)} %get-tuple-element.33.right_ref, bf16[128,1536]{1,0:T(8,128)(2,1)S(1)} %get-tuple-element.34.left_ref), custom_call_target="tpu_custom_call" | custom-call | flops 4950000128 | bytes 524288 | tf_op jit(solution)/shard_map/pallas_call | solution.py:441
  52.5 0.0 copy-start
  52.5 4.2 %shard_map.101.refs_7_ = f32[512,128]{1,0:T(8,128)S(1)} custom-call(f32[1288,128]{1,0:T(8,128)S(1)} %collective-permute-done.2.refs_3_.states_ref, bf16[384,512]{1,0:T(8,128)(2,1)S(1)} %get-tuple-element.33.right_ref, bf16[128,1536]{1,0:T(8,128)(2,1)S(1)} %get-tuple-element.34.left_ref), custom_call_target="tpu_custom_call" | custom-call | flops 4950000128 | bytes 524288 | tf_op jit(solution)/shard_map/pallas_call | solution.py:441
  56.8 0.0 collective-permute-done.5.refs_2_
  56.8 0.0 collective-permute-done.4.refs_1_
  56.8 0.7 collective-permute-start.10
  57.6 0.7 collective-permute-start.8
  58.3 1.3 collective-permute-start.7
  59.6 1.3 collective-permute-start.14
  60.9 0.2 shard_map.110.refs_0_
  61.1 0.7 collective-permute-start.12
  61.8 1.3 collective-permute-start.11
  63.1 1.3 collective-permute-start.9
  64.5 0.0 collective-permute-done.12.states_ref.refs_13_
  64.5 1.3 collective-permute-start.13
  65.8 1.3 collective-permute-start.15
  67.1 14.9 %collective-permute-done.11.refs_10_ = f32[1032,128]{1,0:T(8,128)S(1)} collective-permute-done((f32[1032,128]{1,0:T(8,128)S(1)}, f32[1032,128]{1,0:T(8,128)S(1)}, u32[]{:S(2)}, u32[]{:S(2)}) %collective-permute-start.11) | collective-permute-done | bytes 528416 | tf_op jit(solution)/shard_map/ppermute | solution.py:470
  82.1 1.3 collective-permute-start.16
  83.4 0.0 collective-permute-done.9.refs_9_
  83.4 1.3 collective-permute-start.17
  84.7 4.2 %collective-permute-done.13.refs_11_ = f32[1032,128]{1,0:T(8,128)S(1)} collective-permute-done((f32[1032,128]{1,0:T(8,128)S(1)}, f32[1032,128]{1,0:T(8,128)S(1)}, u32[]{:S(2)}, u32[]{:S(2)}) %collective-permute-start.13) | collective-permute-done | bytes 528416 | tf_op jit(solution)/shard_map/ppermute | solution.py:470
  88.9 4.4 %shard_map.105 = (f32[4096,128]{1,0:T(8,128)S(1)}, f32[4,8,128]{2,1,0:T(8,128)}) custom-call(bf16[8,384,128]{2,1,0:T(8,128)(2,1)S(1)} %get-tuple-element.31.right_ref, bf16[8,128,384]{2,1,0:T(8,128)(2,1)S(1)} %get-tuple-element.32.left_ref, f32[512,128]{1,0:T(8,128)S(1)} %shard_map.94.refs_0_, f32[512,128]{1,0:T(8,128)S(1)} %shard_map.95.refs_1_, ...), custom_call_target="tpu_custom_call" | custom-call | flops 3300000000 | bytes 524288 | tf_op jit(solution)/shard_map/pallas_call | solution.py:441
  93.3 9.0 %collective-permute-done.15.refs_2_ = f32[1032,128]{1,0:T(8,128)S(1)} collective-permute-done((f32[1032,128]{1,0:T(8,128)S(1)}, f32[1032,128]{1,0:T(8,128)S(1)}, u32[]{:S(2)}, u32[]{:S(2)}) %collective-permute-start.15) | collective-permute-done | bytes 528416 | tf_op jit(solution)/shard_map/ppermute | solution.py:470
  102.3 5.7 %collective-permute-done.16.refs_3_ = f32[1032,128]{1,0:T(8,128)S(1)} collective-permute-done((f32[1032,128]{1,0:T(8,128)S(1)}, f32[1032,128]{1,0:T(8,128)S(1)}, u32[]{:S(2)}, u32[]{:S(2)}) %collective-permute-start.16) | collective-permute-done | bytes 528416 | tf_op jit(solution)/shard_map/ppermute | solution.py:470
  108.0 3.6 %shard_map.106 = (f32[4096,128]{1,0:T(8,128)S(1)}, f32[4,8,128]{2,1,0:T(8,128)}) custom-call(bf16[8,384,128]{2,1,0:T(8,128)(2,1)S(1)} %get-tuple-element.31.right_ref, bf16[8,128,384]{2,1,0:T(8,128)(2,1)S(1)} %get-tuple-element.32.left_ref, f32[4096,128]{1,0:T(8,128)S(1)} %get-tuple-element.39.refs_0_, f32[1032,128]{1,0:T(8,128)S(1)} %collective-permute-done.14.refs_1_, ...), custom_call_target="tpu_custom_call" | custom-call | flops 3300000000 | bytes 524288 | tf_op jit(solution)/shard_map/pallas_call | solution.py:441
  111.6 2.0 %collective-permute-done.17.refs_1_ = f32[1032,128]{1,0:T(8,128)S(1)} collective-permute-done((f32[1032,128]{1,0:T(8,128)S(1)}, f32[1032,128]{1,0:T(8,128)S(1)}, u32[]{:S(2)}, u32[]{:S(2)}) %collective-permute-start.17) | collective-permute-done | bytes 528416 | tf_op jit(solution)/shard_map/ppermute | solution.py:470
  113.6 1.6 shard_map.107
  115.2 1.4 collective-permute-start.19
  116.6 1.4 collective-permute-start.20
  118.0 4.3 %collective-permute-start.21 = (f32[2064,128]{1,0:T(8,128)S(1)}, f32[2064,128]{1,0:T(8,128)S(1)}, u32[]{:S(2)}, u32[]{:S(2)}) collective-permute-start(f32[2064,128]{1,0:T(8,128)S(1)} %get-tuple-element.41.states_ref), channel_id=1, source_target_pairs={{4,8},{5,9},{6,10},{7,11},{12,16},{13,17},{14,18},{15,19},{20,24},... | collective-permute-start | bytes 3170312 | tf_op jit(solution)/shard_map/ppermute | solution.py:470
  122.3 1.4 collective-permute-start.22
  123.7 0.1 shard_map.118
  123.8 10.2 %collective-permute-done.21.refs_1_ = f32[2064,128]{1,0:T(8,128)S(1)} collective-permute-done((f32[2064,128]{1,0:T(8,128)S(1)}, f32[2064,128]{1,0:T(8,128)S(1)}, u32[]{:S(2)}, u32[]{:S(2)}) %collective-permute-start.21) | collective-permute-done | bytes 1056800 | tf_op jit(solution)/shard_map/ppermute | solution.py:470
  134.0 11.3 %collective-permute-done.22.refs_2_ = f32[2064,128]{1,0:T(8,128)S(1)} collective-permute-done((f32[2064,128]{1,0:T(8,128)S(1)}, f32[2064,128]{1,0:T(8,128)S(1)}, u32[]{:S(2)}, u32[]{:S(2)}) %collective-permute-start.22) | collective-permute-done | bytes 1056800 | tf_op jit(solution)/shard_map/ppermute | solution.py:470
  145.4 0.7 shard_map.121
  146.1 1.3 collective-permute-start.25
  147.4 8.2 %shard_map.108.refs_0_ = f32[1024,128]{1,0:T(8,128)S(1)} custom-call(f32[2064,128]{1,0:T(8,128)S(1)} %get-tuple-element.41.states_ref, bf16[384,512]{1,0:T(8,128)(2,1)S(1)} %get-tuple-element.33.right_ref, bf16[128,1536]{1,0:T(8,128)(2,1)S(1)} %get-tuple-element.34.left_ref), custom_call_target="tpu_custom_call" | custom-call | flops 9900000256 | bytes 524288 | tf_op jit(solution)/shard_map/pallas_call | solution.py:441
  155.6 1.3 collective-permute-start.23
  156.9 1.3 collective-permute-start.24
  158.2 6.0 %collective-permute-done.23.refs_2_ = f32[512,128]{1,0:T(8,128)S(1)} collective-permute-done((f32[512,128]{1,0:T(8,128)S(1)}, f32[512,128]{1,0:T(8,128)S(1)}, u32[]{:S(2)}, u32[]{:S(2)}) %collective-permute-start.23) | collective-permute-done | bytes 262176 | tf_op jit(solution)/shard_map/ppermute | solution.py:470
  164.2 2.8 %collective-permute-done.24.refs_3_ = f32[512,128]{1,0:T(8,128)S(1)} collective-permute-done((f32[512,128]{1,0:T(8,128)S(1)}, f32[512,128]{1,0:T(8,128)S(1)}, u32[]{:S(2)}, u32[]{:S(2)}) %collective-permute-start.24) | collective-permute-done | bytes 262176 | tf_op jit(solution)/shard_map/ppermute | solution.py:470
  167.0 1.9 %shard_map.122 = f32[1024,128]{1,0:T(8,128)} custom-call(f32[8,128]{1,0:T(8,128)S(1)} %copy-done, bf16[8,384,128]{2,1,0:T(8,128)(2,1)S(1)} %get-tuple-element.31.right_ref, bf16[8,128,384]{2,1,0:T(8,128)(2,1)S(1)} %get-tuple-element.32.left_ref, f32[1024,128]{1,0:T(8,128)S(1)} %shard_map.108.refs_0_, f32[1024,128]{1,0:T(8,128)S(1)} %shard_map.120.refs_1_, ...), custom_call_target="tpu_custom_call" | custom-call | flops 1100000000 | bytes 524288 | tf_op jit(solution)/shard_map/pallas_call | solution.py:441
  (28 shorter events, 0.3 us)
Async XLA Ops:
  0.0 10.4 %copy-start.3 = (f32[128,128]{1,0:T(8,128)S(1)}, f32[128,128]{1,0:T(8,128)}, u32[]{:S(2)}) copy-start(f32[128,128]{1,0:T(8,128)} %ham_ref.1) | copy-start | bytes 196612
  2.0 19.1 %collective-permute-start.1 = (f32[1288,128]{1,0:T(8,128)}, f32[1288,128]{1,0:T(8,128)S(1)}, u32[]{:S(2)}, u32[]{:S(2)}) collective-permute-start(f32[1288,128]{1,0:T(8,128)} %get-tuple-element.30.refs_0_.states_ref), channel_id=1, source_target_pairs={{4,6},{5,7},{6,4},{7,5},{12,14},{13,15},{14,12},{15,13},{20,22},{2... | collective-permute-start | bytes 1978376 | tf_op jit(solution)/shard_map/ppermute | solution.py:470
  6.2 25.9 %collective-permute-start = (f32[1288,128]{1,0:T(8,128)}, f32[1288,128]{1,0:T(8,128)S(1)}, u32[]{:S(2)}, u32[]{:S(2)}) collective-permute-start(f32[1288,128]{1,0:T(8,128)} %get-tuple-element.30.refs_0_.states_ref), channel_id=1, source_target_pairs={{4,5},{5,4},{6,7},{7,6},{12,13},{13,12},{14,15},{15,14},{20,21},{2... | collective-permute-start | bytes 1978376 | tf_op jit(solution)/shard_map/ppermute | solution.py:470
  8.3 2.8 %copy-start.1 = (f32[1288,128]{1,0:T(8,128)S(1)}, f32[1288,128]{1,0:T(8,128)}, u32[]{:S(2)}) copy-start(f32[1288,128]{1,0:T(8,128)} %get-tuple-element.30.refs_0_.states_ref) | copy-start | bytes 1978372
  8.3 32.5 %collective-permute-start.3 = (f32[8,128]{1,0:T(8,128)}, f32[8,128]{1,0:T(8,128)S(1)}, u32[]{:S(2)}, u32[]{:S(2)}) collective-permute-start(f32[8,128]{1,0:T(8,128)} %get-tuple-element.29.own_ref), channel_id=1, source_target_pairs={{4,0},{5,1},{6,2},{7,3},{8,4},{9,5},{10,6},{11,7},{12,8},{13,9},{1... | collective-permute-start | bytes 12296 | tf_op jit(solution)/shard_map/ppermute | solution.py:470
  21.1 19.5 %collective-permute-start.2 = (f32[1288,128]{1,0:T(8,128)S(1)}, f32[1288,128]{1,0:T(8,128)S(1)}, u32[]{:S(2)}, u32[]{:S(2)}) collective-permute-start(f32[1288,128]{1,0:T(8,128)S(1)} %collective-permute-done.1.refs_2_.states_ref), channel_id=1, source_target_pairs={{4,5},{5,4},{6,7},{7,6},{12,13},{13,12},{14,15},{15,14},{20,21},{2... | collective-permute-start | bytes 1978376 | tf_op jit(solution)/shard_map/ppermute | solution.py:470
  36.4 4.2 %copy-start.2 = (f32[2,128,128]{2,1,0:T(8,128)S(1)}, f32[2,128,128]{2,1,0:T(8,128)}, u32[]{:S(2)}) copy-start(f32[2,128,128]{2,1,0:T(8,128)} %param.14) | copy-start | bytes 393220
  43.0 13.7 %collective-permute-start.4 = (f32[1024,128]{1,0:T(8,128)S(1)}, f32[1024,128]{1,0:T(8,128)S(1)}, u32[]{:S(2)}, u32[]{:S(2)}) collective-permute-start(f32[1024,128]{1,0:T(8,128)S(1)} %get-tuple-element.35), channel_id=1, source_target_pairs={{4,0},{5,1},{6,2},{7,3},{12,8},{13,9},{14,10},{15,11},{20,16},{21,... | collective-permute-start | bytes 1572872 | tf_op jit(solution)/shard_map/ppermute | solution.py:470
  44.4 12.4 %collective-permute-start.5 = (f32[512,128]{1,0:T(8,128)S(1)}, f32[512,128]{1,0:T(8,128)S(1)}, u32[]{:S(2)}, u32[]{:S(2)}) collective-permute-start(f32[512,128]{1,0:T(8,128)S(1)} %get-tuple-element.36), channel_id=1, source_target_pairs={{4,8},{5,9},{6,10},{7,11},{12,16},{13,17},{14,18},{15,19},{20,24},... | collective-permute-start | bytes 786440 | tf_op jit(solution)/shard_map/ppermute | solution.py:470
  45.7 11.1 %collective-permute-start.6 = (f32[512,128]{1,0:T(8,128)S(1)}, f32[512,128]{1,0:T(8,128)S(1)}, u32[]{:S(2)}, u32[]{:S(2)}) collective-permute-start(f32[512,128]{1,0:T(8,128)S(1)} %get-tuple-element.37), channel_id=1, source_target_pairs={{4,8},{5,9},{6,10},{7,11},{12,16},{13,17},{14,18},{15,19},{20,24},... | collective-permute-start | bytes 786440 | tf_op jit(solution)/shard_map/ppermute | solution.py:470
  47.0 10.5 %collective-permute-start.18 = (f32[768,128]{1,0:T(8,128)S(1)}, f32[768,128]{1,0:T(8,128)S(1)}, u32[]{:S(2)}, u32[]{:S(2)}) collective-permute-start(f32[768,128]{1,0:T(8,128)S(1)} %get-tuple-element.42), channel_id=1, source_target_pairs={{4,0},{5,1},{6,2},{7,3},{12,8},{13,9},{14,10},{15,11},{20,16},{21,... | collective-permute-start | bytes 1179656 | tf_op jit(solution)/shard_map/ppermute | solution.py:470
  52.5 4.3 %copy-start = (f32[8,128]{1,0:T(8,128)S(1)}, f32[8,128]{1,0:T(8,128)}, u32[]{:S(2)}) copy-start(f32[8,128]{1,0:T(8,128)} %get-tuple-element.29.own_ref) | copy-start | bytes 12292
  56.8 4.3 %collective-permute-start.10 = (f32[1032,128]{1,0:T(8,128)S(1)}, f32[1032,128]{1,0:T(8,128)S(1)}, u32[]{:S(2)}, u32[]{:S(2)}) collective-permute-start(f32[1032,128]{1,0:T(8,128)S(1)} %shard_map.104.states_ref.refs_10_), channel_id=1, source_target_pairs={{0,2},{1,3},{2,0},{3,1},{8,10},{9,11},{10,8},{11,9},{16,18},{17,19... | collective-permute-start | bytes 1585160 | tf_op jit(solution)/shard_map/ppermute | solution.py:470
  57.6 5.6 %collective-permute-start.8 = (f32[1032,128]{1,0:T(8,128)S(1)}, f32[1032,128]{1,0:T(8,128)S(1)}, u32[]{:S(2)}, u32[]{:S(2)}) collective-permute-start(f32[1032,128]{1,0:T(8,128)S(1)} %shard_map.104.states_ref.refs_10_), channel_id=1, source_target_pairs={{0,1},{1,0},{2,3},{3,2},{8,9},{9,8},{10,11},{11,10},{16,17},{17,16... | collective-permute-start | bytes 1585160 | tf_op jit(solution)/shard_map/ppermute | solution.py:470
  58.3 7.5 %collective-permute-start.7 = (f32[1032,128]{1,0:T(8,128)S(1)}, f32[1032,128]{1,0:T(8,128)S(1)}, u32[]{:S(2)}, u32[]{:S(2)}) collective-permute-start(f32[1032,128]{1,0:T(8,128)S(1)} %shard_map.104.states_ref.refs_10_), channel_id=1, source_target_pairs={{0,4},{1,5},{2,6},{3,7},{8,12},{9,13},{10,14},{11,15},{16,20},{17,... | collective-permute-start | bytes 1585160 | tf_op jit(solution)/shard_map/ppermute | solution.py:470
  59.6 33.7 %collective-permute-start.14 = (f32[1032,128]{1,0:T(8,128)S(1)}, f32[1032,128]{1,0:T(8,128)S(1)}, u32[]{:S(2)}, u32[]{:S(2)}) collective-permute-start(f32[1032,128]{1,0:T(8,128)S(1)} %shard_map.104.states_ref.refs_10_), channel_id=1, source_target_pairs={{8,4},{9,5},{10,6},{11,7},{16,12},{17,13},{18,14},{19,15},{24,20},... | collective-permute-start | bytes 1585160 | tf_op jit(solution)/shard_map/ppermute | solution.py:470
  61.1 3.4 %collective-permute-start.12 = (f32[1032,128]{1,0:T(8,128)S(1)}, f32[1032,128]{1,0:T(8,128)S(1)}, u32[]{:S(2)}, u32[]{:S(2)}) collective-permute-start(f32[1032,128]{1,0:T(8,128)S(1)} %collective-permute-done.10.states_ref.refs_12_), channel_id=1, source_target_pairs={{0,1},{1,0},{2,3},{3,2},{8,9},{9,8},{10,11},{11,10},{16,17},{17,16... | collective-permute-start | bytes 1585160 | tf_op jit(solution)/shard_map/ppermute | solution.py:470
  61.8 20.2 %collective-permute-start.11 = (f32[1032,128]{1,0:T(8,128)S(1)}, f32[1032,128]{1,0:T(8,128)S(1)}, u32[]{:S(2)}, u32[]{:S(2)}) collective-permute-start(f32[1032,128]{1,0:T(8,128)S(1)} %collective-permute-done.10.states_ref.refs_12_), channel_id=1, source_target_pairs={{0,4},{1,5},{2,6},{3,7},{8,12},{9,13},{10,14},{11,15},{16,20},{17,... | collective-permute-start | bytes 1585160 | tf_op jit(solution)/shard_map/ppermute | solution.py:470
  63.1 20.3 %collective-permute-start.9 = (f32[1032,128]{1,0:T(8,128)S(1)}, f32[1032,128]{1,0:T(8,128)S(1)}, u32[]{:S(2)}, u32[]{:S(2)}) collective-permute-start(f32[1032,128]{1,0:T(8,128)S(1)} %collective-permute-done.8.states_ref.refs_11_), channel_id=1, source_target_pairs={{0,4},{1,5},{2,6},{3,7},{8,12},{9,13},{10,14},{11,15},{16,20},{17,... | collective-permute-start | bytes 1585160 | tf_op jit(solution)/shard_map/ppermute | solution.py:470
  64.5 24.4 %collective-permute-start.13 = (f32[1032,128]{1,0:T(8,128)S(1)}, f32[1032,128]{1,0:T(8,128)S(1)}, u32[]{:S(2)}, u32[]{:S(2)}) collective-permute-start(f32[1032,128]{1,0:T(8,128)S(1)} %collective-permute-done.12.states_ref.refs_13_), channel_id=1, source_target_pairs={{0,4},{1,5},{2,6},{3,7},{8,12},{9,13},{10,14},{11,15},{16,20},{17,... | collective-permute-start | bytes 1585160 | tf_op jit(solution)/shard_map/ppermute | solution.py:470
  65.8 36.5 %collective-permute-start.15 = (f32[1032,128]{1,0:T(8,128)S(1)}, f32[1032,128]{1,0:T(8,128)S(1)}, u32[]{:S(2)}, u32[]{:S(2)}) collective-permute-start(f32[1032,128]{1,0:T(8,128)S(1)} %collective-permute-done.8.states_ref.refs_11_), channel_id=1, source_target_pairs={{8,4},{9,5},{10,6},{11,7},{16,12},{17,13},{18,14},{19,15},{24,20},... | collective-permute-start | bytes 1585160 | tf_op jit(solution)/shard_map/ppermute | solution.py:470
  82.1 25.9 %collective-permute-start.16 = (f32[1032,128]{1,0:T(8,128)S(1)}, f32[1032,128]{1,0:T(8,128)S(1)}, u32[]{:S(2)}, u32[]{:S(2)}) collective-permute-start(f32[1032,128]{1,0:T(8,128)S(1)} %collective-permute-done.10.states_ref.refs_12_), channel_id=1, source_target_pairs={{8,4},{9,5},{10,6},{11,7},{16,12},{17,13},{18,14},{19,15},{24,20},... | collective-permute-start | bytes 1585160 | tf_op jit(solution)/shard_map/ppermute | solution.py:470
  83.4 30.2 %collective-permute-start.17 = (f32[1032,128]{1,0:T(8,128)S(1)}, f32[1032,128]{1,0:T(8,128)S(1)}, u32[]{:S(2)}, u32[]{:S(2)}) collective-permute-start(f32[1032,128]{1,0:T(8,128)S(1)} %collective-permute-done.12.states_ref.refs_13_), channel_id=1, source_target_pairs={{8,4},{9,5},{10,6},{11,7},{16,12},{17,13},{18,14},{19,15},{24,20},... | collective-permute-start | bytes 1585160 | tf_op jit(solution)/shard_map/ppermute | solution.py:470
  115.2 8.5 %collective-permute-start.19 = (f32[2064,128]{1,0:T(8,128)S(1)}, f32[2064,128]{1,0:T(8,128)S(1)}, u32[]{:S(2)}, u32[]{:S(2)}) collective-permute-start(f32[2064,128]{1,0:T(8,128)S(1)} %get-tuple-element.41.states_ref), channel_id=1, source_target_pairs={{4,0},{5,1},{6,2},{7,3},{12,8},{13,9},{14,10},{15,11},{20,16},{21,... | collective-permute-start | bytes 3170312 | tf_op jit(solution)/shard_map/ppermute | solution.py:470
  116.6 7.1 %collective-permute-start.20 = (f32[2064,128]{1,0:T(8,128)S(1)}, f32[2064,128]{1,0:T(8,128)S(1)}, u32[]{:S(2)}, u32[]{:S(2)}) collective-permute-start(f32[2064,128]{1,0:T(8,128)S(1)} %get-tuple-element.45), channel_id=1, source_target_pairs={{4,0},{5,1},{6,2},{7,3},{12,8},{13,9},{14,10},{15,11},{20,16},{21,... | collective-permute-start | bytes 3170312 | tf_op jit(solution)/shard_map/ppermute | solution.py:470
  118.0 16.0 %collective-permute-start.21 = (f32[2064,128]{1,0:T(8,128)S(1)}, f32[2064,128]{1,0:T(8,128)S(1)}, u32[]{:S(2)}, u32[]{:S(2)}) collective-permute-start(f32[2064,128]{1,0:T(8,128)S(1)} %get-tuple-element.41.states_ref), channel_id=1, source_target_pairs={{4,8},{5,9},{6,10},{7,11},{12,16},{13,17},{14,18},{15,19},{20,24},... | collective-permute-start | bytes 3170312 | tf_op jit(solution)/shard_map/ppermute | solution.py:470
  122.3 23.1 %collective-permute-start.22 = (f32[2064,128]{1,0:T(8,128)S(1)}, f32[2064,128]{1,0:T(8,128)S(1)}, u32[]{:S(2)}, u32[]{:S(2)}) collective-permute-start(f32[2064,128]{1,0:T(8,128)S(1)} %get-tuple-element.45), channel_id=1, source_target_pairs={{4,8},{5,9},{6,10},{7,11},{12,16},{13,17},{14,18},{15,19},{20,24},... | collective-permute-start | bytes 3170312 | tf_op jit(solution)/shard_map/ppermute | solution.py:470
  146.1 20.9 %collective-permute-start.25 = (f32[1024,128]{1,0:T(8,128)S(1)}, f32[1024,128]{1,0:T(8,128)S(1)}, u32[]{:S(2)}, u32[]{:S(2)}) collective-permute-start(f32[1024,128]{1,0:T(8,128)S(1)} %get-tuple-element.52), channel_id=1, source_target_pairs={{0,4},{1,5},{2,6},{3,7},{8,12},{9,13},{10,14},{11,15},{16,20},{17,... | collective-permute-start | bytes 1572872 | tf_op jit(solution)/shard_map/ppermute | solution.py:470
  155.6 8.6 %collective-permute-start.23 = (f32[512,128]{1,0:T(8,128)S(1)}, f32[512,128]{1,0:T(8,128)S(1)}, u32[]{:S(2)}, u32[]{:S(2)}) collective-permute-start(f32[512,128]{1,0:T(8,128)S(1)} %get-tuple-element.50), channel_id=1, source_target_pairs={{8,4},{9,5},{10,6},{11,7},{16,12},{17,13},{18,14},{19,15},{24,20},... | collective-permute-start | bytes 786440 | tf_op jit(solution)/shard_map/ppermute | solution.py:470
  156.9 10.1 %collective-permute-start.24 = (f32[512,128]{1,0:T(8,128)S(1)}, f32[512,128]{1,0:T(8,128)S(1)}, u32[]{:S(2)}, u32[]{:S(2)}) collective-permute-start(f32[512,128]{1,0:T(8,128)S(1)} %get-tuple-element.51), channel_id=1, source_target_pairs={{8,4},{9,5},{10,6},{11,7},{16,12},{17,13},{18,14},{19,15},{24,20},... | collective-permute-start | bytes 786440 | tf_op jit(solution)/shard_map/ppermute | solution.py:470

commit v3 on v2

--- a/solution.py
+++ b/solution.py
@@ -281,23 +281,32 @@
     return parts[s // size], 2 * (s % size)
 
 
-def send_kernel(sender, slots, group, modes, sum_parts, pick_parts, near_ref, right_ref, left_ref, *refs):
+def pick_kernel(sender, slots, group, parts, near_ref, *refs):
+    tab, sem_ref = refs[-2:]
+    picks = refs[-2 - parts : -2]
+    groups = Layout(refs[: -2 - parts], slots, group)
+
+    @pl.when(odd_depth() == sender)
+    def _():
+        pull([narrow(near_ref)], tab, sem_ref)
+        for s in range(slots):
+            pick, at = part_of(picks, s)
+            groups.fetch(parent_of(tab, s, slots), pick, at)
+
+
+def send_kernel(sender, slots, group, modes, parts, right_ref, left_ref, *refs):
     acc_ref, stage_ref, list_ref, tab, sem_ref = refs[-5:]
     tabs_ref = refs[-6]
     n = acc_ref.shape[1]
-    outs = refs[-6 - sum_parts - pick_parts : -6]
-    sums, picks = outs[:sum_parts], outs[sum_parts:]
-    groups = Layout(refs[: -6 - sum_parts - pick_parts], slots, group)
+    sums = refs[-6 - parts : -6]
+    groups = Layout(refs[: -6 - parts], slots, group)
 
     @pl.when(odd_depth() == sender)
     def _():
-        pull([groups.table(k) for k in range(group)] + [narrow(near_ref)], tab, sem_ref)
+        pull([groups.table(k) for k in range(group)], tab, sem_ref)
         for k in range(group):
             groups.copy_table(k, tabs_ref, k)
         acc_ref[...] = jnp.zeros_like(acc_ref)
-        for s in range(slots):
-            pick, at = part_of(picks, s)
-            groups.fetch(parent_of(tab, group * slots + s, slots), pick, at)
 
         def collect(c, count):
             mine = parent_of(tab, c, slots) < slots
@@ -533,17 +542,25 @@
     def free_parts(states, parity, times):
         return [free(states, parity, times, part, split_hop) for part in range(split_hop)]
 
-    def send(groups, sender, sum_parts, pick_parts, operators):
-        shapes = [mats(plain // sum_parts)] * sum_parts + [mats(plain // pick_parts)] * pick_parts
+    def pick(groups, sender, parts):
+        return call(
+            functools.partial(pick_kernel, sender, slots, group, parts),
+            [mats(plain // parts)] * parts,
+            limit,
+            (near_table, *groups),
+            scratch=tables(1),
+        )
+
+    def send(groups, sender, parts, operators):
         outs = call(
-            functools.partial(send_kernel, sender, slots, group, modes, sum_parts, pick_parts),
-            [*shapes, sds(group, ROWS, n)],
+            functools.partial(send_kernel, sender, slots, group, modes, parts),
+            [mats(plain // parts)] * parts + [sds(group, ROWS, n)],
             limit,
-            (near_table, *operators, *groups),
+            (*operators, *groups),
             us=2,
-            scratch=[stage, stage, SMEM((total,), jnp.int32), *tables(group + 1)],
+            scratch=[stage, stage, SMEM((total,), jnp.int32), *tables(group)],
         )
-        return outs[:sum_parts], outs[sum_parts:-1], outs[-1]
+        return outs[:parts], outs[-1]
 
     def join(frees, sums, picks, receiver, operators):
         return call(
@@ -568,8 +585,8 @@
 
     free_even = free(packed, 0, 1)
     free_odd = [part for k in ranks for part in free_parts(first[k], 1, 2)]
-    sums, picks, tabs_odd = send(first, 1, 1, split_hop, operators_odd)
-    picks = [shift(value, 1, 1) for value in picks]
+    picks = [shift(value, 1, 1) for value in pick(first, 1, split_hop)]
+    sums, tabs_odd = send(first, 1, 1, operators_odd)
     sums = [shift(value, -1, 1) for value in sums]
     own_state = join([free_even], sums, picks, 0, operators_odd)
 
@@ -577,9 +594,9 @@
     from_below = [shift(value, -1, 0) for value in gathered]
     from_above = [shift(value, 1, 0) for value in gathered]
     free_even = [part for k in ranks for part in free_parts(gathered[k], 0, 2)]
-    states, _ = side("parents", free_odd, from_above, [tabs_odd], 1, operators_odd)
     ready = group - 1
-    states, _ = side("children", [states], from_below[:ready], [tabs_odd], 1, operators_odd, span=(0, ready))
+    states, _ = side("children", free_odd, from_below[:ready], [tabs_odd], 1, operators_odd, span=(0, ready))
+    states, _ = side("parents", [states], from_above, [tabs_odd], 1, operators_odd)
     states = side("children", [states], from_below[ready:], [tabs_odd], 1, operators_odd, second=True, span=(ready, 1))
 
     from_above = [shift(value, 1, 1) for value in states]
@@ -592,9 +609,9 @@
     states, tabs_even = side("children", free_even, from_below, gathered, 0, operators_even)
     states = side("parents", [states], from_above, [tabs_even], 0, operators_even, second=True)
 
-    sums, picks, _ = send(states, 0, split_hop, 1, operators_even)
+    sums, _ = send(states, 0, split_hop, operators_even)
     sums = [shift(value, -1, 0) for value in sums]
-    picks = [shift(value, 1, 0) for value in picks]
+    picks = [shift(value, 1, 0) for value in pick(states, 0, 1)]
     last_even = free(states[0], 0, 1)
     return join([last_odd, last_even], sums, picks, 1, operators_odd).reshape(blocks.shape)
 

time: 170 us -> 171 us (level)
  the two profiles are of different devices: /device:TPU:11 before, /device:TPU:3 now
where the time goes in v3:
time: 171 us; the launch traced here: 170 us
  waiting for transfers between devices  65.8 us (38%)
  Pallas kernels  61.3 us (36%)
  starting transfers between devices  42 us (25%)
    ppermute x26, waiting for transfers between devices, permute(): return lax.ppermute(value, AXES, pairs)  65.8 us
    pallas_call x34, Pallas kernels, call(): pl.pallas_call(kernel, out_shape=out_shapes, in_specs=specs, out_specs=ja...  61.3 us
    ppermute x26, starting transfers between devices, permute(): return lax.ppermute(value, AXES, pairs)  42 us
  transfers between devices with their start and end apart: 26, of which 12 were waited for; matrix products, arithmetic and copies ran while one was open for 0% of the time, Pallas kernels for 33%

profile of v3, /device:TPU:3, one launch (start us, length us, event | category | flops | bytes accessed | tf_op | source)
XLA Modules:
  0.0 170.4 jit_solution(4348418618309901481)
XLA Ops:
  0.0 2.0 %shard_map.91 = (f32[1288,128]{1,0:T(8,128)}, f32[8,128]{1,0:T(8,128)}) custom-call(s32[4]{0:T(128)} %live_ref.1, s32[4]{0:T(128)} %parent_ref.1, s32[4]{0:T(128)} %mode_ref.1, f32[4]{0:T(128)} %damping_ref.1, f32[4]{0:T(128)} %weight_ref.1, f32[2,2]{1,0:T(2,128)} %corr_ref.1, f32[1024,128]{1,0:T(8,128)} %bitcast.6, f32[256,128]{1,0:T(8,128)} %bitcast.3), custom_call_target="tpu_custom_call" | custom-call | flops 1100000000 | bytes 524288 | tf_op jit(solution)/shard_map/pallas_call | solution.py:450
  2.0 4.2 %collective-permute-start.1 = (f32[1288,128]{1,0:T(8,128)}, f32[1288,128]{1,0:T(8,128)S(1)}, u32[]{:S(2)}, u32[]{:S(2)}) collective-permute-start(f32[1288,128]{1,0:T(8,128)} %get-tuple-element.29.refs_0_.states_ref), channel_id=1, source_target_pairs={{4,6},{5,7},{6,4},{7,5},{12,14},{13,15},{14,12},{15,13},{20,22},{2... | collective-permute-start | bytes 1978376 | tf_op jit(solution)/shard_map/ppermute | solution.py:479
  6.2 3.2 %collective-permute-start = (f32[1288,128]{1,0:T(8,128)}, f32[1288,128]{1,0:T(8,128)S(1)}, u32[]{:S(2)}, u32[]{:S(2)}) collective-permute-start(f32[1288,128]{1,0:T(8,128)} %get-tuple-element.29.refs_0_.states_ref), channel_id=1, source_target_pairs={{4,5},{5,4},{6,7},{7,6},{12,13},{13,12},{14,15},{15,14},{20,21},{2... | collective-permute-start | bytes 1978376 | tf_op jit(solution)/shard_map/ppermute | solution.py:479
  9.5 2.1 %collective-permute-start.4 = (f32[8,128]{1,0:T(8,128)}, f32[8,128]{1,0:T(8,128)S(1)}, u32[]{:S(2)}, u32[]{:S(2)}) collective-permute-start(f32[8,128]{1,0:T(8,128)} %get-tuple-element.28.own_ref), channel_id=1, source_target_pairs={{4,0},{5,1},{6,2},{7,3},{8,4},{9,5},{10,6},{11,7},{12,8},{13,9},{1... | collective-permute-start | bytes 12296 | tf_op jit(solution)/shard_map/ppermute | solution.py:479
  11.5 0.7 shard_map.93
  12.3 4.2 %shard_map.94.refs_0_ = f32[512,128]{1,0:T(8,128)S(1)} custom-call(f32[1288,128]{1,0:T(8,128)S(1)} %copy-done.1, bf16[384,512]{1,0:T(8,128)(2,1)S(1)} %get-tuple-element.32.right_ref, bf16[128,1536]{1,0:T(8,128)(2,1)S(1)} %get-tuple-element.33.left_ref), custom_call_target="tpu_custom_call" | custom-call | flops 4950000128 | bytes 524288 | tf_op jit(solution)/shard_map/pallas_call | solution.py:450
  16.5 4.2 %shard_map.95.refs_1_ = f32[512,128]{1,0:T(8,128)S(1)} custom-call(f32[1288,128]{1,0:T(8,128)S(1)} %copy-done.1, bf16[384,512]{1,0:T(8,128)(2,1)S(1)} %get-tuple-element.32.right_ref, bf16[128,1536]{1,0:T(8,128)(2,1)S(1)} %get-tuple-element.33.left_ref), custom_call_target="tpu_custom_call" | custom-call | flops 4950000128 | bytes 524288 | tf_op jit(solution)/shard_map/pallas_call | solution.py:450
  20.7 0.9 collective-permute-done.1.refs_2_.states_ref
  21.7 2.6 %collective-permute-start.2 = (f32[1288,128]{1,0:T(8,128)S(1)}, f32[1288,128]{1,0:T(8,128)S(1)}, u32[]{:S(2)}, u32[]{:S(2)}) collective-permute-start(f32[1288,128]{1,0:T(8,128)S(1)} %collective-permute-done.1.refs_2_.states_ref), channel_id=1, source_target_pairs={{4,5},{5,4},{6,7},{7,6},{12,13},{13,12},{14,15},{15,14},{20,21},{2... | collective-permute-start | bytes 1978376 | tf_op jit(solution)/shard_map/ppermute | solution.py:479
  24.3 4.2 %shard_map.98.refs_4_ = f32[512,128]{1,0:T(8,128)S(1)} custom-call(f32[1288,128]{1,0:T(8,128)S(1)} %collective-permute-done.1.refs_2_.states_ref, bf16[384,512]{1,0:T(8,128)(2,1)S(1)} %get-tuple-element.32.right_ref, bf16[128,1536]{1,0:T(8,128)(2,1)S(1)} %get-tuple-element.33.left_ref), custom_call_target="tpu_custom_call" | custom-call | flops 4950000128 | bytes 524288 | tf_op jit(solution)/shard_map/pallas_call | solution.py:450
  28.5 4.2 %shard_map.99.refs_5_ = f32[512,128]{1,0:T(8,128)S(1)} custom-call(f32[1288,128]{1,0:T(8,128)S(1)} %collective-permute-done.1.refs_2_.states_ref, bf16[384,512]{1,0:T(8,128)(2,1)S(1)} %get-tuple-element.32.right_ref, bf16[128,1536]{1,0:T(8,128)(2,1)S(1)} %get-tuple-element.33.left_ref), custom_call_target="tpu_custom_call" | custom-call | flops 4950000128 | bytes 524288 | tf_op jit(solution)/shard_map/pallas_call | solution.py:450
  32.7 0.0 collective-permute-done.refs_1_.states_ref
  32.7 4.2 %shard_map.96.refs_2_ = f32[512,128]{1,0:T(8,128)S(1)} custom-call(f32[1288,128]{1,0:T(8,128)S(1)} %collective-permute-done.refs_1_.states_ref, bf16[384,512]{1,0:T(8,128)(2,1)S(1)} %get-tuple-element.32.right_ref, bf16[128,1536]{1,0:T(8,128)(2,1)S(1)} %get-tuple-element.33.left_ref), custom_call_target="tpu_custom_call" | custom-call | flops 4950000128 | bytes 524288 | tf_op jit(solution)/shard_map/pallas_call | solution.py:450
  36.9 0.0 copy-start.2
  37.0 4.2 %shard_map.97.refs_3_ = f32[512,128]{1,0:T(8,128)S(1)} custom-call(f32[1288,128]{1,0:T(8,128)S(1)} %collective-permute-done.refs_1_.states_ref, bf16[384,512]{1,0:T(8,128)(2,1)S(1)} %get-tuple-element.32.right_ref, bf16[128,1536]{1,0:T(8,128)(2,1)S(1)} %get-tuple-element.33.left_ref), custom_call_target="tpu_custom_call" | custom-call | flops 4950000128 | bytes 524288 | tf_op jit(solution)/shard_map/pallas_call | solution.py:450
  41.2 0.0 collective-permute-done.2.refs_3_.states_ref
  41.2 0.2 shard_map.92
  41.4 2.6 %shard_map.103 = (f32[1024,128]{1,0:T(8,128)S(1)}, f32[4,8,128]{2,1,0:T(8,128)S(1)}) custom-call(bf16[8,384,128]{2,1,0:T(8,128)(2,1)S(1)} %get-tuple-element.30.right_ref, bf16[8,128,384]{2,1,0:T(8,128)(2,1)S(1)} %get-tuple-element.31.left_ref, f32[1288,128]{1,0:T(8,128)S(1)} %copy-done.1, f32[1288,128]{1,0:T(8,128)S(1)} %collective-permute-done.refs_1_.states_ref, ...), custom_call_target="tpu_custom_call" | custom-call | flops 2200000000 | bytes 524288 | tf_op jit(solution)/shard_map/pallas_call | solution.py:450
  44.1 1.3 collective-permute-start.3
  45.4 0.8 shard_map.104
  46.2 1.3 collective-permute-start.5
  47.5 1.3 collective-permute-start.6
  48.8 1.3 collective-permute-start.18
  50.1 4.2 %shard_map.100.refs_6_ = f32[512,128]{1,0:T(8,128)S(1)} custom-call(f32[1288,128]{1,0:T(8,128)S(1)} %collective-permute-done.2.refs_3_.states_ref, bf16[384,512]{1,0:T(8,128)(2,1)S(1)} %get-tuple-element.32.right_ref, bf16[128,1536]{1,0:T(8,128)(2,1)S(1)} %get-tuple-element.33.left_ref), custom_call_target="tpu_custom_call" | custom-call | flops 4950000128 | bytes 524288 | tf_op jit(solution)/shard_map/pallas_call | solution.py:450
  54.3 4.2 %shard_map.101.refs_7_ = f32[512,128]{1,0:T(8,128)S(1)} custom-call(f32[1288,128]{1,0:T(8,128)S(1)} %collective-permute-done.2.refs_3_.states_ref, bf16[384,512]{1,0:T(8,128)(2,1)S(1)} %get-tuple-element.32.right_ref, bf16[128,1536]{1,0:T(8,128)(2,1)S(1)} %get-tuple-element.33.left_ref), custom_call_target="tpu_custom_call" | custom-call | flops 4950000128 | bytes 524288 | tf_op jit(solution)/shard_map/pallas_call | solution.py:450
  58.6 0.0 copy-start
  58.6 0.6 copy-done
  59.3 0.7 collective-permute-start.10
  60.0 0.7 collective-permute-start.8
  60.7 1.3 collective-permute-start.7
  62.0 1.3 collective-permute-start.12
  63.3 0.2 shard_map.111.refs_0_
  63.5 1.3 collective-permute-start.11
  64.8 0.7 collective-permute-start.15
  65.5 1.3 collective-permute-start.9
  66.9 6.0 %collective-permute-done.7.refs_8_ = f32[1032,128]{1,0:T(8,128)S(1)} collective-permute-done((f32[1032,128]{1,0:T(8,128)S(1)}, f32[1032,128]{1,0:T(8,128)S(1)}, u32[]{:S(2)}, u32[]{:S(2)}) %collective-permute-start.7) | collective-permute-done | bytes 528416 | tf_op jit(solution)/shard_map/ppermute | solution.py:479
  72.9 1.3 collective-permute-start.13
  74.2 9.8 %collective-permute-done.11.refs_10_ = f32[1032,128]{1,0:T(8,128)S(1)} collective-permute-done((f32[1032,128]{1,0:T(8,128)S(1)}, f32[1032,128]{1,0:T(8,128)S(1)}, u32[]{:S(2)}, u32[]{:S(2)}) %collective-permute-start.11) | collective-permute-done | bytes 528416 | tf_op jit(solution)/shard_map/ppermute | solution.py:479
  84.1 1.3 collective-permute-start.14
  85.4 1.3 collective-permute-start.16
  86.7 3.0 %collective-permute-done.9.refs_9_ = f32[1032,128]{1,0:T(8,128)S(1)} collective-permute-done((f32[1032,128]{1,0:T(8,128)S(1)}, f32[1032,128]{1,0:T(8,128)S(1)}, u32[]{:S(2)}, u32[]{:S(2)}) %collective-permute-start.9) | collective-permute-done | bytes 528416 | tf_op jit(solution)/shard_map/ppermute | solution.py:479
  89.7 1.3 collective-permute-start.17
  91.0 3.7 %shard_map.106 = (f32[4096,128]{1,0:T(8,128)S(1)}, f32[4,8,128]{2,1,0:T(8,128)}) custom-call(bf16[8,384,128]{2,1,0:T(8,128)(2,1)S(1)} %get-tuple-element.30.right_ref, bf16[8,128,384]{2,1,0:T(8,128)(2,1)S(1)} %get-tuple-element.31.left_ref, f32[512,128]{1,0:T(8,128)S(1)} %shard_map.94.refs_0_, f32[512,128]{1,0:T(8,128)S(1)} %shard_map.95.refs_1_, ...), custom_call_target="tpu_custom_call" | custom-call | flops 3300000000 | bytes 524288 | tf_op jit(solution)/shard_map/pallas_call | solution.py:450
  94.7 5.0 %collective-permute-done.13.refs_2_ = f32[1032,128]{1,0:T(8,128)S(1)} collective-permute-done((f32[1032,128]{1,0:T(8,128)S(1)}, f32[1032,128]{1,0:T(8,128)S(1)}, u32[]{:S(2)}, u32[]{:S(2)}) %collective-permute-start.13) | collective-permute-done | bytes 528416 | tf_op jit(solution)/shard_map/ppermute | solution.py:479
  99.7 1.3 collective-permute-done.14.refs_3_
  101.0 1.3 collective-permute-done.16.refs_4_
  102.3 4.4 %shard_map.107 = (f32[4096,128]{1,0:T(8,128)S(1)}, f32[4,8,128]{2,1,0:T(8,128)}) custom-call(bf16[8,384,128]{2,1,0:T(8,128)(2,1)S(1)} %get-tuple-element.30.right_ref, bf16[8,128,384]{2,1,0:T(8,128)(2,1)S(1)} %get-tuple-element.31.left_ref, f32[4096,128]{1,0:T(8,128)S(1)} %get-tuple-element.38.refs_0_, f32[1032,128]{1,0:T(8,128)S(1)} %collective-permute-done.12.refs_1_, ...), custom_call_target="tpu_custom_call" | custom-call | flops 3300000000 | bytes 524288 | tf_op jit(solution)/shard_map/pallas_call | solution.py:450
  106.7 8.6 %collective-permute-done.17.refs_1_ = f32[1032,128]{1,0:T(8,128)S(1)} collective-permute-done((f32[1032,128]{1,0:T(8,128)S(1)}, f32[1032,128]{1,0:T(8,128)S(1)}, u32[]{:S(2)}, u32[]{:S(2)}) %collective-permute-start.17) | collective-permute-done | bytes 528416 | tf_op jit(solution)/shard_map/ppermute | solution.py:479
  115.4 1.6 shard_map.108
  117.0 1.4 collective-permute-start.19
  118.4 1.4 collective-permute-start.20
  119.8 4.3 %collective-permute-start.21 = (f32[2064,128]{1,0:T(8,128)S(1)}, f32[2064,128]{1,0:T(8,128)S(1)}, u32[]{:S(2)}, u32[]{:S(2)}) collective-permute-start(f32[2064,128]{1,0:T(8,128)S(1)} %get-tuple-element.40.states_ref), channel_id=1, source_target_pairs={{4,8},{5,9},{6,10},{7,11},{12,16},{13,17},{14,18},{15,19},{20,24},... | collective-permute-start | bytes 3170312 | tf_op jit(solution)/shard_map/ppermute | solution.py:479
  124.1 1.4 collective-permute-start.22
  125.4 8.2 %shard_map.109.refs_0_ = f32[1024,128]{1,0:T(8,128)S(1)} custom-call(f32[2064,128]{1,0:T(8,128)S(1)} %get-tuple-element.40.states_ref, bf16[384,512]{1,0:T(8,128)(2,1)S(1)} %get-tuple-element.32.right_ref, bf16[128,1536]{1,0:T(8,128)(2,1)S(1)} %get-tuple-element.33.left_ref), custom_call_target="tpu_custom_call" | custom-call | flops 9900000256 | bytes 524288 | tf_op jit(solution)/shard_map/pallas_call | solution.py:450
  133.6 0.3 shard_map.119
  134.0 1.8 %collective-permute-done.21.refs_1_ = f32[2064,128]{1,0:T(8,128)S(1)} collective-permute-done((f32[2064,128]{1,0:T(8,128)S(1)}, f32[2064,128]{1,0:T(8,128)S(1)}, u32[]{:S(2)}, u32[]{:S(2)}) %collective-permute-start.21) | collective-permute-done | bytes 1056800 | tf_op jit(solution)/shard_map/ppermute | solution.py:479
  135.8 11.3 %collective-permute-done.22.refs_2_ = f32[2064,128]{1,0:T(8,128)S(1)} collective-permute-done((f32[2064,128]{1,0:T(8,128)S(1)}, f32[2064,128]{1,0:T(8,128)S(1)}, u32[]{:S(2)}, u32[]{:S(2)}) %collective-permute-start.22) | collective-permute-done | bytes 1056800 | tf_op jit(solution)/shard_map/ppermute | solution.py:479
  147.2 1.3 collective-permute-start.25
  148.5 0.7 shard_map.122
  149.2 1.3 collective-permute-start.23
  150.5 1.3 collective-permute-start.24
  151.8 13.7 %collective-permute-done.23.refs_2_ = f32[512,128]{1,0:T(8,128)S(1)} collective-permute-done((f32[512,128]{1,0:T(8,128)S(1)}, f32[512,128]{1,0:T(8,128)S(1)}, u32[]{:S(2)}, u32[]{:S(2)}) %collective-permute-start.23) | collective-permute-done | bytes 262176 | tf_op jit(solution)/shard_map/ppermute | solution.py:479
  165.5 2.8 %collective-permute-done.24.refs_3_ = f32[512,128]{1,0:T(8,128)S(1)} collective-permute-done((f32[512,128]{1,0:T(8,128)S(1)}, f32[512,128]{1,0:T(8,128)S(1)}, u32[]{:S(2)}, u32[]{:S(2)}) %collective-permute-start.24) | collective-permute-done | bytes 262176 | tf_op jit(solution)/shard_map/ppermute | solution.py:479
  168.3 1.9 %shard_map.124 = f32[1024,128]{1,0:T(8,128)} custom-call(f32[8,128]{1,0:T(8,128)S(1)} %copy-done, bf16[8,384,128]{2,1,0:T(8,128)(2,1)S(1)} %get-tuple-element.30.right_ref, bf16[8,128,384]{2,1,0:T(8,128)(2,1)S(1)} %get-tuple-element.31.left_ref, f32[1024,128]{1,0:T(8,128)S(1)} %shard_map.109.refs_0_, f32[1024,128]{1,0:T(8,128)S(1)} %shard_map.121.refs_1_, ...), custom_call_target="tpu_custom_call" | custom-call | flops 1100000000 | bytes 524288 | tf_op jit(solution)/shard_map/pallas_call | solution.py:450
  (30 shorter events, 0.3 us)
Async XLA Ops:
  0.0 11.5 %copy-start.3 = (f32[128,128]{1,0:T(8,128)S(1)}, f32[128,128]{1,0:T(8,128)}, u32[]{:S(2)}) copy-start(f32[128,128]{1,0:T(8,128)} %ham_ref.1) | copy-start | bytes 196612
  2.0 19.6 %collective-permute-start.1 = (f32[1288,128]{1,0:T(8,128)}, f32[1288,128]{1,0:T(8,128)S(1)}, u32[]{:S(2)}, u32[]{:S(2)}) collective-permute-start(f32[1288,128]{1,0:T(8,128)} %get-tuple-element.29.refs_0_.states_ref), channel_id=1, source_target_pairs={{4,6},{5,7},{6,4},{7,5},{12,14},{13,15},{14,12},{15,13},{20,22},{2... | collective-permute-start | bytes 1978376 | tf_op jit(solution)/shard_map/ppermute | solution.py:479
  6.2 26.5 %collective-permute-start = (f32[1288,128]{1,0:T(8,128)}, f32[1288,128]{1,0:T(8,128)S(1)}, u32[]{:S(2)}, u32[]{:S(2)}) collective-permute-start(f32[1288,128]{1,0:T(8,128)} %get-tuple-element.29.refs_0_.states_ref), channel_id=1, source_target_pairs={{4,5},{5,4},{6,7},{7,6},{12,13},{13,12},{14,15},{15,14},{20,21},{2... | collective-permute-start | bytes 1978376 | tf_op jit(solution)/shard_map/ppermute | solution.py:479
  9.4 2.8 %copy-start.1 = (f32[1288,128]{1,0:T(8,128)S(1)}, f32[1288,128]{1,0:T(8,128)}, u32[]{:S(2)}) copy-start(f32[1288,128]{1,0:T(8,128)} %get-tuple-element.29.refs_0_.states_ref) | copy-start | bytes 1978372
  9.5 35.9 %collective-permute-start.4 = (f32[8,128]{1,0:T(8,128)}, f32[8,128]{1,0:T(8,128)S(1)}, u32[]{:S(2)}, u32[]{:S(2)}) collective-permute-start(f32[8,128]{1,0:T(8,128)} %get-tuple-element.28.own_ref), channel_id=1, source_target_pairs={{4,0},{5,1},{6,2},{7,3},{8,4},{9,5},{10,6},{11,7},{12,8},{13,9},{1... | collective-permute-start | bytes 12296 | tf_op jit(solution)/shard_map/ppermute | solution.py:479
  21.7 19.5 %collective-permute-start.2 = (f32[1288,128]{1,0:T(8,128)S(1)}, f32[1288,128]{1,0:T(8,128)S(1)}, u32[]{:S(2)}, u32[]{:S(2)}) collective-permute-start(f32[1288,128]{1,0:T(8,128)S(1)} %collective-permute-done.1.refs_2_.states_ref), channel_id=1, source_target_pairs={{4,5},{5,4},{6,7},{7,6},{12,13},{13,12},{14,15},{15,14},{20,21},{2... | collective-permute-start | bytes 1978376 | tf_op jit(solution)/shard_map/ppermute | solution.py:479
  36.9 4.2 %copy-start.2 = (f32[2,128,128]{2,1,0:T(8,128)S(1)}, f32[2,128,128]{2,1,0:T(8,128)}, u32[]{:S(2)}) copy-start(f32[2,128,128]{2,1,0:T(8,128)} %param.14) | copy-start | bytes 393220
  44.1 14.6 %collective-permute-start.3 = (f32[1024,128]{1,0:T(8,128)S(1)}, f32[1024,128]{1,0:T(8,128)S(1)}, u32[]{:S(2)}, u32[]{:S(2)}) collective-permute-start(f32[1024,128]{1,0:T(8,128)S(1)} %get-tuple-element.34), channel_id=1, source_target_pairs={{4,0},{5,1},{6,2},{7,3},{12,8},{13,9},{14,10},{15,11},{20,16},{21,... | collective-permute-start | bytes 1572872 | tf_op jit(solution)/shard_map/ppermute | solution.py:479
  46.2 12.4 %collective-permute-start.5 = (f32[512,128]{1,0:T(8,128)S(1)}, f32[512,128]{1,0:T(8,128)S(1)}, u32[]{:S(2)}, u32[]{:S(2)}) collective-permute-start(f32[512,128]{1,0:T(8,128)S(1)} %get-tuple-element.35), channel_id=1, source_target_pairs={{4,8},{5,9},{6,10},{7,11},{12,16},{13,17},{14,18},{15,19},{20,24},... | collective-permute-start | bytes 786440 | tf_op jit(solution)/shard_map/ppermute | solution.py:479
  47.5 11.1 %collective-permute-start.6 = (f32[512,128]{1,0:T(8,128)S(1)}, f32[512,128]{1,0:T(8,128)S(1)}, u32[]{:S(2)}, u32[]{:S(2)}) collective-permute-start(f32[512,128]{1,0:T(8,128)S(1)} %get-tuple-element.36), channel_id=1, source_target_pairs={{4,8},{5,9},{6,10},{7,11},{12,16},{13,17},{14,18},{15,19},{20,24},... | collective-permute-start | bytes 786440 | tf_op jit(solution)/shard_map/ppermute | solution.py:479
  48.8 9.8 %collective-permute-start.18 = (f32[768,128]{1,0:T(8,128)S(1)}, f32[768,128]{1,0:T(8,128)S(1)}, u32[]{:S(2)}, u32[]{:S(2)}) collective-permute-start(f32[768,128]{1,0:T(8,128)S(1)} %get-tuple-element.41), channel_id=1, source_target_pairs={{4,0},{5,1},{6,2},{7,3},{12,8},{13,9},{14,10},{15,11},{20,16},{21,... | collective-permute-start | bytes 1179656 | tf_op jit(solution)/shard_map/ppermute | solution.py:479
  58.6 0.7 copy-start
  59.3 4.2 %collective-permute-start.10 = (f32[1032,128]{1,0:T(8,128)S(1)}, f32[1032,128]{1,0:T(8,128)S(1)}, u32[]{:S(2)}, u32[]{:S(2)}) collective-permute-start(f32[1032,128]{1,0:T(8,128)S(1)} %shard_map.105.states_ref.refs_10_), channel_id=1, source_target_pairs={{0,2},{1,3},{2,0},{3,1},{8,10},{9,11},{10,8},{11,9},{16,18},{17,19... | collective-permute-start | bytes 1585160 | tf_op jit(solution)/shard_map/ppermute | solution.py:479
  60.0 5.6 %collective-permute-start.8 = (f32[1032,128]{1,0:T(8,128)S(1)}, f32[1032,128]{1,0:T(8,128)S(1)}, u32[]{:S(2)}, u32[]{:S(2)}) collective-permute-start(f32[1032,128]{1,0:T(8,128)S(1)} %shard_map.105.states_ref.refs_10_), channel_id=1, source_target_pairs={{0,1},{1,0},{2,3},{3,2},{8,9},{9,8},{10,11},{11,10},{16,17},{17,16... | collective-permute-start | bytes 1585160 | tf_op jit(solution)/shard_map/ppermute | solution.py:479
  60.7 12.3 %collective-permute-start.7 = (f32[1032,128]{1,0:T(8,128)S(1)}, f32[1032,128]{1,0:T(8,128)S(1)}, u32[]{:S(2)}, u32[]{:S(2)}) collective-permute-start(f32[1032,128]{1,0:T(8,128)S(1)} %shard_map.105.states_ref.refs_10_), channel_id=1, source_target_pairs={{8,4},{9,5},{10,6},{11,7},{16,12},{17,13},{18,14},{19,15},{24,20},... | collective-permute-start | bytes 1585160 | tf_op jit(solution)/shard_map/ppermute | solution.py:479
  62.0 32.7 %collective-permute-start.12 = (f32[1032,128]{1,0:T(8,128)S(1)}, f32[1032,128]{1,0:T(8,128)S(1)}, u32[]{:S(2)}, u32[]{:S(2)}) collective-permute-start(f32[1032,128]{1,0:T(8,128)S(1)} %shard_map.105.states_ref.refs_10_), channel_id=1, source_target_pairs={{0,4},{1,5},{2,6},{3,7},{8,12},{9,13},{10,14},{11,15},{16,20},{17,... | collective-permute-start | bytes 1585160 | tf_op jit(solution)/shard_map/ppermute | solution.py:479
  63.5 20.5 %collective-permute-start.11 = (f32[1032,128]{1,0:T(8,128)S(1)}, f32[1032,128]{1,0:T(8,128)S(1)}, u32[]{:S(2)}, u32[]{:S(2)}) collective-permute-start(f32[1032,128]{1,0:T(8,128)S(1)} %collective-permute-done.10.states_ref.refs_12_), channel_id=1, source_target_pairs={{8,4},{9,5},{10,6},{11,7},{16,12},{17,13},{18,14},{19,15},{24,20},... | collective-permute-start | bytes 1585160 | tf_op jit(solution)/shard_map/ppermute | solution.py:479
  64.8 20.5 %collective-permute-start.15 = (f32[1032,128]{1,0:T(8,128)S(1)}, f32[1032,128]{1,0:T(8,128)S(1)}, u32[]{:S(2)}, u32[]{:S(2)}) collective-permute-start(f32[1032,128]{1,0:T(8,128)S(1)} %collective-permute-done.10.states_ref.refs_12_), channel_id=1, source_target_pairs={{0,1},{1,0},{2,3},{3,2},{8,9},{9,8},{10,11},{11,10},{16,17},{17,16... | collective-permute-start | bytes 1585160 | tf_op jit(solution)/shard_map/ppermute | solution.py:479
  65.5 24.2 %collective-permute-start.9 = (f32[1032,128]{1,0:T(8,128)S(1)}, f32[1032,128]{1,0:T(8,128)S(1)}, u32[]{:S(2)}, u32[]{:S(2)}) collective-permute-start(f32[1032,128]{1,0:T(8,128)S(1)} %collective-permute-done.8.states_ref.refs_11_), channel_id=1, source_target_pairs={{8,4},{9,5},{10,6},{11,7},{16,12},{17,13},{18,14},{19,15},{24,20},... | collective-permute-start | bytes 1585160 | tf_op jit(solution)/shard_map/ppermute | solution.py:479
  72.9 26.7 %collective-permute-start.13 = (f32[1032,128]{1,0:T(8,128)S(1)}, f32[1032,128]{1,0:T(8,128)S(1)}, u32[]{:S(2)}, u32[]{:S(2)}) collective-permute-start(f32[1032,128]{1,0:T(8,128)S(1)} %collective-permute-done.8.states_ref.refs_11_), channel_id=1, source_target_pairs={{0,4},{1,5},{2,6},{3,7},{8,12},{9,13},{10,14},{11,15},{16,20},{17,... | collective-permute-start | bytes 1585160 | tf_op jit(solution)/shard_map/ppermute | solution.py:479
  84.1 17.0 %collective-permute-start.14 = (f32[1032,128]{1,0:T(8,128)S(1)}, f32[1032,128]{1,0:T(8,128)S(1)}, u32[]{:S(2)}, u32[]{:S(2)}) collective-permute-start(f32[1032,128]{1,0:T(8,128)S(1)} %collective-permute-done.10.states_ref.refs_12_), channel_id=1, source_target_pairs={{0,4},{1,5},{2,6},{3,7},{8,12},{9,13},{10,14},{11,15},{16,20},{17,... | collective-permute-start | bytes 1585160 | tf_op jit(solution)/shard_map/ppermute | solution.py:479
  85.4 17.0 %collective-permute-start.16 = (f32[1032,128]{1,0:T(8,128)S(1)}, f32[1032,128]{1,0:T(8,128)S(1)}, u32[]{:S(2)}, u32[]{:S(2)}) collective-permute-start(f32[1032,128]{1,0:T(8,128)S(1)} %collective-permute-done.15.states_ref.refs_13_), channel_id=1, source_target_pairs={{0,4},{1,5},{2,6},{3,7},{8,12},{9,13},{10,14},{11,15},{16,20},{17,... | collective-permute-start | bytes 1585160 | tf_op jit(solution)/shard_map/ppermute | solution.py:479
  89.7 25.7 %collective-permute-start.17 = (f32[1032,128]{1,0:T(8,128)S(1)}, f32[1032,128]{1,0:T(8,128)S(1)}, u32[]{:S(2)}, u32[]{:S(2)}) collective-permute-start(f32[1032,128]{1,0:T(8,128)S(1)} %collective-permute-done.15.states_ref.refs_13_), channel_id=1, source_target_pairs={{8,4},{9,5},{10,6},{11,7},{16,12},{17,13},{18,14},{19,15},{24,20},... | collective-permute-start | bytes 1585160 | tf_op jit(solution)/shard_map/ppermute | solution.py:479
  117.0 16.6 %collective-permute-start.19 = (f32[2064,128]{1,0:T(8,128)S(1)}, f32[2064,128]{1,0:T(8,128)S(1)}, u32[]{:S(2)}, u32[]{:S(2)}) collective-permute-start(f32[2064,128]{1,0:T(8,128)S(1)} %get-tuple-element.40.states_ref), channel_id=1, source_target_pairs={{4,0},{5,1},{6,2},{7,3},{12,8},{13,9},{14,10},{15,11},{20,16},{21,... | collective-permute-start | bytes 3170312 | tf_op jit(solution)/shard_map/ppermute | solution.py:479
  118.4 15.3 %collective-permute-start.20 = (f32[2064,128]{1,0:T(8,128)S(1)}, f32[2064,128]{1,0:T(8,128)S(1)}, u32[]{:S(2)}, u32[]{:S(2)}) collective-permute-start(f32[2064,128]{1,0:T(8,128)S(1)} %get-tuple-element.44), channel_id=1, source_target_pairs={{4,0},{5,1},{6,2},{7,3},{12,8},{13,9},{14,10},{15,11},{20,16},{21,... | collective-permute-start | bytes 3170312 | tf_op jit(solution)/shard_map/ppermute | solution.py:479
  119.8 16.1 %collective-permute-start.21 = (f32[2064,128]{1,0:T(8,128)S(1)}, f32[2064,128]{1,0:T(8,128)S(1)}, u32[]{:S(2)}, u32[]{:S(2)}) collective-permute-start(f32[2064,128]{1,0:T(8,128)S(1)} %get-tuple-element.40.states_ref), channel_id=1, source_target_pairs={{4,8},{5,9},{6,10},{7,11},{12,16},{13,17},{14,18},{15,19},{20,24},... | collective-permute-start | bytes 3170312 | tf_op jit(solution)/shard_map/ppermute | solution.py:479
  124.1 23.1 %collective-permute-start.22 = (f32[2064,128]{1,0:T(8,128)S(1)}, f32[2064,128]{1,0:T(8,128)S(1)}, u32[]{:S(2)}, u32[]{:S(2)}) collective-permute-start(f32[2064,128]{1,0:T(8,128)S(1)} %get-tuple-element.44), channel_id=1, source_target_pairs={{4,8},{5,9},{6,10},{7,11},{12,16},{13,17},{14,18},{15,19},{20,24},... | collective-permute-start | bytes 3170312 | tf_op jit(solution)/shard_map/ppermute | solution.py:479
  147.2 21.1 %collective-permute-start.25 = (f32[1024,128]{1,0:T(8,128)S(1)}, f32[1024,128]{1,0:T(8,128)S(1)}, u32[]{:S(2)}, u32[]{:S(2)}) collective-permute-start(f32[1024,128]{1,0:T(8,128)S(1)} %shard_map.123), channel_id=1, source_target_pairs={{0,4},{1,5},{2,6},{3,7},{8,12},{9,13},{10,14},{11,15},{16,20},{17,... | collective-permute-start | bytes 1572872 | tf_op jit(solution)/shard_map/ppermute | solution.py:479
  149.2 16.3 %collective-permute-start.23 = (f32[512,128]{1,0:T(8,128)S(1)}, f32[512,128]{1,0:T(8,128)S(1)}, u32[]{:S(2)}, u32[]{:S(2)}) collective-permute-start(f32[512,128]{1,0:T(8,128)S(1)} %get-tuple-element.49), channel_id=1, source_target_pairs={{8,4},{9,5},{10,6},{11,7},{16,12},{17,13},{18,14},{19,15},{24,20},... | collective-permute-start | bytes 786440 | tf_op jit(solution)/shard_map/ppermute | solution.py:479
  150.5 17.8 %collective-permute-start.24 = (f32[512,128]{1,0:T(8,128)S(1)}, f32[512,128]{1,0:T(8,128)S(1)}, u32[]{:S(2)}, u32[]{:S(2)}) collective-permute-start(f32[512,128]{1,0:T(8,128)S(1)} %get-tuple-element.50), channel_id=1, source_target_pairs={{8,4},{9,5},{10,6},{11,7},{16,12},{17,13},{18,14},{19,15},{24,20},... | collective-permute-start | bytes 786440 | tf_op jit(solution)/shard_map/ppermute | solution.py:479

commit v4 on v3

--- a/solution.py
+++ b/solution.py
@@ -56,11 +56,9 @@
     return pl.ds(at, count * n)
 
 
-def pack_kernel(live_ref, parent_ref, mode_ref, damping_ref, weight_ref, corr_ref, blocks_ref, coupling_ref, out_ref, table_ref):
-    slots, n = live_ref.shape[0], blocks_ref.shape[1]
-    size = blocks_ref.shape[0]
-    out_ref[pl.ds(0, size)] = blocks_ref[...]
-    out_ref[pl.ds(size + ROWS, coupling_ref.shape[0])] = coupling_ref[...]
+def pack_kernel(live_ref, parent_ref, mode_ref, damping_ref, weight_ref, corr_ref, coupling_ref, out_ref, table_ref):
+    slots, n = live_ref.shape[0], coupling_ref.shape[1]
+    out_ref[pl.ds(ROWS, coupling_ref.shape[0])] = coupling_ref[...]
     row = lax.broadcasted_iota(jnp.int32, (ROWS, n), 0)
     lane = lax.broadcasted_iota(jnp.int32, (ROWS, n), 1)
     table = jnp.zeros((ROWS, n), f32)
@@ -83,7 +81,7 @@
     live_row = table[LIVE : LIVE + 1]
     table = jnp.where(row == FACTOR, live_row * jnp.exp(table), table)
     table_ref[...] = table
-    out_ref[pl.ds(size, ROWS)] = table
+    out_ref[pl.ds(0, ROWS)] = table
 
 
 def powers_kernel(ham_ref, right_ref, left_ref):
@@ -98,24 +96,40 @@
         left_ref[:, (k - 1) * 3 * n : k * 3 * n] = stack_cols(scaled)
 
 
+def single(group):
+    return [[k] for k in range(group)]
+
+
+def joined(group):
+    return [[0], list(range(2, group)), [1]]
+
+
 class Layout:
-    def __init__(self, refs, slots, group):
-        self.refs, self.slots, self.group = refs, slots, group
+    def __init__(self, refs, slots, split, notes=()):
+        self.refs, self.slots, self.split, self.notes = refs, slots, split, notes
+        self.group = sum(len(held) for held in split)
         self.n = refs[0].shape[1]
-        self.held = group // len(refs)
         self.size = 2 * slots * self.n
         self.stride = self.size + ROWS
 
     def base(self, k):
-        return self.refs[k // self.held], (k % self.held) * self.stride
+        for ref, held in zip(self.refs, self.split):
+            if k in held:
+                return ref, held.index(k) * self.stride
+
+    def table_rows(self, k):
+        if self.notes:
+            return self.notes[k], pl.ds(0, ROWS)
+        ref, base = self.base(k)
+        return ref, pl.ds(base + self.size, ROWS)
 
     def table(self, k):
-        ref, base = self.base(k)
-        return ref.at[pl.ds(base + self.size, ROWS), pl.ds(0, LANES)]
+        ref, where = self.table_rows(k)
+        return ref.at[where, pl.ds(0, LANES)]
 
     def copy_table(self, k, target_ref, at):
-        ref, base = self.base(k)
-        target_ref[at] = ref[pl.ds(base + self.size, ROWS)]
+        ref, where = self.table_rows(k)
+        target_ref[at] = ref[where]
 
     def fetch(self, index, stage_ref, at):
         for k in range(self.group):
@@ -139,7 +153,7 @@
     return ref.at[pl.ds(0, ROWS), pl.ds(0, LANES)]
 
 
-def operators_kernel(slots, group, modes, parity, own_ref, *refs):
+def operators_kernel(group, modes, parity, own_ref, *refs):
     outs = refs[-2 - (parity is None) :]
     sources = refs[: -len(outs)]
     right_ref, left_ref = outs[0], outs[1]
@@ -156,11 +170,9 @@
 
     if parity is None:
         own()
-        groups = Layout(sources, slots, group)
         for k in range(1, group):
-            ref, base = groups.base(k)
             for i in range(modes):
-                value = ref[rows(base + groups.stride + i * n, n)]
+                value = sources[k][rows(ROWS + i * n, n)]
                 put(k * modes + i, value)
                 outs[2][rows(((k - 1) * modes + i) * n, n)] = value
     else:
@@ -206,30 +218,35 @@
     return u_real + done[:, :n], u_imag + done[:, n:]
 
 
-def free_kernel(run_parity, times, slots, first, states_ref, right_ref, left_ref, out_ref):
+def free_kernel(run_parity, times, first, table_row, states_ref, table_ref, right_ref, left_ref, *refs):
+    out_ref = refs[-1]
     n = out_ref.shape[1]
-    count = out_ref.shape[0] // (2 * n)
+    ahead = first if len(refs) > 1 else 0
+    count = out_ref.shape[0] // (2 * n) - ahead
     pair = 2 if count % 2 == 0 else 1
 
     @pl.when(odd_depth() == run_parity)
     def _():
         right, left = right_ref[...], left_ref[...]
-        out_ref[...] = states_ref[pl.ds(2 * first * n, 2 * count * n)]
+        if ahead:
+            out_ref[pl.ds(0, 2 * ahead * n)] = refs[0][...]
+        out_ref[pl.ds(2 * ahead * n, 2 * count * n)] = states_ref[pl.ds(2 * first * n, 2 * count * n)]
 
         @pl.loop(0, count // pair)
         def _(step):
             @pl.loop(0, times * SUBSTEPS)
             def _(turn):
-                at = [(rows(2 * s * n, n), rows((2 * s + 1) * n, n)) for s in [step * pair + u for u in range(pair)]]
+                blocks = [ahead + step * pair + u for u in range(pair)]
+                at = [(rows(2 * s * n, n), rows((2 * s + 1) * n, n)) for s in blocks]
                 done = [taylor(out_ref[r], out_ref[i], right, left) for r, i in at]
                 for (r, i), (real, imag) in zip(at, done):
                     out_ref[r] = real
                     out_ref[i] = imag
 
-        factors = states_ref[pl.ds(2 * slots * n, ROWS)][FACTOR : FACTOR + 1]
+        factors = table_ref[pl.ds(table_row, ROWS)][FACTOR : FACTOR + 1]
         for s in range(count):
             scale = factors[:, first + s : first + s + 1] ** times
-            at = rows(2 * s * n, n, 2)
+            at = rows(2 * (ahead + s) * n, n, 2)
             out_ref[at] = out_ref[at] * scale
 
 
@@ -281,10 +298,10 @@
     return parts[s // size], 2 * (s % size)
 
 
-def pick_kernel(sender, slots, group, parts, near_ref, *refs):
+def pick_kernel(sender, slots, split, parts, near_ref, *refs):
     tab, sem_ref = refs[-2:]
     picks = refs[-2 - parts : -2]
-    groups = Layout(refs[: -2 - parts], slots, group)
+    groups = Layout(refs[: -2 - parts], slots, split)
 
     @pl.when(odd_depth() == sender)
     def _():
@@ -294,12 +311,13 @@
             groups.fetch(parent_of(tab, s, slots), pick, at)
 
 
-def send_kernel(sender, slots, group, modes, parts, right_ref, left_ref, *refs):
+def send_kernel(sender, slots, group, split, modes, parts, noted, right_ref, left_ref, *refs):
     acc_ref, stage_ref, list_ref, tab, sem_ref = refs[-5:]
     tabs_ref = refs[-6]
     n = acc_ref.shape[1]
     sums = refs[-6 - parts : -6]
-    groups = Layout(refs[: -6 - parts], slots, group)
+    held = refs[: -6 - parts]
+    groups = Layout(held[: len(split)], slots, split, held[len(split) :] if noted else ())
 
     @pl.when(odd_depth() == sender)
     def _():
@@ -371,20 +389,19 @@
             out_ref[...] = frees[1][...]
 
 
-def side_kernel(side, receiver, slots, group, modes, span, base_count, group_count, tab_count, right_ref, left_ref, *refs):
+def side_kernel(side, receiver, slots, group, modes, span, split, base_count, group_count, tab_count, right_ref, left_ref, *refs):
     stage_ref, tab, sem_ref = refs[-3:]
-    start, count = span
+    start, step, count = span
     bases = refs[:base_count]
-    groups = Layout(refs[base_count : base_count + group_count], slots, count)
+    groups = Layout(refs[base_count : base_count + group_count], slots, split)
     tab_refs = refs[base_count + group_count : base_count + group_count + tab_count]
     outs = refs[base_count + group_count + tab_count : -3]
     second = len(outs[-1].shape) == 2
     n = stage_ref.shape[1]
     size = 2 * slots * n
-    gathered = Layout(tab_refs, slots, group) if tab_count > 1 else None
+    gathered = Layout(tab_refs, slots, single(group)) if tab_count > 1 else None
     own_tables = [gathered.table(k) if gathered else tab_refs[0].at[k, pl.ds(0, ROWS), pl.ds(0, LANES)] for k in range(group)]
-    held = group // len(outs) if second else group
-    stride = size + ROWS if second else size
+    out = Layout(outs, slots, joined(group)) if second else None
 
     @pl.when(odd_depth() == receiver)
     def _():
@@ -392,7 +409,7 @@
         pull(own_tables + below, tab, sem_ref)
         if second:
             for k in range(group):
-                ref, base = outs[k // held], (k % held) * stride
+                ref, base = out.base(k)
                 ref[pl.ds(base, size)] = bases[0][pl.ds(k * size, size)]
                 ref[pl.ds(base + size, ROWS)] = tab_refs[0][k]
         else:
@@ -410,11 +427,11 @@
             if not second:
                 add_pair(outs[0], 2 * index * n, pair)
                 return
-            for half, ref in enumerate(outs):
-                local = index - half * held * slots
-                at = lax.div(local, slots) * stride + lax.rem(local, slots) * (2 * n)
-
-                @pl.when(jnp.logical_and(local >= 0, local < held * slots))
+            for ref, held in zip(outs, out.split):
+                local = index - held[0] * slots
+                at = lax.div(local, slots) * out.stride + lax.rem(local, slots) * (2 * n)
+
+                @pl.when(jnp.logical_and(local >= 0, local < len(held) * slots))
                 def _():
                     add_pair(ref, at, pair)
 
@@ -431,7 +448,7 @@
                     b = c + group * slots
                     target = parent_of(tab, b, slots)
                     weight = entry(tab, WEIGHT, b, slots) * (entry(tab, LIVE, target, slots) * couple_step)
-                    mode = operator_of(tab, b, slots, modes) + (start - group) * modes
+                    mode = entry(tab, MODE, b, slots).astype(jnp.int32) + (start + k * step) * modes
                     terms.append(child_pair(stage_ref, 2 * s, mode, weight, right_ref, left_ref))
                 else:
                     target = c
@@ -495,6 +512,10 @@
         ]
         return permute(value, pairs)
 
+    def neighbour(value, parity):
+        pairs = [(place(d, m), place(d, m ^ 1)) for d in range(parity, depths, 2) for m in ranks]
+        return permute(value, pairs)
+
     def mats(count, tables=0):
         return jax.ShapeDtypeStruct((count * n + tables * ROWS, n), f32)
 
@@ -510,53 +531,64 @@
     operator_shapes = (sds(group * modes, 3 * n, n, dtype=bf16), sds(group * modes, n, 3 * n, dtype=bf16))
     couplings = coupling.reshape(modes * n, n)
 
+    states = blocks.reshape(plain * n, n)
+    first = gather(states, 1)
     packed, own_table = call(
         pack_kernel,
-        (mats(plain + modes, 1), sds(ROWS, n)),
+        (mats(modes, 1), sds(ROWS, n)),
         PACK_LIMIT,
-        (live_slots, parent_index, bath_mode, damping, link_weight, correlation, blocks.reshape(plain * n, n), couplings),
+        (live_slots, parent_index, bath_mode, damping, link_weight, correlation, couplings),
         smem=6,
     )
-    first = gather(packed, 1)
+    notes = gather(packed, 1)
     near_table = shift(own_table, -1)
     powers = call(
         powers_kernel, (sds(3 * n, ORDER * n, dtype=bf16), sds(n, 3 * ORDER * n, dtype=bf16)), limit, (hamiltonian,)
     )
     *operators_odd, raw = call(
-        functools.partial(operators_kernel, slots, group, modes, None),
+        functools.partial(operators_kernel, group, modes, None),
         (*operator_shapes, mats((group - 1) * modes)),
         limit,
-        (couplings, *first),
+        (couplings, *notes),
     )
 
-    def free(states, parity, times, part=0, parts=1):
+    def free(states, parity, times, part=0, parts=1, prior=None, note=None):
         count = slots // parts
+        table, row = (states, plain * n) if note is None else (note, 0)
         return call(
-            functools.partial(free_kernel, parity, times, slots, part * count),
-            mats(2 * count),
+            functools.partial(free_kernel, parity, times, part * count, row),
+            mats(2 * count * (1 if prior is None else part + 1)),
             limit,
-            (states, *powers),
+            (states, table, *powers) if prior is None else (states, table, *powers, prior),
             us=4.5 * times / parts,
         )
 
-    def free_parts(states, parity, times):
-        return [free(states, parity, times, part, split_hop) for part in range(split_hop)]
+    def free_parts(states, parity, times, note):
+        return [free(states, parity, times, part, split_hop, note=note) for part in range(split_hop)]
+
+    def free_chain(states, parity, times):
+        done = None
+        for part in range(split_hop):
+            done = free(states, parity, times, part, split_hop, done)
+        return done
+
+    splits = {group: single(group), len(joined(group)): joined(group)}
 
     def pick(groups, sender, parts):
         return call(
-            functools.partial(pick_kernel, sender, slots, group, parts),
+            functools.partial(pick_kernel, sender, slots, splits[len(groups)], parts),
             [mats(plain // parts)] * parts,
             limit,
             (near_table, *groups),
             scratch=tables(1),
         )
 
-    def send(groups, sender, parts, operators):
+    def send(groups, sender, parts, operators, notes=()):
         outs = call(
-            functools.partial(send_kernel, sender, slots, group, modes, parts),
+            functools.partial(send_kernel, sender, slots, group, splits[len(groups)], modes, parts, bool(notes)),
             [mats(plain // parts)] * parts + [sds(group, ROWS, n)],
             limit,
-            (*operators, *groups),
+            (*operators, *groups, *notes),
             us=2,
             scratch=[stage, stage, SMEM((total,), jnp.int32), *tables(group)],
         )
@@ -572,39 +604,46 @@
         )
 
     def side(kind, bases, groups, tabs, receiver, operators, second=False, span=None):
-        halves = 2 if group % 2 == 0 else 1
-        span = (0, group) if span is None else span
+        split = splits[len(groups)] if span is None else single(len(groups))
+        span = (0, 1, group) if span is None else span
         return call(
-            functools.partial(side_kernel, kind, receiver, slots, group, modes, span, len(bases), len(groups), len(tabs)),
-            [mats(2 * total // halves, group // halves)] * halves if second else [mats(2 * total), sds(group, ROWS, n)],
+            functools.partial(
+                side_kernel, kind, receiver, slots, group, modes, span, split, len(bases), len(groups), len(tabs)
+            ),
+            [mats(plain * len(held), len(held)) for held in joined(group)]
+            if second
+            else [mats(2 * total), sds(group, ROWS, n)],
             limit,
             (*operators, *bases, *groups, *tabs),
             us=3,
-            scratch=[stage, *tables(group + (span[1] if kind == "children" else 0))],
+            scratch=[stage, *tables(group + (span[2] if kind == "children" else 0))],
         )
 
-    free_even = free(packed, 0, 1)
-    free_odd = [part for k in ranks for part in free_parts(first[k], 1, 2)]
+    free_even = free(states, 0, 1, note=packed)
+    free_odd = [part for k in ranks for part in free_parts(first[k], 1, 2, notes[k])]
     picks = [shift(value, 1, 1) for value in pick(first, 1, split_hop)]
-    sums, tabs_odd = send(first, 1, 1, operators_odd)
+    sums, tabs_odd = send(first, 1, 1, operators_odd, notes)
     sums = [shift(value, -1, 1) for value in sums]
-    own_state = join([free_even], sums, picks, 0, operators_odd)
-
-    gathered = gather(own_state, 0)
-    from_below = [shift(value, -1, 0) for value in gathered]
-    from_above = [shift(value, 1, 0) for value in gathered]
-    free_even = [part for k in ranks for part in free_parts(gathered[k], 0, 2)]
-    ready = group - 1
-    states, _ = side("children", free_odd, from_below[:ready], [tabs_odd], 1, operators_odd, span=(0, ready))
-    states, _ = side("parents", [states], from_above, [tabs_odd], 1, operators_odd)
-    states = side("children", [states], from_below[ready:], [tabs_odd], 1, operators_odd, second=True, span=(ready, 1))
-
-    from_above = [shift(value, 1, 1) for value in states]
-    from_below = [shift(value, -1, 1) for value in states]
     passed = shift(raw, -1, 1)
     operators_even = call(
-        functools.partial(operators_kernel, slots, group, modes, 0), operator_shapes, limit, (couplings, passed)
+        functools.partial(operators_kernel, group, modes, 0), operator_shapes, limit, (couplings, passed)
     )
+    own_state = join([free_even], sums, picks, 0, operators_odd)
+
+    gathered = gather(own_state, 0)
+    from_below = [shift(value, -1, 0) for value in gathered[:-1]]
+    from_below.append(neighbour(from_below[group - 2], 1))
+    from_above = [shift(value, 1, 0) for value in gathered]
+    free_own = free_chain(gathered[0], 0, 2)
+    free_even = [free_own, neighbour(free_own, 0)] + [free(gathered[k], 0, 2) for k in range(2, group)]
+    evens, odds = (0, 2, group // 2), (1, 2, group // 2)
+    states, _ = side("children", free_odd, from_below[::2], [tabs_odd], 1, operators_odd, span=evens)
+    states, _ = side("parents", [states], from_above, [tabs_odd], 1, operators_odd)
+    states = side("children", [states], from_below[1::2], [tabs_odd], 1, operators_odd, second=True, span=odds)
+
+    from_above = [shift(value, 1, 1) for value in states[:2]]
+    from_above.append(neighbour(from_above[0], 0))
+    from_below = [shift(value, -1, 1) for value in states]
     last_odd = free(states[0], 1, 2)
     states, tabs_even = side("children", free_even, from_below, gathered, 0, operators_even)
     states = side("parents", [states], from_above, [tabs_even], 0, operators_even, second=True)

time: 171 us -> 162 us (0.947)
  the two profiles are of different devices: /device:TPU:3 before, /device:TPU:19 now
where the time goes in v4:
time: 162 us
  Pallas kernels  60 us (37%)
  starting transfers between devices  55.3 us (34%)
  waiting for transfers between devices  45.3 us (28%)
    pallas_call x30, Pallas kernels, call(): pl.pallas_call(kernel, out_shape=out_shapes, in_specs=specs, out_specs=ja...  60 us
    ppermute x32, starting transfers between devices, permute(): return lax.ppermute(value, AXES, pairs)  55.3 us
    ppermute x32, waiting for transfers between devices, permute(): return lax.ppermute(value, AXES, pairs)  45.3 us
  transfers between devices with their start and end apart: 32, of which 8 were waited for; matrix products, arithmetic and copies ran while one was open for 0% of the time, Pallas kernels for 35%

profile of v4, /device:TPU:19, one launch (start us, length us, event | category | flops | bytes accessed | tf_op | source)
XLA Modules:
  0.0 161.7 jit_solution(15405065203425630845)
XLA Ops:
  0.0 1.7 %shard_map.91 = (f32[264,128]{1,0:T(8,128)}, f32[8,128]{1,0:T(8,128)}) custom-call(s32[4]{0:T(128)} %live_ref.1, s32[4]{0:T(128)} %parent_ref.1, s32[4]{0:T(128)} %mode_ref.1, f32[4]{0:T(128)} %damping_ref.1, f32[4]{0:T(128)} %weight_ref.1, f32[2,2]{1,0:T(2,128)} %corr_ref.1, f32[256,128]{1,0:T(8,128)} %bitcast.10), custom_call_target="tpu_custom_call" | custom-call | flops 1100000000 | bytes 524288 | tf_op jit(solution)/shard_map/pallas_call | solution.py:467
  1.7 2.0 %collective-permute-start.1 = (f32[264,128]{1,0:T(8,128)}, f32[264,128]{1,0:T(8,128)S(1)}, u32[]{:S(2)}, u32[]{:S(2)}) collective-permute-start(f32[264,128]{1,0:T(8,128)} %get-tuple-element.31.refs_0_.table_ref.refs_4_), channel_id=1, source_target_pairs={{4,6},{5,7},{6,4},{7,5},{12,14},{13,15},{14,12},{15,13},{20,22},{2... | collective-permute-start | bytes 405512 | tf_op jit(solution)/shard_map/ppermute | solution.py:496
  3.6 3.2 %collective-permute-start = (f32[264,128]{1,0:T(8,128)}, f32[264,128]{1,0:T(8,128)S(1)}, u32[]{:S(2)}, u32[]{:S(2)}) collective-permute-start(f32[264,128]{1,0:T(8,128)} %get-tuple-element.31.refs_0_.table_ref.refs_4_), channel_id=1, source_target_pairs={{4,5},{5,4},{6,7},{7,6},{12,13},{13,12},{14,15},{15,14},{20,21},{2... | collective-permute-start | bytes 405512 | tf_op jit(solution)/shard_map/ppermute | solution.py:496
  6.9 4.2 %collective-permute-start.4 = (f32[1024,128]{1,0:T(8,128)S(1)}, f32[1024,128]{1,0:T(8,128)S(1)}, u32[]{:S(2)}, u32[]{:S(2)}) collective-permute-start(f32[1024,128]{1,0:T(8,128)S(1)} %bitcast.3), channel_id=1, source_target_pairs={{4,6},{5,7},{6,4},{7,5},{12,14},{13,15},{14,12},{15,13},{20,22},{2... | collective-permute-start | bytes 1572872 | tf_op jit(solution)/shard_map/ppermute | solution.py:496
  11.1 2.1 %collective-permute-start.3 = (f32[1024,128]{1,0:T(8,128)S(1)}, f32[1024,128]{1,0:T(8,128)S(1)}, u32[]{:S(2)}, u32[]{:S(2)}) collective-permute-start(f32[1024,128]{1,0:T(8,128)S(1)} %bitcast.4), channel_id=1, source_target_pairs={{4,5},{5,4},{6,7},{7,6},{12,13},{13,12},{14,15},{15,14},{20,21},{2... | collective-permute-start | bytes 1572872 | tf_op jit(solution)/shard_map/ppermute | solution.py:496
  13.2 0.0 copy-start.2
  13.2 2.1 %collective-permute-start.7 = (f32[8,128]{1,0:T(8,128)}, f32[8,128]{1,0:T(8,128)S(1)}, u32[]{:S(2)}, u32[]{:S(2)}) collective-permute-start(f32[8,128]{1,0:T(8,128)} %get-tuple-element.30.own_ref), channel_id=1, source_target_pairs={{4,0},{5,1},{6,2},{7,3},{8,4},{9,5},{10,6},{11,7},{12,8},{13,9},{1... | collective-permute-start | bytes 12296 | tf_op jit(solution)/shard_map/ppermute | solution.py:496
  15.3 0.7 shard_map.93
  16.0 4.2 %shard_map.94.refs_0_ = f32[512,128]{1,0:T(8,128)S(1)} custom-call(f32[1024,128]{1,0:T(8,128)S(1)} %bitcast.6, f32[264,128]{1,0:T(8,128)S(1)} %copy-done.2, bf16[384,512]{1,0:T(8,128)(2,1)S(1)} %get-tuple-element.34.right_ref, bf16[128,1536]{1,0:T(8,128)(2,1)S(1)} %get-tuple-element.35.left_ref), custom_call_target="tpu_custom_call" | custom-call | flops 4950000128 | bytes 524288 | tf_op jit(solution)/shard_map/pallas_call | solution.py:467
  20.2 0.0 copy-start.3
  20.3 3.3 %collective-permute-start.2 = (f32[264,128]{1,0:T(8,128)S(1)}, f32[264,128]{1,0:T(8,128)S(1)}, u32[]{:S(2)}, u32[]{:S(2)}) collective-permute-start(f32[264,128]{1,0:T(8,128)S(1)} %collective-permute-done.1.refs_2_.table_ref.refs_6_), channel_id=1, source_target_pairs={{4,5},{5,4},{6,7},{7,6},{12,13},{13,12},{14,15},{15,14},{20,21},{2... | collective-permute-start | bytes 405512 | tf_op jit(solution)/shard_map/ppermute | solution.py:496
  23.6 4.2 %shard_map.95.refs_1_ = f32[512,128]{1,0:T(8,128)S(1)} custom-call(f32[1024,128]{1,0:T(8,128)S(1)} %bitcast.7, f32[264,128]{1,0:T(8,128)S(1)} %copy-done.2, bf16[384,512]{1,0:T(8,128)(2,1)S(1)} %get-tuple-element.34.right_ref, bf16[128,1536]{1,0:T(8,128)(2,1)S(1)} %get-tuple-element.35.left_ref), custom_call_target="tpu_custom_call" | custom-call | flops 4950000128 | bytes 524288 | tf_op jit(solution)/shard_map/pallas_call | solution.py:467
  27.8 0.0 collective-permute-done.refs_1_.table_ref.refs_5_
  27.9 0.2 shard_map.92
  28.1 1.3 collective-permute-start.21
  29.4 2.1 %collective-permute-start.5 = (f32[1024,128]{1,0:T(8,128)S(1)}, f32[1024,128]{1,0:T(8,128)S(1)}, u32[]{:S(2)}, u32[]{:S(2)}) collective-permute-start(f32[1024,128]{1,0:T(8,128)S(1)} %collective-permute-done.4.states_ref.refs_2_), channel_id=1, source_target_pairs={{4,5},{5,4},{6,7},{7,6},{12,13},{13,12},{14,15},{15,14},{20,21},{2... | collective-permute-start | bytes 1572872 | tf_op jit(solution)/shard_map/ppermute | solution.py:496
  31.5 4.2 %shard_map.98.refs_4_ = f32[512,128]{1,0:T(8,128)S(1)} custom-call(f32[1024,128]{1,0:T(8,128)S(1)} %collective-permute-done.4.states_ref.refs_2_, f32[264,128]{1,0:T(8,128)S(1)} %collective-permute-done.1.refs_2_.table_ref.refs_6_, bf16[384,512]{1,0:T(8,128)(2,1)S(1)} %get-tuple-element.34.right_ref, bf16[128,1536]{1,0:T(8,128)(2,1)S(1)} %get-tuple-element.35.left_ref), custom_call_target="tpu_custom_call" | custom-call | flops 4950000128 | bytes 524288 | tf_op jit(solution)/shard_map/pallas_call | solution.py:467
  35.7 4.2 %shard_map.99.refs_5_ = f32[512,128]{1,0:T(8,128)S(1)} custom-call(f32[1024,128]{1,0:T(8,128)S(1)} %collective-permute-done.4.states_ref.refs_2_, f32[264,128]{1,0:T(8,128)S(1)} %collective-permute-done.1.refs_2_.table_ref.refs_6_, bf16[384,512]{1,0:T(8,128)(2,1)S(1)} %get-tuple-element.34.right_ref, bf16[128,1536]{1,0:T(8,128)(2,1)S(1)} %get-tuple-element.35.left_ref), custom_call_target="tpu_custom_call" | custom-call | flops 4950000128 | bytes 524288 | tf_op jit(solution)/shard_map/pallas_call | solution.py:467
  39.9 4.2 %shard_map.96.refs_2_ = f32[512,128]{1,0:T(8,128)S(1)} custom-call(f32[1024,128]{1,0:T(8,128)S(1)} %collective-permute-done.3.states_ref.refs_1_, f32[264,128]{1,0:T(8,128)S(1)} %collective-permute-done.refs_1_.table_ref.refs_5_, bf16[384,512]{1,0:T(8,128)(2,1)S(1)} %get-tuple-element.34.right_ref, bf16[128,1536]{1,0:T(8,128)(2,1)S(1)} %get-tuple-element.35.left_ref), custom_call_target="tpu_custom_call" | custom-call | flops 4950000128 | bytes 524288 | tf_op jit(solution)/shard_map/pallas_call | solution.py:467
  44.1 1.9 %shard_map.103 = (f32[1024,128]{1,0:T(8,128)S(1)}, f32[4,8,128]{2,1,0:T(8,128)S(1)}) custom-call(bf16[8,384,128]{2,1,0:T(8,128)(2,1)S(1)} %get-tuple-element.32.right_ref, bf16[8,128,384]{2,1,0:T(8,128)(2,1)S(1)} %get-tuple-element.33.left_ref, f32[1024,128]{1,0:T(8,128)S(1)} %bitcast.8, f32[1024,128]{1,0:T(8,128)S(1)} %collective-permute-done.3.states_ref.refs_1_, ...), custom_call_target="tpu_custom_call" | custom-call | flops 2200000000 | bytes 524288 | tf_op jit(solution)/shard_map/pallas_call | solution.py:467
  46.1 1.3 collective-permute-start.6
  47.4 0.8 shard_map.104
  48.2 1.3 collective-permute-start.8
  49.5 1.3 collective-permute-start.9
  50.9 4.2 %shard_map.97.refs_3_ = f32[512,128]{1,0:T(8,128)S(1)} custom-call(f32[1024,128]{1,0:T(8,128)S(1)} %collective-permute-done.3.states_ref.refs_1_, f32[264,128]{1,0:T(8,128)S(1)} %collective-permute-done.refs_1_.table_ref.refs_5_, bf16[384,512]{1,0:T(8,128)(2,1)S(1)} %get-tuple-element.34.right_ref, bf16[128,1536]{1,0:T(8,128)(2,1)S(1)} %get-tuple-element.35.left_ref), custom_call_target="tpu_custom_call" | custom-call | flops 4950000128 | bytes 524288 | tf_op jit(solution)/shard_map/pallas_call | solution.py:467
  55.1 0.5 collective-permute-done.9.refs_3_
  55.6 0.1 copy-done
  55.8 0.7 collective-permute-start.11
  56.5 4.2 %shard_map.100.refs_6_ = f32[512,128]{1,0:T(8,128)S(1)} custom-call(f32[1024,128]{1,0:T(8,128)S(1)} %collective-permute-done.5.states_ref.refs_3_, f32[264,128]{1,0:T(8,128)S(1)} %collective-permute-done.2.refs_3_.table_ref.refs_7_, bf16[384,512]{1,0:T(8,128)(2,1)S(1)} %get-tuple-element.34.right_ref, bf16[128,1536]{1,0:T(8,128)(2,1)S(1)} %get-tuple-element.35.left_ref), custom_call_target="tpu_custom_call" | custom-call | flops 4950000128 | bytes 524288 | tf_op jit(solution)/shard_map/pallas_call | solution.py:467
  60.7 4.2 %shard_map.101.refs_7_ = f32[512,128]{1,0:T(8,128)S(1)} custom-call(f32[1024,128]{1,0:T(8,128)S(1)} %collective-permute-done.5.states_ref.refs_3_, f32[264,128]{1,0:T(8,128)S(1)} %collective-permute-done.2.refs_3_.table_ref.refs_7_, bf16[384,512]{1,0:T(8,128)(2,1)S(1)} %get-tuple-element.34.right_ref, bf16[128,1536]{1,0:T(8,128)(2,1)S(1)} %get-tuple-element.35.left_ref), custom_call_target="tpu_custom_call" | custom-call | flops 4950000128 | bytes 524288 | tf_op jit(solution)/shard_map/pallas_call | solution.py:467
  64.9 1.3 collective-permute-start.10
  66.2 0.7 collective-permute-start.14
  66.9 0.9 collective-permute-start.17
  67.8 1.3 collective-permute-start.13
  69.1 1.3 collective-permute-start.12
  70.4 5.9 %collective-permute-done.10.refs_8_ = f32[1032,128]{1,0:T(8,128)S(1)} collective-permute-done((f32[1032,128]{1,0:T(8,128)S(1)}, f32[1032,128]{1,0:T(8,128)S(1)}, u32[]{:S(2)}, u32[]{:S(2)}) %collective-permute-start.10) | collective-permute-done | bytes 528416 | tf_op jit(solution)/shard_map/ppermute | solution.py:496
  76.3 1.3 collective-permute-start.16
  77.6 1.3 collective-permute-start.15
  79.0 1.3 collective-permute-start.18
  80.3 6.1 %collective-permute-done.13.refs_1_ = f32[1032,128]{1,0:T(8,128)S(1)} collective-permute-done((f32[1032,128]{1,0:T(8,128)S(1)}, f32[1032,128]{1,0:T(8,128)S(1)}, u32[]{:S(2)}, u32[]{:S(2)}) %collective-permute-start.13) | collective-permute-done | bytes 528416 | tf_op jit(solution)/shard_map/ppermute | solution.py:496
  86.4 1.3 collective-permute-start.19
  87.7 11.8 %collective-permute-done.12.refs_9_ = f32[1032,128]{1,0:T(8,128)S(1)} collective-permute-done((f32[1032,128]{1,0:T(8,128)S(1)}, f32[1032,128]{1,0:T(8,128)S(1)}, u32[]{:S(2)}, u32[]{:S(2)}) %collective-permute-start.12) | collective-permute-done | bytes 528416 | tf_op jit(solution)/shard_map/ppermute | solution.py:496
  99.4 1.9 %collective-permute-start.20 = (f32[1032,128]{1,0:T(8,128)S(1)}, f32[1032,128]{1,0:T(8,128)S(1)}, u32[]{:S(2)}, u32[]{:S(2)}) collective-permute-start(f32[1032,128]{1,0:T(8,128)S(1)} %collective-permute-done.12.refs_9_), channel_id=1, source_target_pairs={{4,5},{5,4},{6,7},{7,6},{12,13},{13,12},{14,15},{15,14},{20,21},{2... | collective-permute-start | bytes 1585160 | tf_op jit(solution)/shard_map/ppermute | solution.py:496
  101.4 3.0 %shard_map.106 = (f32[4096,128]{1,0:T(8,128)S(1)}, f32[4,8,128]{2,1,0:T(8,128)}) custom-call(bf16[8,384,128]{2,1,0:T(8,128)(2,1)S(1)} %get-tuple-element.32.right_ref, bf16[8,128,384]{2,1,0:T(8,128)(2,1)S(1)} %get-tuple-element.33.left_ref, f32[512,128]{1,0:T(8,128)S(1)} %shard_map.94.refs_0_, f32[512,128]{1,0:T(8,128)S(1)} %shard_map.95.refs_1_, ...), custom_call_target="tpu_custom_call" | custom-call | flops 3300000000 | bytes 524288 | tf_op jit(solution)/shard_map/pallas_call | solution.py:467
  104.3 0.7 collective-permute-start.22
  105.1 4.4 %shard_map.107 = (f32[4096,128]{1,0:T(8,128)S(1)}, f32[4,8,128]{2,1,0:T(8,128)}) custom-call(bf16[8,384,128]{2,1,0:T(8,128)(2,1)S(1)} %get-tuple-element.32.right_ref, bf16[8,128,384]{2,1,0:T(8,128)(2,1)S(1)} %get-tuple-element.33.left_ref, f32[4096,128]{1,0:T(8,128)S(1)} %get-tuple-element.40.refs_0_, f32[1032,128]{1,0:T(8,128)S(1)} %collective-permute-done.13.refs_1_, ...), custom_call_target="tpu_custom_call" | custom-call | flops 3300000000 | bytes 524288 | tf_op jit(solution)/shard_map/pallas_call | solution.py:467
  109.5 3.6 %collective-permute-done.19.refs_1_ = f32[1032,128]{1,0:T(8,128)S(1)} collective-permute-done((f32[1032,128]{1,0:T(8,128)S(1)}, f32[1032,128]{1,0:T(8,128)S(1)}, u32[]{:S(2)}, u32[]{:S(2)}) %collective-permute-start.19) | collective-permute-done | bytes 528416 | tf_op jit(solution)/shard_map/ppermute | solution.py:496
  113.1 2.6 %shard_map.108 = (f32[1032,128]{1,0:T(8,128)S(1)}, f32[2064,128]{1,0:T(8,128)S(1)}, f32[1032,128]{1,0:T(8,128)S(1)}) custom-call(bf16[8,384,128]{2,1,0:T(8,128)(2,1)S(1)} %get-tuple-element.32.right_ref, bf16[8,128,384]{2,1,0:T(8,128)(2,1)S(1)} %get-tuple-element.33.left_ref, f32[4096,128]{1,0:T(8,128)S(1)} %get-tuple-element.41.refs_0_, ...), custom_call_target="tpu_custom_call" | custom-call | flops 3300000000 | bytes 524288 | tf_op jit(solution)/shard_map/pallas_call | solution.py:467
  115.7 1.4 collective-permute-start.24
  117.0 1.3 collective-permute-start.26
  118.4 5.4 %collective-permute-start.23 = (f32[1032,128]{1,0:T(8,128)S(1)}, f32[1032,128]{1,0:T(8,128)S(1)}, u32[]{:S(2)}, u32[]{:S(2)}) collective-permute-start(f32[1032,128]{1,0:T(8,128)S(1)} %get-tuple-element.42.states_ref.table_ref), channel_id=1, source_target_pairs={{4,0},{5,1},{6,2},{7,3},{12,8},{13,9},{14,10},{15,11},{20,16},{21,... | collective-permute-start | bytes 1585160 | tf_op jit(solution)/shard_map/ppermute | solution.py:496
  123.8 3.3 %collective-permute-start.27 = (f32[2064,128]{1,0:T(8,128)S(1)}, f32[2064,128]{1,0:T(8,128)S(1)}, u32[]{:S(2)}, u32[]{:S(2)}) collective-permute-start(f32[2064,128]{1,0:T(8,128)S(1)} %get-tuple-element.46), channel_id=1, source_target_pairs={{4,8},{5,9},{6,10},{7,11},{12,16},{13,17},{14,18},{15,19},{20,24},... | collective-permute-start | bytes 3170312 | tf_op jit(solution)/shard_map/ppermute | solution.py:496
  127.1 1.3 collective-permute-start.25
  128.5 0.7 collective-permute-start.28
  129.2 8.2 %shard_map.109.refs_0_ = f32[1024,128]{1,0:T(8,128)S(1)} custom-call(f32[1032,128]{1,0:T(8,128)S(1)} %get-tuple-element.42.states_ref.table_ref, f32[1032,128]{1,0:T(8,128)S(1)} %get-tuple-element.42.states_ref.table_ref, bf16[384,512]{1,0:T(8,128)(2,1)S(1)} %get-tuple-element.34.right_ref, bf16[128,1536]{1,0:T(8,128)(2,1)S(1)} %get-tuple-element.35.left_ref), custom_call_target="tpu_custom_call" | custom-call | flops 9900000256 | bytes 524288 | tf_op jit(solution)/shard_map/pallas_call | solution.py:467
  137.4 0.1 shard_map.115
  137.5 1.3 collective-permute-done.27.refs_2_
  138.9 1.3 collective-permute-start.31
  140.2 0.7 shard_map.118
  140.9 1.3 collective-permute-start.29
  142.2 1.3 collective-permute-start.30
  143.5 13.2 %collective-permute-done.29.refs_2_ = f32[512,128]{1,0:T(8,128)S(1)} collective-permute-done((f32[512,128]{1,0:T(8,128)S(1)}, f32[512,128]{1,0:T(8,128)S(1)}, u32[]{:S(2)}, u32[]{:S(2)}) %collective-permute-start.29) | collective-permute-done | bytes 262176 | tf_op jit(solution)/shard_map/ppermute | solution.py:496
  156.8 2.8 %collective-permute-done.30.refs_3_ = f32[512,128]{1,0:T(8,128)S(1)} collective-permute-done((f32[512,128]{1,0:T(8,128)S(1)}, f32[512,128]{1,0:T(8,128)S(1)}, u32[]{:S(2)}, u32[]{:S(2)}) %collective-permute-start.30) | collective-permute-done | bytes 262176 | tf_op jit(solution)/shard_map/ppermute | solution.py:496
  159.6 1.9 %shard_map.120 = f32[1024,128]{1,0:T(8,128)} custom-call(f32[8,128]{1,0:T(8,128)S(1)} %copy-done, bf16[8,384,128]{2,1,0:T(8,128)(2,1)S(1)} %get-tuple-element.32.right_ref, bf16[8,128,384]{2,1,0:T(8,128)(2,1)S(1)} %get-tuple-element.33.left_ref, f32[1024,128]{1,0:T(8,128)S(1)} %shard_map.109.refs_0_, f32[1024,128]{1,0:T(8,128)S(1)} %shard_map.117.refs_1_, ...), custom_call_target="tpu_custom_call" | custom-call | flops 1100000000 | bytes 524288 | tf_op jit(solution)/shard_map/pallas_call | solution.py:467
  (40 shorter events, 0.3 us)
Async XLA Ops:
  0.0 6.9 %copy-start.1 = (f32[4,2,128,128]{3,2,1,0:T(8,128)S(1)}, f32[4,2,128,128]{3,2,1,0:T(8,128)}, u32[]{:S(2)}) copy-start(f32[4,2,128,128]{3,2,1,0:T(8,128)} %param.9) | copy-start | bytes 1572868
  0.0 15.3 %copy-start.4 = (f32[128,128]{1,0:T(8,128)S(1)}, f32[128,128]{1,0:T(8,128)}, u32[]{:S(2)}) copy-start(f32[128,128]{1,0:T(8,128)} %ham_ref.1) | copy-start | bytes 196612
  1.7 18.6 %collective-permute-start.1 = (f32[264,128]{1,0:T(8,128)}, f32[264,128]{1,0:T(8,128)S(1)}, u32[]{:S(2)}, u32[]{:S(2)}) collective-permute-start(f32[264,128]{1,0:T(8,128)} %get-tuple-element.31.refs_0_.table_ref.refs_4_), channel_id=1, source_target_pairs={{4,6},{5,7},{6,4},{7,5},{12,14},{13,15},{14,12},{15,13},{20,22},{2... | collective-permute-start | bytes 405512 | tf_op jit(solution)/shard_map/ppermute | solution.py:496
  3.6 24.2 %collective-permute-start = (f32[264,128]{1,0:T(8,128)}, f32[264,128]{1,0:T(8,128)S(1)}, u32[]{:S(2)}, u32[]{:S(2)}) collective-permute-start(f32[264,128]{1,0:T(8,128)} %get-tuple-element.31.refs_0_.table_ref.refs_4_), channel_id=1, source_target_pairs={{4,5},{5,4},{6,7},{7,6},{12,13},{13,12},{14,15},{15,14},{20,21},{2... | collective-permute-start | bytes 405512 | tf_op jit(solution)/shard_map/ppermute | solution.py:496
  6.9 22.5 %collective-permute-start.4 = (f32[1024,128]{1,0:T(8,128)S(1)}, f32[1024,128]{1,0:T(8,128)S(1)}, u32[]{:S(2)}, u32[]{:S(2)}) collective-permute-start(f32[1024,128]{1,0:T(8,128)S(1)} %bitcast.3), channel_id=1, source_target_pairs={{4,6},{5,7},{6,4},{7,5},{12,14},{13,15},{14,12},{15,13},{20,22},{2... | collective-permute-start | bytes 1572872 | tf_op jit(solution)/shard_map/ppermute | solution.py:496
  11.1 28.8 %collective-permute-start.3 = (f32[1024,128]{1,0:T(8,128)S(1)}, f32[1024,128]{1,0:T(8,128)S(1)}, u32[]{:S(2)}, u32[]{:S(2)}) collective-permute-start(f32[1024,128]{1,0:T(8,128)S(1)} %bitcast.4), channel_id=1, source_target_pairs={{4,5},{5,4},{6,7},{7,6},{12,13},{13,12},{14,15},{15,14},{20,21},{2... | collective-permute-start | bytes 1572872 | tf_op jit(solution)/shard_map/ppermute | solution.py:496
  13.2 2.8 %copy-start.2 = (f32[264,128]{1,0:T(8,128)S(1)}, f32[264,128]{1,0:T(8,128)}, u32[]{:S(2)}) copy-start(f32[264,128]{1,0:T(8,128)} %get-tuple-element.31.refs_0_.table_ref.refs_4_) | copy-start | bytes 405508
  13.2 34.2 %collective-permute-start.7 = (f32[8,128]{1,0:T(8,128)}, f32[8,128]{1,0:T(8,128)S(1)}, u32[]{:S(2)}, u32[]{:S(2)}) collective-permute-start(f32[8,128]{1,0:T(8,128)} %get-tuple-element.30.own_ref), channel_id=1, source_target_pairs={{4,0},{5,1},{6,2},{7,3},{8,4},{9,5},{10,6},{11,7},{12,8},{13,9},{1... | collective-permute-start | bytes 12296 | tf_op jit(solution)/shard_map/ppermute | solution.py:496
  20.2 7.6 %copy-start.3 = (f32[2,128,128]{2,1,0:T(8,128)S(1)}, f32[2,128,128]{2,1,0:T(8,128)}, u32[]{:S(2)}) copy-start(f32[2,128,128]{2,1,0:T(8,128)} %param.14) | copy-start | bytes 393220
  20.3 7.6 %collective-permute-start.2 = (f32[264,128]{1,0:T(8,128)S(1)}, f32[264,128]{1,0:T(8,128)S(1)}, u32[]{:S(2)}, u32[]{:S(2)}) collective-permute-start(f32[264,128]{1,0:T(8,128)S(1)} %collective-permute-done.1.refs_2_.table_ref.refs_6_), channel_id=1, source_target_pairs={{4,5},{5,4},{6,7},{7,6},{12,13},{13,12},{14,15},{15,14},{20,21},{2... | collective-permute-start | bytes 405512 | tf_op jit(solution)/shard_map/ppermute | solution.py:496
  28.1 27.0 %collective-permute-start.21 = (f32[768,128]{1,0:T(8,128)S(1)}, f32[768,128]{1,0:T(8,128)S(1)}, u32[]{:S(2)}, u32[]{:S(2)}) collective-permute-start(f32[768,128]{1,0:T(8,128)S(1)} %get-tuple-element.43), channel_id=1, source_target_pairs={{4,0},{5,1},{6,2},{7,3},{12,8},{13,9},{14,10},{15,11},{20,16},{21,... | collective-permute-start | bytes 1179656 | tf_op jit(solution)/shard_map/ppermute | solution.py:496
  29.4 14.7 %collective-permute-start.5 = (f32[1024,128]{1,0:T(8,128)S(1)}, f32[1024,128]{1,0:T(8,128)S(1)}, u32[]{:S(2)}, u32[]{:S(2)}) collective-permute-start(f32[1024,128]{1,0:T(8,128)S(1)} %collective-permute-done.4.states_ref.refs_2_), channel_id=1, source_target_pairs={{4,5},{5,4},{6,7},{7,6},{12,13},{13,12},{14,15},{15,14},{20,21},{2... | collective-permute-start | bytes 1572872 | tf_op jit(solution)/shard_map/ppermute | solution.py:496
  46.1 9.5 %collective-permute-start.6 = (f32[1024,128]{1,0:T(8,128)S(1)}, f32[1024,128]{1,0:T(8,128)S(1)}, u32[]{:S(2)}, u32[]{:S(2)}) collective-permute-start(f32[1024,128]{1,0:T(8,128)S(1)} %get-tuple-element.36), channel_id=1, source_target_pairs={{4,0},{5,1},{6,2},{7,3},{12,8},{13,9},{14,10},{15,11},{20,16},{21,... | collective-permute-start | bytes 1572872 | tf_op jit(solution)/shard_map/ppermute | solution.py:496
  48.2 6.9 %collective-permute-start.8 = (f32[512,128]{1,0:T(8,128)S(1)}, f32[512,128]{1,0:T(8,128)S(1)}, u32[]{:S(2)}, u32[]{:S(2)}) collective-permute-start(f32[512,128]{1,0:T(8,128)S(1)} %get-tuple-element.37), channel_id=1, source_target_pairs={{4,8},{5,9},{6,10},{7,11},{12,16},{13,17},{14,18},{15,19},{20,24},... | collective-permute-start | bytes 786440 | tf_op jit(solution)/shard_map/ppermute | solution.py:496
  49.5 6.1 %collective-permute-start.9 = (f32[512,128]{1,0:T(8,128)S(1)}, f32[512,128]{1,0:T(8,128)S(1)}, u32[]{:S(2)}, u32[]{:S(2)}) collective-permute-start(f32[512,128]{1,0:T(8,128)S(1)} %get-tuple-element.38), channel_id=1, source_target_pairs={{4,8},{5,9},{6,10},{7,11},{12,16},{13,17},{14,18},{15,19},{20,24},... | collective-permute-start | bytes 786440 | tf_op jit(solution)/shard_map/ppermute | solution.py:496
  55.1 0.7 copy-start
  55.8 11.1 %collective-permute-start.11 = (f32[1032,128]{1,0:T(8,128)S(1)}, f32[1032,128]{1,0:T(8,128)S(1)}, u32[]{:S(2)}, u32[]{:S(2)}) collective-permute-start(f32[1032,128]{1,0:T(8,128)S(1)} %shard_map.105.states_ref.table_ref.refs_7_), channel_id=1, source_target_pairs={{0,2},{1,3},{2,0},{3,1},{8,10},{9,11},{10,8},{11,9},{16,18},{17,19... | collective-permute-start | bytes 1585160 | tf_op jit(solution)/shard_map/ppermute | solution.py:496
  64.9 11.4 %collective-permute-start.10 = (f32[1032,128]{1,0:T(8,128)S(1)}, f32[1032,128]{1,0:T(8,128)S(1)}, u32[]{:S(2)}, u32[]{:S(2)}) collective-permute-start(f32[1032,128]{1,0:T(8,128)S(1)} %shard_map.105.states_ref.table_ref.refs_7_), channel_id=1, source_target_pairs={{8,4},{9,5},{10,6},{11,7},{16,12},{17,13},{18,14},{19,15},{24,20},... | collective-permute-start | bytes 1585160 | tf_op jit(solution)/shard_map/ppermute | solution.py:496
  66.2 11.4 %collective-permute-start.14 = (f32[1032,128]{1,0:T(8,128)S(1)}, f32[1032,128]{1,0:T(8,128)S(1)}, u32[]{:S(2)}, u32[]{:S(2)}) collective-permute-start(f32[1032,128]{1,0:T(8,128)S(1)} %shard_map.105.states_ref.table_ref.refs_7_), channel_id=1, source_target_pairs={{0,1},{1,0},{2,3},{3,2},{8,9},{9,8},{10,11},{11,10},{16,17},{17,16... | collective-permute-start | bytes 1585160 | tf_op jit(solution)/shard_map/ppermute | solution.py:496
  66.9 12.0 %collective-permute-start.17 = (f32[1032,128]{1,0:T(8,128)S(1)}, f32[1032,128]{1,0:T(8,128)S(1)}, u32[]{:S(2)}, u32[]{:S(2)}) collective-permute-start(f32[1032,128]{1,0:T(8,128)S(1)} %collective-permute-done.11.states_ref.table_ref.refs_9_), channel_id=1, source_target_pairs={{0,1},{1,0},{2,3},{3,2},{8,9},{9,8},{10,11},{11,10},{16,17},{17,16... | collective-permute-start | bytes 1585160 | tf_op jit(solution)/shard_map/ppermute | solution.py:496
  67.8 18.6 %collective-permute-start.13 = (f32[1032,128]{1,0:T(8,128)S(1)}, f32[1032,128]{1,0:T(8,128)S(1)}, u32[]{:S(2)}, u32[]{:S(2)}) collective-permute-start(f32[1032,128]{1,0:T(8,128)S(1)} %shard_map.105.states_ref.table_ref.refs_7_), channel_id=1, source_target_pairs={{0,4},{1,5},{2,6},{3,7},{8,12},{9,13},{10,14},{11,15},{16,20},{17,... | collective-permute-start | bytes 1585160 | tf_op jit(solution)/shard_map/ppermute | solution.py:496
  69.1 30.3 %collective-permute-start.12 = (f32[1032,128]{1,0:T(8,128)S(1)}, f32[1032,128]{1,0:T(8,128)S(1)}, u32[]{:S(2)}, u32[]{:S(2)}) collective-permute-start(f32[1032,128]{1,0:T(8,128)S(1)} %collective-permute-done.11.states_ref.table_ref.refs_9_), channel_id=1, source_target_pairs={{8,4},{9,5},{10,6},{11,7},{16,12},{17,13},{18,14},{19,15},{24,20},... | collective-permute-start | bytes 1585160 | tf_op jit(solution)/shard_map/ppermute | solution.py:496
  76.3 28.7 %collective-permute-start.16 = (f32[1032,128]{1,0:T(8,128)S(1)}, f32[1032,128]{1,0:T(8,128)S(1)}, u32[]{:S(2)}, u32[]{:S(2)}) collective-permute-start(f32[1032,128]{1,0:T(8,128)S(1)} %collective-permute-done.11.states_ref.table_ref.refs_9_), channel_id=1, source_target_pairs={{0,4},{1,5},{2,6},{3,7},{8,12},{9,13},{10,14},{11,15},{16,20},{17,... | collective-permute-start | bytes 1585160 | tf_op jit(solution)/shard_map/ppermute | solution.py:496
  77.6 26.7 %collective-permute-start.15 = (f32[1032,128]{1,0:T(8,128)S(1)}, f32[1032,128]{1,0:T(8,128)S(1)}, u32[]{:S(2)}, u32[]{:S(2)}) collective-permute-start(f32[1032,128]{1,0:T(8,128)S(1)} %collective-permute-done.14.refs_8_), channel_id=1, source_target_pairs={{0,4},{1,5},{2,6},{3,7},{8,12},{9,13},{10,14},{11,15},{16,20},{17,... | collective-permute-start | bytes 1585160 | tf_op jit(solution)/shard_map/ppermute | solution.py:496
  79.0 26.1 %collective-permute-start.18 = (f32[1032,128]{1,0:T(8,128)S(1)}, f32[1032,128]{1,0:T(8,128)S(1)}, u32[]{:S(2)}, u32[]{:S(2)}) collective-permute-start(f32[1032,128]{1,0:T(8,128)S(1)} %collective-permute-done.17.states_ref.table_ref.refs_10_), channel_id=1, source_target_pairs={{0,4},{1,5},{2,6},{3,7},{8,12},{9,13},{10,14},{11,15},{16,20},{17,... | collective-permute-start | bytes 1585160 | tf_op jit(solution)/shard_map/ppermute | solution.py:496
  86.4 26.7 %collective-permute-start.19 = (f32[1032,128]{1,0:T(8,128)S(1)}, f32[1032,128]{1,0:T(8,128)S(1)}, u32[]{:S(2)}, u32[]{:S(2)}) collective-permute-start(f32[1032,128]{1,0:T(8,128)S(1)} %collective-permute-done.14.refs_8_), channel_id=1, source_target_pairs={{8,4},{9,5},{10,6},{11,7},{16,12},{17,13},{18,14},{19,15},{24,20},... | collective-permute-start | bytes 1585160 | tf_op jit(solution)/shard_map/ppermute | solution.py:496
  99.4 13.6 %collective-permute-start.20 = (f32[1032,128]{1,0:T(8,128)S(1)}, f32[1032,128]{1,0:T(8,128)S(1)}, u32[]{:S(2)}, u32[]{:S(2)}) collective-permute-start(f32[1032,128]{1,0:T(8,128)S(1)} %collective-permute-done.12.refs_9_), channel_id=1, source_target_pairs={{4,5},{5,4},{6,7},{7,6},{12,13},{13,12},{14,15},{15,14},{20,21},{2... | collective-permute-start | bytes 1585160 | tf_op jit(solution)/shard_map/ppermute | solution.py:496
  104.3 22.8 %collective-permute-start.22 = (f32[1024,128]{1,0:T(8,128)S(1)}, f32[1024,128]{1,0:T(8,128)S(1)}, u32[]{:S(2)}, u32[]{:S(2)}) collective-permute-start(f32[1024,128]{1,0:T(8,128)S(1)} %shard_map.112.refs_0_), channel_id=1, source_target_pairs={{0,1},{1,0},{2,3},{3,2},{8,9},{9,8},{10,11},{11,10},{16,17},{17,16... | collective-permute-start | bytes 1572872 | tf_op jit(solution)/shard_map/ppermute | solution.py:496
  115.7 21.7 %collective-permute-start.24 = (f32[2064,128]{1,0:T(8,128)S(1)}, f32[2064,128]{1,0:T(8,128)S(1)}, u32[]{:S(2)}, u32[]{:S(2)}) collective-permute-start(f32[2064,128]{1,0:T(8,128)S(1)} %get-tuple-element.46), channel_id=1, source_target_pairs={{4,0},{5,1},{6,2},{7,3},{12,8},{13,9},{14,10},{15,11},{20,16},{21,... | collective-permute-start | bytes 3170312 | tf_op jit(solution)/shard_map/ppermute | solution.py:496
  117.0 11.4 %collective-permute-start.26 = (f32[1032,128]{1,0:T(8,128)S(1)}, f32[1032,128]{1,0:T(8,128)S(1)}, u32[]{:S(2)}, u32[]{:S(2)}) collective-permute-start(f32[1032,128]{1,0:T(8,128)S(1)} %get-tuple-element.42.states_ref.table_ref), channel_id=1, source_target_pairs={{4,8},{5,9},{6,10},{7,11},{12,16},{13,17},{14,18},{15,19},{20,24},... | collective-permute-start | bytes 1585160 | tf_op jit(solution)/shard_map/ppermute | solution.py:496
  118.4 19.0 %collective-permute-start.23 = (f32[1032,128]{1,0:T(8,128)S(1)}, f32[1032,128]{1,0:T(8,128)S(1)}, u32[]{:S(2)}, u32[]{:S(2)}) collective-permute-start(f32[1032,128]{1,0:T(8,128)S(1)} %get-tuple-element.42.states_ref.table_ref), channel_id=1, source_target_pairs={{4,0},{5,1},{6,2},{7,3},{12,8},{13,9},{14,10},{15,11},{20,16},{21,... | collective-permute-start | bytes 1585160 | tf_op jit(solution)/shard_map/ppermute | solution.py:496
  123.8 15.1 %collective-permute-start.27 = (f32[2064,128]{1,0:T(8,128)S(1)}, f32[2064,128]{1,0:T(8,128)S(1)}, u32[]{:S(2)}, u32[]{:S(2)}) collective-permute-start(f32[2064,128]{1,0:T(8,128)S(1)} %get-tuple-element.46), channel_id=1, source_target_pairs={{4,8},{5,9},{6,10},{7,11},{12,16},{13,17},{14,18},{15,19},{20,24},... | collective-permute-start | bytes 3170312 | tf_op jit(solution)/shard_map/ppermute | solution.py:496
  127.1 10.3 %collective-permute-start.25 = (f32[1032,128]{1,0:T(8,128)S(1)}, f32[1032,128]{1,0:T(8,128)S(1)}, u32[]{:S(2)}, u32[]{:S(2)}) collective-permute-start(f32[1032,128]{1,0:T(8,128)S(1)} %get-tuple-element.47), channel_id=1, source_target_pairs={{4,0},{5,1},{6,2},{7,3},{12,8},{13,9},{14,10},{15,11},{20,16},{21,... | collective-permute-start | bytes 1585160 | tf_op jit(solution)/shard_map/ppermute | solution.py:496
  128.5 9.0 %collective-permute-start.28 = (f32[1032,128]{1,0:T(8,128)S(1)}, f32[1032,128]{1,0:T(8,128)S(1)}, u32[]{:S(2)}, u32[]{:S(2)}) collective-permute-start(f32[1032,128]{1,0:T(8,128)S(1)} %collective-permute-done.26.refs_1_), channel_id=1, source_target_pairs={{0,1},{1,0},{2,3},{3,2},{8,9},{9,8},{10,11},{11,10},{16,17},{17,16... | collective-permute-start | bytes 1585160 | tf_op jit(solution)/shard_map/ppermute | solution.py:496
  138.9 20.6 %collective-permute-start.31 = (f32[1024,128]{1,0:T(8,128)S(1)}, f32[1024,128]{1,0:T(8,128)S(1)}, u32[]{:S(2)}, u32[]{:S(2)}) collective-permute-start(f32[1024,128]{1,0:T(8,128)S(1)} %shard_map.119), channel_id=1, source_target_pairs={{0,4},{1,5},{2,6},{3,7},{8,12},{9,13},{10,14},{11,15},{16,20},{17,... | collective-permute-start | bytes 1572872 | tf_op jit(solution)/shard_map/ppermute | solution.py:496
  140.9 15.9 %collective-permute-start.29 = (f32[512,128]{1,0:T(8,128)S(1)}, f32[512,128]{1,0:T(8,128)S(1)}, u32[]{:S(2)}, u32[]{:S(2)}) collective-permute-start(f32[512,128]{1,0:T(8,128)S(1)} %get-tuple-element.53), channel_id=1, source_target_pairs={{8,4},{9,5},{10,6},{11,7},{16,12},{17,13},{18,14},{19,15},{24,20},... | collective-permute-start | bytes 786440 | tf_op jit(solution)/shard_map/ppermute | solution.py:496
  142.2 17.4 %collective-permute-start.30 = (f32[512,128]{1,0:T(8,128)S(1)}, f32[512,128]{1,0:T(8,128)S(1)}, u32[]{:S(2)}, u32[]{:S(2)}) collective-permute-start(f32[512,128]{1,0:T(8,128)S(1)} %get-tuple-element.54), channel_id=1, source_target_pairs={{8,4},{9,5},{10,6},{11,7},{16,12},{17,13},{18,14},{19,15},{24,20},... | collective-permute-start | bytes 786440 | tf_op jit(solution)/shard_map/ppermute | solution.py:496

commit v5 on v4

--- a/solution.py
+++ b/solution.py
@@ -56,9 +56,11 @@
     return pl.ds(at, count * n)
 
 
-def pack_kernel(live_ref, parent_ref, mode_ref, damping_ref, weight_ref, corr_ref, coupling_ref, out_ref, table_ref):
-    slots, n = live_ref.shape[0], coupling_ref.shape[1]
-    out_ref[pl.ds(ROWS, coupling_ref.shape[0])] = coupling_ref[...]
+def pack_kernel(live_ref, parent_ref, mode_ref, damping_ref, weight_ref, corr_ref, blocks_ref, coupling_ref, out_ref, table_ref):
+    slots, n = live_ref.shape[0], blocks_ref.shape[1]
+    size = blocks_ref.shape[0]
+    out_ref[pl.ds(0, size)] = blocks_ref[...]
+    out_ref[pl.ds(size + ROWS, coupling_ref.shape[0])] = coupling_ref[...]
     row = lax.broadcasted_iota(jnp.int32, (ROWS, n), 0)
     lane = lax.broadcasted_iota(jnp.int32, (ROWS, n), 1)
     table = jnp.zeros((ROWS, n), f32)
@@ -81,7 +83,7 @@
     live_row = table[LIVE : LIVE + 1]
     table = jnp.where(row == FACTOR, live_row * jnp.exp(table), table)
     table_ref[...] = table
-    out_ref[pl.ds(0, ROWS)] = table
+    out_ref[pl.ds(size, ROWS)] = table
 
 
 def powers_kernel(ham_ref, right_ref, left_ref):
@@ -105,8 +107,8 @@
 
 
 class Layout:
-    def __init__(self, refs, slots, split, notes=()):
-        self.refs, self.slots, self.split, self.notes = refs, slots, split, notes
+    def __init__(self, refs, slots, split):
+        self.refs, self.slots, self.split = refs, slots, split
         self.group = sum(len(held) for held in split)
         self.n = refs[0].shape[1]
         self.size = 2 * slots * self.n
@@ -117,19 +119,13 @@
             if k in held:
                 return ref, held.index(k) * self.stride
 
-    def table_rows(self, k):
-        if self.notes:
-            return self.notes[k], pl.ds(0, ROWS)
+    def table(self, k):
         ref, base = self.base(k)
-        return ref, pl.ds(base + self.size, ROWS)
-
-    def table(self, k):
-        ref, where = self.table_rows(k)
-        return ref.at[where, pl.ds(0, LANES)]
+        return ref.at[pl.ds(base + self.size, ROWS), pl.ds(0, LANES)]
 
     def copy_table(self, k, target_ref, at):
-        ref, where = self.table_rows(k)
-        target_ref[at] = ref[where]
+        ref, base = self.base(k)
+        target_ref[at] = ref[pl.ds(base + self.size, ROWS)]
 
     def fetch(self, index, stage_ref, at):
         for k in range(self.group):
@@ -153,7 +149,7 @@
     return ref.at[pl.ds(0, ROWS), pl.ds(0, LANES)]
 
 
-def operators_kernel(group, modes, parity, own_ref, *refs):
+def operators_kernel(slots, group, modes, parity, own_ref, *refs):
     outs = refs[-2 - (parity is None) :]
     sources = refs[: -len(outs)]
     right_ref, left_ref = outs[0], outs[1]
@@ -170,9 +166,11 @@
 
     if parity is None:
         own()
+        groups = Layout(sources, slots, single(group))
         for k in range(1, group):
+            ref, base = groups.base(k)
             for i in range(modes):
-                value = sources[k][rows(ROWS + i * n, n)]
+                value = ref[rows(base + groups.stride + i * n, n)]
                 put(k * modes + i, value)
                 outs[2][rows(((k - 1) * modes + i) * n, n)] = value
     else:
@@ -218,7 +216,7 @@
     return u_real + done[:, :n], u_imag + done[:, n:]
 
 
-def free_kernel(run_parity, times, first, table_row, states_ref, table_ref, right_ref, left_ref, *refs):
+def free_kernel(run_parity, times, slots, first, states_ref, right_ref, left_ref, *refs):
     out_ref = refs[-1]
     n = out_ref.shape[1]
     ahead = first if len(refs) > 1 else 0
@@ -243,7 +241,7 @@
                     out_ref[r] = real
                     out_ref[i] = imag
 
-        factors = table_ref[pl.ds(table_row, ROWS)][FACTOR : FACTOR + 1]
+        factors = states_ref[pl.ds(2 * slots * n, ROWS)][FACTOR : FACTOR + 1]
         for s in range(count):
             scale = factors[:, first + s : first + s + 1] ** times
             at = rows(2 * (ahead + s) * n, n, 2)
@@ -311,13 +309,12 @@
             groups.fetch(parent_of(tab, s, slots), pick, at)
 
 
-def send_kernel(sender, slots, group, split, modes, parts, noted, right_ref, left_ref, *refs):
+def send_kernel(sender, slots, group, split, modes, parts, right_ref, left_ref, *refs):
     acc_ref, stage_ref, list_ref, tab, sem_ref = refs[-5:]
     tabs_ref = refs[-6]
     n = acc_ref.shape[1]
     sums = refs[-6 - parts : -6]
-    held = refs[: -6 - parts]
-    groups = Layout(held[: len(split)], slots, split, held[len(split) :] if noted else ())
+    groups = Layout(refs[: -6 - parts], slots, split)
 
     @pl.when(odd_depth() == sender)
     def _():
@@ -531,40 +528,37 @@
     operator_shapes = (sds(group * modes, 3 * n, n, dtype=bf16), sds(group * modes, n, 3 * n, dtype=bf16))
     couplings = coupling.reshape(modes * n, n)
 
-    states = blocks.reshape(plain * n, n)
-    first = gather(states, 1)
     packed, own_table = call(
         pack_kernel,
-        (mats(modes, 1), sds(ROWS, n)),
+        (mats(plain + modes, 1), sds(ROWS, n)),
         PACK_LIMIT,
-        (live_slots, parent_index, bath_mode, damping, link_weight, correlation, couplings),
+        (live_slots, parent_index, bath_mode, damping, link_weight, correlation, blocks.reshape(plain * n, n), couplings),
         smem=6,
     )
-    notes = gather(packed, 1)
+    first = gather(packed, 1)
     near_table = shift(own_table, -1)
     powers = call(
         powers_kernel, (sds(3 * n, ORDER * n, dtype=bf16), sds(n, 3 * ORDER * n, dtype=bf16)), limit, (hamiltonian,)
     )
     *operators_odd, raw = call(
-        functools.partial(operators_kernel, group, modes, None),
+        functools.partial(operators_kernel, slots, group, modes, None),
         (*operator_shapes, mats((group - 1) * modes)),
         limit,
-        (couplings, *notes),
+        (couplings, *first),
     )
 
-    def free(states, parity, times, part=0, parts=1, prior=None, note=None):
+    def free(states, parity, times, part=0, parts=1, prior=None):
         count = slots // parts
-        table, row = (states, plain * n) if note is None else (note, 0)
         return call(
-            functools.partial(free_kernel, parity, times, part * count, row),
+            functools.partial(free_kernel, parity, times, slots, part * count),
             mats(2 * count * (1 if prior is None else part + 1)),
             limit,
-            (states, table, *powers) if prior is None else (states, table, *powers, prior),
+            (states, *powers) if prior is None else (states, *powers, prior),
             us=4.5 * times / parts,
         )
 
-    def free_parts(states, parity, times, note):
-        return [free(states, parity, times, part, split_hop, note=note) for part in range(split_hop)]
+    def free_parts(states, parity, times):
+        return [free(states, parity, times, part, split_hop) for part in range(split_hop)]
 
     def free_chain(states, parity, times):
         done = None
@@ -583,12 +577,12 @@
             scratch=tables(1),
         )
 
-    def send(groups, sender, parts, operators, notes=()):
+    def send(groups, sender, parts, operators):
         outs = call(
-            functools.partial(send_kernel, sender, slots, group, splits[len(groups)], modes, parts, bool(notes)),
+            functools.partial(send_kernel, sender, slots, group, splits[len(groups)], modes, parts),
             [mats(plain // parts)] * parts + [sds(group, ROWS, n)],
             limit,
-            (*operators, *groups, *notes),
+            (*operators, *groups),
             us=2,
             scratch=[stage, stage, SMEM((total,), jnp.int32), *tables(group)],
         )
@@ -619,23 +613,22 @@
             scratch=[stage, *tables(group + (span[2] if kind == "children" else 0))],
         )
 
-    free_even = free(states, 0, 1, note=packed)
-    free_odd = [part for k in ranks for part in free_parts(first[k], 1, 2, notes[k])]
+    free_even = free(packed, 0, 1)
+    free_odd = [part for k in ranks for part in free_parts(first[k], 1, 2)]
     picks = [shift(value, 1, 1) for value in pick(first, 1, split_hop)]
-    sums, tabs_odd = send(first, 1, 1, operators_odd, notes)
+    sums, tabs_odd = send(first, 1, 1, operators_odd)
     sums = [shift(value, -1, 1) for value in sums]
     passed = shift(raw, -1, 1)
     operators_even = call(
-        functools.partial(operators_kernel, group, modes, 0), operator_shapes, limit, (couplings, passed)
+        functools.partial(operators_kernel, slots, group, modes, 0), operator_shapes, limit, (couplings, passed)
     )
     own_state = join([free_even], sums, picks, 0, operators_odd)
 
     gathered = gather(own_state, 0)
-    from_below = [shift(value, -1, 0) for value in gathered[:-1]]
-    from_below.append(neighbour(from_below[group - 2], 1))
+    from_below = [shift(value, -1, 0) for value in gathered]
     from_above = [shift(value, 1, 0) for value in gathered]
-    free_own = free_chain(gathered[0], 0, 2)
-    free_even = [free_own, neighbour(free_own, 0)] + [free(gathered[k], 0, 2) for k in range(2, group)]
+    free_even = [free_chain(gathered[0], 0, 2)] + [free(gathered[k], 0, 2) for k in range(2, group, 2)]
+    free_even = [value for own in free_even for value in (own, neighbour(own, 0))]
     evens, odds = (0, 2, group // 2), (1, 2, group // 2)
     states, _ = side("children", free_odd, from_below[::2], [tabs_odd], 1, operators_odd, span=evens)
     states, _ = side("parents", [states], from_above, [tabs_odd], 1, operators_odd)

time: 162 us -> 155 us (0.957)
  the two profiles are of different devices: /device:TPU:19 before, /device:TPU:3 now
where the time goes in v5:
time: 155 us; the launch traced here: 154 us
  Pallas kernels  61.1 us (39%)
  starting transfers between devices  52.8 us (34%)
  waiting for transfers between devices  39.8 us (26%)
    pallas_call x29, Pallas kernels, call(): pl.pallas_call(kernel, out_shape=out_shapes, in_specs=specs, out_specs=ja...  61.1 us
    ppermute x30, starting transfers between devices, permute(): return lax.ppermute(value, AXES, pairs)  52.8 us
    ppermute x30, waiting for transfers between devices, permute(): return lax.ppermute(value, AXES, pairs)  39.8 us
  transfers between devices with their start and end apart: 30, of which 11 were waited for; matrix products, arithmetic and copies ran while one was open for 0% of the time, Pallas kernels for 37%

profile of v5, /device:TPU:3, one launch (start us, length us, event | category | flops | bytes accessed | tf_op | source)
XLA Modules:
  0.0 154.5 jit_solution(7423278091921596602)
XLA Ops:
  0.0 2.0 %shard_map.91 = (f32[1288,128]{1,0:T(8,128)}, f32[8,128]{1,0:T(8,128)}) custom-call(s32[4]{0:T(128)} %live_ref.1, s32[4]{0:T(128)} %parent_ref.1, s32[4]{0:T(128)} %mode_ref.1, f32[4]{0:T(128)} %damping_ref.1, f32[4]{0:T(128)} %weight_ref.1, f32[2,2]{1,0:T(2,128)} %corr_ref.1, f32[1024,128]{1,0:T(8,128)} %bitcast.6, f32[256,128]{1,0:T(8,128)} %bitcast.3), custom_call_target="tpu_custom_call" | custom-call | flops 1100000000 | bytes 524288 | tf_op jit(solution)/shard_map/pallas_call | solution.py:464
  2.0 4.2 %collective-permute-start.1 = (f32[1288,128]{1,0:T(8,128)}, f32[1288,128]{1,0:T(8,128)S(1)}, u32[]{:S(2)}, u32[]{:S(2)}) collective-permute-start(f32[1288,128]{1,0:T(8,128)} %get-tuple-element.31.refs_0_.states_ref), channel_id=1, source_target_pairs={{4,6},{5,7},{6,4},{7,5},{12,14},{13,15},{14,12},{15,13},{20,22},{2... | collective-permute-start | bytes 1978376 | tf_op jit(solution)/shard_map/ppermute | solution.py:493
  6.2 3.2 %collective-permute-start = (f32[1288,128]{1,0:T(8,128)}, f32[1288,128]{1,0:T(8,128)S(1)}, u32[]{:S(2)}, u32[]{:S(2)}) collective-permute-start(f32[1288,128]{1,0:T(8,128)} %get-tuple-element.31.refs_0_.states_ref), channel_id=1, source_target_pairs={{4,5},{5,4},{6,7},{7,6},{12,13},{13,12},{14,15},{15,14},{20,21},{2... | collective-permute-start | bytes 1978376 | tf_op jit(solution)/shard_map/ppermute | solution.py:493
  9.4 2.1 %collective-permute-start.4 = (f32[8,128]{1,0:T(8,128)}, f32[8,128]{1,0:T(8,128)S(1)}, u32[]{:S(2)}, u32[]{:S(2)}) collective-permute-start(f32[8,128]{1,0:T(8,128)} %get-tuple-element.30.own_ref), channel_id=1, source_target_pairs={{4,0},{5,1},{6,2},{7,3},{8,4},{9,5},{10,6},{11,7},{12,8},{13,9},{1... | collective-permute-start | bytes 12296 | tf_op jit(solution)/shard_map/ppermute | solution.py:493
  11.5 0.7 shard_map.93
  12.3 4.2 %shard_map.94.refs_0_ = f32[512,128]{1,0:T(8,128)S(1)} custom-call(f32[1288,128]{1,0:T(8,128)S(1)} %copy-done.1, bf16[384,512]{1,0:T(8,128)(2,1)S(1)} %get-tuple-element.34.right_ref, bf16[128,1536]{1,0:T(8,128)(2,1)S(1)} %get-tuple-element.35.left_ref), custom_call_target="tpu_custom_call" | custom-call | flops 4950000128 | bytes 524288 | tf_op jit(solution)/shard_map/pallas_call | solution.py:464
  16.5 4.2 %shard_map.95.refs_1_ = f32[512,128]{1,0:T(8,128)S(1)} custom-call(f32[1288,128]{1,0:T(8,128)S(1)} %copy-done.1, bf16[384,512]{1,0:T(8,128)(2,1)S(1)} %get-tuple-element.34.right_ref, bf16[128,1536]{1,0:T(8,128)(2,1)S(1)} %get-tuple-element.35.left_ref), custom_call_target="tpu_custom_call" | custom-call | flops 4950000128 | bytes 524288 | tf_op jit(solution)/shard_map/pallas_call | solution.py:464
  20.7 0.9 collective-permute-done.1.refs_2_.states_ref
  21.6 2.6 %collective-permute-start.2 = (f32[1288,128]{1,0:T(8,128)S(1)}, f32[1288,128]{1,0:T(8,128)S(1)}, u32[]{:S(2)}, u32[]{:S(2)}) collective-permute-start(f32[1288,128]{1,0:T(8,128)S(1)} %collective-permute-done.1.refs_2_.states_ref), channel_id=1, source_target_pairs={{4,5},{5,4},{6,7},{7,6},{12,13},{13,12},{14,15},{15,14},{20,21},{2... | collective-permute-start | bytes 1978376 | tf_op jit(solution)/shard_map/ppermute | solution.py:493
  24.3 4.2 %shard_map.98.refs_4_ = f32[512,128]{1,0:T(8,128)S(1)} custom-call(f32[1288,128]{1,0:T(8,128)S(1)} %collective-permute-done.1.refs_2_.states_ref, bf16[384,512]{1,0:T(8,128)(2,1)S(1)} %get-tuple-element.34.right_ref, bf16[128,1536]{1,0:T(8,128)(2,1)S(1)} %get-tuple-element.35.left_ref), custom_call_target="tpu_custom_call" | custom-call | flops 4950000128 | bytes 524288 | tf_op jit(solution)/shard_map/pallas_call | solution.py:464
  28.5 0.0 copy-start.2
  28.5 4.2 %shard_map.99.refs_5_ = f32[512,128]{1,0:T(8,128)S(1)} custom-call(f32[1288,128]{1,0:T(8,128)S(1)} %collective-permute-done.1.refs_2_.states_ref, bf16[384,512]{1,0:T(8,128)(2,1)S(1)} %get-tuple-element.34.right_ref, bf16[128,1536]{1,0:T(8,128)(2,1)S(1)} %get-tuple-element.35.left_ref), custom_call_target="tpu_custom_call" | custom-call | flops 4950000128 | bytes 524288 | tf_op jit(solution)/shard_map/pallas_call | solution.py:464
  32.7 0.3 collective-permute-done.2.refs_3_.states_ref
  33.0 0.2 shard_map.92
  33.2 2.6 %shard_map.103 = (f32[1024,128]{1,0:T(8,128)S(1)}, f32[4,8,128]{2,1,0:T(8,128)S(1)}) custom-call(bf16[8,384,128]{2,1,0:T(8,128)(2,1)S(1)} %get-tuple-element.32.right_ref, bf16[8,128,384]{2,1,0:T(8,128)(2,1)S(1)} %get-tuple-element.33.left_ref, f32[1288,128]{1,0:T(8,128)S(1)} %copy-done.1, f32[1288,128]{1,0:T(8,128)S(1)} %collective-permute-done.refs_1_.states_ref, ...), custom_call_target="tpu_custom_call" | custom-call | flops 2200000000 | bytes 524288 | tf_op jit(solution)/shard_map/pallas_call | solution.py:464
  35.8 1.3 collective-permute-start.3
  37.2 0.8 shard_map.104
  38.0 1.3 collective-permute-start.5
  39.3 0.0 copy-start
  39.3 1.3 collective-permute-start.6
  40.6 4.2 %shard_map.96.refs_2_ = f32[512,128]{1,0:T(8,128)S(1)} custom-call(f32[1288,128]{1,0:T(8,128)S(1)} %collective-permute-done.refs_1_.states_ref, bf16[384,512]{1,0:T(8,128)(2,1)S(1)} %get-tuple-element.34.right_ref, bf16[128,1536]{1,0:T(8,128)(2,1)S(1)} %get-tuple-element.35.left_ref), custom_call_target="tpu_custom_call" | custom-call | flops 4950000128 | bytes 524288 | tf_op jit(solution)/shard_map/pallas_call | solution.py:464
  44.8 0.6 collective-permute-done.6.refs_3_
  45.4 0.7 collective-permute-start.8
  46.1 4.2 %shard_map.97.refs_3_ = f32[512,128]{1,0:T(8,128)S(1)} custom-call(f32[1288,128]{1,0:T(8,128)S(1)} %collective-permute-done.refs_1_.states_ref, bf16[384,512]{1,0:T(8,128)(2,1)S(1)} %get-tuple-element.34.right_ref, bf16[128,1536]{1,0:T(8,128)(2,1)S(1)} %get-tuple-element.35.left_ref), custom_call_target="tpu_custom_call" | custom-call | flops 4950000128 | bytes 524288 | tf_op jit(solution)/shard_map/pallas_call | solution.py:464
  50.3 4.2 %shard_map.100.refs_6_ = f32[512,128]{1,0:T(8,128)S(1)} custom-call(f32[1288,128]{1,0:T(8,128)S(1)} %collective-permute-done.2.refs_3_.states_ref, bf16[384,512]{1,0:T(8,128)(2,1)S(1)} %get-tuple-element.34.right_ref, bf16[128,1536]{1,0:T(8,128)(2,1)S(1)} %get-tuple-element.35.left_ref), custom_call_target="tpu_custom_call" | custom-call | flops 4950000128 | bytes 524288 | tf_op jit(solution)/shard_map/pallas_call | solution.py:464
  54.5 1.3 collective-permute-start.7
  55.8 0.7 collective-permute-start.11
  56.5 0.7 collective-permute-start.14
  57.2 4.2 %shard_map.101.refs_7_ = f32[512,128]{1,0:T(8,128)S(1)} custom-call(f32[1288,128]{1,0:T(8,128)S(1)} %collective-permute-done.2.refs_3_.states_ref, bf16[384,512]{1,0:T(8,128)(2,1)S(1)} %get-tuple-element.34.right_ref, bf16[128,1536]{1,0:T(8,128)(2,1)S(1)} %get-tuple-element.35.left_ref), custom_call_target="tpu_custom_call" | custom-call | flops 4950000128 | bytes 524288 | tf_op jit(solution)/shard_map/pallas_call | solution.py:464
  61.4 1.3 collective-permute-start.10
  62.7 1.3 collective-permute-start.9
  64.0 0.2 shard_map.111.refs_0_
  64.2 1.7 %collective-permute-done.7.refs_8_ = f32[1032,128]{1,0:T(8,128)S(1)} collective-permute-done((f32[1032,128]{1,0:T(8,128)S(1)}, f32[1032,128]{1,0:T(8,128)S(1)}, u32[]{:S(2)}, u32[]{:S(2)}) %collective-permute-start.7) | collective-permute-done | bytes 528416 | tf_op jit(solution)/shard_map/ppermute | solution.py:493
  65.9 1.3 collective-permute-start.13
  67.2 1.3 collective-permute-start.12
  68.6 1.3 collective-permute-start.15
  69.9 0.4 collective-permute-done.10.refs_1_
  70.3 1.3 collective-permute-start.16
  71.6 7.5 %collective-permute-done.9.refs_9_ = f32[1032,128]{1,0:T(8,128)S(1)} collective-permute-done((f32[1032,128]{1,0:T(8,128)S(1)}, f32[1032,128]{1,0:T(8,128)S(1)}, u32[]{:S(2)}, u32[]{:S(2)}) %collective-permute-start.9) | collective-permute-done | bytes 528416 | tf_op jit(solution)/shard_map/ppermute | solution.py:493
  79.1 1.3 collective-permute-start.17
  80.4 2.9 %shard_map.106 = (f32[4096,128]{1,0:T(8,128)S(1)}, f32[4,8,128]{2,1,0:T(8,128)}) custom-call(bf16[8,384,128]{2,1,0:T(8,128)(2,1)S(1)} %get-tuple-element.32.right_ref, bf16[8,128,384]{2,1,0:T(8,128)(2,1)S(1)} %get-tuple-element.33.left_ref, f32[512,128]{1,0:T(8,128)S(1)} %shard_map.94.refs_0_, f32[512,128]{1,0:T(8,128)S(1)} %shard_map.95.refs_1_, ...), custom_call_target="tpu_custom_call" | custom-call | flops 3300000000 | bytes 524288 | tf_op jit(solution)/shard_map/pallas_call | solution.py:464
  83.3 0.7 collective-permute-start.19
  84.1 4.4 %shard_map.107 = (f32[4096,128]{1,0:T(8,128)S(1)}, f32[4,8,128]{2,1,0:T(8,128)}) custom-call(bf16[8,384,128]{2,1,0:T(8,128)(2,1)S(1)} %get-tuple-element.32.right_ref, bf16[8,128,384]{2,1,0:T(8,128)(2,1)S(1)} %get-tuple-element.33.left_ref, f32[4096,128]{1,0:T(8,128)S(1)} %get-tuple-element.40.refs_0_, f32[1032,128]{1,0:T(8,128)S(1)} %collective-permute-done.10.refs_1_, ...), custom_call_target="tpu_custom_call" | custom-call | flops 3300000000 | bytes 524288 | tf_op jit(solution)/shard_map/pallas_call | solution.py:464
  88.5 4.6 %collective-permute-done.16.refs_1_ = f32[1032,128]{1,0:T(8,128)S(1)} collective-permute-done((f32[1032,128]{1,0:T(8,128)S(1)}, f32[1032,128]{1,0:T(8,128)S(1)}, u32[]{:S(2)}, u32[]{:S(2)}) %collective-permute-start.16) | collective-permute-done | bytes 528416 | tf_op jit(solution)/shard_map/ppermute | solution.py:493
  93.1 5.7 %collective-permute-done.17.refs_2_ = f32[1032,128]{1,0:T(8,128)S(1)} collective-permute-done((f32[1032,128]{1,0:T(8,128)S(1)}, f32[1032,128]{1,0:T(8,128)S(1)}, u32[]{:S(2)}, u32[]{:S(2)}) %collective-permute-start.17) | collective-permute-done | bytes 528416 | tf_op jit(solution)/shard_map/ppermute | solution.py:493
  98.7 2.6 %shard_map.108 = (f32[1032,128]{1,0:T(8,128)S(1)}, f32[2064,128]{1,0:T(8,128)S(1)}, f32[1032,128]{1,0:T(8,128)S(1)}) custom-call(bf16[8,384,128]{2,1,0:T(8,128)(2,1)S(1)} %get-tuple-element.32.right_ref, bf16[8,128,384]{2,1,0:T(8,128)(2,1)S(1)} %get-tuple-element.33.left_ref, f32[4096,128]{1,0:T(8,128)S(1)} %get-tuple-element.41.refs_0_, ...), custom_call_target="tpu_custom_call" | custom-call | flops 3300000000 | bytes 524288 | tf_op jit(solution)/shard_map/pallas_call | solution.py:464
  101.3 1.3 collective-permute-start.24
  102.7 0.7 collective-permute-start.20
  103.4 8.0 %collective-permute-start.18 = (f32[768,128]{1,0:T(8,128)S(1)}, f32[768,128]{1,0:T(8,128)S(1)}, u32[]{:S(2)}, u32[]{:S(2)}) collective-permute-start(f32[768,128]{1,0:T(8,128)S(1)} %get-tuple-element.43), channel_id=1, source_target_pairs={{4,0},{5,1},{6,2},{7,3},{12,8},{13,9},{14,10},{15,11},{20,16},{21,... | collective-permute-start | bytes 1179656 | tf_op jit(solution)/shard_map/ppermute | solution.py:493
  111.4 1.4 collective-permute-start.22
  112.8 2.4 %collective-permute-start.21 = (f32[1032,128]{1,0:T(8,128)S(1)}, f32[1032,128]{1,0:T(8,128)S(1)}, u32[]{:S(2)}, u32[]{:S(2)}) collective-permute-start(f32[1032,128]{1,0:T(8,128)S(1)} %get-tuple-element.42.states_ref), channel_id=1, source_target_pairs={{4,0},{5,1},{6,2},{7,3},{12,8},{13,9},{14,10},{15,11},{20,16},{21,... | collective-permute-start | bytes 1585160 | tf_op jit(solution)/shard_map/ppermute | solution.py:493
  115.3 3.9 %collective-permute-start.25 = (f32[2064,128]{1,0:T(8,128)S(1)}, f32[2064,128]{1,0:T(8,128)S(1)}, u32[]{:S(2)}, u32[]{:S(2)}) collective-permute-start(f32[2064,128]{1,0:T(8,128)S(1)} %get-tuple-element.46), channel_id=1, source_target_pairs={{4,8},{5,9},{6,10},{7,11},{12,16},{13,17},{14,18},{15,19},{20,24},... | collective-permute-start | bytes 3170312 | tf_op jit(solution)/shard_map/ppermute | solution.py:493
  119.2 1.3 collective-permute-start.23
  120.6 0.7 collective-permute-start.26
  121.3 8.2 %shard_map.109.refs_0_ = f32[1024,128]{1,0:T(8,128)S(1)} custom-call(f32[1032,128]{1,0:T(8,128)S(1)} %get-tuple-element.42.states_ref, bf16[384,512]{1,0:T(8,128)(2,1)S(1)} %get-tuple-element.34.right_ref, bf16[128,1536]{1,0:T(8,128)(2,1)S(1)} %get-tuple-element.35.left_ref), custom_call_target="tpu_custom_call" | custom-call | flops 9900000256 | bytes 524288 | tf_op jit(solution)/shard_map/pallas_call | solution.py:464
  129.5 0.1 shard_map.114
  129.6 1.3 collective-permute-done.25.refs_2_
  131.1 1.3 collective-permute-start.29
  132.4 0.7 shard_map.117
  133.0 1.3 collective-permute-start.27
  134.3 1.3 collective-permute-start.28
  135.7 13.9 %collective-permute-done.27.refs_2_ = f32[512,128]{1,0:T(8,128)S(1)} collective-permute-done((f32[512,128]{1,0:T(8,128)S(1)}, f32[512,128]{1,0:T(8,128)S(1)}, u32[]{:S(2)}, u32[]{:S(2)}) %collective-permute-start.27) | collective-permute-done | bytes 262176 | tf_op jit(solution)/shard_map/ppermute | solution.py:493
  149.6 2.8 %collective-permute-done.28.refs_3_ = f32[512,128]{1,0:T(8,128)S(1)} collective-permute-done((f32[512,128]{1,0:T(8,128)S(1)}, f32[512,128]{1,0:T(8,128)S(1)}, u32[]{:S(2)}, u32[]{:S(2)}) %collective-permute-start.28) | collective-permute-done | bytes 262176 | tf_op jit(solution)/shard_map/ppermute | solution.py:493
  152.4 1.9 %shard_map.119 = f32[1024,128]{1,0:T(8,128)} custom-call(f32[8,128]{1,0:T(8,128)S(1)} %copy-done, bf16[8,384,128]{2,1,0:T(8,128)(2,1)S(1)} %get-tuple-element.32.right_ref, bf16[8,128,384]{2,1,0:T(8,128)(2,1)S(1)} %get-tuple-element.33.left_ref, f32[1024,128]{1,0:T(8,128)S(1)} %shard_map.109.refs_0_, f32[1024,128]{1,0:T(8,128)S(1)} %shard_map.116.refs_1_, ...), custom_call_target="tpu_custom_call" | custom-call | flops 1100000000 | bytes 524288 | tf_op jit(solution)/shard_map/pallas_call | solution.py:464
  (33 shorter events, 0.2 us)
Async XLA Ops:
  0.0 11.5 %copy-start.3 = (f32[128,128]{1,0:T(8,128)S(1)}, f32[128,128]{1,0:T(8,128)}, u32[]{:S(2)}) copy-start(f32[128,128]{1,0:T(8,128)} %ham_ref.1) | copy-start | bytes 196612
  2.0 19.6 %collective-permute-start.1 = (f32[1288,128]{1,0:T(8,128)}, f32[1288,128]{1,0:T(8,128)S(1)}, u32[]{:S(2)}, u32[]{:S(2)}) collective-permute-start(f32[1288,128]{1,0:T(8,128)} %get-tuple-element.31.refs_0_.states_ref), channel_id=1, source_target_pairs={{4,6},{5,7},{6,4},{7,5},{12,14},{13,15},{14,12},{15,13},{20,22},{2... | collective-permute-start | bytes 1978376 | tf_op jit(solution)/shard_map/ppermute | solution.py:493
  6.2 26.5 %collective-permute-start = (f32[1288,128]{1,0:T(8,128)}, f32[1288,128]{1,0:T(8,128)S(1)}, u32[]{:S(2)}, u32[]{:S(2)}) collective-permute-start(f32[1288,128]{1,0:T(8,128)} %get-tuple-element.31.refs_0_.states_ref), channel_id=1, source_target_pairs={{4,5},{5,4},{6,7},{7,6},{12,13},{13,12},{14,15},{15,14},{20,21},{2... | collective-permute-start | bytes 1978376 | tf_op jit(solution)/shard_map/ppermute | solution.py:493
  9.4 2.8 %copy-start.1 = (f32[1288,128]{1,0:T(8,128)S(1)}, f32[1288,128]{1,0:T(8,128)}, u32[]{:S(2)}) copy-start(f32[1288,128]{1,0:T(8,128)} %get-tuple-element.31.refs_0_.states_ref) | copy-start | bytes 1978372
  9.4 27.7 %collective-permute-start.4 = (f32[8,128]{1,0:T(8,128)}, f32[8,128]{1,0:T(8,128)S(1)}, u32[]{:S(2)}, u32[]{:S(2)}) collective-permute-start(f32[8,128]{1,0:T(8,128)} %get-tuple-element.30.own_ref), channel_id=1, source_target_pairs={{4,0},{5,1},{6,2},{7,3},{8,4},{9,5},{10,6},{11,7},{12,8},{13,9},{1... | collective-permute-start | bytes 12296 | tf_op jit(solution)/shard_map/ppermute | solution.py:493
  21.6 11.4 %collective-permute-start.2 = (f32[1288,128]{1,0:T(8,128)S(1)}, f32[1288,128]{1,0:T(8,128)S(1)}, u32[]{:S(2)}, u32[]{:S(2)}) collective-permute-start(f32[1288,128]{1,0:T(8,128)S(1)} %collective-permute-done.1.refs_2_.states_ref), channel_id=1, source_target_pairs={{4,5},{5,4},{6,7},{7,6},{12,13},{13,12},{14,15},{15,14},{20,21},{2... | collective-permute-start | bytes 1978376 | tf_op jit(solution)/shard_map/ppermute | solution.py:493
  28.5 4.5 %copy-start.2 = (f32[2,128,128]{2,1,0:T(8,128)S(1)}, f32[2,128,128]{2,1,0:T(8,128)}, u32[]{:S(2)}) copy-start(f32[2,128,128]{2,1,0:T(8,128)} %param.14) | copy-start | bytes 393220
  35.8 9.5 %collective-permute-start.3 = (f32[1024,128]{1,0:T(8,128)S(1)}, f32[1024,128]{1,0:T(8,128)S(1)}, u32[]{:S(2)}, u32[]{:S(2)}) collective-permute-start(f32[1024,128]{1,0:T(8,128)S(1)} %get-tuple-element.36), channel_id=1, source_target_pairs={{4,0},{5,1},{6,2},{7,3},{12,8},{13,9},{14,10},{15,11},{20,16},{21,... | collective-permute-start | bytes 1572872 | tf_op jit(solution)/shard_map/ppermute | solution.py:493
  38.0 6.8 %collective-permute-start.5 = (f32[512,128]{1,0:T(8,128)S(1)}, f32[512,128]{1,0:T(8,128)S(1)}, u32[]{:S(2)}, u32[]{:S(2)}) collective-permute-start(f32[512,128]{1,0:T(8,128)S(1)} %get-tuple-element.37), channel_id=1, source_target_pairs={{4,8},{5,9},{6,10},{7,11},{12,16},{13,17},{14,18},{15,19},{20,24},... | collective-permute-start | bytes 786440 | tf_op jit(solution)/shard_map/ppermute | solution.py:493
  39.3 6.1 %copy-start = (f32[8,128]{1,0:T(8,128)S(1)}, f32[8,128]{1,0:T(8,128)}, u32[]{:S(2)}) copy-start(f32[8,128]{1,0:T(8,128)} %get-tuple-element.30.own_ref) | copy-start | bytes 12292
  39.3 6.1 %collective-permute-start.6 = (f32[512,128]{1,0:T(8,128)S(1)}, f32[512,128]{1,0:T(8,128)S(1)}, u32[]{:S(2)}, u32[]{:S(2)}) collective-permute-start(f32[512,128]{1,0:T(8,128)S(1)} %get-tuple-element.38), channel_id=1, source_target_pairs={{4,8},{5,9},{6,10},{7,11},{12,16},{13,17},{14,18},{15,19},{20,24},... | collective-permute-start | bytes 786440 | tf_op jit(solution)/shard_map/ppermute | solution.py:493
  45.4 11.1 %collective-permute-start.8 = (f32[1032,128]{1,0:T(8,128)S(1)}, f32[1032,128]{1,0:T(8,128)S(1)}, u32[]{:S(2)}, u32[]{:S(2)}) collective-permute-start(f32[1032,128]{1,0:T(8,128)S(1)} %shard_map.105.states_ref.refs_7_), channel_id=1, source_target_pairs={{0,2},{1,3},{2,0},{3,1},{8,10},{9,11},{10,8},{11,9},{16,18},{17,19... | collective-permute-start | bytes 1585160 | tf_op jit(solution)/shard_map/ppermute | solution.py:493
  54.5 11.4 %collective-permute-start.7 = (f32[1032,128]{1,0:T(8,128)S(1)}, f32[1032,128]{1,0:T(8,128)S(1)}, u32[]{:S(2)}, u32[]{:S(2)}) collective-permute-start(f32[1032,128]{1,0:T(8,128)S(1)} %shard_map.105.states_ref.refs_7_), channel_id=1, source_target_pairs={{8,4},{9,5},{10,6},{11,7},{16,12},{17,13},{18,14},{19,15},{24,20},... | collective-permute-start | bytes 1585160 | tf_op jit(solution)/shard_map/ppermute | solution.py:493
  55.8 11.4 %collective-permute-start.11 = (f32[1032,128]{1,0:T(8,128)S(1)}, f32[1032,128]{1,0:T(8,128)S(1)}, u32[]{:S(2)}, u32[]{:S(2)}) collective-permute-start(f32[1032,128]{1,0:T(8,128)S(1)} %shard_map.105.states_ref.refs_7_), channel_id=1, source_target_pairs={{0,1},{1,0},{2,3},{3,2},{8,9},{9,8},{10,11},{11,10},{16,17},{17,16... | collective-permute-start | bytes 1585160 | tf_op jit(solution)/shard_map/ppermute | solution.py:493
  56.5 12.0 %collective-permute-start.14 = (f32[1032,128]{1,0:T(8,128)S(1)}, f32[1032,128]{1,0:T(8,128)S(1)}, u32[]{:S(2)}, u32[]{:S(2)}) collective-permute-start(f32[1032,128]{1,0:T(8,128)S(1)} %collective-permute-done.8.states_ref.refs_9_), channel_id=1, source_target_pairs={{0,1},{1,0},{2,3},{3,2},{8,9},{9,8},{10,11},{11,10},{16,17},{17,16... | collective-permute-start | bytes 1585160 | tf_op jit(solution)/shard_map/ppermute | solution.py:493
  61.4 8.8 %collective-permute-start.10 = (f32[1032,128]{1,0:T(8,128)S(1)}, f32[1032,128]{1,0:T(8,128)S(1)}, u32[]{:S(2)}, u32[]{:S(2)}) collective-permute-start(f32[1032,128]{1,0:T(8,128)S(1)} %shard_map.105.states_ref.refs_7_), channel_id=1, source_target_pairs={{0,4},{1,5},{2,6},{3,7},{8,12},{9,13},{10,14},{11,15},{16,20},{17,... | collective-permute-start | bytes 1585160 | tf_op jit(solution)/shard_map/ppermute | solution.py:493
  62.7 16.4 %collective-permute-start.9 = (f32[1032,128]{1,0:T(8,128)S(1)}, f32[1032,128]{1,0:T(8,128)S(1)}, u32[]{:S(2)}, u32[]{:S(2)}) collective-permute-start(f32[1032,128]{1,0:T(8,128)S(1)} %collective-permute-done.8.states_ref.refs_9_), channel_id=1, source_target_pairs={{8,4},{9,5},{10,6},{11,7},{16,12},{17,13},{18,14},{19,15},{24,20},... | collective-permute-start | bytes 1585160 | tf_op jit(solution)/shard_map/ppermute | solution.py:493
  65.9 18.1 %collective-permute-start.13 = (f32[1032,128]{1,0:T(8,128)S(1)}, f32[1032,128]{1,0:T(8,128)S(1)}, u32[]{:S(2)}, u32[]{:S(2)}) collective-permute-start(f32[1032,128]{1,0:T(8,128)S(1)} %collective-permute-done.8.states_ref.refs_9_), channel_id=1, source_target_pairs={{0,4},{1,5},{2,6},{3,7},{8,12},{9,13},{10,14},{11,15},{16,20},{17,... | collective-permute-start | bytes 1585160 | tf_op jit(solution)/shard_map/ppermute | solution.py:493
  67.2 16.1 %collective-permute-start.12 = (f32[1032,128]{1,0:T(8,128)S(1)}, f32[1032,128]{1,0:T(8,128)S(1)}, u32[]{:S(2)}, u32[]{:S(2)}) collective-permute-start(f32[1032,128]{1,0:T(8,128)S(1)} %collective-permute-done.11.refs_8_), channel_id=1, source_target_pairs={{0,4},{1,5},{2,6},{3,7},{8,12},{9,13},{10,14},{11,15},{16,20},{17,... | collective-permute-start | bytes 1585160 | tf_op jit(solution)/shard_map/ppermute | solution.py:493
  68.6 15.5 %collective-permute-start.15 = (f32[1032,128]{1,0:T(8,128)S(1)}, f32[1032,128]{1,0:T(8,128)S(1)}, u32[]{:S(2)}, u32[]{:S(2)}) collective-permute-start(f32[1032,128]{1,0:T(8,128)S(1)} %collective-permute-done.14.refs_10_), channel_id=1, source_target_pairs={{0,4},{1,5},{2,6},{3,7},{8,12},{9,13},{10,14},{11,15},{16,20},{17,... | collective-permute-start | bytes 1585160 | tf_op jit(solution)/shard_map/ppermute | solution.py:493
  70.3 22.8 %collective-permute-start.16 = (f32[1032,128]{1,0:T(8,128)S(1)}, f32[1032,128]{1,0:T(8,128)S(1)}, u32[]{:S(2)}, u32[]{:S(2)}) collective-permute-start(f32[1032,128]{1,0:T(8,128)S(1)} %collective-permute-done.11.refs_8_), channel_id=1, source_target_pairs={{8,4},{9,5},{10,6},{11,7},{16,12},{17,13},{18,14},{19,15},{24,20},... | collective-permute-start | bytes 1585160 | tf_op jit(solution)/shard_map/ppermute | solution.py:493
  79.1 19.6 %collective-permute-start.17 = (f32[1032,128]{1,0:T(8,128)S(1)}, f32[1032,128]{1,0:T(8,128)S(1)}, u32[]{:S(2)}, u32[]{:S(2)}) collective-permute-start(f32[1032,128]{1,0:T(8,128)S(1)} %collective-permute-done.14.refs_10_), channel_id=1, source_target_pairs={{8,4},{9,5},{10,6},{11,7},{16,12},{17,13},{18,14},{19,15},{24,20},... | collective-permute-start | bytes 1585160 | tf_op jit(solution)/shard_map/ppermute | solution.py:493
  83.3 31.9 %collective-permute-start.19 = (f32[1024,128]{1,0:T(8,128)S(1)}, f32[1024,128]{1,0:T(8,128)S(1)}, u32[]{:S(2)}, u32[]{:S(2)}) collective-permute-start(f32[1024,128]{1,0:T(8,128)S(1)} %shard_map.112.refs_0_), channel_id=1, source_target_pairs={{0,1},{1,0},{2,3},{3,2},{8,9},{9,8},{10,11},{11,10},{16,17},{17,16... | collective-permute-start | bytes 1572872 | tf_op jit(solution)/shard_map/ppermute | solution.py:493
  101.3 19.2 %collective-permute-start.24 = (f32[1032,128]{1,0:T(8,128)S(1)}, f32[1032,128]{1,0:T(8,128)S(1)}, u32[]{:S(2)}, u32[]{:S(2)}) collective-permute-start(f32[1032,128]{1,0:T(8,128)S(1)} %get-tuple-element.42.states_ref), channel_id=1, source_target_pairs={{4,8},{5,9},{6,10},{7,11},{12,16},{13,17},{14,18},{15,19},{20,24},... | collective-permute-start | bytes 1585160 | tf_op jit(solution)/shard_map/ppermute | solution.py:493
  102.7 16.5 %collective-permute-start.20 = (f32[1024,128]{1,0:T(8,128)S(1)}, f32[1024,128]{1,0:T(8,128)S(1)}, u32[]{:S(2)}, u32[]{:S(2)}) collective-permute-start(f32[1024,128]{1,0:T(8,128)S(1)} %shard_map.113.refs_2_), channel_id=1, source_target_pairs={{0,1},{1,0},{2,3},{3,2},{8,9},{9,8},{10,11},{11,10},{16,17},{17,16... | collective-permute-start | bytes 1572872 | tf_op jit(solution)/shard_map/ppermute | solution.py:493
  103.4 9.4 %collective-permute-start.18 = (f32[768,128]{1,0:T(8,128)S(1)}, f32[768,128]{1,0:T(8,128)S(1)}, u32[]{:S(2)}, u32[]{:S(2)}) collective-permute-start(f32[768,128]{1,0:T(8,128)S(1)} %get-tuple-element.43), channel_id=1, source_target_pairs={{4,0},{5,1},{6,2},{7,3},{12,8},{13,9},{14,10},{15,11},{20,16},{21,... | collective-permute-start | bytes 1179656 | tf_op jit(solution)/shard_map/ppermute | solution.py:493
  111.4 18.1 %collective-permute-start.22 = (f32[2064,128]{1,0:T(8,128)S(1)}, f32[2064,128]{1,0:T(8,128)S(1)}, u32[]{:S(2)}, u32[]{:S(2)}) collective-permute-start(f32[2064,128]{1,0:T(8,128)S(1)} %get-tuple-element.46), channel_id=1, source_target_pairs={{4,0},{5,1},{6,2},{7,3},{12,8},{13,9},{14,10},{15,11},{20,16},{21,... | collective-permute-start | bytes 3170312 | tf_op jit(solution)/shard_map/ppermute | solution.py:493
  112.8 16.7 %collective-permute-start.21 = (f32[1032,128]{1,0:T(8,128)S(1)}, f32[1032,128]{1,0:T(8,128)S(1)}, u32[]{:S(2)}, u32[]{:S(2)}) collective-permute-start(f32[1032,128]{1,0:T(8,128)S(1)} %get-tuple-element.42.states_ref), channel_id=1, source_target_pairs={{4,0},{5,1},{6,2},{7,3},{12,8},{13,9},{14,10},{15,11},{20,16},{21,... | collective-permute-start | bytes 1585160 | tf_op jit(solution)/shard_map/ppermute | solution.py:493
  115.3 15.7 %collective-permute-start.25 = (f32[2064,128]{1,0:T(8,128)S(1)}, f32[2064,128]{1,0:T(8,128)S(1)}, u32[]{:S(2)}, u32[]{:S(2)}) collective-permute-start(f32[2064,128]{1,0:T(8,128)S(1)} %get-tuple-element.46), channel_id=1, source_target_pairs={{4,8},{5,9},{6,10},{7,11},{12,16},{13,17},{14,18},{15,19},{20,24},... | collective-permute-start | bytes 3170312 | tf_op jit(solution)/shard_map/ppermute | solution.py:493
  119.2 10.3 %collective-permute-start.23 = (f32[1032,128]{1,0:T(8,128)S(1)}, f32[1032,128]{1,0:T(8,128)S(1)}, u32[]{:S(2)}, u32[]{:S(2)}) collective-permute-start(f32[1032,128]{1,0:T(8,128)S(1)} %get-tuple-element.47), channel_id=1, source_target_pairs={{4,0},{5,1},{6,2},{7,3},{12,8},{13,9},{14,10},{15,11},{20,16},{21,... | collective-permute-start | bytes 1585160 | tf_op jit(solution)/shard_map/ppermute | solution.py:493
  120.6 9.0 %collective-permute-start.26 = (f32[1032,128]{1,0:T(8,128)S(1)}, f32[1032,128]{1,0:T(8,128)S(1)}, u32[]{:S(2)}, u32[]{:S(2)}) collective-permute-start(f32[1032,128]{1,0:T(8,128)S(1)} %collective-permute-done.24.refs_1_), channel_id=1, source_target_pairs={{0,1},{1,0},{2,3},{3,2},{8,9},{9,8},{10,11},{11,10},{16,17},{17,16... | collective-permute-start | bytes 1585160 | tf_op jit(solution)/shard_map/ppermute | solution.py:493
  131.1 21.3 %collective-permute-start.29 = (f32[1024,128]{1,0:T(8,128)S(1)}, f32[1024,128]{1,0:T(8,128)S(1)}, u32[]{:S(2)}, u32[]{:S(2)}) collective-permute-start(f32[1024,128]{1,0:T(8,128)S(1)} %shard_map.118), channel_id=1, source_target_pairs={{0,4},{1,5},{2,6},{3,7},{8,12},{9,13},{10,14},{11,15},{16,20},{17,... | collective-permute-start | bytes 1572872 | tf_op jit(solution)/shard_map/ppermute | solution.py:493
  133.0 16.5 %collective-permute-start.27 = (f32[512,128]{1,0:T(8,128)S(1)}, f32[512,128]{1,0:T(8,128)S(1)}, u32[]{:S(2)}, u32[]{:S(2)}) collective-permute-start(f32[512,128]{1,0:T(8,128)S(1)} %get-tuple-element.53), channel_id=1, source_target_pairs={{8,4},{9,5},{10,6},{11,7},{16,12},{17,13},{18,14},{19,15},{24,20},... | collective-permute-start | bytes 786440 | tf_op jit(solution)/shard_map/ppermute | solution.py:493
  134.3 18.0 %collective-permute-start.28 = (f32[512,128]{1,0:T(8,128)S(1)}, f32[512,128]{1,0:T(8,128)S(1)}, u32[]{:S(2)}, u32[]{:S(2)}) collective-permute-start(f32[512,128]{1,0:T(8,128)S(1)} %get-tuple-element.54), channel_id=1, source_target_pairs={{8,4},{9,5},{10,6},{11,7},{16,12},{17,13},{18,14},{19,15},{24,20},... | collective-permute-start | bytes 786440 | tf_op jit(solution)/shard_map/ppermute | solution.py:493

commit v6 on v5

--- a/solution.py
+++ b/solution.py
@@ -360,26 +360,28 @@
     sums = refs[-3 - pick_parts - sum_parts : -3 - pick_parts]
     frees = refs[: -3 - pick_parts - sum_parts]
     n = frees[0].shape[1]
-    final = len(frees) > 1
 
     @pl.when(odd_depth() == receiver)
     def _():
         pull([narrow(own_ref)], tab, sem_ref)
         terms = []
-        for s in range(slots):
+        for s in range(slots if picks else 0):
             pick, at = part_of(picks, s)
             wa, wc = tab[0, WEIGHT_A, s], tab[0, WEIGHT_C, s]
             terms.append(parent_pair(pick, at, operator_of(tab, s, slots, modes), wa, wc, right_ref, left_ref))
         for s in range(slots):
             scale = tab[0, LIVE, s] * couple_step
-            part, at = part_of(sums, s)
             for i in range(2):
                 here = rows((2 * s + i) * n, n)
-                out_ref[here] = frees[0][here] + scale * (part[rows((at + i) * n, n)] + terms[s][i])
-        if not final:
+                added = terms[s][i] if picks else 0.0
+                if sums:
+                    part, at = part_of(sums, s)
+                    added = part[rows((at + i) * n, n)] + added
+                out_ref[here] = frees[0][here] + scale * added
+        if out_ref.shape[0] > 2 * slots * n:
             out_ref[pl.ds(2 * slots * n, ROWS)] = own_ref[...]
 
-    if final:
+    if len(frees) > 1:
 
         @pl.when(odd_depth() != receiver)
         def _():
@@ -588,10 +590,10 @@
         )
         return outs[:parts], outs[-1]
 
-    def join(frees, sums, picks, receiver, operators):
+    def join(frees, sums, picks, receiver, operators, noted=0):
         return call(
             functools.partial(join_kernel, receiver, slots, modes, len(sums), len(picks)),
-            mats(plain) if len(frees) > 1 else mats(plain, 1),
+            mats(plain, noted),
             limit,
             (own_table, *operators, *frees, *sums, *picks),
             scratch=tables(1),
@@ -622,13 +624,12 @@
     operators_even = call(
         functools.partial(operators_kernel, slots, group, modes, 0), operator_shapes, limit, (couplings, passed)
     )
-    own_state = join([free_even], sums, picks, 0, operators_odd)
+    own_state = join([free_even], sums, picks, 0, operators_odd, 1)
 
     gathered = gather(own_state, 0)
     from_below = [shift(value, -1, 0) for value in gathered]
     from_above = [shift(value, 1, 0) for value in gathered]
-    free_even = [free_chain(gathered[0], 0, 2)] + [free(gathered[k], 0, 2) for k in range(2, group, 2)]
-    free_even = [value for own in free_even for value in (own, neighbour(own, 0))]
+    free_even = gather(free_chain(gathered[0], 0, 2), 0)
     evens, odds = (0, 2, group // 2), (1, 2, group // 2)
     states, _ = side("children", free_odd, from_below[::2], [tabs_odd], 1, operators_odd, span=evens)
     states, _ = side("parents", [states], from_above, [tabs_odd], 1, operators_odd)
@@ -645,7 +646,8 @@
     sums = [shift(value, -1, 0) for value in sums]
     picks = [shift(value, 1, 0) for value in pick(states, 0, 1)]
     last_even = free(states[0], 0, 1)
-    return join([last_odd, last_even], sums, picks, 1, operators_odd).reshape(blocks.shape)
+    last_odd = join([last_odd], [], picks, 1, operators_odd)
+    return join([last_odd, last_even], sums, [], 1, operators_odd).reshape(blocks.shape)
 
 
 def solution(mesh):

time: 155 us -> 151 us (0.974)
  starting transfers between devices: 52.8 us -> 49.5 us
    ppermute x30 -> x31, starting transfers between devices: 52.8 us -> 49.5 us  [permute(): return lax.ppermute(value, AXES, pairs)]
    ppermute x30 -> x31, waiting for transfers between devices: 39.8 us -> 38.3 us  [permute(): return lax.ppermute(value, AXES, pairs)]
  transfers between devices with their start and end apart: 30 -> 31, of which waited for: 11 -> 12; matrix products, arithmetic and copies ran while one was open for 0% -> 0% of each run, Pallas kernels for 37% -> 39%
where the time goes in v6:
time: 151 us; the launch traced here: 150 us
  Pallas kernels  61.7 us (41%)
  starting transfers between devices  49.5 us (33%)
  waiting for transfers between devices  38.3 us (25%)
    pallas_call x29, Pallas kernels, call(): pl.pallas_call(kernel, out_shape=out_shapes, in_specs=specs, out_specs=ja...  61.7 us
    ppermute x31, starting transfers between devices, permute(): return lax.ppermute(value, AXES, pairs)  49.5 us
    ppermute x31, waiting for transfers between devices, permute(): return lax.ppermute(value, AXES, pairs)  38.3 us
  transfers between devices with their start and end apart: 31, of which 12 were waited for; matrix products, arithmetic and copies ran while one was open for 0% of the time, Pallas kernels for 39%

profile of v6, /device:TPU:3, one launch (start us, length us, event | category | flops | bytes accessed | tf_op | source)
XLA Modules:
  0.0 150.3 jit_solution(17623613161402448794)
XLA Ops:
  0.0 2.0 %shard_map.91 = (f32[1288,128]{1,0:T(8,128)}, f32[8,128]{1,0:T(8,128)}) custom-call(s32[4]{0:T(128)} %live_ref.1, s32[4]{0:T(128)} %parent_ref.1, s32[4]{0:T(128)} %mode_ref.1, f32[4]{0:T(128)} %damping_ref.1, f32[4]{0:T(128)} %weight_ref.1, f32[2,2]{1,0:T(2,128)} %corr_ref.1, f32[1024,128]{1,0:T(8,128)} %bitcast.6, f32[256,128]{1,0:T(8,128)} %bitcast.3), custom_call_target="tpu_custom_call" | custom-call | flops 1100000000 | bytes 524288 | tf_op jit(solution)/shard_map/pallas_call | solution.py:466
  2.0 4.2 %collective-permute-start.1 = (f32[1288,128]{1,0:T(8,128)}, f32[1288,128]{1,0:T(8,128)S(1)}, u32[]{:S(2)}, u32[]{:S(2)}) collective-permute-start(f32[1288,128]{1,0:T(8,128)} %get-tuple-element.31.refs_0_.states_ref), channel_id=1, source_target_pairs={{4,6},{5,7},{6,4},{7,5},{12,14},{13,15},{14,12},{15,13},{20,22},{2... | collective-permute-start | bytes 1978376 | tf_op jit(solution)/shard_map/ppermute | solution.py:495
  6.2 3.2 %collective-permute-start = (f32[1288,128]{1,0:T(8,128)}, f32[1288,128]{1,0:T(8,128)S(1)}, u32[]{:S(2)}, u32[]{:S(2)}) collective-permute-start(f32[1288,128]{1,0:T(8,128)} %get-tuple-element.31.refs_0_.states_ref), channel_id=1, source_target_pairs={{4,5},{5,4},{6,7},{7,6},{12,13},{13,12},{14,15},{15,14},{20,21},{2... | collective-permute-start | bytes 1978376 | tf_op jit(solution)/shard_map/ppermute | solution.py:495
  9.4 2.1 %collective-permute-start.4 = (f32[8,128]{1,0:T(8,128)}, f32[8,128]{1,0:T(8,128)S(1)}, u32[]{:S(2)}, u32[]{:S(2)}) collective-permute-start(f32[8,128]{1,0:T(8,128)} %get-tuple-element.30.own_ref), channel_id=1, source_target_pairs={{4,0},{5,1},{6,2},{7,3},{8,4},{9,5},{10,6},{11,7},{12,8},{13,9},{1... | collective-permute-start | bytes 12296 | tf_op jit(solution)/shard_map/ppermute | solution.py:495
  11.5 0.7 shard_map.93
  12.3 4.2 %shard_map.94.refs_0_ = f32[512,128]{1,0:T(8,128)S(1)} custom-call(f32[1288,128]{1,0:T(8,128)S(1)} %copy-done, bf16[384,512]{1,0:T(8,128)(2,1)S(1)} %get-tuple-element.34.right_ref, bf16[128,1536]{1,0:T(8,128)(2,1)S(1)} %get-tuple-element.35.left_ref), custom_call_target="tpu_custom_call" | custom-call | flops 4950000128 | bytes 524288 | tf_op jit(solution)/shard_map/pallas_call | solution.py:466
  16.5 4.2 %shard_map.95.refs_1_ = f32[512,128]{1,0:T(8,128)S(1)} custom-call(f32[1288,128]{1,0:T(8,128)S(1)} %copy-done, bf16[384,512]{1,0:T(8,128)(2,1)S(1)} %get-tuple-element.34.right_ref, bf16[128,1536]{1,0:T(8,128)(2,1)S(1)} %get-tuple-element.35.left_ref), custom_call_target="tpu_custom_call" | custom-call | flops 4950000128 | bytes 524288 | tf_op jit(solution)/shard_map/pallas_call | solution.py:466
  20.7 0.9 collective-permute-done.1.refs_2_.states_ref
  21.6 2.6 %collective-permute-start.2 = (f32[1288,128]{1,0:T(8,128)S(1)}, f32[1288,128]{1,0:T(8,128)S(1)}, u32[]{:S(2)}, u32[]{:S(2)}) collective-permute-start(f32[1288,128]{1,0:T(8,128)S(1)} %collective-permute-done.1.refs_2_.states_ref), channel_id=1, source_target_pairs={{4,5},{5,4},{6,7},{7,6},{12,13},{13,12},{14,15},{15,14},{20,21},{2... | collective-permute-start | bytes 1978376 | tf_op jit(solution)/shard_map/ppermute | solution.py:495
  24.3 4.2 %shard_map.98.refs_4_ = f32[512,128]{1,0:T(8,128)S(1)} custom-call(f32[1288,128]{1,0:T(8,128)S(1)} %collective-permute-done.1.refs_2_.states_ref, bf16[384,512]{1,0:T(8,128)(2,1)S(1)} %get-tuple-element.34.right_ref, bf16[128,1536]{1,0:T(8,128)(2,1)S(1)} %get-tuple-element.35.left_ref), custom_call_target="tpu_custom_call" | custom-call | flops 4950000128 | bytes 524288 | tf_op jit(solution)/shard_map/pallas_call | solution.py:466
  28.5 4.2 %shard_map.99.refs_5_ = f32[512,128]{1,0:T(8,128)S(1)} custom-call(f32[1288,128]{1,0:T(8,128)S(1)} %collective-permute-done.1.refs_2_.states_ref, bf16[384,512]{1,0:T(8,128)(2,1)S(1)} %get-tuple-element.34.right_ref, bf16[128,1536]{1,0:T(8,128)(2,1)S(1)} %get-tuple-element.35.left_ref), custom_call_target="tpu_custom_call" | custom-call | flops 4950000128 | bytes 524288 | tf_op jit(solution)/shard_map/pallas_call | solution.py:466
  32.7 0.3 collective-permute-done.2.refs_3_.states_ref
  33.0 0.2 shard_map.92
  33.2 2.6 %shard_map.103 = (f32[1024,128]{1,0:T(8,128)S(1)}, f32[4,8,128]{2,1,0:T(8,128)S(1)}) custom-call(bf16[8,384,128]{2,1,0:T(8,128)(2,1)S(1)} %get-tuple-element.32.right_ref, bf16[8,128,384]{2,1,0:T(8,128)(2,1)S(1)} %get-tuple-element.33.left_ref, f32[1288,128]{1,0:T(8,128)S(1)} %copy-done, f32[1288,128]{1,0:T(8,128)S(1)} %collective-permute-done.refs_1_.states_ref, ...), custom_call_target="tpu_custom_call" | custom-call | flops 2200000000 | bytes 524288 | tf_op jit(solution)/shard_map/pallas_call | solution.py:466
  35.9 1.3 collective-permute-start.3
  37.2 0.8 shard_map.104
  38.0 1.3 collective-permute-start.5
  39.3 1.3 collective-permute-start.6
  40.6 4.2 %shard_map.96.refs_2_ = f32[512,128]{1,0:T(8,128)S(1)} custom-call(f32[1288,128]{1,0:T(8,128)S(1)} %collective-permute-done.refs_1_.states_ref, bf16[384,512]{1,0:T(8,128)(2,1)S(1)} %get-tuple-element.34.right_ref, bf16[128,1536]{1,0:T(8,128)(2,1)S(1)} %get-tuple-element.35.left_ref), custom_call_target="tpu_custom_call" | custom-call | flops 4950000128 | bytes 524288 | tf_op jit(solution)/shard_map/pallas_call | solution.py:466
  44.8 0.6 collective-permute-done.6.refs_3_
  45.4 0.7 collective-permute-start.8
  46.1 4.2 %shard_map.97.refs_3_ = f32[512,128]{1,0:T(8,128)S(1)} custom-call(f32[1288,128]{1,0:T(8,128)S(1)} %collective-permute-done.refs_1_.states_ref, bf16[384,512]{1,0:T(8,128)(2,1)S(1)} %get-tuple-element.34.right_ref, bf16[128,1536]{1,0:T(8,128)(2,1)S(1)} %get-tuple-element.35.left_ref), custom_call_target="tpu_custom_call" | custom-call | flops 4950000128 | bytes 524288 | tf_op jit(solution)/shard_map/pallas_call | solution.py:466
  50.3 4.2 %shard_map.100.refs_6_ = f32[512,128]{1,0:T(8,128)S(1)} custom-call(f32[1288,128]{1,0:T(8,128)S(1)} %collective-permute-done.2.refs_3_.states_ref, bf16[384,512]{1,0:T(8,128)(2,1)S(1)} %get-tuple-element.34.right_ref, bf16[128,1536]{1,0:T(8,128)(2,1)S(1)} %get-tuple-element.35.left_ref), custom_call_target="tpu_custom_call" | custom-call | flops 4950000128 | bytes 524288 | tf_op jit(solution)/shard_map/pallas_call | solution.py:466
  54.5 1.3 collective-permute-start.7
  55.8 0.7 collective-permute-start.11
  56.5 0.7 collective-permute-start.14
  57.2 4.2 %shard_map.101.refs_7_ = f32[512,128]{1,0:T(8,128)S(1)} custom-call(f32[1288,128]{1,0:T(8,128)S(1)} %collective-permute-done.2.refs_3_.states_ref, bf16[384,512]{1,0:T(8,128)(2,1)S(1)} %get-tuple-element.34.right_ref, bf16[128,1536]{1,0:T(8,128)(2,1)S(1)} %get-tuple-element.35.left_ref), custom_call_target="tpu_custom_call" | custom-call | flops 4950000128 | bytes 524288 | tf_op jit(solution)/shard_map/pallas_call | solution.py:466
  61.4 1.3 collective-permute-start.10
  62.7 1.3 collective-permute-start.9
  64.0 0.2 shard_map.111.refs_0_
  64.2 1.7 %collective-permute-done.7.refs_8_ = f32[1032,128]{1,0:T(8,128)S(1)} collective-permute-done((f32[1032,128]{1,0:T(8,128)S(1)}, f32[1032,128]{1,0:T(8,128)S(1)}, u32[]{:S(2)}, u32[]{:S(2)}) %collective-permute-start.7) | collective-permute-done | bytes 528416 | tf_op jit(solution)/shard_map/ppermute | solution.py:495
  66.0 1.3 collective-permute-start.13
  67.3 1.3 collective-permute-start.12
  68.6 1.3 collective-permute-start.15
  69.9 0.4 collective-permute-done.10.refs_1_
  70.3 1.3 collective-permute-start.16
  71.6 7.5 %collective-permute-done.9.refs_9_ = f32[1032,128]{1,0:T(8,128)S(1)} collective-permute-done((f32[1032,128]{1,0:T(8,128)S(1)}, f32[1032,128]{1,0:T(8,128)S(1)}, u32[]{:S(2)}, u32[]{:S(2)}) %collective-permute-start.9) | collective-permute-done | bytes 528416 | tf_op jit(solution)/shard_map/ppermute | solution.py:495
  79.1 1.3 collective-permute-start.17
  80.4 2.9 %shard_map.106 = (f32[4096,128]{1,0:T(8,128)S(1)}, f32[4,8,128]{2,1,0:T(8,128)}) custom-call(bf16[8,384,128]{2,1,0:T(8,128)(2,1)S(1)} %get-tuple-element.32.right_ref, bf16[8,128,384]{2,1,0:T(8,128)(2,1)S(1)} %get-tuple-element.33.left_ref, f32[512,128]{1,0:T(8,128)S(1)} %shard_map.94.refs_0_, f32[512,128]{1,0:T(8,128)S(1)} %shard_map.95.refs_1_, ...), custom_call_target="tpu_custom_call" | custom-call | flops 3300000000 | bytes 524288 | tf_op jit(solution)/shard_map/pallas_call | solution.py:466
  83.3 0.7 collective-permute-start.20
  84.1 4.4 %shard_map.107 = (f32[4096,128]{1,0:T(8,128)S(1)}, f32[4,8,128]{2,1,0:T(8,128)}) custom-call(bf16[8,384,128]{2,1,0:T(8,128)(2,1)S(1)} %get-tuple-element.32.right_ref, bf16[8,128,384]{2,1,0:T(8,128)(2,1)S(1)} %get-tuple-element.33.left_ref, f32[4096,128]{1,0:T(8,128)S(1)} %get-tuple-element.40.refs_0_, f32[1032,128]{1,0:T(8,128)S(1)} %collective-permute-done.10.refs_1_, ...), custom_call_target="tpu_custom_call" | custom-call | flops 3300000000 | bytes 524288 | tf_op jit(solution)/shard_map/pallas_call | solution.py:466
  88.5 4.9 %collective-permute-done.16.refs_1_ = f32[1032,128]{1,0:T(8,128)S(1)} collective-permute-done((f32[1032,128]{1,0:T(8,128)S(1)}, f32[1032,128]{1,0:T(8,128)S(1)}, u32[]{:S(2)}, u32[]{:S(2)}) %collective-permute-start.16) | collective-permute-done | bytes 528416 | tf_op jit(solution)/shard_map/ppermute | solution.py:495
  93.4 5.7 %collective-permute-done.17.refs_2_ = f32[1032,128]{1,0:T(8,128)S(1)} collective-permute-done((f32[1032,128]{1,0:T(8,128)S(1)}, f32[1032,128]{1,0:T(8,128)S(1)}, u32[]{:S(2)}, u32[]{:S(2)}) %collective-permute-start.17) | collective-permute-done | bytes 528416 | tf_op jit(solution)/shard_map/ppermute | solution.py:495
  99.0 2.6 %shard_map.108 = (f32[1032,128]{1,0:T(8,128)S(1)}, f32[2064,128]{1,0:T(8,128)S(1)}, f32[1032,128]{1,0:T(8,128)S(1)}) custom-call(bf16[8,384,128]{2,1,0:T(8,128)(2,1)S(1)} %get-tuple-element.32.right_ref, bf16[8,128,384]{2,1,0:T(8,128)(2,1)S(1)} %get-tuple-element.33.left_ref, f32[4096,128]{1,0:T(8,128)S(1)} %get-tuple-element.41.refs_0_, ...), custom_call_target="tpu_custom_call" | custom-call | flops 3300000000 | bytes 524288 | tf_op jit(solution)/shard_map/pallas_call | solution.py:466
  101.6 1.3 collective-permute-start.25
  102.9 0.7 collective-permute-start.19
  103.7 0.7 collective-permute-start.21
  104.4 4.0 %collective-permute-start.18 = (f32[768,128]{1,0:T(8,128)S(1)}, f32[768,128]{1,0:T(8,128)S(1)}, u32[]{:S(2)}, u32[]{:S(2)}) collective-permute-start(f32[768,128]{1,0:T(8,128)S(1)} %get-tuple-element.43), channel_id=1, source_target_pairs={{4,0},{5,1},{6,2},{7,3},{12,8},{13,9},{14,10},{15,11},{20,16},{21,... | collective-permute-start | bytes 1179656 | tf_op jit(solution)/shard_map/ppermute | solution.py:495
  108.3 1.4 collective-permute-start.23
  109.7 2.4 %collective-permute-start.22 = (f32[1032,128]{1,0:T(8,128)S(1)}, f32[1032,128]{1,0:T(8,128)S(1)}, u32[]{:S(2)}, u32[]{:S(2)}) collective-permute-start(f32[1032,128]{1,0:T(8,128)S(1)} %get-tuple-element.42.states_ref), channel_id=1, source_target_pairs={{4,0},{5,1},{6,2},{7,3},{12,8},{13,9},{14,10},{15,11},{20,16},{21,... | collective-permute-start | bytes 1585160 | tf_op jit(solution)/shard_map/ppermute | solution.py:495
  112.2 3.3 %collective-permute-start.26 = (f32[2064,128]{1,0:T(8,128)S(1)}, f32[2064,128]{1,0:T(8,128)S(1)}, u32[]{:S(2)}, u32[]{:S(2)}) collective-permute-start(f32[2064,128]{1,0:T(8,128)S(1)} %get-tuple-element.46), channel_id=1, source_target_pairs={{4,8},{5,9},{6,10},{7,11},{12,16},{13,17},{14,18},{15,19},{20,24},... | collective-permute-start | bytes 3170312 | tf_op jit(solution)/shard_map/ppermute | solution.py:495
  115.5 2.0 %collective-permute-start.24 = (f32[1032,128]{1,0:T(8,128)S(1)}, f32[1032,128]{1,0:T(8,128)S(1)}, u32[]{:S(2)}, u32[]{:S(2)}) collective-permute-start(f32[1032,128]{1,0:T(8,128)S(1)} %get-tuple-element.47), channel_id=1, source_target_pairs={{4,0},{5,1},{6,2},{7,3},{12,8},{13,9},{14,10},{15,11},{20,16},{21,... | collective-permute-start | bytes 1585160 | tf_op jit(solution)/shard_map/ppermute | solution.py:495
  117.6 0.7 collective-permute-start.27
  118.3 8.2 %shard_map.109.refs_0_ = f32[1024,128]{1,0:T(8,128)S(1)} custom-call(f32[1032,128]{1,0:T(8,128)S(1)} %get-tuple-element.42.states_ref, bf16[384,512]{1,0:T(8,128)(2,1)S(1)} %get-tuple-element.34.right_ref, bf16[128,1536]{1,0:T(8,128)(2,1)S(1)} %get-tuple-element.35.left_ref), custom_call_target="tpu_custom_call" | custom-call | flops 9900000256 | bytes 524288 | tf_op jit(solution)/shard_map/pallas_call | solution.py:466
  126.6 0.7 collective-permute-done.26.refs_2_
  127.4 1.3 collective-permute-start.28
  128.7 0.7 shard_map.118
  129.3 1.3 collective-permute-start.29
  130.6 1.3 collective-permute-start.30
  132.0 4.1 %collective-permute-done.28.refs_1_ = f32[1024,128]{1,0:T(8,128)S(1)} collective-permute-done((f32[1024,128]{1,0:T(8,128)S(1)}, f32[1024,128]{1,0:T(8,128)S(1)}, u32[]{:S(2)}, u32[]{:S(2)}) %collective-permute-start.28) | collective-permute-done | bytes 524320 | tf_op jit(solution)/shard_map/ppermute | solution.py:495
  136.0 1.1 shard_map.116.refs_0_
  137.2 8.7 %collective-permute-done.29.refs_2_ = f32[512,128]{1,0:T(8,128)S(1)} collective-permute-done((f32[512,128]{1,0:T(8,128)S(1)}, f32[512,128]{1,0:T(8,128)S(1)}, u32[]{:S(2)}, u32[]{:S(2)}) %collective-permute-start.29) | collective-permute-done | bytes 262176 | tf_op jit(solution)/shard_map/ppermute | solution.py:495
  145.9 2.8 %collective-permute-done.30.refs_3_ = f32[512,128]{1,0:T(8,128)S(1)} collective-permute-done((f32[512,128]{1,0:T(8,128)S(1)}, f32[512,128]{1,0:T(8,128)S(1)}, u32[]{:S(2)}, u32[]{:S(2)}) %collective-permute-start.30) | collective-permute-done | bytes 262176 | tf_op jit(solution)/shard_map/ppermute | solution.py:495
  148.7 1.5 shard_map.119
  (35 shorter events, 0.3 us)
Async XLA Ops:
  0.0 11.5 %copy-start.2 = (f32[128,128]{1,0:T(8,128)S(1)}, f32[128,128]{1,0:T(8,128)}, u32[]{:S(2)}) copy-start(f32[128,128]{1,0:T(8,128)} %ham_ref.1) | copy-start | bytes 196612
  2.0 19.6 %collective-permute-start.1 = (f32[1288,128]{1,0:T(8,128)}, f32[1288,128]{1,0:T(8,128)S(1)}, u32[]{:S(2)}, u32[]{:S(2)}) collective-permute-start(f32[1288,128]{1,0:T(8,128)} %get-tuple-element.31.refs_0_.states_ref), channel_id=1, source_target_pairs={{4,6},{5,7},{6,4},{7,5},{12,14},{13,15},{14,12},{15,13},{20,22},{2... | collective-permute-start | bytes 1978376 | tf_op jit(solution)/shard_map/ppermute | solution.py:495
  6.2 26.5 %collective-permute-start = (f32[1288,128]{1,0:T(8,128)}, f32[1288,128]{1,0:T(8,128)S(1)}, u32[]{:S(2)}, u32[]{:S(2)}) collective-permute-start(f32[1288,128]{1,0:T(8,128)} %get-tuple-element.31.refs_0_.states_ref), channel_id=1, source_target_pairs={{4,5},{5,4},{6,7},{7,6},{12,13},{13,12},{14,15},{15,14},{20,21},{2... | collective-permute-start | bytes 1978376 | tf_op jit(solution)/shard_map/ppermute | solution.py:495
  9.4 2.8 %copy-start = (f32[1288,128]{1,0:T(8,128)S(1)}, f32[1288,128]{1,0:T(8,128)}, u32[]{:S(2)}) copy-start(f32[1288,128]{1,0:T(8,128)} %get-tuple-element.31.refs_0_.states_ref) | copy-start | bytes 1978372
  9.4 27.8 %collective-permute-start.4 = (f32[8,128]{1,0:T(8,128)}, f32[8,128]{1,0:T(8,128)S(1)}, u32[]{:S(2)}, u32[]{:S(2)}) collective-permute-start(f32[8,128]{1,0:T(8,128)} %get-tuple-element.30.own_ref), channel_id=1, source_target_pairs={{4,0},{5,1},{6,2},{7,3},{8,4},{9,5},{10,6},{11,7},{12,8},{13,9},{1... | collective-permute-start | bytes 12296 | tf_op jit(solution)/shard_map/ppermute | solution.py:495
  21.6 11.4 %collective-permute-start.2 = (f32[1288,128]{1,0:T(8,128)S(1)}, f32[1288,128]{1,0:T(8,128)S(1)}, u32[]{:S(2)}, u32[]{:S(2)}) collective-permute-start(f32[1288,128]{1,0:T(8,128)S(1)} %collective-permute-done.1.refs_2_.states_ref), channel_id=1, source_target_pairs={{4,5},{5,4},{6,7},{7,6},{12,13},{13,12},{14,15},{15,14},{20,21},{2... | collective-permute-start | bytes 1978376 | tf_op jit(solution)/shard_map/ppermute | solution.py:495
  28.5 4.5 %copy-start.1 = (f32[2,128,128]{2,1,0:T(8,128)S(1)}, f32[2,128,128]{2,1,0:T(8,128)}, u32[]{:S(2)}) copy-start(f32[2,128,128]{2,1,0:T(8,128)} %param.14) | copy-start | bytes 393220
  35.9 9.5 %collective-permute-start.3 = (f32[1024,128]{1,0:T(8,128)S(1)}, f32[1024,128]{1,0:T(8,128)S(1)}, u32[]{:S(2)}, u32[]{:S(2)}) collective-permute-start(f32[1024,128]{1,0:T(8,128)S(1)} %get-tuple-element.36), channel_id=1, source_target_pairs={{4,0},{5,1},{6,2},{7,3},{12,8},{13,9},{14,10},{15,11},{20,16},{21,... | collective-permute-start | bytes 1572872 | tf_op jit(solution)/shard_map/ppermute | solution.py:495
  38.0 6.8 %collective-permute-start.5 = (f32[512,128]{1,0:T(8,128)S(1)}, f32[512,128]{1,0:T(8,128)S(1)}, u32[]{:S(2)}, u32[]{:S(2)}) collective-permute-start(f32[512,128]{1,0:T(8,128)S(1)} %get-tuple-element.37), channel_id=1, source_target_pairs={{4,8},{5,9},{6,10},{7,11},{12,16},{13,17},{14,18},{15,19},{20,24},... | collective-permute-start | bytes 786440 | tf_op jit(solution)/shard_map/ppermute | solution.py:495
  39.3 6.1 %copy-start.3 = (f32[8,128]{1,0:T(8,128)S(1)}, f32[8,128]{1,0:T(8,128)}, u32[]{:S(2)}) copy-start(f32[8,128]{1,0:T(8,128)} %get-tuple-element.30.own_ref) | copy-start | bytes 12292
  39.3 6.1 %collective-permute-start.6 = (f32[512,128]{1,0:T(8,128)S(1)}, f32[512,128]{1,0:T(8,128)S(1)}, u32[]{:S(2)}, u32[]{:S(2)}) collective-permute-start(f32[512,128]{1,0:T(8,128)S(1)} %get-tuple-element.38), channel_id=1, source_target_pairs={{4,8},{5,9},{6,10},{7,11},{12,16},{13,17},{14,18},{15,19},{20,24},... | collective-permute-start | bytes 786440 | tf_op jit(solution)/shard_map/ppermute | solution.py:495
  45.4 11.1 %collective-permute-start.8 = (f32[1032,128]{1,0:T(8,128)S(1)}, f32[1032,128]{1,0:T(8,128)S(1)}, u32[]{:S(2)}, u32[]{:S(2)}) collective-permute-start(f32[1032,128]{1,0:T(8,128)S(1)} %shard_map.105.states_ref.refs_7_), channel_id=1, source_target_pairs={{0,2},{1,3},{2,0},{3,1},{8,10},{9,11},{10,8},{11,9},{16,18},{17,19... | collective-permute-start | bytes 1585160 | tf_op jit(solution)/shard_map/ppermute | solution.py:495
  54.5 11.4 %collective-permute-start.7 = (f32[1032,128]{1,0:T(8,128)S(1)}, f32[1032,128]{1,0:T(8,128)S(1)}, u32[]{:S(2)}, u32[]{:S(2)}) collective-permute-start(f32[1032,128]{1,0:T(8,128)S(1)} %shard_map.105.states_ref.refs_7_), channel_id=1, source_target_pairs={{8,4},{9,5},{10,6},{11,7},{16,12},{17,13},{18,14},{19,15},{24,20},... | collective-permute-start | bytes 1585160 | tf_op jit(solution)/shard_map/ppermute | solution.py:495
  55.8 11.4 %collective-permute-start.11 = (f32[1032,128]{1,0:T(8,128)S(1)}, f32[1032,128]{1,0:T(8,128)S(1)}, u32[]{:S(2)}, u32[]{:S(2)}) collective-permute-start(f32[1032,128]{1,0:T(8,128)S(1)} %shard_map.105.states_ref.refs_7_), channel_id=1, source_target_pairs={{0,1},{1,0},{2,3},{3,2},{8,9},{9,8},{10,11},{11,10},{16,17},{17,16... | collective-permute-start | bytes 1585160 | tf_op jit(solution)/shard_map/ppermute | solution.py:495
  56.5 12.0 %collective-permute-start.14 = (f32[1032,128]{1,0:T(8,128)S(1)}, f32[1032,128]{1,0:T(8,128)S(1)}, u32[]{:S(2)}, u32[]{:S(2)}) collective-permute-start(f32[1032,128]{1,0:T(8,128)S(1)} %collective-permute-done.8.refs_9_), channel_id=1, source_target_pairs={{0,1},{1,0},{2,3},{3,2},{8,9},{9,8},{10,11},{11,10},{16,17},{17,16... | collective-permute-start | bytes 1585160 | tf_op jit(solution)/shard_map/ppermute | solution.py:495
  61.4 8.9 %collective-permute-start.10 = (f32[1032,128]{1,0:T(8,128)S(1)}, f32[1032,128]{1,0:T(8,128)S(1)}, u32[]{:S(2)}, u32[]{:S(2)}) collective-permute-start(f32[1032,128]{1,0:T(8,128)S(1)} %shard_map.105.states_ref.refs_7_), channel_id=1, source_target_pairs={{0,4},{1,5},{2,6},{3,7},{8,12},{9,13},{10,14},{11,15},{16,20},{17,... | collective-permute-start | bytes 1585160 | tf_op jit(solution)/shard_map/ppermute | solution.py:495
  62.7 16.4 %collective-permute-start.9 = (f32[1032,128]{1,0:T(8,128)S(1)}, f32[1032,128]{1,0:T(8,128)S(1)}, u32[]{:S(2)}, u32[]{:S(2)}) collective-permute-start(f32[1032,128]{1,0:T(8,128)S(1)} %collective-permute-done.8.refs_9_), channel_id=1, source_target_pairs={{8,4},{9,5},{10,6},{11,7},{16,12},{17,13},{18,14},{19,15},{24,20},... | collective-permute-start | bytes 1585160 | tf_op jit(solution)/shard_map/ppermute | solution.py:495
  66.0 18.1 %collective-permute-start.13 = (f32[1032,128]{1,0:T(8,128)S(1)}, f32[1032,128]{1,0:T(8,128)S(1)}, u32[]{:S(2)}, u32[]{:S(2)}) collective-permute-start(f32[1032,128]{1,0:T(8,128)S(1)} %collective-permute-done.8.refs_9_), channel_id=1, source_target_pairs={{0,4},{1,5},{2,6},{3,7},{8,12},{9,13},{10,14},{11,15},{16,20},{17,... | collective-permute-start | bytes 1585160 | tf_op jit(solution)/shard_map/ppermute | solution.py:495
  67.3 16.1 %collective-permute-start.12 = (f32[1032,128]{1,0:T(8,128)S(1)}, f32[1032,128]{1,0:T(8,128)S(1)}, u32[]{:S(2)}, u32[]{:S(2)}) collective-permute-start(f32[1032,128]{1,0:T(8,128)S(1)} %collective-permute-done.11.refs_8_), channel_id=1, source_target_pairs={{0,4},{1,5},{2,6},{3,7},{8,12},{9,13},{10,14},{11,15},{16,20},{17,... | collective-permute-start | bytes 1585160 | tf_op jit(solution)/shard_map/ppermute | solution.py:495
  68.6 15.5 %collective-permute-start.15 = (f32[1032,128]{1,0:T(8,128)S(1)}, f32[1032,128]{1,0:T(8,128)S(1)}, u32[]{:S(2)}, u32[]{:S(2)}) collective-permute-start(f32[1032,128]{1,0:T(8,128)S(1)} %collective-permute-done.14.refs_10_), channel_id=1, source_target_pairs={{0,4},{1,5},{2,6},{3,7},{8,12},{9,13},{10,14},{11,15},{16,20},{17,... | collective-permute-start | bytes 1585160 | tf_op jit(solution)/shard_map/ppermute | solution.py:495
  70.3 23.1 %collective-permute-start.16 = (f32[1032,128]{1,0:T(8,128)S(1)}, f32[1032,128]{1,0:T(8,128)S(1)}, u32[]{:S(2)}, u32[]{:S(2)}) collective-permute-start(f32[1032,128]{1,0:T(8,128)S(1)} %collective-permute-done.11.refs_8_), channel_id=1, source_target_pairs={{8,4},{9,5},{10,6},{11,7},{16,12},{17,13},{18,14},{19,15},{24,20},... | collective-permute-start | bytes 1585160 | tf_op jit(solution)/shard_map/ppermute | solution.py:495
  79.1 19.9 %collective-permute-start.17 = (f32[1032,128]{1,0:T(8,128)S(1)}, f32[1032,128]{1,0:T(8,128)S(1)}, u32[]{:S(2)}, u32[]{:S(2)}) collective-permute-start(f32[1032,128]{1,0:T(8,128)S(1)} %collective-permute-done.14.refs_10_), channel_id=1, source_target_pairs={{8,4},{9,5},{10,6},{11,7},{16,12},{17,13},{18,14},{19,15},{24,20},... | collective-permute-start | bytes 1585160 | tf_op jit(solution)/shard_map/ppermute | solution.py:495
  83.3 20.3 %collective-permute-start.20 = (f32[1024,128]{1,0:T(8,128)S(1)}, f32[1024,128]{1,0:T(8,128)S(1)}, u32[]{:S(2)}, u32[]{:S(2)}) collective-permute-start(f32[1024,128]{1,0:T(8,128)S(1)} %shard_map.112.refs_0_), channel_id=1, source_target_pairs={{0,2},{1,3},{2,0},{3,1},{8,10},{9,11},{10,8},{11,9},{16,18},{17,19... | collective-permute-start | bytes 1572872 | tf_op jit(solution)/shard_map/ppermute | solution.py:495
  101.6 16.0 %collective-permute-start.25 = (f32[1032,128]{1,0:T(8,128)S(1)}, f32[1032,128]{1,0:T(8,128)S(1)}, u32[]{:S(2)}, u32[]{:S(2)}) collective-permute-start(f32[1032,128]{1,0:T(8,128)S(1)} %get-tuple-element.42.states_ref), channel_id=1, source_target_pairs={{4,8},{5,9},{6,10},{7,11},{12,16},{13,17},{14,18},{15,19},{20,24},... | collective-permute-start | bytes 1585160 | tf_op jit(solution)/shard_map/ppermute | solution.py:495
  102.9 9.3 %collective-permute-start.19 = (f32[1024,128]{1,0:T(8,128)S(1)}, f32[1024,128]{1,0:T(8,128)S(1)}, u32[]{:S(2)}, u32[]{:S(2)}) collective-permute-start(f32[1024,128]{1,0:T(8,128)S(1)} %shard_map.112.refs_0_), channel_id=1, source_target_pairs={{0,1},{1,0},{2,3},{3,2},{8,9},{9,8},{10,11},{11,10},{16,17},{17,16... | collective-permute-start | bytes 1572872 | tf_op jit(solution)/shard_map/ppermute | solution.py:495
  103.7 11.9 %collective-permute-start.21 = (f32[1024,128]{1,0:T(8,128)S(1)}, f32[1024,128]{1,0:T(8,128)S(1)}, u32[]{:S(2)}, u32[]{:S(2)}) collective-permute-start(f32[1024,128]{1,0:T(8,128)S(1)} %collective-permute-done.20.refs_2_), channel_id=1, source_target_pairs={{0,1},{1,0},{2,3},{3,2},{8,9},{9,8},{10,11},{11,10},{16,17},{17,16... | collective-permute-start | bytes 1572872 | tf_op jit(solution)/shard_map/ppermute | solution.py:495
  104.4 5.4 %collective-permute-start.18 = (f32[768,128]{1,0:T(8,128)S(1)}, f32[768,128]{1,0:T(8,128)S(1)}, u32[]{:S(2)}, u32[]{:S(2)}) collective-permute-start(f32[768,128]{1,0:T(8,128)S(1)} %get-tuple-element.43), channel_id=1, source_target_pairs={{4,0},{5,1},{6,2},{7,3},{12,8},{13,9},{14,10},{15,11},{20,16},{21,... | collective-permute-start | bytes 1179656 | tf_op jit(solution)/shard_map/ppermute | solution.py:495
  108.3 18.2 %collective-permute-start.23 = (f32[2064,128]{1,0:T(8,128)S(1)}, f32[2064,128]{1,0:T(8,128)S(1)}, u32[]{:S(2)}, u32[]{:S(2)}) collective-permute-start(f32[2064,128]{1,0:T(8,128)S(1)} %get-tuple-element.46), channel_id=1, source_target_pairs={{4,0},{5,1},{6,2},{7,3},{12,8},{13,9},{14,10},{15,11},{20,16},{21,... | collective-permute-start | bytes 3170312 | tf_op jit(solution)/shard_map/ppermute | solution.py:495
  109.7 16.7 %collective-permute-start.22 = (f32[1032,128]{1,0:T(8,128)S(1)}, f32[1032,128]{1,0:T(8,128)S(1)}, u32[]{:S(2)}, u32[]{:S(2)}) collective-permute-start(f32[1032,128]{1,0:T(8,128)S(1)} %get-tuple-element.42.states_ref), channel_id=1, source_target_pairs={{4,0},{5,1},{6,2},{7,3},{12,8},{13,9},{14,10},{15,11},{20,16},{21,... | collective-permute-start | bytes 1585160 | tf_op jit(solution)/shard_map/ppermute | solution.py:495
  112.2 15.1 %collective-permute-start.26 = (f32[2064,128]{1,0:T(8,128)S(1)}, f32[2064,128]{1,0:T(8,128)S(1)}, u32[]{:S(2)}, u32[]{:S(2)}) collective-permute-start(f32[2064,128]{1,0:T(8,128)S(1)} %get-tuple-element.46), channel_id=1, source_target_pairs={{4,8},{5,9},{6,10},{7,11},{12,16},{13,17},{14,18},{15,19},{20,24},... | collective-permute-start | bytes 3170312 | tf_op jit(solution)/shard_map/ppermute | solution.py:495
  115.5 11.0 %collective-permute-start.24 = (f32[1032,128]{1,0:T(8,128)S(1)}, f32[1032,128]{1,0:T(8,128)S(1)}, u32[]{:S(2)}, u32[]{:S(2)}) collective-permute-start(f32[1032,128]{1,0:T(8,128)S(1)} %get-tuple-element.47), channel_id=1, source_target_pairs={{4,0},{5,1},{6,2},{7,3},{12,8},{13,9},{14,10},{15,11},{20,16},{21,... | collective-permute-start | bytes 1585160 | tf_op jit(solution)/shard_map/ppermute | solution.py:495
  117.6 9.0 %collective-permute-start.27 = (f32[1032,128]{1,0:T(8,128)S(1)}, f32[1032,128]{1,0:T(8,128)S(1)}, u32[]{:S(2)}, u32[]{:S(2)}) collective-permute-start(f32[1032,128]{1,0:T(8,128)S(1)} %collective-permute-done.25.refs_1_), channel_id=1, source_target_pairs={{0,1},{1,0},{2,3},{3,2},{8,9},{9,8},{10,11},{11,10},{16,17},{17,16... | collective-permute-start | bytes 1585160 | tf_op jit(solution)/shard_map/ppermute | solution.py:495
  127.4 8.7 %collective-permute-start.28 = (f32[1024,128]{1,0:T(8,128)S(1)}, f32[1024,128]{1,0:T(8,128)S(1)}, u32[]{:S(2)}, u32[]{:S(2)}) collective-permute-start(f32[1024,128]{1,0:T(8,128)S(1)} %shard_map.115), channel_id=1, source_target_pairs={{0,4},{1,5},{2,6},{3,7},{8,12},{9,13},{10,14},{11,15},{16,20},{17,... | collective-permute-start | bytes 1572872 | tf_op jit(solution)/shard_map/ppermute | solution.py:495
  129.3 16.5 %collective-permute-start.29 = (f32[512,128]{1,0:T(8,128)S(1)}, f32[512,128]{1,0:T(8,128)S(1)}, u32[]{:S(2)}, u32[]{:S(2)}) collective-permute-start(f32[512,128]{1,0:T(8,128)S(1)} %get-tuple-element.53), channel_id=1, source_target_pairs={{8,4},{9,5},{10,6},{11,7},{16,12},{17,13},{18,14},{19,15},{24,20},... | collective-permute-start | bytes 786440 | tf_op jit(solution)/shard_map/ppermute | solution.py:495
  130.6 18.0 %collective-permute-start.30 = (f32[512,128]{1,0:T(8,128)S(1)}, f32[512,128]{1,0:T(8,128)S(1)}, u32[]{:S(2)}, u32[]{:S(2)}) collective-permute-start(f32[512,128]{1,0:T(8,128)S(1)} %get-tuple-element.54), channel_id=1, source_target_pairs={{8,4},{9,5},{10,6},{11,7},{16,12},{17,13},{18,14},{19,15},{24,20},... | collective-permute-start | bytes 786440 | tf_op jit(solution)/shard_map/ppermute | solution.py:495

commit v7 on v6

--- a/solution.py
+++ b/solution.py
@@ -18,7 +18,7 @@
 bf16 = jnp.bfloat16
 f32 = jnp.float32
 
-PARENT, MODE, LIVE, FACTOR, WEIGHT, WEIGHT_A, WEIGHT_C = range(7)
+PARENT, MODE, LIVE, FACTOR, WEIGHT, WEIGHT_A, WEIGHT_C, DIAGONAL = range(8)
 ROWS, LANES = 8, 128
 PACK_LIMIT = 56 << 20
 
@@ -56,11 +56,24 @@
     return pl.ds(at, count * n)
 
 
+def symmetric(value):
+    return (value + value.T) * 0.5
+
+
+def paired(operators):
+    return [tuple(operators)] if len(operators) == 2 else operators
+
+
 def pack_kernel(live_ref, parent_ref, mode_ref, damping_ref, weight_ref, corr_ref, blocks_ref, coupling_ref, out_ref, table_ref):
     slots, n = live_ref.shape[0], blocks_ref.shape[1]
     size = blocks_ref.shape[0]
     out_ref[pl.ds(0, size)] = blocks_ref[...]
-    out_ref[pl.ds(size + ROWS, coupling_ref.shape[0])] = coupling_ref[...]
+    corner_row, corner_lane = (lax.broadcasted_iota(jnp.int32, (n, n), axis) for axis in range(2))
+    operators = [symmetric(coupling_ref[pl.ds(i * n, n)]) for i in range(corr_ref.shape[0])]
+    for i, value in enumerate(paired(operators)):
+        if isinstance(value, tuple):
+            value = jnp.where(corner_row <= corner_lane, *value)
+        out_ref[pl.ds(size + ROWS + i * n, n)] = value
     row = lax.broadcasted_iota(jnp.int32, (ROWS, n), 0)
     lane = lax.broadcasted_iota(jnp.int32, (ROWS, n), 1)
     table = jnp.zeros((ROWS, n), f32)
@@ -80,6 +93,10 @@
         }
         for at, value in values.items():
             table = jnp.where(jnp.logical_and(row == at, lane == s), value, table)
+    for value in paired(operators):
+        if isinstance(value, tuple):
+            second = jnp.sum(jnp.where(corner_row == corner_lane, value[1], 0.0), axis=0, keepdims=True)
+            table = jnp.where(row == DIAGONAL, second, table)
     live_row = table[LIVE : LIVE + 1]
     table = jnp.where(row == FACTOR, live_row * jnp.exp(table), table)
     table_ref[...] = table
@@ -154,32 +171,42 @@
     sources = refs[: -len(outs)]
     right_ref, left_ref = outs[0], outs[1]
     n = own_ref.shape[1]
-
-    def put(at, value):
-        sym = (value + value.T) * 0.5
+    size = 2 * slots * n
+    squares = len(paired([None] * modes))
+    block = ROWS + squares * n
+    row, lane = (lax.broadcasted_iota(jnp.int32, (n, n), axis) for axis in range(2))
+
+    def put(at, sym):
         right_ref[at] = stack_rows(sym)
         left_ref[at] = stack_cols(sym)
 
     def own():
         for i in range(modes):
-            put(i, own_ref[rows(i * n, n)])
+            put(i, symmetric(own_ref[rows(i * n, n)]))
+
+    def unpack(k, ref, base):
+        if squares == modes:
+            for i in range(modes):
+                put(k * modes + i, ref[rows(base + ROWS + i * n, n)])
+            return
+        square = ref[rows(base + ROWS, n)]
+        turned = square.T
+        diagonal = ref[pl.ds(base, ROWS)][DIAGONAL : DIAGONAL + 1]
+        put(k * modes, jnp.where(row <= lane, square, turned))
+        put(k * modes + 1, jnp.where(row == lane, diagonal, jnp.where(row > lane, square, turned)))
 
     if parity is None:
         own()
-        groups = Layout(sources, slots, single(group))
         for k in range(1, group):
-            ref, base = groups.base(k)
-            for i in range(modes):
-                value = ref[rows(base + groups.stride + i * n, n)]
-                put(k * modes + i, value)
-                outs[2][rows(((k - 1) * modes + i) * n, n)] = value
+            unpack(k, sources[k], size)
+            outs[2][pl.ds((k - 1) * block, block)] = sources[k][pl.ds(size, block)]
     else:
 
         @pl.when(odd_depth() == parity)
         def _():
             own()
-            for at in range(modes, group * modes):
-                put(at, sources[0][rows((at - modes) * n, n)])
+            for k in range(1, group):
+                unpack(k, sources[0], (k - 1) * block)
 
 
 def taylor(real, imag, right, left):
@@ -409,10 +436,15 @@
         if second:
             for k in range(group):
                 ref, base = out.base(k)
-                ref[pl.ds(base, size)] = bases[0][pl.ds(k * size, size)]
+                start_value = bases[0][pl.ds(k * size, size)]
+                if base_count > 1:
+                    start_value = start_value + bases[1 + k][...]
+                ref[pl.ds(base, size)] = start_value
                 ref[pl.ds(base + size, ROWS)] = tab_refs[0][k]
         else:
             offset = 0
+            if not bases:
+                outs[0][...] = jnp.zeros_like(outs[0])
             for base in bases:
                 outs[0][pl.ds(offset, base.shape[0])] = base[...]
                 offset += base.shape[0]
@@ -529,10 +561,11 @@
 
     operator_shapes = (sds(group * modes, 3 * n, n, dtype=bf16), sds(group * modes, n, 3 * n, dtype=bf16))
     couplings = coupling.reshape(modes * n, n)
+    squares = len(paired([None] * modes))
 
     packed, own_table = call(
         pack_kernel,
-        (mats(plain + modes, 1), sds(ROWS, n)),
+        (mats(plain + squares, 1), sds(ROWS, n)),
         PACK_LIMIT,
         (live_slots, parent_index, bath_mode, damping, link_weight, correlation, blocks.reshape(plain * n, n), couplings),
         smem=6,
@@ -544,7 +577,7 @@
     )
     *operators_odd, raw = call(
         functools.partial(operators_kernel, slots, group, modes, None),
-        (*operator_shapes, mats((group - 1) * modes)),
+        (*operator_shapes, mats((group - 1) * squares, group - 1)),
         limit,
         (couplings, *first),
     )
@@ -639,8 +672,8 @@
     from_above.append(neighbour(from_above[0], 0))
     from_below = [shift(value, -1, 1) for value in states]
     last_odd = free(states[0], 1, 2)
-    states, tabs_even = side("children", free_even, from_below, gathered, 0, operators_even)
-    states = side("parents", [states], from_above, [tabs_even], 0, operators_even, second=True)
+    states, tabs_even = side("children", [], from_below, gathered, 0, operators_even)
+    states = side("parents", [states, *free_even], from_above, [tabs_even], 0, operators_even, second=True)
 
     sums, _ = send(states, 0, split_hop, operators_even)
     sums = [shift(value, -1, 0) for value in sums]

time: 151 us -> 167 us (1.11)
  starting transfers between devices: 49.5 us -> 61.7 us
  waiting for transfers between devices: 38.3 us -> 42.1 us
    ppermute x31, starting transfers between devices: 49.5 us -> 61.7 us  [permute(): return lax.ppermute(value, AXES, pairs)]
    ppermute x31, waiting for transfers between devices: 38.3 us -> 42.1 us  [permute(): return lax.ppermute(value, AXES, pairs)]
  transfers between devices with their start and end apart: 31 -> 31, of which waited for: 12 -> 11; matrix products, arithmetic and copies ran while one was open for 0% -> 0% of each run, Pallas kernels for 39% -> 33%
where the time goes in v7:
time: 167 us; the launch traced here: 166 us
  Pallas kernels  61.7 us (37%)
  starting transfers between devices  61.7 us (37%)
  waiting for transfers between devices  42.1 us (25%)
    pallas_call x29, Pallas kernels, call(): pl.pallas_call(kernel, out_shape=out_shapes, in_specs=specs, out_specs=ja...  61.7 us
    ppermute x31, starting transfers between devices, permute(): return lax.ppermute(value, AXES, pairs)  61.7 us
    ppermute x31, waiting for transfers between devices, permute(): return lax.ppermute(value, AXES, pairs)  42.1 us
  transfers between devices with their start and end apart: 31, of which 11 were waited for; matrix products, arithmetic and copies ran while one was open for 0% of the time, Pallas kernels for 33%

profile of v7, /device:TPU:3, one launch (start us, length us, event | category | flops | bytes accessed | tf_op | source)
XLA Modules:
  0.0 166.4 jit_solution(4883641538716530115)
XLA Ops:
  0.0 2.0 %shard_map.91 = (f32[1160,128]{1,0:T(8,128)}, f32[8,128]{1,0:T(8,128)}) custom-call(s32[4]{0:T(128)} %live_ref.1, s32[4]{0:T(128)} %parent_ref.1, s32[4]{0:T(128)} %mode_ref.1, f32[4]{0:T(128)} %damping_ref.1, f32[4]{0:T(128)} %weight_ref.1, f32[2,2]{1,0:T(2,128)} %corr_ref.1, f32[1024,128]{1,0:T(8,128)} %bitcast.6, f32[256,128]{1,0:T(8,128)} %bitcast.3), custom_call_target="tpu_custom_call" | custom-call | flops 1100000000 | bytes 524288 | tf_op jit(solution)/shard_map/pallas_call | solution.py:498
  2.1 3.2 %collective-permute-start = (f32[1160,128]{1,0:T(8,128)}, f32[1160,128]{1,0:T(8,128)S(1)}, u32[]{:S(2)}, u32[]{:S(2)}) collective-permute-start(f32[1160,128]{1,0:T(8,128)} %get-tuple-element.31.refs_0_.states_ref), channel_id=1, source_target_pairs={{4,5},{5,4},{6,7},{7,6},{12,13},{13,12},{14,15},{15,14},{20,21},{2... | collective-permute-start | bytes 1781768 | tf_op jit(solution)/shard_map/ppermute | solution.py:527
  5.3 4.2 %collective-permute-start.1 = (f32[1160,128]{1,0:T(8,128)}, f32[1160,128]{1,0:T(8,128)S(1)}, u32[]{:S(2)}, u32[]{:S(2)}) collective-permute-start(f32[1160,128]{1,0:T(8,128)} %get-tuple-element.31.refs_0_.states_ref), channel_id=1, source_target_pairs={{4,6},{5,7},{6,4},{7,5},{12,14},{13,15},{14,12},{15,13},{20,22},{2... | collective-permute-start | bytes 1781768 | tf_op jit(solution)/shard_map/ppermute | solution.py:527
  9.5 2.1 %collective-permute-start.4 = (f32[8,128]{1,0:T(8,128)}, f32[8,128]{1,0:T(8,128)S(1)}, u32[]{:S(2)}, u32[]{:S(2)}) collective-permute-start(f32[8,128]{1,0:T(8,128)} %get-tuple-element.30.own_ref), channel_id=1, source_target_pairs={{4,0},{5,1},{6,2},{7,3},{8,4},{9,5},{10,6},{11,7},{12,8},{13,9},{1... | collective-permute-start | bytes 12296 | tf_op jit(solution)/shard_map/ppermute | solution.py:527
  11.6 0.7 shard_map.93
  12.3 4.2 %shard_map.94.refs_0_ = f32[512,128]{1,0:T(8,128)S(1)} custom-call(f32[1160,128]{1,0:T(8,128)S(1)} %copy-done, bf16[384,512]{1,0:T(8,128)(2,1)S(1)} %get-tuple-element.34.right_ref, bf16[128,1536]{1,0:T(8,128)(2,1)S(1)} %get-tuple-element.35.left_ref), custom_call_target="tpu_custom_call" | custom-call | flops 4950000128 | bytes 524288 | tf_op jit(solution)/shard_map/pallas_call | solution.py:498
  16.5 4.2 %shard_map.95.refs_1_ = f32[512,128]{1,0:T(8,128)S(1)} custom-call(f32[1160,128]{1,0:T(8,128)S(1)} %copy-done, bf16[384,512]{1,0:T(8,128)(2,1)S(1)} %get-tuple-element.34.right_ref, bf16[128,1536]{1,0:T(8,128)(2,1)S(1)} %get-tuple-element.35.left_ref), custom_call_target="tpu_custom_call" | custom-call | flops 4950000128 | bytes 524288 | tf_op jit(solution)/shard_map/pallas_call | solution.py:498
  20.7 2.7 %collective-permute-done.1.refs_2_.states_ref = f32[1160,128]{1,0:T(8,128)S(1)} collective-permute-done((f32[1160,128]{1,0:T(8,128)}, f32[1160,128]{1,0:T(8,128)S(1)}, u32[]{:S(2)}, u32[]{:S(2)}) %collective-permute-start.1) | collective-permute-done | bytes 593952 | tf_op jit(solution)/shard_map/ppermute | solution.py:527
  23.4 1.9 %collective-permute-start.2 = (f32[1160,128]{1,0:T(8,128)S(1)}, f32[1160,128]{1,0:T(8,128)S(1)}, u32[]{:S(2)}, u32[]{:S(2)}) collective-permute-start(f32[1160,128]{1,0:T(8,128)S(1)} %collective-permute-done.1.refs_2_.states_ref), channel_id=1, source_target_pairs={{4,5},{5,4},{6,7},{7,6},{12,13},{13,12},{14,15},{15,14},{20,21},{2... | collective-permute-start | bytes 1781768 | tf_op jit(solution)/shard_map/ppermute | solution.py:527
  25.4 0.0 copy-start.1
  25.4 4.2 %shard_map.96.refs_2_ = f32[512,128]{1,0:T(8,128)S(1)} custom-call(f32[1160,128]{1,0:T(8,128)S(1)} %collective-permute-done.refs_1_.states_ref, bf16[384,512]{1,0:T(8,128)(2,1)S(1)} %get-tuple-element.34.right_ref, bf16[128,1536]{1,0:T(8,128)(2,1)S(1)} %get-tuple-element.35.left_ref), custom_call_target="tpu_custom_call" | custom-call | flops 4950000128 | bytes 524288 | tf_op jit(solution)/shard_map/pallas_call | solution.py:498
  29.6 4.5 %collective-permute-done.2.refs_3_.states_ref = f32[1160,128]{1,0:T(8,128)S(1)} collective-permute-done((f32[1160,128]{1,0:T(8,128)S(1)}, f32[1160,128]{1,0:T(8,128)S(1)}, u32[]{:S(2)}, u32[]{:S(2)}) %collective-permute-start.2) | collective-permute-done | bytes 593952 | tf_op jit(solution)/shard_map/ppermute | solution.py:527
  34.1 0.2 shard_map.92
  34.3 2.6 %shard_map.103 = (f32[1024,128]{1,0:T(8,128)S(1)}, f32[4,8,128]{2,1,0:T(8,128)S(1)}) custom-call(bf16[8,384,128]{2,1,0:T(8,128)(2,1)S(1)} %get-tuple-element.32.right_ref, bf16[8,128,384]{2,1,0:T(8,128)(2,1)S(1)} %get-tuple-element.33.left_ref, f32[1160,128]{1,0:T(8,128)S(1)} %copy-done, f32[1160,128]{1,0:T(8,128)S(1)} %collective-permute-done.refs_1_.states_ref, ...), custom_call_target="tpu_custom_call" | custom-call | flops 2200000000 | bytes 524288 | tf_op jit(solution)/shard_map/pallas_call | solution.py:498
  37.0 1.3 collective-permute-start.3
  38.3 0.8 shard_map.104
  39.1 1.3 collective-permute-start.5
  40.4 1.3 collective-permute-start.6
  41.8 4.2 %shard_map.97.refs_3_ = f32[512,128]{1,0:T(8,128)S(1)} custom-call(f32[1160,128]{1,0:T(8,128)S(1)} %collective-permute-done.refs_1_.states_ref, bf16[384,512]{1,0:T(8,128)(2,1)S(1)} %get-tuple-element.34.right_ref, bf16[128,1536]{1,0:T(8,128)(2,1)S(1)} %get-tuple-element.35.left_ref), custom_call_target="tpu_custom_call" | custom-call | flops 4950000128 | bytes 524288 | tf_op jit(solution)/shard_map/pallas_call | solution.py:498
  46.0 0.6 collective-permute-done.6.refs_3_
  46.5 0.7 collective-permute-start.8
  47.2 4.2 %shard_map.98.refs_4_ = f32[512,128]{1,0:T(8,128)S(1)} custom-call(f32[1160,128]{1,0:T(8,128)S(1)} %collective-permute-done.1.refs_2_.states_ref, bf16[384,512]{1,0:T(8,128)(2,1)S(1)} %get-tuple-element.34.right_ref, bf16[128,1536]{1,0:T(8,128)(2,1)S(1)} %get-tuple-element.35.left_ref), custom_call_target="tpu_custom_call" | custom-call | flops 4950000128 | bytes 524288 | tf_op jit(solution)/shard_map/pallas_call | solution.py:498
  51.4 4.2 %shard_map.99.refs_5_ = f32[512,128]{1,0:T(8,128)S(1)} custom-call(f32[1160,128]{1,0:T(8,128)S(1)} %collective-permute-done.1.refs_2_.states_ref, bf16[384,512]{1,0:T(8,128)(2,1)S(1)} %get-tuple-element.34.right_ref, bf16[128,1536]{1,0:T(8,128)(2,1)S(1)} %get-tuple-element.35.left_ref), custom_call_target="tpu_custom_call" | custom-call | flops 4950000128 | bytes 524288 | tf_op jit(solution)/shard_map/pallas_call | solution.py:498
  55.7 1.3 collective-permute-start.7
  57.0 0.7 collective-permute-start.11
  57.7 0.7 collective-permute-start.14
  58.4 4.2 %shard_map.100.refs_6_ = f32[512,128]{1,0:T(8,128)S(1)} custom-call(f32[1160,128]{1,0:T(8,128)S(1)} %collective-permute-done.2.refs_3_.states_ref, bf16[384,512]{1,0:T(8,128)(2,1)S(1)} %get-tuple-element.34.right_ref, bf16[128,1536]{1,0:T(8,128)(2,1)S(1)} %get-tuple-element.35.left_ref), custom_call_target="tpu_custom_call" | custom-call | flops 4950000128 | bytes 524288 | tf_op jit(solution)/shard_map/pallas_call | solution.py:498
  62.6 1.3 collective-permute-start.10
  63.9 1.3 collective-permute-start.9
  65.2 4.2 %shard_map.101.refs_7_ = f32[512,128]{1,0:T(8,128)S(1)} custom-call(f32[1160,128]{1,0:T(8,128)S(1)} %collective-permute-done.2.refs_3_.states_ref, bf16[384,512]{1,0:T(8,128)(2,1)S(1)} %get-tuple-element.34.right_ref, bf16[128,1536]{1,0:T(8,128)(2,1)S(1)} %get-tuple-element.35.left_ref), custom_call_target="tpu_custom_call" | custom-call | flops 4950000128 | bytes 524288 | tf_op jit(solution)/shard_map/pallas_call | solution.py:498
  69.4 1.3 collective-permute-start.13
  70.7 1.5 collective-permute-start.12
  72.2 1.3 collective-permute-start.15
  73.5 1.3 collective-permute-start.16
  74.8 4.5 %collective-permute-done.9.refs_9_ = f32[1032,128]{1,0:T(8,128)S(1)} collective-permute-done((f32[1032,128]{1,0:T(8,128)S(1)}, f32[1032,128]{1,0:T(8,128)S(1)}, u32[]{:S(2)}, u32[]{:S(2)}) %collective-permute-start.9) | collective-permute-done | bytes 528416 | tf_op jit(solution)/shard_map/ppermute | solution.py:527
  79.4 1.3 collective-permute-start.17
  80.7 3.0 %shard_map.106 = (f32[4096,128]{1,0:T(8,128)S(1)}, f32[4,8,128]{2,1,0:T(8,128)}) custom-call(bf16[8,384,128]{2,1,0:T(8,128)(2,1)S(1)} %get-tuple-element.32.right_ref, bf16[8,128,384]{2,1,0:T(8,128)(2,1)S(1)} %get-tuple-element.33.left_ref, f32[512,128]{1,0:T(8,128)S(1)} %shard_map.94.refs_0_, f32[512,128]{1,0:T(8,128)S(1)} %shard_map.95.refs_1_, ...), custom_call_target="tpu_custom_call" | custom-call | flops 3300000000 | bytes 524288 | tf_op jit(solution)/shard_map/pallas_call | solution.py:498
  83.7 4.4 %shard_map.107 = (f32[4096,128]{1,0:T(8,128)S(1)}, f32[4,8,128]{2,1,0:T(8,128)}) custom-call(bf16[8,384,128]{2,1,0:T(8,128)(2,1)S(1)} %get-tuple-element.32.right_ref, bf16[8,128,384]{2,1,0:T(8,128)(2,1)S(1)} %get-tuple-element.33.left_ref, f32[4096,128]{1,0:T(8,128)S(1)} %get-tuple-element.40.refs_0_, f32[1032,128]{1,0:T(8,128)S(1)} %collective-permute-done.10.refs_1_, ...), custom_call_target="tpu_custom_call" | custom-call | flops 3300000000 | bytes 524288 | tf_op jit(solution)/shard_map/pallas_call | solution.py:498
  88.1 4.7 %collective-permute-done.16.refs_1_ = f32[1032,128]{1,0:T(8,128)S(1)} collective-permute-done((f32[1032,128]{1,0:T(8,128)S(1)}, f32[1032,128]{1,0:T(8,128)S(1)}, u32[]{:S(2)}, u32[]{:S(2)}) %collective-permute-start.16) | collective-permute-done | bytes 528416 | tf_op jit(solution)/shard_map/ppermute | solution.py:527
  92.8 5.7 %collective-permute-done.17.refs_2_ = f32[1032,128]{1,0:T(8,128)S(1)} collective-permute-done((f32[1032,128]{1,0:T(8,128)S(1)}, f32[1032,128]{1,0:T(8,128)S(1)}, u32[]{:S(2)}, u32[]{:S(2)}) %collective-permute-start.17) | collective-permute-done | bytes 528416 | tf_op jit(solution)/shard_map/ppermute | solution.py:527
  98.5 2.6 %shard_map.108 = (f32[1032,128]{1,0:T(8,128)S(1)}, f32[2064,128]{1,0:T(8,128)S(1)}, f32[1032,128]{1,0:T(8,128)S(1)}) custom-call(bf16[8,384,128]{2,1,0:T(8,128)(2,1)S(1)} %get-tuple-element.32.right_ref, bf16[8,128,384]{2,1,0:T(8,128)(2,1)S(1)} %get-tuple-element.33.left_ref, f32[4096,128]{1,0:T(8,128)S(1)} %get-tuple-element.41.refs_0_, ...), custom_call_target="tpu_custom_call" | custom-call | flops 3300000000 | bytes 524288 | tf_op jit(solution)/shard_map/pallas_call | solution.py:498
  101.1 1.3 collective-permute-start.19
  102.4 1.3 collective-permute-start.25
  103.7 1.3 collective-permute-start.21
  105.1 0.7 collective-permute-start.23
  105.8 3.4 %collective-permute-start.18 = (f32[408,128]{1,0:T(8,128)S(1)}, f32[408,128]{1,0:T(8,128)S(1)}, u32[]{:S(2)}, u32[]{:S(2)}) collective-permute-start(f32[408,128]{1,0:T(8,128)S(1)} %get-tuple-element.43), channel_id=1, source_target_pairs={{4,0},{5,1},{6,2},{7,3},{12,8},{13,9},{14,10},{15,11},{20,16},{21,... | collective-permute-start | bytes 626696 | tf_op jit(solution)/shard_map/ppermute | solution.py:527
  109.2 1.1 collective-permute-done.18.refs_0_
  110.3 2.3 %collective-permute-start.20 = (f32[2064,128]{1,0:T(8,128)S(1)}, f32[2064,128]{1,0:T(8,128)S(1)}, u32[]{:S(2)}, u32[]{:S(2)}) collective-permute-start(f32[2064,128]{1,0:T(8,128)S(1)} %get-tuple-element.46), channel_id=1, source_target_pairs={{4,0},{5,1},{6,2},{7,3},{12,8},{13,9},{14,10},{15,11},{20,16},{21,... | collective-permute-start | bytes 3170312 | tf_op jit(solution)/shard_map/ppermute | solution.py:527
  112.7 0.7 collective-permute-start.22
  113.4 0.7 collective-permute-start.24
  114.1 17.4 %collective-permute-start.26 = (f32[2064,128]{1,0:T(8,128)S(1)}, f32[2064,128]{1,0:T(8,128)S(1)}, u32[]{:S(2)}, u32[]{:S(2)}) collective-permute-start(f32[2064,128]{1,0:T(8,128)S(1)} %get-tuple-element.46), channel_id=1, source_target_pairs={{4,8},{5,9},{6,10},{7,11},{12,16},{13,17},{14,18},{15,19},{20,24},... | collective-permute-start | bytes 3170312 | tf_op jit(solution)/shard_map/ppermute | solution.py:527
  131.5 0.7 collective-permute-start.27
  132.2 8.2 %shard_map.109.refs_0_ = f32[1024,128]{1,0:T(8,128)S(1)} custom-call(f32[1032,128]{1,0:T(8,128)S(1)} %get-tuple-element.42.states_ref, bf16[384,512]{1,0:T(8,128)(2,1)S(1)} %get-tuple-element.34.right_ref, bf16[128,1536]{1,0:T(8,128)(2,1)S(1)} %get-tuple-element.35.left_ref), custom_call_target="tpu_custom_call" | custom-call | flops 9900000256 | bytes 524288 | tf_op jit(solution)/shard_map/pallas_call | solution.py:498
  140.4 0.1 shard_map.111
  140.6 2.7 %collective-permute-done.26.refs_6_ = f32[2064,128]{1,0:T(8,128)S(1)} collective-permute-done((f32[2064,128]{1,0:T(8,128)S(1)}, f32[2064,128]{1,0:T(8,128)S(1)}, u32[]{:S(2)}, u32[]{:S(2)}) %collective-permute-start.26) | collective-permute-done | bytes 1056800 | tf_op jit(solution)/shard_map/ppermute | solution.py:527
  143.3 1.3 collective-permute-start.28
  144.6 0.7 shard_map.118
  145.3 1.3 collective-permute-start.29
  146.6 1.3 collective-permute-start.30
  147.9 4.2 %collective-permute-done.28.refs_1_ = f32[1024,128]{1,0:T(8,128)S(1)} collective-permute-done((f32[1024,128]{1,0:T(8,128)S(1)}, f32[1024,128]{1,0:T(8,128)S(1)}, u32[]{:S(2)}, u32[]{:S(2)}) %collective-permute-start.28) | collective-permute-done | bytes 524320 | tf_op jit(solution)/shard_map/ppermute | solution.py:527
  152.1 1.1 shard_map.116.refs_0_
  153.3 8.7 %collective-permute-done.29.refs_2_ = f32[512,128]{1,0:T(8,128)S(1)} collective-permute-done((f32[512,128]{1,0:T(8,128)S(1)}, f32[512,128]{1,0:T(8,128)S(1)}, u32[]{:S(2)}, u32[]{:S(2)}) %collective-permute-start.29) | collective-permute-done | bytes 262176 | tf_op jit(solution)/shard_map/ppermute | solution.py:527
  162.0 2.8 %collective-permute-done.30.refs_3_ = f32[512,128]{1,0:T(8,128)S(1)} collective-permute-done((f32[512,128]{1,0:T(8,128)S(1)}, f32[512,128]{1,0:T(8,128)S(1)}, u32[]{:S(2)}, u32[]{:S(2)}) %collective-permute-start.30) | collective-permute-done | bytes 262176 | tf_op jit(solution)/shard_map/ppermute | solution.py:527
  164.8 1.5 shard_map.119
  (35 shorter events, 0.2 us)
Async XLA Ops:
  0.0 11.5 %copy-start.2 = (f32[128,128]{1,0:T(8,128)S(1)}, f32[128,128]{1,0:T(8,128)}, u32[]{:S(2)}) copy-start(f32[128,128]{1,0:T(8,128)} %ham_ref.1) | copy-start | bytes 196612
  2.1 23.4 %collective-permute-start = (f32[1160,128]{1,0:T(8,128)}, f32[1160,128]{1,0:T(8,128)S(1)}, u32[]{:S(2)}, u32[]{:S(2)}) collective-permute-start(f32[1160,128]{1,0:T(8,128)} %get-tuple-element.31.refs_0_.states_ref), channel_id=1, source_target_pairs={{4,5},{5,4},{6,7},{7,6},{12,13},{13,12},{14,15},{15,14},{20,21},{2... | collective-permute-start | bytes 1781768 | tf_op jit(solution)/shard_map/ppermute | solution.py:527
  5.3 18.2 %collective-permute-start.1 = (f32[1160,128]{1,0:T(8,128)}, f32[1160,128]{1,0:T(8,128)S(1)}, u32[]{:S(2)}, u32[]{:S(2)}) collective-permute-start(f32[1160,128]{1,0:T(8,128)} %get-tuple-element.31.refs_0_.states_ref), channel_id=1, source_target_pairs={{4,6},{5,7},{6,4},{7,5},{12,14},{13,15},{14,12},{15,13},{20,22},{2... | collective-permute-start | bytes 1781768 | tf_op jit(solution)/shard_map/ppermute | solution.py:527
  9.5 2.8 %copy-start = (f32[1160,128]{1,0:T(8,128)S(1)}, f32[1160,128]{1,0:T(8,128)}, u32[]{:S(2)}) copy-start(f32[1160,128]{1,0:T(8,128)} %get-tuple-element.31.refs_0_.states_ref) | copy-start | bytes 1781764
  9.5 28.8 %collective-permute-start.4 = (f32[8,128]{1,0:T(8,128)}, f32[8,128]{1,0:T(8,128)S(1)}, u32[]{:S(2)}, u32[]{:S(2)}) collective-permute-start(f32[8,128]{1,0:T(8,128)} %get-tuple-element.30.own_ref), channel_id=1, source_target_pairs={{4,0},{5,1},{6,2},{7,3},{8,4},{9,5},{10,6},{11,7},{12,8},{13,9},{1... | collective-permute-start | bytes 12296 | tf_op jit(solution)/shard_map/ppermute | solution.py:527
  23.4 10.7 %collective-permute-start.2 = (f32[1160,128]{1,0:T(8,128)S(1)}, f32[1160,128]{1,0:T(8,128)S(1)}, u32[]{:S(2)}, u32[]{:S(2)}) collective-permute-start(f32[1160,128]{1,0:T(8,128)S(1)} %collective-permute-done.1.refs_2_.states_ref), channel_id=1, source_target_pairs={{4,5},{5,4},{6,7},{7,6},{12,13},{13,12},{14,15},{15,14},{20,21},{2... | collective-permute-start | bytes 1781768 | tf_op jit(solution)/shard_map/ppermute | solution.py:527
  25.4 8.7 %copy-start.1 = (f32[2,128,128]{2,1,0:T(8,128)S(1)}, f32[2,128,128]{2,1,0:T(8,128)}, u32[]{:S(2)}) copy-start(f32[2,128,128]{2,1,0:T(8,128)} %param.14) | copy-start | bytes 393220
  37.0 9.5 %collective-permute-start.3 = (f32[1024,128]{1,0:T(8,128)S(1)}, f32[1024,128]{1,0:T(8,128)S(1)}, u32[]{:S(2)}, u32[]{:S(2)}) collective-permute-start(f32[1024,128]{1,0:T(8,128)S(1)} %get-tuple-element.36), channel_id=1, source_target_pairs={{4,0},{5,1},{6,2},{7,3},{12,8},{13,9},{14,10},{15,11},{20,16},{21,... | collective-permute-start | bytes 1572872 | tf_op jit(solution)/shard_map/ppermute | solution.py:527
  39.1 6.8 %collective-permute-start.5 = (f32[512,128]{1,0:T(8,128)S(1)}, f32[512,128]{1,0:T(8,128)S(1)}, u32[]{:S(2)}, u32[]{:S(2)}) collective-permute-start(f32[512,128]{1,0:T(8,128)S(1)} %get-tuple-element.37), channel_id=1, source_target_pairs={{4,8},{5,9},{6,10},{7,11},{12,16},{13,17},{14,18},{15,19},{20,24},... | collective-permute-start | bytes 786440 | tf_op jit(solution)/shard_map/ppermute | solution.py:527
  40.4 6.1 %copy-start.3 = (f32[8,128]{1,0:T(8,128)S(1)}, f32[8,128]{1,0:T(8,128)}, u32[]{:S(2)}) copy-start(f32[8,128]{1,0:T(8,128)} %get-tuple-element.30.own_ref) | copy-start | bytes 12292
  40.4 6.1 %collective-permute-start.6 = (f32[512,128]{1,0:T(8,128)S(1)}, f32[512,128]{1,0:T(8,128)S(1)}, u32[]{:S(2)}, u32[]{:S(2)}) collective-permute-start(f32[512,128]{1,0:T(8,128)S(1)} %get-tuple-element.38), channel_id=1, source_target_pairs={{4,8},{5,9},{6,10},{7,11},{12,16},{13,17},{14,18},{15,19},{20,24},... | collective-permute-start | bytes 786440 | tf_op jit(solution)/shard_map/ppermute | solution.py:527
  46.5 11.1 %collective-permute-start.8 = (f32[1032,128]{1,0:T(8,128)S(1)}, f32[1032,128]{1,0:T(8,128)S(1)}, u32[]{:S(2)}, u32[]{:S(2)}) collective-permute-start(f32[1032,128]{1,0:T(8,128)S(1)} %shard_map.105.refs_3_.states_ref), channel_id=1, source_target_pairs={{0,2},{1,3},{2,0},{3,1},{8,10},{9,11},{10,8},{11,9},{16,18},{17,19... | collective-permute-start | bytes 1585160 | tf_op jit(solution)/shard_map/ppermute | solution.py:527
  55.7 13.7 %collective-permute-start.7 = (f32[1032,128]{1,0:T(8,128)S(1)}, f32[1032,128]{1,0:T(8,128)S(1)}, u32[]{:S(2)}, u32[]{:S(2)}) collective-permute-start(f32[1032,128]{1,0:T(8,128)S(1)} %shard_map.105.refs_3_.states_ref), channel_id=1, source_target_pairs={{8,4},{9,5},{10,6},{11,7},{16,12},{17,13},{18,14},{19,15},{24,20},... | collective-permute-start | bytes 1585160 | tf_op jit(solution)/shard_map/ppermute | solution.py:527
  57.0 13.7 %collective-permute-start.11 = (f32[1032,128]{1,0:T(8,128)S(1)}, f32[1032,128]{1,0:T(8,128)S(1)}, u32[]{:S(2)}, u32[]{:S(2)}) collective-permute-start(f32[1032,128]{1,0:T(8,128)S(1)} %shard_map.105.refs_3_.states_ref), channel_id=1, source_target_pairs={{0,1},{1,0},{2,3},{3,2},{8,9},{9,8},{10,11},{11,10},{16,17},{17,16... | collective-permute-start | bytes 1585160 | tf_op jit(solution)/shard_map/ppermute | solution.py:527
  57.7 14.5 %collective-permute-start.14 = (f32[1032,128]{1,0:T(8,128)S(1)}, f32[1032,128]{1,0:T(8,128)S(1)}, u32[]{:S(2)}, u32[]{:S(2)}) collective-permute-start(f32[1032,128]{1,0:T(8,128)S(1)} %collective-permute-done.8.refs_5_), channel_id=1, source_target_pairs={{0,1},{1,0},{2,3},{3,2},{8,9},{9,8},{10,11},{11,10},{16,17},{17,16... | collective-permute-start | bytes 1585160 | tf_op jit(solution)/shard_map/ppermute | solution.py:527
  62.6 10.9 %collective-permute-start.10 = (f32[1032,128]{1,0:T(8,128)S(1)}, f32[1032,128]{1,0:T(8,128)S(1)}, u32[]{:S(2)}, u32[]{:S(2)}) collective-permute-start(f32[1032,128]{1,0:T(8,128)S(1)} %shard_map.105.refs_3_.states_ref), channel_id=1, source_target_pairs={{0,4},{1,5},{2,6},{3,7},{8,12},{9,13},{10,14},{11,15},{16,20},{17,... | collective-permute-start | bytes 1585160 | tf_op jit(solution)/shard_map/ppermute | solution.py:527
  63.9 15.5 %collective-permute-start.9 = (f32[1032,128]{1,0:T(8,128)S(1)}, f32[1032,128]{1,0:T(8,128)S(1)}, u32[]{:S(2)}, u32[]{:S(2)}) collective-permute-start(f32[1032,128]{1,0:T(8,128)S(1)} %collective-permute-done.8.refs_5_), channel_id=1, source_target_pairs={{8,4},{9,5},{10,6},{11,7},{16,12},{17,13},{18,14},{19,15},{24,20},... | collective-permute-start | bytes 1585160 | tf_op jit(solution)/shard_map/ppermute | solution.py:527
  69.4 14.2 %collective-permute-start.13 = (f32[1032,128]{1,0:T(8,128)S(1)}, f32[1032,128]{1,0:T(8,128)S(1)}, u32[]{:S(2)}, u32[]{:S(2)}) collective-permute-start(f32[1032,128]{1,0:T(8,128)S(1)} %collective-permute-done.8.refs_5_), channel_id=1, source_target_pairs={{0,4},{1,5},{2,6},{3,7},{8,12},{9,13},{10,14},{11,15},{16,20},{17,... | collective-permute-start | bytes 1585160 | tf_op jit(solution)/shard_map/ppermute | solution.py:527
  70.7 12.9 %collective-permute-start.12 = (f32[1032,128]{1,0:T(8,128)S(1)}, f32[1032,128]{1,0:T(8,128)S(1)}, u32[]{:S(2)}, u32[]{:S(2)}) collective-permute-start(f32[1032,128]{1,0:T(8,128)S(1)} %collective-permute-done.11.refs_4_), channel_id=1, source_target_pairs={{0,4},{1,5},{2,6},{3,7},{8,12},{9,13},{10,14},{11,15},{16,20},{17,... | collective-permute-start | bytes 1585160 | tf_op jit(solution)/shard_map/ppermute | solution.py:527
  72.2 11.5 %collective-permute-start.15 = (f32[1032,128]{1,0:T(8,128)S(1)}, f32[1032,128]{1,0:T(8,128)S(1)}, u32[]{:S(2)}, u32[]{:S(2)}) collective-permute-start(f32[1032,128]{1,0:T(8,128)S(1)} %collective-permute-done.14.refs_6_), channel_id=1, source_target_pairs={{0,4},{1,5},{2,6},{3,7},{8,12},{9,13},{10,14},{11,15},{16,20},{17,... | collective-permute-start | bytes 1585160 | tf_op jit(solution)/shard_map/ppermute | solution.py:527
  73.5 19.3 %collective-permute-start.16 = (f32[1032,128]{1,0:T(8,128)S(1)}, f32[1032,128]{1,0:T(8,128)S(1)}, u32[]{:S(2)}, u32[]{:S(2)}) collective-permute-start(f32[1032,128]{1,0:T(8,128)S(1)} %collective-permute-done.11.refs_4_), channel_id=1, source_target_pairs={{8,4},{9,5},{10,6},{11,7},{16,12},{17,13},{18,14},{19,15},{24,20},... | collective-permute-start | bytes 1585160 | tf_op jit(solution)/shard_map/ppermute | solution.py:527
  79.4 19.1 %collective-permute-start.17 = (f32[1032,128]{1,0:T(8,128)S(1)}, f32[1032,128]{1,0:T(8,128)S(1)}, u32[]{:S(2)}, u32[]{:S(2)}) collective-permute-start(f32[1032,128]{1,0:T(8,128)S(1)} %collective-permute-done.14.refs_6_), channel_id=1, source_target_pairs={{8,4},{9,5},{10,6},{11,7},{16,12},{17,13},{18,14},{19,15},{24,20},... | collective-permute-start | bytes 1585160 | tf_op jit(solution)/shard_map/ppermute | solution.py:527
  101.1 12.3 %collective-permute-start.19 = (f32[1032,128]{1,0:T(8,128)S(1)}, f32[1032,128]{1,0:T(8,128)S(1)}, u32[]{:S(2)}, u32[]{:S(2)}) collective-permute-start(f32[1032,128]{1,0:T(8,128)S(1)} %get-tuple-element.42.states_ref), channel_id=1, source_target_pairs={{4,0},{5,1},{6,2},{7,3},{12,8},{13,9},{14,10},{15,11},{20,16},{21,... | collective-permute-start | bytes 1585160 | tf_op jit(solution)/shard_map/ppermute | solution.py:527
  102.4 29.1 %collective-permute-start.25 = (f32[1032,128]{1,0:T(8,128)S(1)}, f32[1032,128]{1,0:T(8,128)S(1)}, u32[]{:S(2)}, u32[]{:S(2)}) collective-permute-start(f32[1032,128]{1,0:T(8,128)S(1)} %get-tuple-element.42.states_ref), channel_id=1, source_target_pairs={{4,8},{5,9},{6,10},{7,11},{12,16},{13,17},{14,18},{15,19},{20,24},... | collective-permute-start | bytes 1585160 | tf_op jit(solution)/shard_map/ppermute | solution.py:527
  103.7 10.4 %collective-permute-start.21 = (f32[1032,128]{1,0:T(8,128)S(1)}, f32[1032,128]{1,0:T(8,128)S(1)}, u32[]{:S(2)}, u32[]{:S(2)}) collective-permute-start(f32[1032,128]{1,0:T(8,128)S(1)} %get-tuple-element.47), channel_id=1, source_target_pairs={{4,0},{5,1},{6,2},{7,3},{12,8},{13,9},{14,10},{15,11},{20,16},{21,... | collective-permute-start | bytes 1585160 | tf_op jit(solution)/shard_map/ppermute | solution.py:527
  105.1 7.6 %collective-permute-start.23 = (f32[1024,128]{1,0:T(8,128)S(1)}, f32[1024,128]{1,0:T(8,128)S(1)}, u32[]{:S(2)}, u32[]{:S(2)}) collective-permute-start(f32[1024,128]{1,0:T(8,128)S(1)} %shard_map.113.refs_1_), channel_id=1, source_target_pairs={{0,2},{1,3},{2,0},{3,1},{8,10},{9,11},{10,8},{11,9},{16,18},{17,19... | collective-permute-start | bytes 1572872 | tf_op jit(solution)/shard_map/ppermute | solution.py:527
  105.8 4.5 %collective-permute-start.18 = (f32[408,128]{1,0:T(8,128)S(1)}, f32[408,128]{1,0:T(8,128)S(1)}, u32[]{:S(2)}, u32[]{:S(2)}) collective-permute-start(f32[408,128]{1,0:T(8,128)S(1)} %get-tuple-element.43), channel_id=1, source_target_pairs={{4,0},{5,1},{6,2},{7,3},{12,8},{13,9},{14,10},{15,11},{20,16},{21,... | collective-permute-start | bytes 626696 | tf_op jit(solution)/shard_map/ppermute | solution.py:527
  110.3 30.1 %collective-permute-start.20 = (f32[2064,128]{1,0:T(8,128)S(1)}, f32[2064,128]{1,0:T(8,128)S(1)}, u32[]{:S(2)}, u32[]{:S(2)}) collective-permute-start(f32[2064,128]{1,0:T(8,128)S(1)} %get-tuple-element.46), channel_id=1, source_target_pairs={{4,0},{5,1},{6,2},{7,3},{12,8},{13,9},{14,10},{15,11},{20,16},{21,... | collective-permute-start | bytes 3170312 | tf_op jit(solution)/shard_map/ppermute | solution.py:527
  112.7 27.9 %collective-permute-start.22 = (f32[1024,128]{1,0:T(8,128)S(1)}, f32[1024,128]{1,0:T(8,128)S(1)}, u32[]{:S(2)}, u32[]{:S(2)}) collective-permute-start(f32[1024,128]{1,0:T(8,128)S(1)} %shard_map.113.refs_1_), channel_id=1, source_target_pairs={{0,1},{1,0},{2,3},{3,2},{8,9},{9,8},{10,11},{11,10},{16,17},{17,16... | collective-permute-start | bytes 1572872 | tf_op jit(solution)/shard_map/ppermute | solution.py:527
  113.4 27.2 %collective-permute-start.24 = (f32[1024,128]{1,0:T(8,128)S(1)}, f32[1024,128]{1,0:T(8,128)S(1)}, u32[]{:S(2)}, u32[]{:S(2)}) collective-permute-start(f32[1024,128]{1,0:T(8,128)S(1)} %collective-permute-done.23.refs_3_), channel_id=1, source_target_pairs={{0,1},{1,0},{2,3},{3,2},{8,9},{9,8},{10,11},{11,10},{16,17},{17,16... | collective-permute-start | bytes 1572872 | tf_op jit(solution)/shard_map/ppermute | solution.py:527
  114.1 29.2 %collective-permute-start.26 = (f32[2064,128]{1,0:T(8,128)S(1)}, f32[2064,128]{1,0:T(8,128)S(1)}, u32[]{:S(2)}, u32[]{:S(2)}) collective-permute-start(f32[2064,128]{1,0:T(8,128)S(1)} %get-tuple-element.46), channel_id=1, source_target_pairs={{4,8},{5,9},{6,10},{7,11},{12,16},{13,17},{14,18},{15,19},{20,24},... | collective-permute-start | bytes 3170312 | tf_op jit(solution)/shard_map/ppermute | solution.py:527
  131.5 11.7 %collective-permute-start.27 = (f32[1032,128]{1,0:T(8,128)S(1)}, f32[1032,128]{1,0:T(8,128)S(1)}, u32[]{:S(2)}, u32[]{:S(2)}) collective-permute-start(f32[1032,128]{1,0:T(8,128)S(1)} %collective-permute-done.25.refs_5_), channel_id=1, source_target_pairs={{0,1},{1,0},{2,3},{3,2},{8,9},{9,8},{10,11},{11,10},{16,17},{17,16... | collective-permute-start | bytes 1585160 | tf_op jit(solution)/shard_map/ppermute | solution.py:527
  143.3 8.8 %collective-permute-start.28 = (f32[1024,128]{1,0:T(8,128)S(1)}, f32[1024,128]{1,0:T(8,128)S(1)}, u32[]{:S(2)}, u32[]{:S(2)}) collective-permute-start(f32[1024,128]{1,0:T(8,128)S(1)} %shard_map.115), channel_id=1, source_target_pairs={{0,4},{1,5},{2,6},{3,7},{8,12},{9,13},{10,14},{11,15},{16,20},{17,... | collective-permute-start | bytes 1572872 | tf_op jit(solution)/shard_map/ppermute | solution.py:527
  145.3 16.6 %collective-permute-start.29 = (f32[512,128]{1,0:T(8,128)S(1)}, f32[512,128]{1,0:T(8,128)S(1)}, u32[]{:S(2)}, u32[]{:S(2)}) collective-permute-start(f32[512,128]{1,0:T(8,128)S(1)} %get-tuple-element.53), channel_id=1, source_target_pairs={{8,4},{9,5},{10,6},{11,7},{16,12},{17,13},{18,14},{19,15},{24,20},... | collective-permute-start | bytes 786440 | tf_op jit(solution)/shard_map/ppermute | solution.py:527
  146.6 18.2 %collective-permute-start.30 = (f32[512,128]{1,0:T(8,128)S(1)}, f32[512,128]{1,0:T(8,128)S(1)}, u32[]{:S(2)}, u32[]{:S(2)}) collective-permute-start(f32[512,128]{1,0:T(8,128)S(1)} %get-tuple-element.54), channel_id=1, source_target_pairs={{8,4},{9,5},{10,6},{11,7},{16,12},{17,13},{18,14},{19,15},{24,20},... | collective-permute-start | bytes 786440 | tf_op jit(solution)/shard_map/ppermute | solution.py:527

commit v8 on v7

--- a/solution.py
+++ b/solution.py
@@ -436,10 +436,12 @@
         if second:
             for k in range(group):
                 ref, base = out.base(k)
-                start_value = bases[0][pl.ds(k * size, size)]
-                if base_count > 1:
-                    start_value = start_value + bases[1 + k][...]
-                ref[pl.ds(base, size)] = start_value
+                per = (base_count - 1) // group
+                for p in range(per):
+                    piece = size // per
+                    ref[pl.ds(base + p * piece, piece)] = (
+                        bases[0][pl.ds(k * size + p * piece, piece)] + bases[1 + k * per + p][...]
+                    )
                 ref[pl.ds(base + size, ROWS)] = tab_refs[0][k]
         else:
             offset = 0
@@ -653,10 +655,6 @@
     picks = [shift(value, 1, 1) for value in pick(first, 1, split_hop)]
     sums, tabs_odd = send(first, 1, 1, operators_odd)
     sums = [shift(value, -1, 1) for value in sums]
-    passed = shift(raw, -1, 1)
-    operators_even = call(
-        functools.partial(operators_kernel, slots, group, modes, 0), operator_shapes, limit, (couplings, passed)
-    )
     own_state = join([free_even], sums, picks, 0, operators_odd, 1)
 
     gathered = gather(own_state, 0)
@@ -664,13 +662,18 @@
     from_above = [shift(value, 1, 0) for value in gathered]
     free_even = gather(free_chain(gathered[0], 0, 2), 0)
     evens, odds = (0, 2, group // 2), (1, 2, group // 2)
-    states, _ = side("children", free_odd, from_below[::2], [tabs_odd], 1, operators_odd, span=evens)
+    states, _ = side("children", [], from_below[::2], [tabs_odd], 1, operators_odd, span=evens)
     states, _ = side("parents", [states], from_above, [tabs_odd], 1, operators_odd)
-    states = side("children", [states], from_below[1::2], [tabs_odd], 1, operators_odd, second=True, span=odds)
+    far_bases = [states, *free_odd]
+    states = side("children", far_bases, from_below[1::2], [tabs_odd], 1, operators_odd, second=True, span=odds)
 
     from_above = [shift(value, 1, 1) for value in states[:2]]
     from_above.append(neighbour(from_above[0], 0))
     from_below = [shift(value, -1, 1) for value in states]
+    passed = shift(raw, -1, 1)
+    operators_even = call(
+        functools.partial(operators_kernel, slots, group, modes, 0), operator_shapes, limit, (couplings, passed)
+    )
     last_odd = free(states[0], 1, 2)
     states, tabs_even = side("children", [], from_below, gathered, 0, operators_even)
     states = side("parents", [states, *free_even], from_above, [tabs_even], 0, operators_even, second=True)

time: 167 us -> 165 us (0.988)
  waiting for transfers between devices: 42.1 us -> 39.4 us
    ppermute x31, waiting for transfers between devices: 42.1 us -> 39.4 us  [permute(): return lax.ppermute(value, AXES, pairs)]
  transfers between devices with their start and end apart: 31 -> 31, of which waited for: 11 -> 10; matrix products, arithmetic and copies ran while one was open for 0% -> 0% of each run, Pallas kernels for 33% -> 34%
where the time goes in v8:
time: 165 us; the launch traced here: 164 us
  starting transfers between devices  62.5 us (38%)
  Pallas kernels  61.7 us (37%)
  waiting for transfers between devices  39.4 us (24%)
    ppermute x31, starting transfers between devices, permute(): return lax.ppermute(value, AXES, pairs)  62.5 us
    pallas_call x29, Pallas kernels, call(): pl.pallas_call(kernel, out_shape=out_shapes, in_specs=specs, out_specs=ja...  61.7 us
    ppermute x31, waiting for transfers between devices, permute(): return lax.ppermute(value, AXES, pairs)  39.4 us
  transfers between devices with their start and end apart: 31, of which 10 were waited for; matrix products, arithmetic and copies ran while one was open for 0% of the time, Pallas kernels for 34%

profile of v8, /device:TPU:3, one launch (start us, length us, event | category | flops | bytes accessed | tf_op | source)
XLA Modules:
  0.0 164.5 jit_solution(662078915042475803)
XLA Ops:
  0.0 2.0 %shard_map.91 = (f32[1160,128]{1,0:T(8,128)}, f32[8,128]{1,0:T(8,128)}) custom-call(s32[4]{0:T(128)} %live_ref.1, s32[4]{0:T(128)} %parent_ref.1, s32[4]{0:T(128)} %mode_ref.1, f32[4]{0:T(128)} %damping_ref.1, f32[4]{0:T(128)} %weight_ref.1, f32[2,2]{1,0:T(2,128)} %corr_ref.1, f32[1024,128]{1,0:T(8,128)} %bitcast.6, f32[256,128]{1,0:T(8,128)} %bitcast.3), custom_call_target="tpu_custom_call" | custom-call | flops 1100000000 | bytes 524288 | tf_op jit(solution)/shard_map/pallas_call | solution.py:500
  2.1 4.2 %collective-permute-start.1 = (f32[1160,128]{1,0:T(8,128)}, f32[1160,128]{1,0:T(8,128)S(1)}, u32[]{:S(2)}, u32[]{:S(2)}) collective-permute-start(f32[1160,128]{1,0:T(8,128)} %get-tuple-element.31.refs_0_.states_ref), channel_id=1, source_target_pairs={{4,6},{5,7},{6,4},{7,5},{12,14},{13,15},{14,12},{15,13},{20,22},{2... | collective-permute-start | bytes 1781768 | tf_op jit(solution)/shard_map/ppermute | solution.py:529
  6.3 3.2 %collective-permute-start = (f32[1160,128]{1,0:T(8,128)}, f32[1160,128]{1,0:T(8,128)S(1)}, u32[]{:S(2)}, u32[]{:S(2)}) collective-permute-start(f32[1160,128]{1,0:T(8,128)} %get-tuple-element.31.refs_0_.states_ref), channel_id=1, source_target_pairs={{4,5},{5,4},{6,7},{7,6},{12,13},{13,12},{14,15},{15,14},{20,21},{2... | collective-permute-start | bytes 1781768 | tf_op jit(solution)/shard_map/ppermute | solution.py:529
  9.5 2.1 %collective-permute-start.4 = (f32[8,128]{1,0:T(8,128)}, f32[8,128]{1,0:T(8,128)S(1)}, u32[]{:S(2)}, u32[]{:S(2)}) collective-permute-start(f32[8,128]{1,0:T(8,128)} %get-tuple-element.30.own_ref), channel_id=1, source_target_pairs={{4,0},{5,1},{6,2},{7,3},{8,4},{9,5},{10,6},{11,7},{12,8},{13,9},{1... | collective-permute-start | bytes 12296 | tf_op jit(solution)/shard_map/ppermute | solution.py:529
  11.6 0.7 shard_map.93
  12.3 4.2 %shard_map.100.refs_1_ = f32[512,128]{1,0:T(8,128)S(1)} custom-call(f32[1160,128]{1,0:T(8,128)S(1)} %copy-done, bf16[384,512]{1,0:T(8,128)(2,1)S(1)} %get-tuple-element.34.right_ref, bf16[128,1536]{1,0:T(8,128)(2,1)S(1)} %get-tuple-element.35.left_ref), custom_call_target="tpu_custom_call" | custom-call | flops 4950000128 | bytes 524288 | tf_op jit(solution)/shard_map/pallas_call | solution.py:500
  16.5 3.7 %collective-permute-done.1.refs_2_.states_ref = f32[1160,128]{1,0:T(8,128)S(1)} collective-permute-done((f32[1160,128]{1,0:T(8,128)}, f32[1160,128]{1,0:T(8,128)S(1)}, u32[]{:S(2)}, u32[]{:S(2)}) %collective-permute-start.1) | collective-permute-done | bytes 593952 | tf_op jit(solution)/shard_map/ppermute | solution.py:529
  20.3 2.6 %collective-permute-start.2 = (f32[1160,128]{1,0:T(8,128)S(1)}, f32[1160,128]{1,0:T(8,128)S(1)}, u32[]{:S(2)}, u32[]{:S(2)}) collective-permute-start(f32[1160,128]{1,0:T(8,128)S(1)} %collective-permute-done.1.refs_2_.states_ref), channel_id=1, source_target_pairs={{4,5},{5,4},{6,7},{7,6},{12,13},{13,12},{14,15},{15,14},{20,21},{2... | collective-permute-start | bytes 1781768 | tf_op jit(solution)/shard_map/ppermute | solution.py:529
  22.9 4.2 %shard_map.101.refs_2_ = f32[512,128]{1,0:T(8,128)S(1)} custom-call(f32[1160,128]{1,0:T(8,128)S(1)} %copy-done, bf16[384,512]{1,0:T(8,128)(2,1)S(1)} %get-tuple-element.34.right_ref, bf16[128,1536]{1,0:T(8,128)(2,1)S(1)} %get-tuple-element.35.left_ref), custom_call_target="tpu_custom_call" | custom-call | flops 4950000128 | bytes 524288 | tf_op jit(solution)/shard_map/pallas_call | solution.py:500
  27.1 0.0 copy-start.1
  27.1 4.2 %shard_map.104.refs_5_ = f32[512,128]{1,0:T(8,128)S(1)} custom-call(f32[1160,128]{1,0:T(8,128)S(1)} %collective-permute-done.1.refs_2_.states_ref, bf16[384,512]{1,0:T(8,128)(2,1)S(1)} %get-tuple-element.34.right_ref, bf16[128,1536]{1,0:T(8,128)(2,1)S(1)} %get-tuple-element.35.left_ref), custom_call_target="tpu_custom_call" | custom-call | flops 4950000128 | bytes 524288 | tf_op jit(solution)/shard_map/pallas_call | solution.py:500
  31.4 0.2 shard_map.92
  31.6 2.6 %shard_map.95 = (f32[1024,128]{1,0:T(8,128)S(1)}, f32[4,8,128]{2,1,0:T(8,128)S(1)}) custom-call(bf16[8,384,128]{2,1,0:T(8,128)(2,1)S(1)} %get-tuple-element.32.right_ref, bf16[8,128,384]{2,1,0:T(8,128)(2,1)S(1)} %get-tuple-element.33.left_ref, f32[1160,128]{1,0:T(8,128)S(1)} %copy-done, f32[1160,128]{1,0:T(8,128)S(1)} %collective-permute-done.refs_1_.states_ref, ...), custom_call_target="tpu_custom_call" | custom-call | flops 2200000000 | bytes 524288 | tf_op jit(solution)/shard_map/pallas_call | solution.py:500
  34.2 1.3 collective-permute-start.3
  35.6 0.8 shard_map.96
  36.4 1.3 collective-permute-start.5
  37.7 0.0 copy-start.3
  37.7 1.3 collective-permute-start.6
  39.0 4.2 %shard_map.105.refs_6_ = f32[512,128]{1,0:T(8,128)S(1)} custom-call(f32[1160,128]{1,0:T(8,128)S(1)} %collective-permute-done.1.refs_2_.states_ref, bf16[384,512]{1,0:T(8,128)(2,1)S(1)} %get-tuple-element.34.right_ref, bf16[128,1536]{1,0:T(8,128)(2,1)S(1)} %get-tuple-element.35.left_ref), custom_call_target="tpu_custom_call" | custom-call | flops 4950000128 | bytes 524288 | tf_op jit(solution)/shard_map/pallas_call | solution.py:500
  43.2 0.6 collective-permute-done.6.refs_3_
  43.8 0.7 collective-permute-start.8
  44.5 4.2 %shard_map.102.refs_3_ = f32[512,128]{1,0:T(8,128)S(1)} custom-call(f32[1160,128]{1,0:T(8,128)S(1)} %collective-permute-done.refs_1_.states_ref, bf16[384,512]{1,0:T(8,128)(2,1)S(1)} %get-tuple-element.34.right_ref, bf16[128,1536]{1,0:T(8,128)(2,1)S(1)} %get-tuple-element.35.left_ref), custom_call_target="tpu_custom_call" | custom-call | flops 4950000128 | bytes 524288 | tf_op jit(solution)/shard_map/pallas_call | solution.py:500
  48.7 4.2 %shard_map.103.refs_4_ = f32[512,128]{1,0:T(8,128)S(1)} custom-call(f32[1160,128]{1,0:T(8,128)S(1)} %collective-permute-done.refs_1_.states_ref, bf16[384,512]{1,0:T(8,128)(2,1)S(1)} %get-tuple-element.34.right_ref, bf16[128,1536]{1,0:T(8,128)(2,1)S(1)} %get-tuple-element.35.left_ref), custom_call_target="tpu_custom_call" | custom-call | flops 4950000128 | bytes 524288 | tf_op jit(solution)/shard_map/pallas_call | solution.py:500
  52.9 1.3 collective-permute-start.7
  54.2 0.7 collective-permute-start.11
  54.9 0.7 collective-permute-start.14
  55.6 4.2 %shard_map.106.refs_7_ = f32[512,128]{1,0:T(8,128)S(1)} custom-call(f32[1160,128]{1,0:T(8,128)S(1)} %collective-permute-done.2.refs_3_.states_ref, bf16[384,512]{1,0:T(8,128)(2,1)S(1)} %get-tuple-element.34.right_ref, bf16[128,1536]{1,0:T(8,128)(2,1)S(1)} %get-tuple-element.35.left_ref), custom_call_target="tpu_custom_call" | custom-call | flops 4950000128 | bytes 524288 | tf_op jit(solution)/shard_map/pallas_call | solution.py:500
  59.8 1.3 collective-permute-start.10
  61.1 1.3 collective-permute-start.9
  62.4 4.2 %shard_map.107.refs_8_ = f32[512,128]{1,0:T(8,128)S(1)} custom-call(f32[1160,128]{1,0:T(8,128)S(1)} %collective-permute-done.2.refs_3_.states_ref, bf16[384,512]{1,0:T(8,128)(2,1)S(1)} %get-tuple-element.34.right_ref, bf16[128,1536]{1,0:T(8,128)(2,1)S(1)} %get-tuple-element.35.left_ref), custom_call_target="tpu_custom_call" | custom-call | flops 4950000128 | bytes 524288 | tf_op jit(solution)/shard_map/pallas_call | solution.py:500
  66.6 1.3 collective-permute-start.13
  68.0 1.5 collective-permute-start.12
  69.5 1.3 collective-permute-start.15
  70.8 1.3 collective-permute-start.16
  72.1 5.2 %collective-permute-done.9.refs_1_ = f32[1032,128]{1,0:T(8,128)S(1)} collective-permute-done((f32[1032,128]{1,0:T(8,128)S(1)}, f32[1032,128]{1,0:T(8,128)S(1)}, u32[]{:S(2)}, u32[]{:S(2)}) %collective-permute-start.9) | collective-permute-done | bytes 528416 | tf_op jit(solution)/shard_map/ppermute | solution.py:529
  77.3 1.3 collective-permute-start.17
  78.6 3.0 %shard_map.98 = (f32[4096,128]{1,0:T(8,128)S(1)}, f32[4,8,128]{2,1,0:T(8,128)}) custom-call(bf16[8,384,128]{2,1,0:T(8,128)(2,1)S(1)} %get-tuple-element.32.right_ref, bf16[8,128,384]{2,1,0:T(8,128)(2,1)S(1)} %get-tuple-element.33.left_ref, f32[1032,128]{1,0:T(8,128)S(1)} %collective-permute-done.7.refs_0_, f32[1032,128]{1,0:T(8,128)S(1)} %collective-permute-done.9.refs_1_, ...), custom_call_target="tpu_custom_call" | custom-call | flops 3300000000 | bytes 524288 | tf_op jit(solution)/shard_map/pallas_call | solution.py:500
  81.6 4.4 %shard_map.99 = (f32[4096,128]{1,0:T(8,128)S(1)}, f32[4,8,128]{2,1,0:T(8,128)}) custom-call(bf16[8,384,128]{2,1,0:T(8,128)(2,1)S(1)} %get-tuple-element.32.right_ref, bf16[8,128,384]{2,1,0:T(8,128)(2,1)S(1)} %get-tuple-element.33.left_ref, f32[4096,128]{1,0:T(8,128)S(1)} %get-tuple-element.40.refs_0_, f32[1032,128]{1,0:T(8,128)S(1)} %collective-permute-done.10.refs_1_, ...), custom_call_target="tpu_custom_call" | custom-call | flops 3300000000 | bytes 524288 | tf_op jit(solution)/shard_map/pallas_call | solution.py:500
  86.0 4.8 %collective-permute-done.16.refs_9_ = f32[1032,128]{1,0:T(8,128)S(1)} collective-permute-done((f32[1032,128]{1,0:T(8,128)S(1)}, f32[1032,128]{1,0:T(8,128)S(1)}, u32[]{:S(2)}, u32[]{:S(2)}) %collective-permute-start.16) | collective-permute-done | bytes 528416 | tf_op jit(solution)/shard_map/ppermute | solution.py:529
  90.8 5.7 %collective-permute-done.17.refs_10_ = f32[1032,128]{1,0:T(8,128)S(1)} collective-permute-done((f32[1032,128]{1,0:T(8,128)S(1)}, f32[1032,128]{1,0:T(8,128)S(1)}, u32[]{:S(2)}, u32[]{:S(2)}) %collective-permute-start.17) | collective-permute-done | bytes 528416 | tf_op jit(solution)/shard_map/ppermute | solution.py:529
  96.5 2.7 %shard_map.108 = (f32[1032,128]{1,0:T(8,128)S(1)}, f32[2064,128]{1,0:T(8,128)S(1)}, f32[1032,128]{1,0:T(8,128)S(1)}) custom-call(bf16[8,384,128]{2,1,0:T(8,128)(2,1)S(1)} %get-tuple-element.32.right_ref, bf16[8,128,384]{2,1,0:T(8,128)(2,1)S(1)} %get-tuple-element.33.left_ref, f32[4096,128]{1,0:T(8,128)S(1)} %get-tuple-element.41.refs_0_, ...), custom_call_target="tpu_custom_call" | custom-call | flops 3300000000 | bytes 524288 | tf_op jit(solution)/shard_map/pallas_call | solution.py:500
  99.2 1.3 collective-permute-start.19
  100.5 1.3 collective-permute-start.25
  101.8 1.3 collective-permute-start.21
  103.2 0.7 collective-permute-start.23
  103.9 3.5 %collective-permute-start.18 = (f32[408,128]{1,0:T(8,128)S(1)}, f32[408,128]{1,0:T(8,128)S(1)}, u32[]{:S(2)}, u32[]{:S(2)}) collective-permute-start(f32[408,128]{1,0:T(8,128)S(1)} %get-tuple-element.43), channel_id=1, source_target_pairs={{4,0},{5,1},{6,2},{7,3},{12,8},{13,9},{14,10},{15,11},{20,16},{21,... | collective-permute-start | bytes 626696 | tf_op jit(solution)/shard_map/ppermute | solution.py:529
  107.4 1.1 collective-permute-done.18.refs_0_
  108.5 2.3 %collective-permute-start.20 = (f32[2064,128]{1,0:T(8,128)S(1)}, f32[2064,128]{1,0:T(8,128)S(1)}, u32[]{:S(2)}, u32[]{:S(2)}) collective-permute-start(f32[2064,128]{1,0:T(8,128)S(1)} %get-tuple-element.46), channel_id=1, source_target_pairs={{4,0},{5,1},{6,2},{7,3},{12,8},{13,9},{14,10},{15,11},{20,16},{21,... | collective-permute-start | bytes 3170312 | tf_op jit(solution)/shard_map/ppermute | solution.py:529
  110.9 0.7 collective-permute-start.22
  111.6 0.7 collective-permute-start.24
  112.3 17.4 %collective-permute-start.26 = (f32[2064,128]{1,0:T(8,128)S(1)}, f32[2064,128]{1,0:T(8,128)S(1)}, u32[]{:S(2)}, u32[]{:S(2)}) collective-permute-start(f32[2064,128]{1,0:T(8,128)S(1)} %get-tuple-element.46), channel_id=1, source_target_pairs={{4,8},{5,9},{6,10},{7,11},{12,16},{13,17},{14,18},{15,19},{20,24},... | collective-permute-start | bytes 3170312 | tf_op jit(solution)/shard_map/ppermute | solution.py:529
  129.7 0.7 collective-permute-start.27
  130.4 8.2 %shard_map.109.refs_0_ = f32[1024,128]{1,0:T(8,128)S(1)} custom-call(f32[1032,128]{1,0:T(8,128)S(1)} %get-tuple-element.42.states_ref, bf16[384,512]{1,0:T(8,128)(2,1)S(1)} %get-tuple-element.34.right_ref, bf16[128,1536]{1,0:T(8,128)(2,1)S(1)} %get-tuple-element.35.left_ref), custom_call_target="tpu_custom_call" | custom-call | flops 9900000256 | bytes 524288 | tf_op jit(solution)/shard_map/pallas_call | solution.py:500
  138.6 0.1 shard_map.111
  138.7 2.7 %collective-permute-done.26.refs_6_ = f32[2064,128]{1,0:T(8,128)S(1)} collective-permute-done((f32[2064,128]{1,0:T(8,128)S(1)}, f32[2064,128]{1,0:T(8,128)S(1)}, u32[]{:S(2)}, u32[]{:S(2)}) %collective-permute-start.26) | collective-permute-done | bytes 1056800 | tf_op jit(solution)/shard_map/ppermute | solution.py:529
  141.5 1.3 collective-permute-start.28
  142.8 0.7 shard_map.118
  143.5 1.3 collective-permute-start.29
  144.8 1.3 collective-permute-start.30
  146.1 4.1 %collective-permute-done.28.refs_1_ = f32[1024,128]{1,0:T(8,128)S(1)} collective-permute-done((f32[1024,128]{1,0:T(8,128)S(1)}, f32[1024,128]{1,0:T(8,128)S(1)}, u32[]{:S(2)}, u32[]{:S(2)}) %collective-permute-start.28) | collective-permute-done | bytes 524320 | tf_op jit(solution)/shard_map/ppermute | solution.py:529
  150.2 1.1 shard_map.116.refs_0_
  151.3 8.7 %collective-permute-done.29.refs_2_ = f32[512,128]{1,0:T(8,128)S(1)} collective-permute-done((f32[512,128]{1,0:T(8,128)S(1)}, f32[512,128]{1,0:T(8,128)S(1)}, u32[]{:S(2)}, u32[]{:S(2)}) %collective-permute-start.29) | collective-permute-done | bytes 262176 | tf_op jit(solution)/shard_map/ppermute | solution.py:529
  160.1 2.8 %collective-permute-done.30.refs_3_ = f32[512,128]{1,0:T(8,128)S(1)} collective-permute-done((f32[512,128]{1,0:T(8,128)S(1)}, f32[512,128]{1,0:T(8,128)S(1)}, u32[]{:S(2)}, u32[]{:S(2)}) %collective-permute-start.30) | collective-permute-done | bytes 262176 | tf_op jit(solution)/shard_map/ppermute | solution.py:529
  162.9 1.5 shard_map.119
  (35 shorter events, 0.2 us)
Async XLA Ops:
  0.0 11.5 %copy-start.2 = (f32[128,128]{1,0:T(8,128)S(1)}, f32[128,128]{1,0:T(8,128)}, u32[]{:S(2)}) copy-start(f32[128,128]{1,0:T(8,128)} %ham_ref.1) | copy-start | bytes 196612
  2.1 18.2 %collective-permute-start.1 = (f32[1160,128]{1,0:T(8,128)}, f32[1160,128]{1,0:T(8,128)S(1)}, u32[]{:S(2)}, u32[]{:S(2)}) collective-permute-start(f32[1160,128]{1,0:T(8,128)} %get-tuple-element.31.refs_0_.states_ref), channel_id=1, source_target_pairs={{4,6},{5,7},{6,4},{7,5},{12,14},{13,15},{14,12},{15,13},{20,22},{2... | collective-permute-start | bytes 1781768 | tf_op jit(solution)/shard_map/ppermute | solution.py:529
  6.3 25.1 %collective-permute-start = (f32[1160,128]{1,0:T(8,128)}, f32[1160,128]{1,0:T(8,128)S(1)}, u32[]{:S(2)}, u32[]{:S(2)}) collective-permute-start(f32[1160,128]{1,0:T(8,128)} %get-tuple-element.31.refs_0_.states_ref), channel_id=1, source_target_pairs={{4,5},{5,4},{6,7},{7,6},{12,13},{13,12},{14,15},{15,14},{20,21},{2... | collective-permute-start | bytes 1781768 | tf_op jit(solution)/shard_map/ppermute | solution.py:529
  9.5 2.8 %copy-start = (f32[1160,128]{1,0:T(8,128)S(1)}, f32[1160,128]{1,0:T(8,128)}, u32[]{:S(2)}) copy-start(f32[1160,128]{1,0:T(8,128)} %get-tuple-element.31.refs_0_.states_ref) | copy-start | bytes 1781764
  9.5 26.1 %collective-permute-start.4 = (f32[8,128]{1,0:T(8,128)}, f32[8,128]{1,0:T(8,128)S(1)}, u32[]{:S(2)}, u32[]{:S(2)}) collective-permute-start(f32[8,128]{1,0:T(8,128)} %get-tuple-element.30.own_ref), channel_id=1, source_target_pairs={{4,0},{5,1},{6,2},{7,3},{8,4},{9,5},{10,6},{11,7},{12,8},{13,9},{1... | collective-permute-start | bytes 12296 | tf_op jit(solution)/shard_map/ppermute | solution.py:529
  20.3 11.1 %collective-permute-start.2 = (f32[1160,128]{1,0:T(8,128)S(1)}, f32[1160,128]{1,0:T(8,128)S(1)}, u32[]{:S(2)}, u32[]{:S(2)}) collective-permute-start(f32[1160,128]{1,0:T(8,128)S(1)} %collective-permute-done.1.refs_2_.states_ref), channel_id=1, source_target_pairs={{4,5},{5,4},{6,7},{7,6},{12,13},{13,12},{14,15},{15,14},{20,21},{2... | collective-permute-start | bytes 1781768 | tf_op jit(solution)/shard_map/ppermute | solution.py:529
  27.1 4.2 %copy-start.1 = (f32[2,128,128]{2,1,0:T(8,128)S(1)}, f32[2,128,128]{2,1,0:T(8,128)}, u32[]{:S(2)}) copy-start(f32[2,128,128]{2,1,0:T(8,128)} %param.14) | copy-start | bytes 393220
  34.2 9.5 %collective-permute-start.3 = (f32[1024,128]{1,0:T(8,128)S(1)}, f32[1024,128]{1,0:T(8,128)S(1)}, u32[]{:S(2)}, u32[]{:S(2)}) collective-permute-start(f32[1024,128]{1,0:T(8,128)S(1)} %get-tuple-element.36), channel_id=1, source_target_pairs={{4,0},{5,1},{6,2},{7,3},{12,8},{13,9},{14,10},{15,11},{20,16},{21,... | collective-permute-start | bytes 1572872 | tf_op jit(solution)/shard_map/ppermute | solution.py:529
  36.4 6.8 %collective-permute-start.5 = (f32[512,128]{1,0:T(8,128)S(1)}, f32[512,128]{1,0:T(8,128)S(1)}, u32[]{:S(2)}, u32[]{:S(2)}) collective-permute-start(f32[512,128]{1,0:T(8,128)S(1)} %get-tuple-element.37), channel_id=1, source_target_pairs={{4,8},{5,9},{6,10},{7,11},{12,16},{13,17},{14,18},{15,19},{20,24},... | collective-permute-start | bytes 786440 | tf_op jit(solution)/shard_map/ppermute | solution.py:529
  37.7 6.1 %copy-start.3 = (f32[8,128]{1,0:T(8,128)S(1)}, f32[8,128]{1,0:T(8,128)}, u32[]{:S(2)}) copy-start(f32[8,128]{1,0:T(8,128)} %get-tuple-element.30.own_ref) | copy-start | bytes 12292
  37.7 6.1 %collective-permute-start.6 = (f32[512,128]{1,0:T(8,128)S(1)}, f32[512,128]{1,0:T(8,128)S(1)}, u32[]{:S(2)}, u32[]{:S(2)}) collective-permute-start(f32[512,128]{1,0:T(8,128)S(1)} %get-tuple-element.38), channel_id=1, source_target_pairs={{4,8},{5,9},{6,10},{7,11},{12,16},{13,17},{14,18},{15,19},{20,24},... | collective-permute-start | bytes 786440 | tf_op jit(solution)/shard_map/ppermute | solution.py:529
  43.8 11.1 %collective-permute-start.8 = (f32[1032,128]{1,0:T(8,128)S(1)}, f32[1032,128]{1,0:T(8,128)S(1)}, u32[]{:S(2)}, u32[]{:S(2)}) collective-permute-start(f32[1032,128]{1,0:T(8,128)S(1)} %shard_map.97.refs_3_.states_ref), channel_id=1, source_target_pairs={{0,2},{1,3},{2,0},{3,1},{8,10},{9,11},{10,8},{11,9},{16,18},{17,19... | collective-permute-start | bytes 1585160 | tf_op jit(solution)/shard_map/ppermute | solution.py:529
  52.9 13.7 %collective-permute-start.7 = (f32[1032,128]{1,0:T(8,128)S(1)}, f32[1032,128]{1,0:T(8,128)S(1)}, u32[]{:S(2)}, u32[]{:S(2)}) collective-permute-start(f32[1032,128]{1,0:T(8,128)S(1)} %shard_map.97.refs_3_.states_ref), channel_id=1, source_target_pairs={{8,4},{9,5},{10,6},{11,7},{16,12},{17,13},{18,14},{19,15},{24,20},... | collective-permute-start | bytes 1585160 | tf_op jit(solution)/shard_map/ppermute | solution.py:529
  54.2 13.8 %collective-permute-start.11 = (f32[1032,128]{1,0:T(8,128)S(1)}, f32[1032,128]{1,0:T(8,128)S(1)}, u32[]{:S(2)}, u32[]{:S(2)}) collective-permute-start(f32[1032,128]{1,0:T(8,128)S(1)} %shard_map.97.refs_3_.states_ref), channel_id=1, source_target_pairs={{0,1},{1,0},{2,3},{3,2},{8,9},{9,8},{10,11},{11,10},{16,17},{17,16... | collective-permute-start | bytes 1585160 | tf_op jit(solution)/shard_map/ppermute | solution.py:529
  54.9 14.5 %collective-permute-start.14 = (f32[1032,128]{1,0:T(8,128)S(1)}, f32[1032,128]{1,0:T(8,128)S(1)}, u32[]{:S(2)}, u32[]{:S(2)}) collective-permute-start(f32[1032,128]{1,0:T(8,128)S(1)} %collective-permute-done.8.refs_5_), channel_id=1, source_target_pairs={{0,1},{1,0},{2,3},{3,2},{8,9},{9,8},{10,11},{11,10},{16,17},{17,16... | collective-permute-start | bytes 1585160 | tf_op jit(solution)/shard_map/ppermute | solution.py:529
  59.8 11.0 %collective-permute-start.10 = (f32[1032,128]{1,0:T(8,128)S(1)}, f32[1032,128]{1,0:T(8,128)S(1)}, u32[]{:S(2)}, u32[]{:S(2)}) collective-permute-start(f32[1032,128]{1,0:T(8,128)S(1)} %shard_map.97.refs_3_.states_ref), channel_id=1, source_target_pairs={{0,4},{1,5},{2,6},{3,7},{8,12},{9,13},{10,14},{11,15},{16,20},{17,... | collective-permute-start | bytes 1585160 | tf_op jit(solution)/shard_map/ppermute | solution.py:529
  61.1 16.2 %collective-permute-start.9 = (f32[1032,128]{1,0:T(8,128)S(1)}, f32[1032,128]{1,0:T(8,128)S(1)}, u32[]{:S(2)}, u32[]{:S(2)}) collective-permute-start(f32[1032,128]{1,0:T(8,128)S(1)} %collective-permute-done.8.refs_5_), channel_id=1, source_target_pairs={{8,4},{9,5},{10,6},{11,7},{16,12},{17,13},{18,14},{19,15},{24,20},... | collective-permute-start | bytes 1585160 | tf_op jit(solution)/shard_map/ppermute | solution.py:529
  66.6 14.9 %collective-permute-start.13 = (f32[1032,128]{1,0:T(8,128)S(1)}, f32[1032,128]{1,0:T(8,128)S(1)}, u32[]{:S(2)}, u32[]{:S(2)}) collective-permute-start(f32[1032,128]{1,0:T(8,128)S(1)} %collective-permute-done.8.refs_5_), channel_id=1, source_target_pairs={{0,4},{1,5},{2,6},{3,7},{8,12},{9,13},{10,14},{11,15},{16,20},{17,... | collective-permute-start | bytes 1585160 | tf_op jit(solution)/shard_map/ppermute | solution.py:529
  68.0 13.6 %collective-permute-start.12 = (f32[1032,128]{1,0:T(8,128)S(1)}, f32[1032,128]{1,0:T(8,128)S(1)}, u32[]{:S(2)}, u32[]{:S(2)}) collective-permute-start(f32[1032,128]{1,0:T(8,128)S(1)} %collective-permute-done.11.refs_4_), channel_id=1, source_target_pairs={{0,4},{1,5},{2,6},{3,7},{8,12},{9,13},{10,14},{11,15},{16,20},{17,... | collective-permute-start | bytes 1585160 | tf_op jit(solution)/shard_map/ppermute | solution.py:529
  69.5 12.1 %collective-permute-start.15 = (f32[1032,128]{1,0:T(8,128)S(1)}, f32[1032,128]{1,0:T(8,128)S(1)}, u32[]{:S(2)}, u32[]{:S(2)}) collective-permute-start(f32[1032,128]{1,0:T(8,128)S(1)} %collective-permute-done.14.refs_6_), channel_id=1, source_target_pairs={{0,4},{1,5},{2,6},{3,7},{8,12},{9,13},{10,14},{11,15},{16,20},{17,... | collective-permute-start | bytes 1585160 | tf_op jit(solution)/shard_map/ppermute | solution.py:529
  70.8 20.0 %collective-permute-start.16 = (f32[1032,128]{1,0:T(8,128)S(1)}, f32[1032,128]{1,0:T(8,128)S(1)}, u32[]{:S(2)}, u32[]{:S(2)}) collective-permute-start(f32[1032,128]{1,0:T(8,128)S(1)} %collective-permute-done.11.refs_4_), channel_id=1, source_target_pairs={{8,4},{9,5},{10,6},{11,7},{16,12},{17,13},{18,14},{19,15},{24,20},... | collective-permute-start | bytes 1585160 | tf_op jit(solution)/shard_map/ppermute | solution.py:529
  77.3 19.1 %collective-permute-start.17 = (f32[1032,128]{1,0:T(8,128)S(1)}, f32[1032,128]{1,0:T(8,128)S(1)}, u32[]{:S(2)}, u32[]{:S(2)}) collective-permute-start(f32[1032,128]{1,0:T(8,128)S(1)} %collective-permute-done.14.refs_6_), channel_id=1, source_target_pairs={{8,4},{9,5},{10,6},{11,7},{16,12},{17,13},{18,14},{19,15},{24,20},... | collective-permute-start | bytes 1585160 | tf_op jit(solution)/shard_map/ppermute | solution.py:529
  99.2 12.4 %collective-permute-start.19 = (f32[1032,128]{1,0:T(8,128)S(1)}, f32[1032,128]{1,0:T(8,128)S(1)}, u32[]{:S(2)}, u32[]{:S(2)}) collective-permute-start(f32[1032,128]{1,0:T(8,128)S(1)} %get-tuple-element.42.states_ref), channel_id=1, source_target_pairs={{4,0},{5,1},{6,2},{7,3},{12,8},{13,9},{14,10},{15,11},{20,16},{21,... | collective-permute-start | bytes 1585160 | tf_op jit(solution)/shard_map/ppermute | solution.py:529
  100.5 29.2 %collective-permute-start.25 = (f32[1032,128]{1,0:T(8,128)S(1)}, f32[1032,128]{1,0:T(8,128)S(1)}, u32[]{:S(2)}, u32[]{:S(2)}) collective-permute-start(f32[1032,128]{1,0:T(8,128)S(1)} %get-tuple-element.42.states_ref), channel_id=1, source_target_pairs={{4,8},{5,9},{6,10},{7,11},{12,16},{13,17},{14,18},{15,19},{20,24},... | collective-permute-start | bytes 1585160 | tf_op jit(solution)/shard_map/ppermute | solution.py:529
  101.8 10.5 %collective-permute-start.21 = (f32[1032,128]{1,0:T(8,128)S(1)}, f32[1032,128]{1,0:T(8,128)S(1)}, u32[]{:S(2)}, u32[]{:S(2)}) collective-permute-start(f32[1032,128]{1,0:T(8,128)S(1)} %get-tuple-element.47), channel_id=1, source_target_pairs={{4,0},{5,1},{6,2},{7,3},{12,8},{13,9},{14,10},{15,11},{20,16},{21,... | collective-permute-start | bytes 1585160 | tf_op jit(solution)/shard_map/ppermute | solution.py:529
  103.2 7.7 %collective-permute-start.23 = (f32[1024,128]{1,0:T(8,128)S(1)}, f32[1024,128]{1,0:T(8,128)S(1)}, u32[]{:S(2)}, u32[]{:S(2)}) collective-permute-start(f32[1024,128]{1,0:T(8,128)S(1)} %shard_map.113.refs_1_), channel_id=1, source_target_pairs={{0,2},{1,3},{2,0},{3,1},{8,10},{9,11},{10,8},{11,9},{16,18},{17,19... | collective-permute-start | bytes 1572872 | tf_op jit(solution)/shard_map/ppermute | solution.py:529
  103.9 4.6 %collective-permute-start.18 = (f32[408,128]{1,0:T(8,128)S(1)}, f32[408,128]{1,0:T(8,128)S(1)}, u32[]{:S(2)}, u32[]{:S(2)}) collective-permute-start(f32[408,128]{1,0:T(8,128)S(1)} %get-tuple-element.43), channel_id=1, source_target_pairs={{4,0},{5,1},{6,2},{7,3},{12,8},{13,9},{14,10},{15,11},{20,16},{21,... | collective-permute-start | bytes 626696 | tf_op jit(solution)/shard_map/ppermute | solution.py:529
  108.5 30.1 %collective-permute-start.20 = (f32[2064,128]{1,0:T(8,128)S(1)}, f32[2064,128]{1,0:T(8,128)S(1)}, u32[]{:S(2)}, u32[]{:S(2)}) collective-permute-start(f32[2064,128]{1,0:T(8,128)S(1)} %get-tuple-element.46), channel_id=1, source_target_pairs={{4,0},{5,1},{6,2},{7,3},{12,8},{13,9},{14,10},{15,11},{20,16},{21,... | collective-permute-start | bytes 3170312 | tf_op jit(solution)/shard_map/ppermute | solution.py:529
  110.9 27.8 %collective-permute-start.22 = (f32[1024,128]{1,0:T(8,128)S(1)}, f32[1024,128]{1,0:T(8,128)S(1)}, u32[]{:S(2)}, u32[]{:S(2)}) collective-permute-start(f32[1024,128]{1,0:T(8,128)S(1)} %shard_map.113.refs_1_), channel_id=1, source_target_pairs={{0,1},{1,0},{2,3},{3,2},{8,9},{9,8},{10,11},{11,10},{16,17},{17,16... | collective-permute-start | bytes 1572872 | tf_op jit(solution)/shard_map/ppermute | solution.py:529
  111.6 27.1 %collective-permute-start.24 = (f32[1024,128]{1,0:T(8,128)S(1)}, f32[1024,128]{1,0:T(8,128)S(1)}, u32[]{:S(2)}, u32[]{:S(2)}) collective-permute-start(f32[1024,128]{1,0:T(8,128)S(1)} %collective-permute-done.23.refs_3_), channel_id=1, source_target_pairs={{0,1},{1,0},{2,3},{3,2},{8,9},{9,8},{10,11},{11,10},{16,17},{17,16... | collective-permute-start | bytes 1572872 | tf_op jit(solution)/shard_map/ppermute | solution.py:529
  112.3 29.1 %collective-permute-start.26 = (f32[2064,128]{1,0:T(8,128)S(1)}, f32[2064,128]{1,0:T(8,128)S(1)}, u32[]{:S(2)}, u32[]{:S(2)}) collective-permute-start(f32[2064,128]{1,0:T(8,128)S(1)} %get-tuple-element.46), channel_id=1, source_target_pairs={{4,8},{5,9},{6,10},{7,11},{12,16},{13,17},{14,18},{15,19},{20,24},... | collective-permute-start | bytes 3170312 | tf_op jit(solution)/shard_map/ppermute | solution.py:529
  129.7 9.0 %collective-permute-start.27 = (f32[1032,128]{1,0:T(8,128)S(1)}, f32[1032,128]{1,0:T(8,128)S(1)}, u32[]{:S(2)}, u32[]{:S(2)}) collective-permute-start(f32[1032,128]{1,0:T(8,128)S(1)} %collective-permute-done.25.refs_5_), channel_id=1, source_target_pairs={{0,1},{1,0},{2,3},{3,2},{8,9},{9,8},{10,11},{11,10},{16,17},{17,16... | collective-permute-start | bytes 1585160 | tf_op jit(solution)/shard_map/ppermute | solution.py:529
  141.5 8.7 %collective-permute-start.28 = (f32[1024,128]{1,0:T(8,128)S(1)}, f32[1024,128]{1,0:T(8,128)S(1)}, u32[]{:S(2)}, u32[]{:S(2)}) collective-permute-start(f32[1024,128]{1,0:T(8,128)S(1)} %shard_map.115), channel_id=1, source_target_pairs={{0,4},{1,5},{2,6},{3,7},{8,12},{9,13},{10,14},{11,15},{16,20},{17,... | collective-permute-start | bytes 1572872 | tf_op jit(solution)/shard_map/ppermute | solution.py:529
  143.5 16.6 %collective-permute-start.29 = (f32[512,128]{1,0:T(8,128)S(1)}, f32[512,128]{1,0:T(8,128)S(1)}, u32[]{:S(2)}, u32[]{:S(2)}) collective-permute-start(f32[512,128]{1,0:T(8,128)S(1)} %get-tuple-element.53), channel_id=1, source_target_pairs={{8,4},{9,5},{10,6},{11,7},{16,12},{17,13},{18,14},{19,15},{24,20},... | collective-permute-start | bytes 786440 | tf_op jit(solution)/shard_map/ppermute | solution.py:529
  144.8 18.1 %collective-permute-start.30 = (f32[512,128]{1,0:T(8,128)S(1)}, f32[512,128]{1,0:T(8,128)S(1)}, u32[]{:S(2)}, u32[]{:S(2)}) collective-permute-start(f32[512,128]{1,0:T(8,128)S(1)} %get-tuple-element.54), channel_id=1, source_target_pairs={{8,4},{9,5},{10,6},{11,7},{16,12},{17,13},{18,14},{19,15},{24,20},... | collective-permute-start | bytes 786440 | tf_op jit(solution)/shard_map/ppermute | solution.py:529

commit v9 on v8

--- a/solution.py
+++ b/solution.py
@@ -528,13 +528,13 @@
     def permute(value, pairs):
         return lax.ppermute(value, AXES, pairs)
 
-    def gather(value, parity):
+    def gather(value, parity, distances=None):
         held = {0: value}
-        for k in order:
+        for k in distances or order:
             step = k & -k
             pairs = [(place(d, m), place(d, m ^ step)) for d in range(parity, depths, 2) for m in ranks]
             held[k] = permute(held[k ^ step], pairs)
-        return [held[k] for k in ranks]
+        return held if distances else [held[k] for k in ranks]
 
     def shift(value, step, parity=None):
         pairs = [
@@ -660,7 +660,8 @@
     gathered = gather(own_state, 0)
     from_below = [shift(value, -1, 0) for value in gathered]
     from_above = [shift(value, 1, 0) for value in gathered]
-    free_even = gather(free_chain(gathered[0], 0, 2), 0)
+    evolved = gather(free_chain(gathered[0], 0, 2), 0, [k for k in order if k & (k - 1) == 0])
+    free_even = [evolved[k] if k in evolved else free_chain(gathered[k], 0, 2) for k in ranks]
     evens, odds = (0, 2, group // 2), (1, 2, group // 2)
     states, _ = side("children", [], from_below[::2], [tabs_odd], 1, operators_odd, span=evens)
     states, _ = side("parents", [states], from_above, [tabs_odd], 1, operators_odd)

time: 165 us -> 157 us (0.952)
  starting transfers between devices: 62.5 us -> 52 us
  waiting for transfers between devices: 39.4 us -> 41.9 us
    ppermute x31 -> x30, starting transfers between devices: 62.5 us -> 52 us  [permute(): return lax.ppermute(value, AXES, pairs)]
    ppermute x31 -> x30, waiting for transfers between devices: 39.4 us -> 41.9 us  [permute(): return lax.ppermute(value, AXES, pairs)]
    pallas_call x29 -> x31, Pallas kernels: 61.7 us -> 61.7 us  [call(): pl.pallas_call(kernel, out_shape=out_shapes, in_specs=specs, out_specs=ja...]
  transfers between devices with their start and end apart: 31 -> 30, of which waited for: 10 -> 8; matrix products, arithmetic and copies ran while one was open for 0% -> 0% of each run, Pallas kernels for 34% -> 37%
where the time goes in v9:
time: 157 us
  Pallas kernels  61.7 us (39%)
  starting transfers between devices  52 us (33%)
  waiting for transfers between devices  41.9 us (27%)
    pallas_call x31, Pallas kernels, call(): pl.pallas_call(kernel, out_shape=out_shapes, in_specs=specs, out_specs=ja...  61.7 us
    ppermute x30, starting transfers between devices, permute(): return lax.ppermute(value, AXES, pairs)  52 us
    ppermute x30, waiting for transfers between devices, permute(): return lax.ppermute(value, AXES, pairs)  41.9 us
  transfers between devices with their start and end apart: 30, of which 8 were waited for; matrix products, arithmetic and copies ran while one was open for 0% of the time, Pallas kernels for 37%

profile of v9, /device:TPU:3, one launch (start us, length us, event | category | flops | bytes accessed | tf_op | source)
XLA Modules:
  0.0 156.5 jit_solution(10893233656298273236)
XLA Ops:
  0.0 2.1 %shard_map.91 = (f32[1160,128]{1,0:T(8,128)}, f32[8,128]{1,0:T(8,128)}) custom-call(s32[4]{0:T(128)} %live_ref.1, s32[4]{0:T(128)} %parent_ref.1, s32[4]{0:T(128)} %mode_ref.1, f32[4]{0:T(128)} %damping_ref.1, f32[4]{0:T(128)} %weight_ref.1, f32[2,2]{1,0:T(2,128)} %corr_ref.1, f32[1024,128]{1,0:T(8,128)} %bitcast.6, f32[256,128]{1,0:T(8,128)} %bitcast.3), custom_call_target="tpu_custom_call" | custom-call | flops 1100000000 | bytes 524288 | tf_op jit(solution)/shard_map/pallas_call | solution.py:500
  2.1 4.2 %collective-permute-start.1 = (f32[1160,128]{1,0:T(8,128)}, f32[1160,128]{1,0:T(8,128)S(1)}, u32[]{:S(2)}, u32[]{:S(2)}) collective-permute-start(f32[1160,128]{1,0:T(8,128)} %get-tuple-element.31.refs_0_.states_ref), channel_id=1, source_target_pairs={{4,6},{5,7},{6,4},{7,5},{12,14},{13,15},{14,12},{15,13},{20,22},{2... | collective-permute-start | bytes 1781768 | tf_op jit(solution)/shard_map/ppermute | solution.py:529
  6.3 3.2 %collective-permute-start = (f32[1160,128]{1,0:T(8,128)}, f32[1160,128]{1,0:T(8,128)S(1)}, u32[]{:S(2)}, u32[]{:S(2)}) collective-permute-start(f32[1160,128]{1,0:T(8,128)} %get-tuple-element.31.refs_0_.states_ref), channel_id=1, source_target_pairs={{4,5},{5,4},{6,7},{7,6},{12,13},{13,12},{14,15},{15,14},{20,21},{2... | collective-permute-start | bytes 1781768 | tf_op jit(solution)/shard_map/ppermute | solution.py:529
  9.5 2.1 %collective-permute-start.4 = (f32[8,128]{1,0:T(8,128)}, f32[8,128]{1,0:T(8,128)S(1)}, u32[]{:S(2)}, u32[]{:S(2)}) collective-permute-start(f32[8,128]{1,0:T(8,128)} %get-tuple-element.30.own_ref), channel_id=1, source_target_pairs={{4,0},{5,1},{6,2},{7,3},{8,4},{9,5},{10,6},{11,7},{12,8},{13,9},{1... | collective-permute-start | bytes 12296 | tf_op jit(solution)/shard_map/ppermute | solution.py:529
  11.6 0.7 shard_map.93
  12.3 4.2 %shard_map.100.refs_1_ = f32[512,128]{1,0:T(8,128)S(1)} custom-call(f32[1160,128]{1,0:T(8,128)S(1)} %copy-done, bf16[384,512]{1,0:T(8,128)(2,1)S(1)} %get-tuple-element.34.right_ref, bf16[128,1536]{1,0:T(8,128)(2,1)S(1)} %get-tuple-element.35.left_ref), custom_call_target="tpu_custom_call" | custom-call | flops 4950000128 | bytes 524288 | tf_op jit(solution)/shard_map/pallas_call | solution.py:500
  16.5 4.2 %shard_map.101.refs_2_ = f32[512,128]{1,0:T(8,128)S(1)} custom-call(f32[1160,128]{1,0:T(8,128)S(1)} %copy-done, bf16[384,512]{1,0:T(8,128)(2,1)S(1)} %get-tuple-element.34.right_ref, bf16[128,1536]{1,0:T(8,128)(2,1)S(1)} %get-tuple-element.35.left_ref), custom_call_target="tpu_custom_call" | custom-call | flops 4950000128 | bytes 524288 | tf_op jit(solution)/shard_map/pallas_call | solution.py:500
  20.7 0.0 collective-permute-done.1.refs_2_.states_ref
  20.7 2.2 %collective-permute-start.2 = (f32[1160,128]{1,0:T(8,128)S(1)}, f32[1160,128]{1,0:T(8,128)S(1)}, u32[]{:S(2)}, u32[]{:S(2)}) collective-permute-start(f32[1160,128]{1,0:T(8,128)S(1)} %collective-permute-done.1.refs_2_.states_ref), channel_id=1, source_target_pairs={{4,5},{5,4},{6,7},{7,6},{12,13},{13,12},{14,15},{15,14},{20,21},{2... | collective-permute-start | bytes 1781768 | tf_op jit(solution)/shard_map/ppermute | solution.py:529
  22.9 4.2 %shard_map.104.refs_5_ = f32[512,128]{1,0:T(8,128)S(1)} custom-call(f32[1160,128]{1,0:T(8,128)S(1)} %collective-permute-done.1.refs_2_.states_ref, bf16[384,512]{1,0:T(8,128)(2,1)S(1)} %get-tuple-element.34.right_ref, bf16[128,1536]{1,0:T(8,128)(2,1)S(1)} %get-tuple-element.35.left_ref), custom_call_target="tpu_custom_call" | custom-call | flops 4950000128 | bytes 524288 | tf_op jit(solution)/shard_map/pallas_call | solution.py:500
  27.1 4.2 %shard_map.105.refs_6_ = f32[512,128]{1,0:T(8,128)S(1)} custom-call(f32[1160,128]{1,0:T(8,128)S(1)} %collective-permute-done.1.refs_2_.states_ref, bf16[384,512]{1,0:T(8,128)(2,1)S(1)} %get-tuple-element.34.right_ref, bf16[128,1536]{1,0:T(8,128)(2,1)S(1)} %get-tuple-element.35.left_ref), custom_call_target="tpu_custom_call" | custom-call | flops 4950000128 | bytes 524288 | tf_op jit(solution)/shard_map/pallas_call | solution.py:500
  31.3 0.0 copy-start.1
  31.3 4.2 %shard_map.102.refs_3_ = f32[512,128]{1,0:T(8,128)S(1)} custom-call(f32[1160,128]{1,0:T(8,128)S(1)} %collective-permute-done.refs_1_.states_ref, bf16[384,512]{1,0:T(8,128)(2,1)S(1)} %get-tuple-element.34.right_ref, bf16[128,1536]{1,0:T(8,128)(2,1)S(1)} %get-tuple-element.35.left_ref), custom_call_target="tpu_custom_call" | custom-call | flops 4950000128 | bytes 524288 | tf_op jit(solution)/shard_map/pallas_call | solution.py:500
  35.5 0.0 collective-permute-done.2.refs_3_.states_ref
  35.6 0.2 shard_map.92
  35.8 2.6 %shard_map.95 = (f32[1024,128]{1,0:T(8,128)S(1)}, f32[4,8,128]{2,1,0:T(8,128)S(1)}) custom-call(bf16[8,384,128]{2,1,0:T(8,128)(2,1)S(1)} %get-tuple-element.32.right_ref, bf16[8,128,384]{2,1,0:T(8,128)(2,1)S(1)} %get-tuple-element.33.left_ref, f32[1160,128]{1,0:T(8,128)S(1)} %copy-done, f32[1160,128]{1,0:T(8,128)S(1)} %collective-permute-done.refs_1_.states_ref, ...), custom_call_target="tpu_custom_call" | custom-call | flops 2200000000 | bytes 524288 | tf_op jit(solution)/shard_map/pallas_call | solution.py:500
  38.4 1.3 collective-permute-start.3
  39.8 0.8 shard_map.96
  40.6 1.3 collective-permute-start.5
  41.9 0.0 copy-start.3
  41.9 1.3 collective-permute-start.6
  43.2 4.2 %shard_map.103.refs_4_ = f32[512,128]{1,0:T(8,128)S(1)} custom-call(f32[1160,128]{1,0:T(8,128)S(1)} %collective-permute-done.refs_1_.states_ref, bf16[384,512]{1,0:T(8,128)(2,1)S(1)} %get-tuple-element.34.right_ref, bf16[128,1536]{1,0:T(8,128)(2,1)S(1)} %get-tuple-element.35.left_ref), custom_call_target="tpu_custom_call" | custom-call | flops 4950000128 | bytes 524288 | tf_op jit(solution)/shard_map/pallas_call | solution.py:500
  47.4 1.3 collective-permute-start.18
  48.7 0.0 collective-permute-done.5.refs_2_
  48.8 0.7 collective-permute-start.8
  49.5 4.2 %shard_map.106.refs_7_ = f32[512,128]{1,0:T(8,128)S(1)} custom-call(f32[1160,128]{1,0:T(8,128)S(1)} %collective-permute-done.2.refs_3_.states_ref, bf16[384,512]{1,0:T(8,128)(2,1)S(1)} %get-tuple-element.34.right_ref, bf16[128,1536]{1,0:T(8,128)(2,1)S(1)} %get-tuple-element.35.left_ref), custom_call_target="tpu_custom_call" | custom-call | flops 4950000128 | bytes 524288 | tf_op jit(solution)/shard_map/pallas_call | solution.py:500
  53.7 4.2 %shard_map.107.refs_8_ = f32[512,128]{1,0:T(8,128)S(1)} custom-call(f32[1160,128]{1,0:T(8,128)S(1)} %collective-permute-done.2.refs_3_.states_ref, bf16[384,512]{1,0:T(8,128)(2,1)S(1)} %get-tuple-element.34.right_ref, bf16[128,1536]{1,0:T(8,128)(2,1)S(1)} %get-tuple-element.35.left_ref), custom_call_target="tpu_custom_call" | custom-call | flops 4950000128 | bytes 524288 | tf_op jit(solution)/shard_map/pallas_call | solution.py:500
  57.9 1.3 collective-permute-start.7
  59.2 0.7 collective-permute-start.11
  59.9 0.7 collective-permute-start.14
  60.6 1.3 collective-permute-start.10
  61.9 1.5 collective-permute-start.9
  63.5 5.9 %collective-permute-done.7.refs_0_ = f32[1032,128]{1,0:T(8,128)S(1)} collective-permute-done((f32[1032,128]{1,0:T(8,128)S(1)}, f32[1032,128]{1,0:T(8,128)S(1)}, u32[]{:S(2)}, u32[]{:S(2)}) %collective-permute-start.7) | collective-permute-done | bytes 528416 | tf_op jit(solution)/shard_map/ppermute | solution.py:529
  69.3 1.3 collective-permute-start.13
  70.6 1.3 collective-permute-start.12
  71.9 1.3 collective-permute-start.15
  73.3 1.3 collective-permute-start.16
  74.6 7.4 %collective-permute-done.9.refs_1_ = f32[1032,128]{1,0:T(8,128)S(1)} collective-permute-done((f32[1032,128]{1,0:T(8,128)S(1)}, f32[1032,128]{1,0:T(8,128)S(1)}, u32[]{:S(2)}, u32[]{:S(2)}) %collective-permute-start.9) | collective-permute-done | bytes 528416 | tf_op jit(solution)/shard_map/ppermute | solution.py:529
  82.0 1.3 collective-permute-start.17
  83.3 3.0 %shard_map.98 = (f32[4096,128]{1,0:T(8,128)S(1)}, f32[4,8,128]{2,1,0:T(8,128)}) custom-call(bf16[8,384,128]{2,1,0:T(8,128)(2,1)S(1)} %get-tuple-element.32.right_ref, bf16[8,128,384]{2,1,0:T(8,128)(2,1)S(1)} %get-tuple-element.33.left_ref, f32[1032,128]{1,0:T(8,128)S(1)} %collective-permute-done.7.refs_0_, f32[1032,128]{1,0:T(8,128)S(1)} %collective-permute-done.9.refs_1_, ...), custom_call_target="tpu_custom_call" | custom-call | flops 3300000000 | bytes 524288 | tf_op jit(solution)/shard_map/pallas_call | solution.py:500
  86.2 0.7 collective-permute-start.22
  87.0 4.4 %shard_map.99 = (f32[4096,128]{1,0:T(8,128)S(1)}, f32[4,8,128]{2,1,0:T(8,128)}) custom-call(bf16[8,384,128]{2,1,0:T(8,128)(2,1)S(1)} %get-tuple-element.32.right_ref, bf16[8,128,384]{2,1,0:T(8,128)(2,1)S(1)} %get-tuple-element.33.left_ref, f32[4096,128]{1,0:T(8,128)S(1)} %get-tuple-element.40.refs_0_, f32[1032,128]{1,0:T(8,128)S(1)} %collective-permute-done.10.refs_1_, ...), custom_call_target="tpu_custom_call" | custom-call | flops 3300000000 | bytes 524288 | tf_op jit(solution)/shard_map/pallas_call | solution.py:500
  91.4 4.6 %collective-permute-done.16.refs_9_ = f32[1032,128]{1,0:T(8,128)S(1)} collective-permute-done((f32[1032,128]{1,0:T(8,128)S(1)}, f32[1032,128]{1,0:T(8,128)S(1)}, u32[]{:S(2)}, u32[]{:S(2)}) %collective-permute-start.16) | collective-permute-done | bytes 528416 | tf_op jit(solution)/shard_map/ppermute | solution.py:529
  95.9 5.7 %collective-permute-done.17.refs_10_ = f32[1032,128]{1,0:T(8,128)S(1)} collective-permute-done((f32[1032,128]{1,0:T(8,128)S(1)}, f32[1032,128]{1,0:T(8,128)S(1)}, u32[]{:S(2)}, u32[]{:S(2)}) %collective-permute-start.17) | collective-permute-done | bytes 528416 | tf_op jit(solution)/shard_map/ppermute | solution.py:529
  101.6 2.7 %shard_map.108 = (f32[1032,128]{1,0:T(8,128)S(1)}, f32[2064,128]{1,0:T(8,128)S(1)}, f32[1032,128]{1,0:T(8,128)S(1)}) custom-call(bf16[8,384,128]{2,1,0:T(8,128)(2,1)S(1)} %get-tuple-element.32.right_ref, bf16[8,128,384]{2,1,0:T(8,128)(2,1)S(1)} %get-tuple-element.33.left_ref, f32[4096,128]{1,0:T(8,128)S(1)} %get-tuple-element.41.refs_0_, ...), custom_call_target="tpu_custom_call" | custom-call | flops 3300000000 | bytes 524288 | tf_op jit(solution)/shard_map/pallas_call | solution.py:500
  104.3 1.3 collective-permute-start.19
  105.6 1.3 collective-permute-start.24
  106.9 1.3 collective-permute-start.21
  108.3 1.4 collective-permute-start.20
  109.7 0.7 collective-permute-start.23
  110.4 11.3 %collective-permute-start.25 = (f32[2064,128]{1,0:T(8,128)S(1)}, f32[2064,128]{1,0:T(8,128)S(1)}, u32[]{:S(2)}, u32[]{:S(2)}) collective-permute-start(f32[2064,128]{1,0:T(8,128)S(1)} %get-tuple-element.46), channel_id=1, source_target_pairs={{4,8},{5,9},{6,10},{7,11},{12,16},{13,17},{14,18},{15,19},{20,24},... | collective-permute-start | bytes 3170312 | tf_op jit(solution)/shard_map/ppermute | solution.py:529
  121.7 0.7 collective-permute-start.26
  122.4 8.2 %shard_map.109.refs_0_ = f32[1024,128]{1,0:T(8,128)S(1)} custom-call(f32[1032,128]{1,0:T(8,128)S(1)} %get-tuple-element.42.states_ref, bf16[384,512]{1,0:T(8,128)(2,1)S(1)} %get-tuple-element.34.right_ref, bf16[128,1536]{1,0:T(8,128)(2,1)S(1)} %get-tuple-element.35.left_ref), custom_call_target="tpu_custom_call" | custom-call | flops 9900000256 | bytes 524288 | tf_op jit(solution)/shard_map/pallas_call | solution.py:500
  130.6 0.1 shard_map.111
  130.7 2.7 %collective-permute-done.25.refs_6_ = f32[2064,128]{1,0:T(8,128)S(1)} collective-permute-done((f32[2064,128]{1,0:T(8,128)S(1)}, f32[2064,128]{1,0:T(8,128)S(1)}, u32[]{:S(2)}, u32[]{:S(2)}) %collective-permute-start.25) | collective-permute-done | bytes 1056800 | tf_op jit(solution)/shard_map/ppermute | solution.py:529
  133.5 1.3 collective-permute-start.27
  134.8 0.7 shard_map.120
  135.5 1.3 collective-permute-start.28
  136.8 1.3 collective-permute-start.29
  138.1 4.5 %collective-permute-done.27.refs_1_ = f32[1024,128]{1,0:T(8,128)S(1)} collective-permute-done((f32[1024,128]{1,0:T(8,128)S(1)}, f32[1024,128]{1,0:T(8,128)S(1)}, u32[]{:S(2)}, u32[]{:S(2)}) %collective-permute-start.27) | collective-permute-done | bytes 524320 | tf_op jit(solution)/shard_map/ppermute | solution.py:529
  142.6 1.1 shard_map.118.refs_0_
  143.7 8.4 %collective-permute-done.28.refs_2_ = f32[512,128]{1,0:T(8,128)S(1)} collective-permute-done((f32[512,128]{1,0:T(8,128)S(1)}, f32[512,128]{1,0:T(8,128)S(1)}, u32[]{:S(2)}, u32[]{:S(2)}) %collective-permute-start.28) | collective-permute-done | bytes 262176 | tf_op jit(solution)/shard_map/ppermute | solution.py:529
  152.1 2.8 %collective-permute-done.29.refs_3_ = f32[512,128]{1,0:T(8,128)S(1)} collective-permute-done((f32[512,128]{1,0:T(8,128)S(1)}, f32[512,128]{1,0:T(8,128)S(1)}, u32[]{:S(2)}, u32[]{:S(2)}) %collective-permute-start.29) | collective-permute-done | bytes 262176 | tf_op jit(solution)/shard_map/ppermute | solution.py:529
  154.9 1.5 shard_map.121
  (35 shorter events, 0.3 us)
Async XLA Ops:
  0.0 11.6 %copy-start.2 = (f32[128,128]{1,0:T(8,128)S(1)}, f32[128,128]{1,0:T(8,128)}, u32[]{:S(2)}) copy-start(f32[128,128]{1,0:T(8,128)} %ham_ref.1) | copy-start | bytes 196612
  2.1 18.7 %collective-permute-start.1 = (f32[1160,128]{1,0:T(8,128)}, f32[1160,128]{1,0:T(8,128)S(1)}, u32[]{:S(2)}, u32[]{:S(2)}) collective-permute-start(f32[1160,128]{1,0:T(8,128)} %get-tuple-element.31.refs_0_.states_ref), channel_id=1, source_target_pairs={{4,6},{5,7},{6,4},{7,5},{12,14},{13,15},{14,12},{15,13},{20,22},{2... | collective-permute-start | bytes 1781768 | tf_op jit(solution)/shard_map/ppermute | solution.py:529
  6.3 25.1 %collective-permute-start = (f32[1160,128]{1,0:T(8,128)}, f32[1160,128]{1,0:T(8,128)S(1)}, u32[]{:S(2)}, u32[]{:S(2)}) collective-permute-start(f32[1160,128]{1,0:T(8,128)} %get-tuple-element.31.refs_0_.states_ref), channel_id=1, source_target_pairs={{4,5},{5,4},{6,7},{7,6},{12,13},{13,12},{14,15},{15,14},{20,21},{2... | collective-permute-start | bytes 1781768 | tf_op jit(solution)/shard_map/ppermute | solution.py:529
  9.5 2.8 %copy-start = (f32[1160,128]{1,0:T(8,128)S(1)}, f32[1160,128]{1,0:T(8,128)}, u32[]{:S(2)}) copy-start(f32[1160,128]{1,0:T(8,128)} %get-tuple-element.31.refs_0_.states_ref) | copy-start | bytes 1781764
  9.5 30.3 %collective-permute-start.4 = (f32[8,128]{1,0:T(8,128)}, f32[8,128]{1,0:T(8,128)S(1)}, u32[]{:S(2)}, u32[]{:S(2)}) collective-permute-start(f32[8,128]{1,0:T(8,128)} %get-tuple-element.30.own_ref), channel_id=1, source_target_pairs={{4,0},{5,1},{6,2},{7,3},{8,4},{9,5},{10,6},{11,7},{12,8},{13,9},{1... | collective-permute-start | bytes 12296 | tf_op jit(solution)/shard_map/ppermute | solution.py:529
  20.7 14.8 %collective-permute-start.2 = (f32[1160,128]{1,0:T(8,128)S(1)}, f32[1160,128]{1,0:T(8,128)S(1)}, u32[]{:S(2)}, u32[]{:S(2)}) collective-permute-start(f32[1160,128]{1,0:T(8,128)S(1)} %collective-permute-done.1.refs_2_.states_ref), channel_id=1, source_target_pairs={{4,5},{5,4},{6,7},{7,6},{12,13},{13,12},{14,15},{15,14},{20,21},{2... | collective-permute-start | bytes 1781768 | tf_op jit(solution)/shard_map/ppermute | solution.py:529
  31.3 4.2 %copy-start.1 = (f32[2,128,128]{2,1,0:T(8,128)S(1)}, f32[2,128,128]{2,1,0:T(8,128)}, u32[]{:S(2)}) copy-start(f32[2,128,128]{2,1,0:T(8,128)} %param.14) | copy-start | bytes 393220
  38.4 10.3 %collective-permute-start.3 = (f32[1024,128]{1,0:T(8,128)S(1)}, f32[1024,128]{1,0:T(8,128)S(1)}, u32[]{:S(2)}, u32[]{:S(2)}) collective-permute-start(f32[1024,128]{1,0:T(8,128)S(1)} %get-tuple-element.36), channel_id=1, source_target_pairs={{4,0},{5,1},{6,2},{7,3},{12,8},{13,9},{14,10},{15,11},{20,16},{21,... | collective-permute-start | bytes 1572872 | tf_op jit(solution)/shard_map/ppermute | solution.py:529
  40.6 8.2 %collective-permute-start.5 = (f32[512,128]{1,0:T(8,128)S(1)}, f32[512,128]{1,0:T(8,128)S(1)}, u32[]{:S(2)}, u32[]{:S(2)}) collective-permute-start(f32[512,128]{1,0:T(8,128)S(1)} %get-tuple-element.37), channel_id=1, source_target_pairs={{4,8},{5,9},{6,10},{7,11},{12,16},{13,17},{14,18},{15,19},{20,24},... | collective-permute-start | bytes 786440 | tf_op jit(solution)/shard_map/ppermute | solution.py:529
  41.9 6.9 %copy-start.3 = (f32[8,128]{1,0:T(8,128)S(1)}, f32[8,128]{1,0:T(8,128)}, u32[]{:S(2)}) copy-start(f32[8,128]{1,0:T(8,128)} %get-tuple-element.30.own_ref) | copy-start | bytes 12292
  41.9 6.8 %collective-permute-start.6 = (f32[512,128]{1,0:T(8,128)S(1)}, f32[512,128]{1,0:T(8,128)S(1)}, u32[]{:S(2)}, u32[]{:S(2)}) collective-permute-start(f32[512,128]{1,0:T(8,128)S(1)} %get-tuple-element.38), channel_id=1, source_target_pairs={{4,8},{5,9},{6,10},{7,11},{12,16},{13,17},{14,18},{15,19},{20,24},... | collective-permute-start | bytes 786440 | tf_op jit(solution)/shard_map/ppermute | solution.py:529
  47.4 13.2 %collective-permute-start.18 = (f32[408,128]{1,0:T(8,128)S(1)}, f32[408,128]{1,0:T(8,128)S(1)}, u32[]{:S(2)}, u32[]{:S(2)}) collective-permute-start(f32[408,128]{1,0:T(8,128)S(1)} %get-tuple-element.43), channel_id=1, source_target_pairs={{4,0},{5,1},{6,2},{7,3},{12,8},{13,9},{14,10},{15,11},{20,16},{21,... | collective-permute-start | bytes 626696 | tf_op jit(solution)/shard_map/ppermute | solution.py:529
  48.8 11.1 %collective-permute-start.8 = (f32[1032,128]{1,0:T(8,128)S(1)}, f32[1032,128]{1,0:T(8,128)S(1)}, u32[]{:S(2)}, u32[]{:S(2)}) collective-permute-start(f32[1032,128]{1,0:T(8,128)S(1)} %shard_map.97.refs_3_.states_ref), channel_id=1, source_target_pairs={{0,2},{1,3},{2,0},{3,1},{8,10},{9,11},{10,8},{11,9},{16,18},{17,19... | collective-permute-start | bytes 1585160 | tf_op jit(solution)/shard_map/ppermute | solution.py:529
  57.9 11.4 %collective-permute-start.7 = (f32[1032,128]{1,0:T(8,128)S(1)}, f32[1032,128]{1,0:T(8,128)S(1)}, u32[]{:S(2)}, u32[]{:S(2)}) collective-permute-start(f32[1032,128]{1,0:T(8,128)S(1)} %shard_map.97.refs_3_.states_ref), channel_id=1, source_target_pairs={{8,4},{9,5},{10,6},{11,7},{16,12},{17,13},{18,14},{19,15},{24,20},... | collective-permute-start | bytes 1585160 | tf_op jit(solution)/shard_map/ppermute | solution.py:529
  59.2 11.4 %collective-permute-start.11 = (f32[1032,128]{1,0:T(8,128)S(1)}, f32[1032,128]{1,0:T(8,128)S(1)}, u32[]{:S(2)}, u32[]{:S(2)}) collective-permute-start(f32[1032,128]{1,0:T(8,128)S(1)} %shard_map.97.refs_3_.states_ref), channel_id=1, source_target_pairs={{0,1},{1,0},{2,3},{3,2},{8,9},{9,8},{10,11},{11,10},{16,17},{17,16... | collective-permute-start | bytes 1585160 | tf_op jit(solution)/shard_map/ppermute | solution.py:529
  59.9 12.0 %collective-permute-start.14 = (f32[1032,128]{1,0:T(8,128)S(1)}, f32[1032,128]{1,0:T(8,128)S(1)}, u32[]{:S(2)}, u32[]{:S(2)}) collective-permute-start(f32[1032,128]{1,0:T(8,128)S(1)} %collective-permute-done.8.refs_5_), channel_id=1, source_target_pairs={{0,1},{1,0},{2,3},{3,2},{8,9},{9,8},{10,11},{11,10},{16,17},{17,16... | collective-permute-start | bytes 1585160 | tf_op jit(solution)/shard_map/ppermute | solution.py:529
  60.6 12.6 %collective-permute-start.10 = (f32[1032,128]{1,0:T(8,128)S(1)}, f32[1032,128]{1,0:T(8,128)S(1)}, u32[]{:S(2)}, u32[]{:S(2)}) collective-permute-start(f32[1032,128]{1,0:T(8,128)S(1)} %shard_map.97.refs_3_.states_ref), channel_id=1, source_target_pairs={{0,4},{1,5},{2,6},{3,7},{8,12},{9,13},{10,14},{11,15},{16,20},{17,... | collective-permute-start | bytes 1585160 | tf_op jit(solution)/shard_map/ppermute | solution.py:529
  61.9 20.0 %collective-permute-start.9 = (f32[1032,128]{1,0:T(8,128)S(1)}, f32[1032,128]{1,0:T(8,128)S(1)}, u32[]{:S(2)}, u32[]{:S(2)}) collective-permute-start(f32[1032,128]{1,0:T(8,128)S(1)} %collective-permute-done.8.refs_5_), channel_id=1, source_target_pairs={{8,4},{9,5},{10,6},{11,7},{16,12},{17,13},{18,14},{19,15},{24,20},... | collective-permute-start | bytes 1585160 | tf_op jit(solution)/shard_map/ppermute | solution.py:529
  69.3 17.6 %collective-permute-start.13 = (f32[1032,128]{1,0:T(8,128)S(1)}, f32[1032,128]{1,0:T(8,128)S(1)}, u32[]{:S(2)}, u32[]{:S(2)}) collective-permute-start(f32[1032,128]{1,0:T(8,128)S(1)} %collective-permute-done.8.refs_5_), channel_id=1, source_target_pairs={{0,4},{1,5},{2,6},{3,7},{8,12},{9,13},{10,14},{11,15},{16,20},{17,... | collective-permute-start | bytes 1585160 | tf_op jit(solution)/shard_map/ppermute | solution.py:529
  70.6 15.6 %collective-permute-start.12 = (f32[1032,128]{1,0:T(8,128)S(1)}, f32[1032,128]{1,0:T(8,128)S(1)}, u32[]{:S(2)}, u32[]{:S(2)}) collective-permute-start(f32[1032,128]{1,0:T(8,128)S(1)} %collective-permute-done.11.refs_4_), channel_id=1, source_target_pairs={{0,4},{1,5},{2,6},{3,7},{8,12},{9,13},{10,14},{11,15},{16,20},{17,... | collective-permute-start | bytes 1585160 | tf_op jit(solution)/shard_map/ppermute | solution.py:529
  71.9 15.0 %collective-permute-start.15 = (f32[1032,128]{1,0:T(8,128)S(1)}, f32[1032,128]{1,0:T(8,128)S(1)}, u32[]{:S(2)}, u32[]{:S(2)}) collective-permute-start(f32[1032,128]{1,0:T(8,128)S(1)} %collective-permute-done.14.refs_6_.states_ref), channel_id=1, source_target_pairs={{0,4},{1,5},{2,6},{3,7},{8,12},{9,13},{10,14},{11,15},{16,20},{17,... | collective-permute-start | bytes 1585160 | tf_op jit(solution)/shard_map/ppermute | solution.py:529
  73.3 22.7 %collective-permute-start.16 = (f32[1032,128]{1,0:T(8,128)S(1)}, f32[1032,128]{1,0:T(8,128)S(1)}, u32[]{:S(2)}, u32[]{:S(2)}) collective-permute-start(f32[1032,128]{1,0:T(8,128)S(1)} %collective-permute-done.11.refs_4_), channel_id=1, source_target_pairs={{8,4},{9,5},{10,6},{11,7},{16,12},{17,13},{18,14},{19,15},{24,20},... | collective-permute-start | bytes 1585160 | tf_op jit(solution)/shard_map/ppermute | solution.py:529
  82.0 19.6 %collective-permute-start.17 = (f32[1032,128]{1,0:T(8,128)S(1)}, f32[1032,128]{1,0:T(8,128)S(1)}, u32[]{:S(2)}, u32[]{:S(2)}) collective-permute-start(f32[1032,128]{1,0:T(8,128)S(1)} %collective-permute-done.14.refs_6_.states_ref), channel_id=1, source_target_pairs={{8,4},{9,5},{10,6},{11,7},{16,12},{17,13},{18,14},{19,15},{24,20},... | collective-permute-start | bytes 1585160 | tf_op jit(solution)/shard_map/ppermute | solution.py:529
  86.2 44.5 %collective-permute-start.22 = (f32[1024,128]{1,0:T(8,128)S(1)}, f32[1024,128]{1,0:T(8,128)S(1)}, u32[]{:S(2)}, u32[]{:S(2)}) collective-permute-start(f32[1024,128]{1,0:T(8,128)S(1)} %shard_map.113.refs_1_), channel_id=1, source_target_pairs={{0,1},{1,0},{2,3},{3,2},{8,9},{9,8},{10,11},{11,10},{16,17},{17,16... | collective-permute-start | bytes 1572872 | tf_op jit(solution)/shard_map/ppermute | solution.py:529
  104.3 5.4 %collective-permute-start.19 = (f32[1032,128]{1,0:T(8,128)S(1)}, f32[1032,128]{1,0:T(8,128)S(1)}, u32[]{:S(2)}, u32[]{:S(2)}) collective-permute-start(f32[1032,128]{1,0:T(8,128)S(1)} %get-tuple-element.42.states_ref), channel_id=1, source_target_pairs={{4,0},{5,1},{6,2},{7,3},{12,8},{13,9},{14,10},{15,11},{20,16},{21,... | collective-permute-start | bytes 1585160 | tf_op jit(solution)/shard_map/ppermute | solution.py:529
  105.6 16.1 %collective-permute-start.24 = (f32[1032,128]{1,0:T(8,128)S(1)}, f32[1032,128]{1,0:T(8,128)S(1)}, u32[]{:S(2)}, u32[]{:S(2)}) collective-permute-start(f32[1032,128]{1,0:T(8,128)S(1)} %get-tuple-element.42.states_ref), channel_id=1, source_target_pairs={{4,8},{5,9},{6,10},{7,11},{12,16},{13,17},{14,18},{15,19},{20,24},... | collective-permute-start | bytes 1585160 | tf_op jit(solution)/shard_map/ppermute | solution.py:529
  106.9 3.5 %collective-permute-start.21 = (f32[1032,128]{1,0:T(8,128)S(1)}, f32[1032,128]{1,0:T(8,128)S(1)}, u32[]{:S(2)}, u32[]{:S(2)}) collective-permute-start(f32[1032,128]{1,0:T(8,128)S(1)} %get-tuple-element.47), channel_id=1, source_target_pairs={{4,0},{5,1},{6,2},{7,3},{12,8},{13,9},{14,10},{15,11},{20,16},{21,... | collective-permute-start | bytes 1585160 | tf_op jit(solution)/shard_map/ppermute | solution.py:529
  108.3 22.3 %collective-permute-start.20 = (f32[2064,128]{1,0:T(8,128)S(1)}, f32[2064,128]{1,0:T(8,128)S(1)}, u32[]{:S(2)}, u32[]{:S(2)}) collective-permute-start(f32[2064,128]{1,0:T(8,128)S(1)} %get-tuple-element.46), channel_id=1, source_target_pairs={{4,0},{5,1},{6,2},{7,3},{12,8},{13,9},{14,10},{15,11},{20,16},{21,... | collective-permute-start | bytes 3170312 | tf_op jit(solution)/shard_map/ppermute | solution.py:529
  109.7 21.0 %collective-permute-start.23 = (f32[1024,128]{1,0:T(8,128)S(1)}, f32[1024,128]{1,0:T(8,128)S(1)}, u32[]{:S(2)}, u32[]{:S(2)}) collective-permute-start(f32[1024,128]{1,0:T(8,128)S(1)} %shard_map.113.refs_1_), channel_id=1, source_target_pairs={{0,2},{1,3},{2,0},{3,1},{8,10},{9,11},{10,8},{11,9},{16,18},{17,19... | collective-permute-start | bytes 1572872 | tf_op jit(solution)/shard_map/ppermute | solution.py:529
  110.4 23.0 %collective-permute-start.25 = (f32[2064,128]{1,0:T(8,128)S(1)}, f32[2064,128]{1,0:T(8,128)S(1)}, u32[]{:S(2)}, u32[]{:S(2)}) collective-permute-start(f32[2064,128]{1,0:T(8,128)S(1)} %get-tuple-element.46), channel_id=1, source_target_pairs={{4,8},{5,9},{6,10},{7,11},{12,16},{13,17},{14,18},{15,19},{20,24},... | collective-permute-start | bytes 3170312 | tf_op jit(solution)/shard_map/ppermute | solution.py:529
  121.7 9.0 %collective-permute-start.26 = (f32[1032,128]{1,0:T(8,128)S(1)}, f32[1032,128]{1,0:T(8,128)S(1)}, u32[]{:S(2)}, u32[]{:S(2)}) collective-permute-start(f32[1032,128]{1,0:T(8,128)S(1)} %collective-permute-done.24.refs_5_), channel_id=1, source_target_pairs={{0,1},{1,0},{2,3},{3,2},{8,9},{9,8},{10,11},{11,10},{16,17},{17,16... | collective-permute-start | bytes 1585160 | tf_op jit(solution)/shard_map/ppermute | solution.py:529
  133.5 9.1 %collective-permute-start.27 = (f32[1024,128]{1,0:T(8,128)S(1)}, f32[1024,128]{1,0:T(8,128)S(1)}, u32[]{:S(2)}, u32[]{:S(2)}) collective-permute-start(f32[1024,128]{1,0:T(8,128)S(1)} %shard_map.117), channel_id=1, source_target_pairs={{0,4},{1,5},{2,6},{3,7},{8,12},{9,13},{10,14},{11,15},{16,20},{17,... | collective-permute-start | bytes 1572872 | tf_op jit(solution)/shard_map/ppermute | solution.py:529
  135.5 16.6 %collective-permute-start.28 = (f32[512,128]{1,0:T(8,128)S(1)}, f32[512,128]{1,0:T(8,128)S(1)}, u32[]{:S(2)}, u32[]{:S(2)}) collective-permute-start(f32[512,128]{1,0:T(8,128)S(1)} %get-tuple-element.53), channel_id=1, source_target_pairs={{8,4},{9,5},{10,6},{11,7},{16,12},{17,13},{18,14},{19,15},{24,20},... | collective-permute-start | bytes 786440 | tf_op jit(solution)/shard_map/ppermute | solution.py:529
  136.8 18.1 %collective-permute-start.29 = (f32[512,128]{1,0:T(8,128)S(1)}, f32[512,128]{1,0:T(8,128)S(1)}, u32[]{:S(2)}, u32[]{:S(2)}) collective-permute-start(f32[512,128]{1,0:T(8,128)S(1)} %get-tuple-element.54), channel_id=1, source_target_pairs={{8,4},{9,5},{10,6},{11,7},{16,12},{17,13},{18,14},{19,15},{24,20},... | collective-permute-start | bytes 786440 | tf_op jit(solution)/shard_map/ppermute | solution.py:529
